TPU v7x, 32 devices: a whole 2x2x4 slice. The times are simulated.
32 devices in a mesh: head: 4 (over y, x), blk: 8 (over z, core).
Axes of the slice: x: 2, y: 2, z: 4, core: 2. Of those that a mesh axis runs over, the one named last changes fastest.
Arguments:
- pre_tokens: bfloat16 [512, 2048], P('blk'), may hold values from -6 to 6
- dec_tokens: bfloat16 [12, 2048], replicated, may hold values from -6 to 6
- attn_gain: float32 [2048], replicated, may hold values from 0.25 to 1.75
- w_query: bfloat16 [2048, 2048], P(None, 'head'), may hold values from -0.125 to 0.125
- w_key: bfloat16 [2048, 2048], P(None, 'head'), may hold values from -0.125 to 0.125
- w_value: bfloat16 [2048, 2048], P(None, 'head'), may hold values from -0.125 to 0.125
- w_output: bfloat16 [2048, 2048], P('head'), may hold values from -0.125 to 0.125
- cache_keys: bfloat16 [64, 256, 2048], P('blk', None, 'head'), may hold values from -310 to 310
- cache_values: bfloat16 [64, 256, 2048], P('blk', None, 'head'), may hold values from -6 to 6
- block_request: int32 [64], P('blk'), may hold values from 0 to 13, as said below
- block_slot: int32 [64], P('blk'), may hold values from 0 to 15, as said below
- cache_lens: int32 [13], replicated, may hold values from 1 to 4096, as said below
- moe_gain: float32 [2048], replicated, may hold values from 0.25 to 1.75
- expert_ids: int32 [512, 8], P('blk'), may hold values from 0 to 15, all different within a row; in each aligned block of 64 rows (0 to 63, 64 to 127, ...) at most 64 rows name the same one
- expert_gates: bfloat16 [512, 8], P('blk'), may hold values from 0.049804688 to 0.29882812
- dec_expert_ids: int32 [12, 8], replicated, may hold values from 0 to 15, all different within a row
- dec_expert_gates: bfloat16 [12, 8], replicated, may hold values from 0.049804688 to 0.29882812
- w_gate: bfloat16 [16, 2048, 1024], P('blk', None, 'head'), may hold values from -0.125 to 0.125
- w_up: bfloat16 [16, 2048, 1024], P('blk', None, 'head'), may hold values from -0.125 to 0.125
- w_down: bfloat16 [16, 1024, 2048], P('blk', 'head'), may hold values from -0.1875 to 0.1875
Outputs:
- pre_hidden: bfloat16 [512, 2048], P('blk', 'head')
- dec_hidden: bfloat16 [12, 2048], P(None, 'head')
- new_cache: bfloat16 [2, 512, 2048], P(None, 'blk', 'head')
- dec_cache: bfloat16 [2, 12, 2048], P(None, None, 'head')
Inputs may be any that keep to these rules, and one draw needn't show every extreme that they name: `block_request`: 13 marks a free block; request r owns exactly one block for each slot below ceil(cache_lens[r] / 256) and no other. `block_slot`: a block holds positions slot * 256 to slot * 256 + 255 of its request; free blocks have slot 0. `cache_lens`: requests 0 to 0 are the prefill requests, whose new tokens follow their cached ones; one request has exactly 4096 cached tokens, the others at most 1024. `expert_ids`: each row names 8 different experts; among the 64 tokens of one index of blk (aligned blocks of rows) no expert is named more than 64 times. `dec_expert_ids`: each row names 8 different experts.
All inputs are finite; a program needn't handle non-finite values.
Results may differ from a plain program's by a relative error of at most 0.0065.
The roundings to bfloat16 on the way count: a program that leaves them out, or rounds other values in their place, can miss the bound.
Values may be sent and summed in bfloat16 or wider, within the bound.
No kernel may reach another device: no remote copies, remote signals or barrier semaphores. Data moves between devices by JAX's collectives and lax.ppermute only.
A program may use at most 128 MiB of HBM per device.

v0:
```python
import jax
import jax.numpy as jnp
from jax import lax
from jax.sharding import PartitionSpec as P

HD = 128
TOPK = 8
PRE = 1
DEC = 12
REQS = 13


eps_norm = 1e-06
rope_base = 50000.0
neg_fill = -1e30


def rms_scale(row_data, gain_vec):
    values = row_data.astype(jnp.float32)
    meansq = jnp.mean(values * values, axis=-1, keepdims=True)
    return values * lax.rsqrt(meansq + eps_norm) * gain_vec


def rotate(blocks, positions):
    half_dim = blocks.shape[-1] // 2
    frequencies = rope_base ** (-jnp.arange(half_dim, dtype=jnp.float32) / half_dim)
    angles = positions.astype(jnp.float32)[:, None] * frequencies[None, :]
    cosine = jnp.cos(angles)[:, None, :]
    sine_part = jnp.sin(angles)[:, None, :]
    first_half = blocks[..., :half_dim]
    second_half = blocks[..., half_dim:]
    return jnp.concatenate(
        [
            first_half * cosine - second_half * sine_part,
            second_half * cosine + first_half * sine_part,
        ],
        axis=-1,
    )


def project(normed, w_query, w_key, w_value, positions, head_dim):
    row_count = normed.shape[0]
    queries = jnp.dot(normed, w_query, preferred_element_type=jnp.float32).reshape(
        row_count, -1, head_dim
    )
    key_rows = jnp.dot(normed, w_key, preferred_element_type=jnp.float32).reshape(
        row_count, -1, head_dim
    )
    value_rows = jnp.dot(normed, w_value, preferred_element_type=jnp.float32)
    queries = rotate(queries, positions).reshape(row_count, -1).astype(jnp.bfloat16)
    key_rows = rotate(key_rows, positions).reshape(row_count, -1).astype(jnp.bfloat16)
    return (queries, key_rows, value_rows.astype(jnp.bfloat16))


def group_stats(queries, key_rows, value_rows, live_mask, head_dim):
    row_count = queries.shape[0]
    q_heads = queries.reshape(row_count, -1, head_dim)
    k_heads = key_rows.reshape(key_rows.shape[0], -1, head_dim)
    v_heads = value_rows.reshape(value_rows.shape[0], -1, head_dim)
    scores = jnp.einsum(
        "qhd,khd->qhk", q_heads, k_heads, preferred_element_type=jnp.float32
    ) * head_dim ** (-0.5)
    masked = live_mask[:, None, :]
    highest = jnp.max(jnp.where(masked, scores, neg_fill), axis=-1)
    weights = jnp.where(masked, jnp.exp(scores - highest[..., None]), 0.0)
    totals = jnp.sum(weights, axis=-1)
    summed = jnp.einsum(
        "qhk,khd->qhd", weights.astype(jnp.bfloat16), v_heads, preferred_element_type=jnp.float32
    )
    return (highest, totals, summed.reshape(row_count, -1))


def scale_acc(acc_rows, factor, head_dim):
    row_count = acc_rows.shape[0]
    return (acc_rows.reshape(row_count, -1, head_dim) * factor[..., None]).reshape(row_count, -1)


def merge_pair(first_state, second_state, head_dim):
    top_one, total_one, acc_one = first_state
    top_two, total_two, acc_two = second_state
    highest = jnp.maximum(top_one, top_two)
    scale_one = jnp.exp(top_one - highest)
    scale_two = jnp.exp(top_two - highest)
    mixed = scale_acc(acc_one, scale_one, head_dim) + scale_acc(acc_two, scale_two, head_dim)
    return (highest, total_one * scale_one + total_two * scale_two, mixed)


def merge_rows(carried, stats, head_dim):
    current = tuple((member for member in carried))
    updated = merge_pair(current, stats, head_dim)
    return tuple((fresh for fresh in updated))


def normalize(acc_rows, totals, head_dim):
    row_count = acc_rows.shape[0]
    return (
        (acc_rows.reshape(row_count, -1, head_dim) / totals[..., None])
        .reshape(row_count, -1)
        .astype(jnp.bfloat16)
    )


def per_device(
    pre_tokens,
    dec_tokens,
    attn_gain,
    w_query,
    w_key,
    w_value,
    w_output,
    cache_keys,
    cache_values,
    block_request,
    block_slot,
    cache_lens,
    moe_gain,
    expert_ids,
    expert_gates,
    dec_expert_ids,
    dec_expert_gates,
    w_gate,
    w_up,
    w_down,
):
    tok_rows = pre_tokens.shape[0]
    model_width = pre_tokens.shape[1]
    blk_count = lax.axis_size("blk")
    blk_index = lax.axis_index("blk")
    head_count = lax.axis_size("head")
    head_index = lax.axis_index("head")
    head_dim = HD
    local_heads = w_query.shape[1] // head_dim
    all_rows = tok_rows * blk_count
    request_len = all_rows // PRE
    first_row = blk_index * tok_rows
    request_ids = jnp.arange(REQS, dtype=jnp.int32)
    my_request = first_row // request_len
    my_start = my_request * request_len
    my_length = jnp.sum(jnp.where(request_ids == my_request, cache_lens, 0))
    pre_positions = my_length + first_row - my_start + jnp.arange(tok_rows, dtype=jnp.int32)
    dec_positions = cache_lens[PRE : PRE + DEC]
    normed_pre = rms_scale(pre_tokens, attn_gain).astype(jnp.bfloat16)
    normed_dec = rms_scale(dec_tokens, attn_gain).astype(jnp.bfloat16)
    query_pre, key_pre, value_pre = project(
        normed_pre, w_query, w_key, w_value, pre_positions, head_dim
    )
    query_dec, key_dec, value_dec = project(
        normed_dec, w_query, w_key, w_value, dec_positions, head_dim
    )
    new_cache = jnp.stack([key_pre, value_pre])
    dec_cache = jnp.stack([key_dec, value_dec])
    all_queries = lax.all_gather(query_pre, "blk", axis=0, tiled=True)
    pre_state = (
        jnp.full((all_rows, local_heads), neg_fill, jnp.float32),
        jnp.zeros((all_rows, local_heads), jnp.float32),
        jnp.zeros((all_rows, local_heads * head_dim), jnp.float32),
    )
    own_stats = group_stats(
        all_queries, key_pre, value_pre, jnp.ones((1, tok_rows), jnp.bool_), head_dim
    )
    pre_state = merge_rows(pre_state, own_stats, head_dim)
    dec_state = (
        jnp.full((DEC, local_heads), neg_fill, jnp.float32),
        jnp.zeros((DEC, local_heads), jnp.float32),
        jnp.zeros((DEC, local_heads * head_dim), jnp.float32),
    )
    dec_targets = PRE + jnp.arange(DEC, dtype=jnp.int32)
    block_len = cache_keys.shape[1]
    key_offsets = jnp.arange(block_len, dtype=jnp.int32)

    def add_block(block_index, states):
        pre_carry, dec_carry = states
        block_owner = block_request[block_index]
        length_limit = jnp.sum(jnp.where(request_ids == block_owner, cache_lens, 0))
        live_keys = block_slot[block_index] * block_len + key_offsets < length_limit
        block_keys = cache_keys[block_index]
        block_values = cache_values[block_index]

        def prefill_block(carried):
            stats = group_stats(all_queries, block_keys, block_values, live_keys[None, :], head_dim)
            return merge_rows(carried, stats, head_dim)

        pre_carry = lax.cond(block_owner < PRE, prefill_block, lambda carried: carried, pre_carry)
        dec_live = (dec_targets[:, None] == block_owner) & live_keys[None, :]
        dec_carry = merge_pair(
            dec_carry,
            group_stats(query_dec, block_keys, block_values, dec_live, head_dim),
            head_dim,
        )
        return (pre_carry, dec_carry)

    pre_state, dec_state = lax.fori_loop(0, cache_keys.shape[0], add_block, (pre_state, dec_state))
    top_pre, top_dec = (
        lax.pmax(pre_state[0].astype(jnp.bfloat16), "blk").astype(jnp.float32),
        lax.pmax(dec_state[0].astype(jnp.bfloat16), "blk").astype(jnp.float32),
    )
    factor_pre = jnp.exp(pre_state[0] - top_pre)
    factor_dec = jnp.exp(dec_state[0] - top_dec)
    pre_acc, pre_total = (
        lax.psum_scatter(
            scale_acc(pre_state[2], factor_pre, head_dim), "blk", scatter_dimension=0, tiled=True
        ),
        lax.psum_scatter(pre_state[1] * factor_pre, "blk", scatter_dimension=0, tiled=True),
    )
    dec_acc, dec_total = lax.psum(
        (scale_acc(dec_state[2], factor_dec, head_dim), dec_state[1] * factor_dec), "blk"
    )
    dec_state = (top_dec, dec_total, dec_acc)
    own_mask = jnp.arange(DEC)[:, None] == jnp.arange(DEC)[None, :]
    dec_state = merge_pair(
        dec_state, group_stats(query_dec, key_dec, value_dec, own_mask, head_dim), head_dim
    )
    attn_pre = normalize(pre_acc, pre_total, head_dim)
    attn_dec = normalize(dec_state[2], dec_state[1], head_dim)
    out_pre = jnp.dot(attn_pre, w_output, preferred_element_type=jnp.float32)
    out_dec = jnp.dot(attn_dec, w_output, preferred_element_type=jnp.float32)
    part_width = model_width // head_count
    col_start = head_index * part_width
    out_pre, out_dec = lax.psum((out_pre, out_dec), "head")
    mid_pre = pre_tokens.astype(jnp.float32) + out_pre
    mid_dec = dec_tokens.astype(jnp.float32) + out_dec
    moe_in_pre = rms_scale(mid_pre, moe_gain).astype(jnp.bfloat16)
    moe_in_dec = rms_scale(mid_dec, moe_gain).astype(jnp.bfloat16)
    local_experts = w_gate.shape[0]
    all_experts = local_experts * blk_count
    capacity = 2 * tok_rows * TOPK // all_experts
    slot_total = all_experts * capacity
    flat_ids = expert_ids.reshape(-1)
    expert_hits = (flat_ids[:, None] == jnp.arange(all_experts, dtype=jnp.int32)[None, :]).astype(
        jnp.int32
    )
    earlier = jnp.cumsum(expert_hits, axis=0, dtype=jnp.int32) - expert_hits
    slot_of = jnp.sum(earlier * expert_hits, axis=1).reshape(tok_rows, TOPK)
    target = expert_ids * capacity + slot_of
    slot_ids = jnp.arange(slot_total, dtype=jnp.int32)
    dispatch = jnp.any(slot_ids[:, None, None] == target[None, :, :], axis=2).astype(jnp.bfloat16)
    dispatched = jnp.dot(dispatch, moe_in_pre, preferred_element_type=jnp.float32).astype(
        jnp.bfloat16
    )
    dispatched = dispatched.reshape(blk_count, local_experts, capacity, model_width)
    arrived = lax.all_to_all(dispatched, "blk", split_axis=0, concat_axis=0, tiled=True)
    gate_part = jnp.einsum("secd,edf->secf", arrived, w_gate, preferred_element_type=jnp.float32)
    up_part = jnp.einsum("secd,edf->secf", arrived, w_up, preferred_element_type=jnp.float32)
    active = (jax.nn.silu(gate_part) * up_part).astype(jnp.bfloat16)
    produced = jnp.einsum(
        "secf,efd->secd", active, w_down, preferred_element_type=jnp.float32
    ).astype(jnp.bfloat16)
    returned = lax.all_to_all(produced, "blk", split_axis=0, concat_axis=0, tiled=True)
    combine_rows = jnp.sum(
        jnp.where(
            target[:, :, None] == slot_ids[None, None, :],
            expert_gates[:, :, None],
            jnp.zeros((), jnp.bfloat16),
        ),
        axis=1,
    )
    moe_pre = jnp.dot(
        combine_rows, returned.reshape(slot_total, model_width), preferred_element_type=jnp.float32
    )
    local_ids = blk_index * local_experts + jnp.arange(local_experts, dtype=jnp.int32)
    dec_weights = jnp.sum(
        jnp.where(
            dec_expert_ids[:, :, None] == local_ids[None, None, :],
            dec_expert_gates[:, :, None].astype(jnp.float32),
            0.0,
        ),
        axis=1,
    )
    gate_dec = jnp.einsum("td,edf->tef", moe_in_dec, w_gate, preferred_element_type=jnp.float32)
    up_dec = jnp.einsum("td,edf->tef", moe_in_dec, w_up, preferred_element_type=jnp.float32)
    act_dec = (jax.nn.silu(gate_dec) * up_dec).astype(jnp.bfloat16)
    down_dec = jnp.einsum(
        "tef,efd->ted", act_dec, w_down, preferred_element_type=jnp.float32
    ).astype(jnp.bfloat16)
    moe_dec = jnp.sum(down_dec.astype(jnp.float32) * dec_weights[:, :, None], axis=1)
    moe_dec = lax.psum(moe_dec.astype(jnp.bfloat16), "blk").astype(jnp.float32)
    moe_pre, moe_dec = (
        lax.psum(moe_pre.astype(jnp.bfloat16), "head").astype(jnp.float32),
        lax.psum(moe_dec.astype(jnp.bfloat16), "head").astype(jnp.float32),
    )
    pre_hidden = lax.dynamic_slice_in_dim(mid_pre + moe_pre, col_start, part_width, 1).astype(
        jnp.bfloat16
    )
    dec_hidden = lax.dynamic_slice_in_dim(mid_dec + moe_dec, col_start, part_width, 1).astype(
        jnp.bfloat16
    )
    return (pre_hidden, dec_hidden, new_cache, dec_cache)


def solution(mesh):
    placed = (
        P("blk", None),
        P(),
        P(),
        P(None, "head"),
        P(None, "head"),
        P(None, "head"),
        P("head", None),
        P("blk", None, "head"),
        P("blk", None, "head"),
        P("blk"),
        P("blk"),
        P(),
        P(),
        P("blk", None),
        P("blk", None),
        P(),
        P(),
        P("blk", None, "head"),
        P("blk", None, "head"),
        P("blk", "head", None),
    )
    return jax.shard_map(
        per_device,
        mesh=mesh,
        in_specs=placed,
        out_specs=(
            P("blk", "head"),
            P(None, "head"),
            P(None, "blk", "head"),
            P(None, None, "head"),
        ),
        check_vma=False,
    )
```

profile of v0, /device:TPU:0, one launch (start us, length us, event | category | flops | bytes accessed | tf_op | source)
XLA Modules:
  0.0 560.4 jit_solution(17634759153098447598)
XLA Ops:
  8.6 2.3 fusion.139
  16.1 16.6 %all_gather.3 = bf16[512,512]{1,0:T(8,128)(2,1)S(1)} all-gather(bf16[64,512]{1,0:T(8,128)(2,1)S(1)} %copy_bitcast_fusion), channel_id=1, replica_groups=mesh['head'=4,'blk'=8] {'blk'}, dimensions={0}, use_global_device_ids=true | all-gather | bytes 589824 | tf_op jit(solution)/shard_map/all_gather | solution.py:152
  34.0 1.4 fusion.152
  36.7 1.8 convolution_convert_fusion.3
  42.4 2.2 fusion.58
  44.7 110.4 %while.26 = (s32[]{:T(128)}, f32[512,4]{0,1:T(4,128)S(1)}, f32[512,4]{0,1:T(4,128)}, f32[512,512]{0,1:T(8,128)}, f32[12,4]{0,1:T(4,128)}, /*index=5*/f32[12,4]{0...) while((s32[]{:T(128)}, f32[512,4]{0,1:T(4,128)S(1)}, ...), condition=%wide.wide.region_13.14_spmd.clone.clone, body=%wide.wide.region_5.13_spmd.clone.clone.sunk | while | flops 281428288 | bytes 23346496 | solution.py:192
  59.7 1.3 dynamic_slice.66
  65.2 1.3 fusion.200
  68.5 1.4 fusion.202
  73.7 1.3 dynamic_slice.66
  79.2 1.3 fusion.200
  82.5 1.4 fusion.202
  87.7 1.3 dynamic_slice.66
  93.2 1.3 fusion.200
  96.4 1.4 fusion.202
  101.6 1.3 dynamic_slice.66
  107.2 1.3 fusion.200
  110.4 1.4 fusion.202
  115.6 1.3 dynamic_slice.66
  121.1 1.3 fusion.200
  124.4 1.4 fusion.202
  135.1 1.3 fusion.200
  138.4 1.4 fusion.202
  149.1 1.3 fusion.200
  152.3 1.4 fusion.202
  155.8 17.2 %all-reduce.2 = (bf16[512,4]{0,1:T(4,128)(2,1)S(1)}, bf16[12,4]{1,0:T(8,128)(2,1)S(1)}) all-reduce(bf16[512,4]{0,1:T(4,128)(2,1)S(1)} %convert_element_type.189, bf16[12,4]{1,0:T(8,128)(2,1)S(1)} %convert_element_type.202), channel_id=1, replica_groups=mesh['head'=4,'blk'=8] {'blk'}, use_global_device_ids=true, to_apply=%region_14.15 | all-reduce | flops 2096 | bytes 8384 | tf_op jit(solution)/shard_map/pmax | solution.py:194
  174.7 1.4 bitcast_multiply_fusion.1
  176.1 1.3 copy.279
  178.0 26.4 %all-reduce = (f32[12,4]{1,0:T(8,128)S(1)}, f32[12,512]{1,0:T(8,128)S(1)}) all-reduce(f32[12,4]{1,0:T(8,128)S(1)} %get-tuple-element.635, f32[12,512]{1,0:T(8,128)S(1)} %mul.528), channel_id=1, replica_groups=mesh['head'=4,'blk'=8] {'blk'}, use_global_device_ids=true, to_apply=%region_28.29 | all-reduce | flops 6192 | bytes 49536 | tf_op jit(solution)/shard_map/psum | solution.py:205
  204.8 2.0 convolution_convert_fusion.4
  207.4 2.6 fusion.116
  210.9 25.3 %reduce-scatter.7.cloned.1.call-done = f32[64,512]{1,0:T(8,128)} async-done(((f32[512,512]{1,0:T(8,128)}), f32[64,512]{1,0:T(8,128)}) %reduce-scatter.7.cloned.1.call-update) | async-done | bytes 131088
  237.3 2.9 fusion.153
  242.9 43.1 %all-reduce.8.cloned.1.call-done = (f32[64,2048]{1,0:T(8,128)}, f32[12,2048]{1,0:T(8,128)}) async-done(((f32[64,2048]{1,0:T(8,128)}, f32[12,2048]{1,0:T(8,128)}), (f32[64,2048]{1,0:T(8,128)}, f32[12,2048]{1,0:T(8,128)})) %all-reduce.8.cloned.1.call-update) | async-done | bytes 622608 | tf_op jit(solution)/shard_map/psum | solution.py:219
  287.2 1.3 convolution_convert_fusion
  288.5 98.6 %all_to_all.10 = bf16[8,2,64,2048]{3,2,1,0:T(8,128)(2,1)S(1)} all-to-all(bf16[8,2,64,2048]{3,2,1,0:T(8,128)(2,1)S(1)} %bitcast.245), channel_id=1, replica_groups=mesh['head'=4,'blk'=8] {'blk'}, dimensions={0} | all-to-all | bytes 8388608 | tf_op jit(solution)/shard_map/all_to_all | solution.py:241
  387.1 2.0 copy-done.8
  389.1 2.3 fusion.47
  391.4 7.5 %convert_bitcast_fusion = bf16[8,2,64,2048]{3,2,0,1:T(8,128)(2,1)} fusion(bf16[2,256,2048]{2,1,0:T(8,128)(2,1)S(1)} %copy-done, bf16[2,2048,256]{2,1,0:T(8,128)(2,1)} %param.42, bf16[8,2,64,2048]{3,2,1,0:T(8,128)(2,1)} %copy-done.8, f32[8,2,64,256]{3,2,0,1:T(8,128)} %fusion.47), kind=kOutput, calls=%fused_computation.54 | convolution fusion | flops 2151153664 | bytes 13631488 | tf_op jit(solution)/shard_map/secf,efd->secd/dot_general | solution.py:245
  398.8 4.7 copy.256
  403.6 4.7 all-to-all-start.1
  410.9 2.0 fusion.131
  413.0 89.3 %all-to-all-done.1 = bf16[8,2,64,2048]{3,2,1,0:T(8,128)(2,1)} async-done(((bf16[8,2,64,2048]{3,2,1,0:T(8,128)(2,1)}), bf16[8,2,64,2048]{3,2,1,0:T(8,128)(2,1)}, u32[]{:S(2)}, u32[]{:S(2)}) %all-to-all-start.1) | async-done | bytes 4194336 | tf_op jit(solution)/shard_map/all_to_all | solution.py:248
  502.3 3.7 convolution_convert_fusion.1
  506.1 2.4 fusion.70
  508.4 27.2 %psum.54 = bf16[12,2048]{1,0:T(8,128)(2,1)S(1)} all-reduce(bf16[12,2048]{1,0:T(8,128)(2,1)S(1)} %fusion.70), channel_id=1, replica_groups=mesh['head'=4,'blk'=8] {'blk'}, use_global_device_ids=true, to_apply=%region_34.35 | all-reduce | flops 24576 | bytes 98304 | tf_op jit(solution)/shard_map/psum | solution.py:276
  535.6 16.2 %psum.55 = bf16[12,2048]{1,0:T(8,128)(2,1)S(1)} all-reduce(bf16[12,2048]{1,0:T(8,128)(2,1)S(1)} %psum.54), channel_id=1, replica_groups=mesh['head'=4,'blk'=8] {'head'}, use_global_device_ids=true, to_apply=%region_35.36 | all-reduce | flops 24576 | bytes 98304 | tf_op jit(solution)/shard_map/psum | solution.py:279
  552.4 1.5 fusion.95
  (352 shorter events, 99.0 us)
Async XLA Ops:
  7.2 384.2 %copy-start = (bf16[2,256,2048]{2,1,0:T(8,128)(2,1)S(1)}, bf16[2,256,2048]{2,1,0:T(8,128)(2,1)}, u32[]{:S(2)}) copy-start(bf16[2,256,2048]{2,1,0:T(8,128)(2,1)} %param.43) | copy-start | bytes 6291460
  7.2 3.7 copy-start.6
  7.2 3.7 copy-start.17
  7.2 202.9 %reduce-scatter.9.cloned.1.call-start = ((), (), s32[]{:S(2)}) async-start(), calls=%async_computation.6 | async-start | bytes 294912
  7.3 3.6 copy-start.3
  8.6 2.9 copy-start.10
  10.9 1.7 copy-start.4
  11.6 2.1 copy-start.28
  11.6 2.1 copy-start.33
  33.7 3.0 copy-start.5
  34.0 5.3 copy-start.12
  35.5 0.6 copy-start.22
  38.5 6.1 %copy-start.34 = (s32[13]{0:T(128)S(1)}, s32[13]{0:T(128)}, u32[]{:S(2)}) copy-start(s32[13]{0:T(128)} %param.35) | copy-start | bytes 160
  41.8 2.9 copy-start.20
  41.8 2.8 copy-start.26
  56.5 0.7 copy-start.35
  70.5 0.7 copy-start.35
  84.5 0.7 copy-start.35
  98.5 0.7 copy-start.35
  112.4 0.7 copy-start.35
  126.4 0.7 copy-start.35
  140.4 0.7 copy-start.35
  154.4 0.7 copy-start.35
  174.6 61.6 %reduce-scatter.7.cloned.1.call-start = ((), (), s32[]{:S(2)}) async-start(), calls=%async_computation.5 | async-start | bytes 1179648
  176.0 1.5 copy-start.25
  176.0 1.7 copy-start.19
  176.0 1.7 copy-start.21
  176.1 1.9 copy-start.11
  176.1 28.8 %copy-start.18 = (f32[2048]{0:T(1024)S(1)}, f32[2048]{0:T(1024)}, u32[]{:S(2)}) copy-start(f32[2048]{0:T(1024)} %param.26) | copy-start | bytes 24580
  176.1 28.8 %copy-start.29 = (f32[12]{0:T(128)S(1)}, f32[12]{0:T(128)}, u32[]{:S(2)}) copy-start(f32[12]{0:T(128)} %copy-done.28) | copy-start | bytes 148
  177.4 29.8 %copy-start.27 = (s32[64,8]{0,1:T(8,128)S(1)}, s32[64,8]{0,1:T(8,128)}, u32[]{:S(2)}) copy-start(s32[64,8]{0,1:T(8,128)} %param.37) | copy-start | bytes 6148
  177.4 108.5 %all-reduce.8.cloned.1.call-start = ((), (), s32[]{:S(2)}) async-start(), calls=%async_computation.7 | async-start | bytes 1310720 | tf_op jit(solution)/shard_map/psum | solution.py:219
  237.2 48.7 %copy-start.7 = (bf16[64,2048]{1,0:T(8,128)(2,1)S(1)}, bf16[64,2048]{1,0:T(8,128)(2,1)}, u32[]{:S(2)}) copy-start(bf16[64,2048]{1,0:T(8,128)(2,1)} %param.24) | copy-start | bytes 786436
  237.3 49.9 %copy-start.24 = (f32[2048]{0:T(1024)S(1)}, f32[2048]{0:T(1024)}, u32[]{:S(2)}) copy-start(f32[2048]{0:T(1024)} %param.36) | copy-start | bytes 24580
  288.5 100.6 %copy-start.9 = (bf16[2,2048,256]{2,1,0:T(8,128)(2,1)S(1)}, bf16[2,2048,256]{2,1,0:T(8,128)(2,1)}, u32[]{:S(2)}) copy-start(bf16[2,2048,256]{2,1,0:T(8,128)(2,1)} %param.41) | copy-start | bytes 6291460
  387.1 2.0 copy-start.8
  403.6 4.8 copy-start.13
  403.6 4.9 copy-start.31
  403.6 4.9 copy-start.32
  403.6 5.7 %copy-start.30 = (s32[12,8]{0,1:T(8,128)S(1)}, s32[12,8]{0,1:T(8,128)}, u32[]{:S(2)}) copy-start(s32[12,8]{0,1:T(8,128)} %param.39) | copy-start | bytes 1156
  403.6 5.8 %copy-start.14 = (bf16[64,512]{1,0:T(8,128)(2,1)S(1)}, bf16[64,512]{1,0:T(8,128)(2,1)}, u32[]{:S(2)}) copy-start(bf16[64,512]{1,0:T(8,128)(2,1)} %convolution_convert_fusion.3) | copy-start | bytes 196612
  403.6 7.2 %copy-start.23 = (f32[12,2048]{1,0:T(8,128)S(1)}, f32[12,2048]{1,0:T(8,128)}, u32[]{:S(2)}) copy-start(f32[12,2048]{1,0:T(8,128)} %get-tuple-element.617) | copy-start | bytes 294916
  403.6 98.7 %all-to-all-start.1 = ((bf16[8,2,64,2048]{3,2,1,0:T(8,128)(2,1)}), bf16[8,2,64,2048]{3,2,1,0:T(8,128)(2,1)}, u32[]{:S(2)}, u32[]{:S(2)}) async-start(bf16[8,2,64,2048]{3,2,1,0:T(8,128)(2,1)} %copy.256), calls=%async_computation.1 | async-start | bytes 8388608 | tf_op jit(solution)/shard_map/all_to_all | solution.py:248
  408.3 144.1 %all-reduce.6.cloned.1.call-start = ((), (), s32[]{:S(2)}) async-start(), calls=%async_computation.4 | async-start | bytes 524288 | tf_op jit(solution)/shard_map/psum | solution.py:278
Sparse Core Ops, SparseCore 0:
  174.7 28.7 reduce-scatter.8
  205.9 30.2 reduce-scatter.6
  240.4 45.5 all-reduce.7
  506.2 40.8 all-reduce.5
where the time goes:
time: 566 us; the launch traced here: 560 us
  blocking collectives  202 us (36%)
  waiting for transfers between devices  158 us (28%)
  local copies, waits for them, and re-layouts  61.3 us (11%)
  other arithmetic  56.4 us (10%)
  matrix products  51.8 us (9%)
  between operations  15.2 us (3%)
  loops' own time  11 us (2%)
    all_to_all x1, blocking collectives, per_device(): lax.all_to_all(dispatched, 'blk', split_axis=0, concat_axis=0, tiled=True)  98.6 us
    all_to_all x1, waiting for transfers between devices, per_device(): lax.all_to_all(produced, 'blk', split_axis=0, concat_axis=0, tiled=True)  89.3 us
    psum x1, waiting for transfers between devices, per_device(): out_pre, out_dec = lax.psum((out_pre, out_dec), 'head')  43.1 us
    psum x1, blocking collectives, per_device(): moe_dec = lax.psum(moe_dec.astype(jnp.bfloat16), 'blk').astype(jnp.float32)  27.2 us
    psum x1, blocking collectives, per_device(): lax.psum((scale_acc(dec_state[2], factor_dec, head_dim), dec_state[1] * f...  26.4 us
    unnamed x6, waiting for transfers between devices  25.4 us
    pmax x1, blocking collectives, per_device(): lax.pmax(pre_state[0].astype(jnp.bfloat16), 'blk').astype(jnp.float32)  17.2 us
    all_gather x1, blocking collectives, per_device(): all_queries = lax.all_gather(query_pre, 'blk', axis=0, tiled=True)  16.6 us
  transfers between devices with their start and end apart: 5, of which 3 were waited for; matrix products, arithmetic and copies ran while one was open for 3% of the time, Pallas kernels for 0%

commit v1 on v0

v1 whole, which is shorter than its diff:
```python
import functools

import jax
import jax.numpy as jnp
from jax import lax
from jax.experimental import pallas as pl
from jax.experimental.pallas import tpu as pltpu
from jax.sharding import PartitionSpec as P

HD = 128
PRE = 1
DEC = 12
REQS = 13
DPAD = 16
TILE = 256

eps_norm = 1e-06
rope_base = 50000.0
neg_fill = -1e30
bf16 = jnp.bfloat16
f32 = jnp.float32


def rms_scale(row_data, gain_vec):
    values = row_data.astype(f32)
    meansq = jnp.mean(values * values, axis=-1, keepdims=True)
    return values * lax.rsqrt(meansq + eps_norm) * gain_vec


def rotate(flat, cosine, sine):
    rows = flat.shape[0]
    blocks = flat.reshape(rows, -1, HD)
    first = blocks[..., : HD // 2]
    second = blocks[..., HD // 2 :]
    return jnp.concatenate(
        [first * cosine - second * sine, second * cosine + first * sine], axis=-1
    ).reshape(rows, -1)


def swap(value, axis, mask):
    count = lax.axis_size(axis)
    return lax.ppermute(value, axis, [(i, i ^ mask) for i in range(count)])


def span(index, size):
    return pl.ds(pl.multiple_of(index * size, size), size)


def lanes(head):
    return slice(head * HD, (head + 1) * HD)


def group(query, keys, values, live):
    scores = lax.dot_general(
        query, keys, (((1,), (1,)), ((), ())), preferred_element_type=f32
    ) * HD ** (-0.5)
    top = jnp.max(scores if live is None else jnp.where(live, scores, neg_fill), axis=-1, keepdims=True)
    weights = jnp.exp(scores - top)
    if live is not None:
        weights = jnp.where(live, weights, 0.0)
    total = jnp.sum(weights, axis=-1, keepdims=True)
    acc = jnp.dot(weights.astype(bf16), values, preferred_element_type=f32)
    return top, total, acc


def attention_kernel(
    owner_ref,
    live_ref,
    first_ref,
    query_a,
    query_b,
    query_d,
    key_new,
    value_new,
    key_dec,
    value_dec,
    cache_k,
    cache_v,
    keep,
    send,
    tops,
    totals,
):
    step = pl.program_id(0)
    half = query_a.shape[0]
    heads = query_a.shape[1] // HD
    tile = min(TILE, half)
    sides = ((query_a, keep, 0), (query_b, send, half))

    def over_tiles(body):
        for side in sides:
            if half == tile:
                body(side, 0)
            else:

                @pl.loop(0, half // tile)
                def _(index):
                    body(side, pl.multiple_of(index * tile, tile))

    def merge(acc_ref, row, size, state_row, head, found):
        top, total, acc = found
        rows = pl.ds(row, size)
        state = pl.ds(state_row, size)
        old_top = tops[head, state, :]
        best = jnp.maximum(old_top, top)
        old_scale = jnp.exp(old_top - best)
        scale = jnp.exp(top - best)
        tops[head, state, :] = best
        totals[head, state, :] = totals[head, state, :] * old_scale + total * scale
        acc_ref[rows, lanes(head)] = acc_ref[rows, lanes(head)] * old_scale + acc * scale

    @pl.when(step == 0)
    def _():
        def start(side, row):
            query, acc_ref, base = side
            for head in range(heads):
                top, total, acc = group(
                    query[pl.ds(row, tile), lanes(head)],
                    key_new[:, lanes(head)],
                    value_new[:, lanes(head)],
                    None,
                )
                tops[head, pl.ds(base + row, tile), :] = top
                totals[head, pl.ds(base + row, tile), :] = total
                acc_ref[pl.ds(row, tile), lanes(head)] = acc

        over_tiles(start)
        mine = first_ref[0] == 1
        for head in range(heads):
            own = jnp.sum(
                query_d[:, lanes(head)].astype(f32) * key_dec[:, lanes(head)].astype(f32),
                axis=-1,
                keepdims=True,
            ) * HD ** (-0.5)
            tops[head, pl.ds(2 * half, DPAD), :] = jnp.where(mine, own, neg_fill)
            totals[head, pl.ds(2 * half, DPAD), :] = jnp.where(
                mine, jnp.ones_like(own), jnp.zeros_like(own)
            )
            keep[pl.ds(half, DPAD), lanes(head)] = jnp.where(
                mine, value_dec[:, lanes(head)].astype(f32), 0.0
            )

    owner = owner_ref[step]
    count = live_ref[step]

    @pl.when(owner < PRE)
    def _():
        live = lax.broadcasted_iota(jnp.int32, (tile, cache_k.shape[1]), 1) < count

        def add(side, row):
            query, acc_ref, base = side
            for head in range(heads):
                found = group(
                    query[pl.ds(row, tile), lanes(head)],
                    cache_k[0, :, lanes(head)],
                    cache_v[0, :, lanes(head)],
                    live,
                )
                merge(acc_ref, row, tile, base + row, head, found)

        over_tiles(add)

    @pl.when((owner >= PRE) & (owner < REQS))
    def _():
        shape = (DPAD, cache_k.shape[1])
        live = (lax.broadcasted_iota(jnp.int32, shape, 1) < count) & (
            lax.broadcasted_iota(jnp.int32, shape, 0) == owner - PRE
        )
        for head in range(heads):
            found = group(
                query_d[:, lanes(head)],
                cache_k[0, :, lanes(head)],
                cache_v[0, :, lanes(head)],
                live,
            )
            merge(keep, half, DPAD, 2 * half, head, found)

    @pl.when(step == pl.num_programs(0) - 1)
    def _():
        width = heads * HD
        for ref, base in ((keep, 0), (send, half)):
            for row, size, state in ((0, half, base), (half, DPAD, 2 * half)):
                place = lax.broadcasted_iota(jnp.int32, (size, HD), 1)
                packed = jnp.zeros((size, HD), f32)
                for head in range(heads):
                    packed = jnp.where(place == head, tops[head, pl.ds(state, size), :], packed)
                    packed = jnp.where(
                        place == heads + head, totals[head, pl.ds(state, size), :], packed
                    )
                ref[pl.ds(row, size), width : width + HD] = packed
        send[pl.ds(half, DPAD), :width] = keep[pl.ds(half, DPAD), :width]


def attention(queries, query_d, new, dec, cache_keys, cache_values, owner, count, first):
    query_a, query_b = queries
    half, width = query_a.shape
    heads = width // HD
    blocks, block_len = cache_keys.shape[:2]
    whole = lambda arr: pl.BlockSpec(arr.shape, lambda *_: (0,) * arr.ndim)
    block = pl.BlockSpec((1, block_len, width), lambda i, *_: (i, 0, 0))
    fixed = (query_a, query_b, query_d, *new, *dec)
    shape = jax.ShapeDtypeStruct((half + DPAD, width + HD), f32)
    return pl.pallas_call(
        attention_kernel,
        out_shape=(shape, shape),
        grid_spec=pltpu.PrefetchScalarGridSpec(
            num_scalar_prefetch=3,
            grid=(blocks,),
            in_specs=[*(whole(arr) for arr in fixed), block, block],
            out_specs=(whole(shape), whole(shape)),
            scratch_shapes=[
                pltpu.VMEM((heads, 2 * half + DPAD, 1), f32),
                pltpu.VMEM((heads, 2 * half + DPAD, 1), f32),
            ],
        ),
        compiler_params=pltpu.CompilerParams(
            dimension_semantics=("arbitrary",), vmem_limit_bytes=40 << 20
        ),
        name="attention",
    )(owner, count, first, *fixed, cache_keys, cache_values)


def merge_core_kernel(mine, other, *outs):
    rows, full = mine.shape
    width = full - HD
    heads = width // HD
    place = lax.broadcasted_iota(jnp.int32, (rows, HD), 1)
    packed = jnp.zeros((rows, HD), f32)
    stats_a = mine[:, width:]
    stats_b = other[:, width:]
    tok = (rows - DPAD) // len(outs)

    def put(where, value):
        for index, out in enumerate(outs):
            out[0:tok, where] = value[index * tok : (index + 1) * tok]
            out[tok : tok + DPAD, where] = value[rows - DPAD :]

    for head in range(heads):
        top_a, top_b = stats_a[:, head : head + 1], stats_b[:, head : head + 1]
        sum_a = stats_a[:, heads + head : heads + head + 1]
        sum_b = stats_b[:, heads + head : heads + head + 1]
        best = jnp.maximum(top_a, top_b)
        scale_a = jnp.exp(top_a - best)
        scale_b = jnp.exp(top_b - best)
        packed = jnp.where(place == head, best, packed)
        packed = jnp.where(place == heads + head, sum_a * scale_a + sum_b * scale_b, packed)
        put(lanes(head), (mine[:, lanes(head)] * scale_a + other[:, lanes(head)] * scale_b).astype(bf16))
    high = packed.astype(bf16).astype(f32)
    middle = (packed - high).astype(bf16).astype(f32)
    low = (packed - high) - middle
    coded = high + pltpu.roll(middle, 2 * heads, 1) + pltpu.roll(low, 4 * heads, 1)
    put(slice(width, full), coded.astype(bf16))


def merge_core(mine, other, parts):
    rows, full = mine.shape
    tok = (rows - DPAD) // parts
    shape = jax.ShapeDtypeStruct((tok + DPAD, full), bf16)
    return pl.pallas_call(
        merge_core_kernel,
        out_shape=(shape,) * parts,
        compiler_params=pltpu.CompilerParams(vmem_limit_bytes=40 << 20),
        name="merge_core",
    )(mine, other)


def tree_sum(values):
    values = list(values)
    while len(values) > 1:
        values = [a + b for a, b in zip(values[::2], values[1::2])]
    return values[0]


def project_kernel(parts, head_ref, *refs):
    pieces = refs[:parts]
    weight = refs[parts]
    outs = refs[parts + 1 :]
    rows, full = pieces[0].shape
    width = full - HD
    heads = width // HD
    columns = outs[0].shape[1]
    stats = []
    for piece in pieces:
        coded = piece[:, width:].astype(f32)
        stats.append(
            (coded + pltpu.roll(coded, HD - 2 * heads, 1)) + pltpu.roll(coded, HD - 4 * heads, 1)
        )
    attended = []
    for head in range(heads):
        tops = [s[:, head : head + 1] for s in stats]
        best = functools.reduce(jnp.maximum, tops)
        scales = [jnp.exp(top - best) for top in tops]
        total = tree_sum([s[:, heads + head : heads + head + 1] * c for s, c in zip(stats, scales)])
        acc = tree_sum([piece[:, lanes(head)].astype(f32) * c for piece, c in zip(pieces, scales)])
        attended.append((acc / total).astype(bf16))
    attended = jnp.concatenate(attended, axis=1)
    for offset, out in enumerate(outs):
        place = lax.bitwise_xor(head_ref[0], offset)
        out[...] = jnp.dot(attended, weight[:, span(place, columns)], preferred_element_type=f32)


def project_out(pieces, w_output, head_index, head_count):
    rows = pieces[0].shape[0]
    columns = w_output.shape[1] // head_count
    shape = jax.ShapeDtypeStruct((rows, columns), f32)
    vmem = pl.BlockSpec(memory_space=pltpu.VMEM)
    return pl.pallas_call(
        functools.partial(project_kernel, len(pieces)),
        out_shape=(shape,) * head_count,
        in_specs=[pl.BlockSpec(memory_space=pltpu.SMEM)] + [vmem] * (len(pieces) + 1),
        out_specs=(vmem,) * head_count,
        compiler_params=pltpu.CompilerParams(vmem_limit_bytes=32 << 20),
        name="project_out",
    )(head_index, *pieces, w_output)


def experts_kernel(chunks, head_ref, *refs):
    own = refs[:chunks]
    other = refs[chunks : 2 * chunks]
    gates_own, gates_other, w_gate, w_up, w_down = refs[2 * chunks : 2 * chunks + 5]
    keep = refs[2 * chunks + 5 : 3 * chunks + 5]
    send = refs[3 * chunks + 5 :]
    experts = w_gate.shape[0]
    width = own[0].shape[1]
    half = own[0].shape[0] - DPAD
    tile = min(TILE, half)
    places = [lax.bitwise_xor(head_ref[0], offset) for offset in range(chunks)]

    def run(parts, gates, row, size):
        rows = pl.ds(row, size)
        total = [None] * chunks
        for expert in range(experts):
            gate = up = None
            for part, place in zip(parts, places):
                data = part[rows, :]
                g = jnp.dot(data, w_gate[expert, span(place, width), :], preferred_element_type=f32)
                u = jnp.dot(data, w_up[expert, span(place, width), :], preferred_element_type=f32)
                gate = g if gate is None else gate + g
                up = u if up is None else up + u
            act = (gate / (1.0 + jnp.exp(-gate)) * up).astype(bf16)
            factor = gates[rows, expert : expert + 1]
            for index, place in enumerate(places):
                down = jnp.dot(act, w_down[expert, :, span(place, width)], preferred_element_type=f32)
                down = down.astype(bf16).astype(f32) * factor
                total[index] = down if total[index] is None else total[index] + down
        return total

    for row in range(0, half, tile):
        for index, value in enumerate(run(other, gates_other, row, tile)):
            send[index][row : row + tile, :] = value.astype(bf16)
    for row in range(0, half, tile):
        size = tile + (DPAD if row + tile == half else 0)
        for index, value in enumerate(run(own, gates_own, row, size)):
            value = value.astype(bf16)
            keep[index][row : row + size, :] = value
            if size > tile:
                send[index][half : half + DPAD, :] = value[tile:]


def run_experts(own, other, gates_own, gates_other, w_gate, w_up, w_down, head_index):
    chunks = len(own)
    shape = jax.ShapeDtypeStruct(own[0].shape, bf16)
    vmem = pl.BlockSpec(memory_space=pltpu.VMEM)
    outs = pl.pallas_call(
        functools.partial(experts_kernel, chunks),
        out_shape=(shape,) * (2 * chunks),
        in_specs=[pl.BlockSpec(memory_space=pltpu.SMEM)] + [vmem] * (2 * chunks + 5),
        out_specs=(vmem,) * (2 * chunks),
        compiler_params=pltpu.CompilerParams(vmem_limit_bytes=48 << 20),
        name="experts",
    )(head_index, *own, *other, gates_own, gates_other, w_gate, w_up, w_down)
    return outs[:chunks], outs[chunks:]


def per_device(
    pre_tokens,
    dec_tokens,
    attn_gain,
    w_query,
    w_key,
    w_value,
    w_output,
    cache_keys,
    cache_values,
    block_request,
    block_slot,
    cache_lens,
    moe_gain,
    expert_ids,
    expert_gates,
    dec_expert_ids,
    dec_expert_gates,
    w_gate,
    w_up,
    w_down,
):
    tok, model_width = pre_tokens.shape
    blk_count = lax.axis_size("blk")
    blk_index = lax.axis_index("blk")
    head_count = lax.axis_size("head")
    head_index = lax.axis_index("head")
    chips = blk_count // 2
    head_scalar = head_index.reshape(1).astype(jnp.int32)
    part_width = model_width // head_count

    request_len = tok * blk_count // PRE
    first_row = blk_index * tok
    request_ids = jnp.arange(REQS, dtype=jnp.int32)
    my_request = first_row // request_len
    my_length = jnp.sum(jnp.where(request_ids == my_request, cache_lens, 0))
    pre_positions = my_length + first_row - my_request * request_len + jnp.arange(tok, dtype=jnp.int32)
    positions = jnp.concatenate(
        [pre_positions, cache_lens[PRE : PRE + DEC], jnp.zeros((DPAD - DEC,), jnp.int32)]
    )
    frequencies = rope_base ** (-jnp.arange(HD // 2, dtype=f32) / (HD // 2))
    angles = positions.astype(f32)[:, None] * frequencies[None, :]
    cosine = jnp.cos(angles)[:, None, :]
    sine = jnp.sin(angles)[:, None, :]

    tokens = jnp.concatenate(
        [pre_tokens, dec_tokens, jnp.zeros((DPAD - DEC, model_width), bf16)], axis=0
    )
    normed = rms_scale(tokens, attn_gain).astype(bf16)
    query = rotate(jnp.dot(normed, w_query, preferred_element_type=f32), cosine, sine).astype(bf16)
    key = rotate(jnp.dot(normed, w_key, preferred_element_type=f32), cosine, sine).astype(bf16)
    value = jnp.dot(normed, w_value, preferred_element_type=f32).astype(bf16)
    new_cache = jnp.stack([key[:tok], value[:tok]])
    dec_cache = jnp.stack([key[tok : tok + DEC], value[tok : tok + DEC]])

    def gather_chips(piece):
        return [piece] + [swap(piece, "blk", 2 * o) for o in range(1, chips)]

    query_a = jnp.concatenate(gather_chips(query[:tok]), axis=0)
    query_b = swap(query_a, "blk", 1)

    experts_all = w_gate.shape[0] * blk_count
    expert_range = jnp.arange(experts_all, dtype=jnp.int32)

    def gate_table(ids, gates):
        return jnp.sum(
            jnp.where(ids[:, :, None] == expert_range, gates.astype(f32)[:, :, None], 0.0), axis=1
        )

    table = gate_table(expert_ids, expert_gates).astype(bf16)
    table_a = jnp.concatenate(gather_chips(table), axis=0)
    table_b = swap(table_a, "blk", 1)
    table_d = jnp.concatenate(
        [
            gate_table(dec_expert_ids, dec_expert_gates).astype(bf16),
            jnp.zeros((DPAD - DEC, experts_all), bf16),
        ],
        axis=0,
    )

    def local_gates(rows):
        mine = blk_index * w_gate.shape[0] + jnp.arange(w_gate.shape[0], dtype=jnp.int32)
        return jnp.sum(
            jnp.where(expert_range[None, None, :] == mine[None, :, None], rows.astype(f32)[:, None, :], 0.0),
            axis=2,
        )

    gates_own = local_gates(jnp.concatenate([table_a, table_d], axis=0))
    gates_other = local_gates(table_b)

    lengths = jnp.sum(jnp.where(request_ids[None, :] == block_request[:, None], cache_lens[None, :], 0), axis=1)
    count = jnp.clip(lengths - block_slot * cache_keys.shape[1], 0, cache_keys.shape[1]).astype(jnp.int32)
    first = (blk_index == 0).astype(jnp.int32).reshape(1)
    keep, send = attention(
        (query_a, query_b),
        query[tok:],
        (key[:tok], value[:tok]),
        (key[tok:], value[tok:]),
        cache_keys,
        cache_values,
        block_request,
        count,
        first,
    )
    pieces = merge_core(keep, swap(send, "blk", 1), chips)
    pieces = [pieces[0]] + [swap(pieces[o], "blk", 2 * o) for o in range(1, chips)]
    partial = project_out(pieces, w_output, head_scalar, head_count)
    arrived = [partial[0]] + [swap(partial[o], "head", o) for o in range(1, head_count)]

    def own_columns(arr):
        return lax.dynamic_slice_in_dim(arr, head_index * part_width, part_width, arr.ndim - 1)

    mid = own_columns(tokens).astype(f32) + tree_sum(arrived)
    square = jnp.sum(mid * mid, axis=1)[None, :]
    square = tree_sum([square] + [swap(square, "head", o) for o in range(1, head_count)])
    scale = lax.rsqrt(square[0][:, None] / model_width + eps_norm)
    moe_in = (mid * scale * own_columns(moe_gain)).astype(bf16)

    rows_own = jnp.concatenate([*gather_chips(moe_in[:tok]), moe_in[tok:]], axis=0)
    own = [rows_own] + [swap(rows_own, "head", o) for o in range(1, head_count)]
    other = [swap(chunk, "blk", 1) for chunk in own]
    keep, send = run_experts(own, other, gates_own, gates_other, w_gate, w_up, w_down, head_scalar)
    summed = [
        (a.astype(f32) + swap(b, "blk", 1).astype(f32)).astype(bf16) for a, b in zip(keep, send)
    ]
    summed = [summed[0]] + [swap(summed[o], "head", o) for o in range(1, head_count)]
    half = tok * chips
    merged = tree_sum([s.astype(f32) for s in summed]).astype(bf16)
    final = [
        jnp.concatenate([merged[o * tok : (o + 1) * tok], merged[half:]], axis=0) for o in range(chips)
    ]
    final = [final[0]] + [swap(final[o], "blk", 2 * o) for o in range(1, chips)]
    hidden = (mid + tree_sum([s.astype(f32) for s in final])).astype(bf16)
    return (hidden[:tok], hidden[tok : tok + DEC], new_cache, dec_cache)


def solution(mesh):
    placed = (
        P("blk", None),
        P(),
        P(),
        P(None, "head"),
        P(None, "head"),
        P(None, "head"),
        P("head", None),
        P("blk", None, "head"),
        P("blk", None, "head"),
        P("blk"),
        P("blk"),
        P(),
        P(),
        P("blk", None),
        P("blk", None),
        P(),
        P(),
        P("blk", None, "head"),
        P("blk", None, "head"),
        P("blk", "head", None),
    )
    return jax.shard_map(
        per_device,
        mesh=mesh,
        in_specs=placed,
        out_specs=(
            P("blk", "head"),
            P(None, "head"),
            P(None, "blk", "head"),
            P(None, None, "head"),
        ),
        check_vma=False,
    )
```

time: 566 us -> 139 us (0.25)
  blocking collectives: 202 us -> 0 us
  waiting for transfers between devices: 158 us -> 42.5 us
  other arithmetic: 56.4 us -> 9.84 us
  matrix products: 51.8 us -> 5.47 us
  local copies, waits for them, and re-layouts: 61.3 us -> 16.3 us
  starting transfers between devices: 4.85 us -> 38.7 us
  Pallas kernels: 0 us -> 23 us
  between operations: 15.2 us -> 1.89 us
  loops' own time: 11 us -> 0 us
    all_to_all x1 -> x0, blocking collectives: 98.6 us -> none  [per_device(): lax.all_to_all(dispatched, 'blk', split_axis=0, concat_axis=0, tiled=True)]
    all_to_all x1 -> x0, waiting for transfers between devices: 89.3 us -> none  [per_device(): lax.all_to_all(produced, 'blk', split_axis=0, concat_axis=0, tiled=True)]
    psum x3 -> x0, blocking collectives: 69.8 us -> none  [the longest x1 27.2 us: per_device(): moe_dec = lax.psum(moe_dec.astype(jnp.bfloat16), 'blk').astype(jnp.float32)]
    dot_general x34 -> x3, matrix products: 51.8 us -> 5.47 us  [the longest x1 2.13 us: per_device(): jnp.dot(normed, w_query, preferred_element_type=f32)]
    psum x2 -> x0, waiting for transfers between devices: 43.1 us -> none  [the longest x1 43.1 us: per_device(): out_pre, out_dec = lax.psum((out_pre, out_dec), 'head')]
    ppermute x0 -> x38, waiting for transfers between devices: none -> 42.5 us  [swap(): return lax.ppermute(value, axis, [(i, i ^ mask) for i in range(count)])]
    ppermute x0 -> x38, starting transfers between devices: none -> 38.7 us  [swap(): return lax.ppermute(value, axis, [(i, i ^ mask) for i in range(count)])]
    dynamic_slice x40 -> x1, local copies, waits for them, and re-layouts: 31.1 us -> 0.76 us  [own_columns(): lax.dynamic_slice_in_dim(arr, head_index * part_width, part_width, arr.nd...]
  transfers between devices with their start and end apart: 5 -> 38, of which waited for: 3 -> 19; matrix products, arithmetic and copies ran while one was open for 3% -> 10% of each run, Pallas kernels for 0% -> 0%
where the time goes in v1:
time: 139 us; the launch traced here: 138 us
  waiting for transfers between devices  42.5 us (31%)
  starting transfers between devices  38.7 us (28%)
  Pallas kernels  23 us (17%)
  local copies, waits for them, and re-layouts  16.3 us (12%)
  other arithmetic  9.84 us (7%)
  matrix products  5.47 us (4%)
  between operations  1.89 us (1%)
    ppermute x38, waiting for transfers between devices, swap(): return lax.ppermute(value, axis, [(i, i ^ mask) for i in range(count)])  42.5 us
    ppermute x38, starting transfers between devices, swap(): return lax.ppermute(value, axis, [(i, i ^ mask) for i in range(count)])  38.7 us
    pallas_call x1, Pallas kernels, attention(): pl.pallas_call(attention_kernel, out_shape=(shape, shape), grid_spec=pltp...  13.3 us
    unnamed x60, local copies, waits for them, and re-layouts  10.6 us
    pallas_call x1, Pallas kernels, run_experts(): pl.pallas_call(functools.partial(experts_kernel, chunks), out_shape=(shap...  7.96 us
  transfers between devices with their start and end apart: 38, of which 19 were waited for; matrix products, arithmetic and copies ran while one was open for 10% of the time, Pallas kernels for 0%

profile of v1, /device:TPU:0, one launch (start us, length us, event | category | flops | bytes accessed | tf_op | source)
XLA Modules:
  0.0 137.7 jit_solution(1790693563813419184)
XLA Ops:
  1.6 1.3 fusion.5
  3.6 1.3 fusion
  4.9 1.2 fusion.7
  6.2 2.1 %fusion.9 = f32[80,512]{1,0:T(8,128)S(1)} fusion(bf16[2048,512]{1,0:T(8,128)(2,1)} %param.23, bf16[80,2048]{1,0:T(8,128)(2,1)S(1)} %get-tuple-element.55, f32[2048]{0:T(1024)S(1)} %copy-done.21, f32[80]{0:T(128)S(1)} %add_rsqrt_fusion), kind=kOutput, calls=%fused_computation.71 | convolution fusion | flops 168427520 | bytes 2597184 | tf_op jit(solution)/shard_map/dot_general | solution.py:424
  9.3 5.1 %collective-permute-start.2 = (bf16[64,512]{1,0:T(8,128)(2,1)S(1)}, bf16[64,512]{1,0:T(8,128)(2,1)S(1)}, u32[]{:S(2)}, u32[]{:S(2)}) collective-permute-start(bf16[64,512]{1,0:T(8,128)(2,1)S(1)} %bitcast.39), channel_id=1, source_target_pairs={{0,6},{1,7},{2,4},{3,5},{4,2},{5,3},{6,0},{7,1},{8,14},{9,15},{10,... | collective-permute-start | bytes 196616 | tf_op jit(solution)/shard_map/ppermute | solution.py:42
  15.3 2.1 %convolution_convert_fusion = bf16[80,512]{1,0:T(8,128)(2,1)S(1)} fusion(bf16[2048,512]{1,0:T(8,128)(2,1)} %param.25, bf16[80,2048]{1,0:T(8,128)(2,1)S(1)} %get-tuple-element.55, f32[2048]{0:T(1024)S(1)} %copy-done.21, f32[80]{0:T(128)S(1)} %add_rsqrt_fusion), kind=kOutput, calls=%fused_computation | convolution fusion | flops 168468480 | bytes 2515264 | tf_op jit(solution)/shard_map/dot_general | solution.py:426
  17.4 1.3 collective-permute-done
  18.7 1.3 collective-permute-done.1
  21.7 1.6 %copy-done.1 = bf16[8,256,512]{2,1,0:T(8,128)(2,1)S(1)} copy-done((bf16[8,256,512]{2,1,0:T(8,128)(2,1)S(1)}, bf16[8,256,512]{2,1,0:T(8,128)(2,1)}, u32[]{:S(2)}) %copy-start.1) | copy-done | bytes 2097176
  23.3 1.6 %copy-done.2 = bf16[8,256,512]{2,1,0:T(8,128)(2,1)S(1)} copy-done((bf16[8,256,512]{2,1,0:T(8,128)(2,1)S(1)}, bf16[8,256,512]{2,1,0:T(8,128)(2,1)}, u32[]{:S(2)}) %copy-start.2) | copy-done | bytes 2097176
  24.8 13.3 %attention.1 = (f32[272,640]{1,0:T(8,128)S(1)}, f32[272,640]{1,0:T(8,128)S(1)}) custom-call(s32[8]{0:T(128)S(1)} %copy-done.10, s32[8]{0:T(128)S(1)} %subtract_clamp_fusion.live_ref, s32[1]{0:T(128)} %bitcast.1.first_ref, bf16[256,512]{1,0:T(8,128)(2,1)S(1)} %constant_dynamic-update-slice_fusion.query_a, ...), custom_call_target="tpu_custom_call" | custom-call | tf_op jit(solution)/shard_map/attention/pallas_call | solution.py:203
  38.2 2.1 %collective-permute-done.4.other = f32[272,640]{1,0:T(8,128)S(1)} collective-permute-done((f32[272,640]{1,0:T(8,128)S(1)}, f32[272,640]{1,0:T(8,128)S(1)}, u32[]{:S(2)}, u32[]{:S(2)}) %collective-permute-start.4) | collective-permute-done | bytes 696352 | tf_op jit(solution)/shard_map/ppermute | solution.py:42
  41.3 1.0 collective-permute-start.6
  42.3 3.4 %collective-permute-start.7 = (bf16[80,640]{1,0:T(8,128)(2,1)S(1)}, bf16[80,640]{1,0:T(8,128)(2,1)S(1)}, u32[]{:S(2)}, u32[]{:S(2)}) collective-permute-start(bf16[80,640]{1,0:T(8,128)(2,1)S(1)} %get-tuple-element.27), channel_id=1, source_target_pairs={{0,6},{1,7},{2,4},{3,5},{4,2},{5,3},{6,0},{7,1},{8,14},{9,15},{10,... | collective-permute-start | bytes 307208 | tf_op jit(solution)/shard_map/ppermute | solution.py:42
  45.7 1.7 %collective-permute-done.5.refs_1_ = bf16[80,640]{1,0:T(8,128)(2,1)S(1)} collective-permute-done((bf16[80,640]{1,0:T(8,128)(2,1)S(1)}, bf16[80,640]{1,0:T(8,128)(2,1)S(1)}, u32[]{:S(2)}, u32[]{:S(2)}) %collective-permute-start.5) | collective-permute-done | bytes 102432 | tf_op jit(solution)/shard_map/ppermute | solution.py:42
  47.4 5.0 %collective-permute-done.6.refs_2_ = bf16[80,640]{1,0:T(8,128)(2,1)S(1)} collective-permute-done((bf16[80,640]{1,0:T(8,128)(2,1)S(1)}, bf16[80,640]{1,0:T(8,128)(2,1)S(1)}, u32[]{:S(2)}, u32[]{:S(2)}) %collective-permute-start.6) | collective-permute-done | bytes 102432 | tf_op jit(solution)/shard_map/ppermute | solution.py:42
  52.4 1.6 %copy-done.3 = bf16[512,2048]{1,0:T(8,128)(2,1)S(1)} copy-done((bf16[512,2048]{1,0:T(8,128)(2,1)S(1)}, bf16[512,2048]{1,0:T(8,128)(2,1)}, u32[]{:S(2)}) %copy-start.3) | copy-done | bytes 2097176
  54.0 0.9 project_out.1
  54.9 1.6 %collective-permute-start.8 = (f32[80,512]{1,0:T(8,128)S(1)}, f32[80,512]{1,0:T(8,128)S(1)}, u32[]{:S(2)}, u32[]{:S(2)}) collective-permute-start(f32[80,512]{1,0:T(8,128)S(1)} %get-tuple-element.29), channel_id=1, source_target_pairs={{0,8},{8,0},{16,24},{24,16},{1,9},{9,1},{17,25},{25,17},{2,10},{10... | collective-permute-start | bytes 491528 | tf_op jit(solution)/shard_map/ppermute | solution.py:42
  56.5 1.5 %collective-permute-start.9 = (f32[80,512]{1,0:T(8,128)S(1)}, f32[80,512]{1,0:T(8,128)S(1)}, u32[]{:S(2)}, u32[]{:S(2)}) collective-permute-start(f32[80,512]{1,0:T(8,128)S(1)} %get-tuple-element.30), channel_id=1, source_target_pairs={{0,16},{8,24},{16,0},{24,8},{1,17},{9,25},{17,1},{25,9},{2,18},{10... | collective-permute-start | bytes 491528 | tf_op jit(solution)/shard_map/ppermute | solution.py:42
  59.8 1.4 %collective-permute-start.26 = (bf16[64,16]{0,1:T(8,128)(2,1)S(1)}, bf16[64,16]{0,1:T(8,128)(2,1)S(1)}, u32[]{:S(2)}, u32[]{:S(2)}) collective-permute-start(bf16[64,16]{0,1:T(8,128)(2,1)S(1)} %select_reduce_fusion), channel_id=1, source_target_pairs={{0,6},{1,7},{2,4},{3,5},{4,2},{5,3},{6,0},{7,1},{8,14},{9,15},{10,... | collective-permute-start | bytes 6152 | tf_op jit(solution)/shard_map/ppermute | solution.py:42
  61.3 2.0 %collective-permute-start.25 = (bf16[64,16]{0,1:T(8,128)(2,1)S(1)}, bf16[64,16]{0,1:T(8,128)(2,1)S(1)}, u32[]{:S(2)}, u32[]{:S(2)}) collective-permute-start(bf16[64,16]{0,1:T(8,128)(2,1)S(1)} %select_reduce_fusion), channel_id=1, source_target_pairs={{0,4},{1,5},{2,6},{3,7},{4,0},{5,1},{6,2},{7,3},{8,12},{9,13},{10,... | collective-permute-start | bytes 6152 | tf_op jit(solution)/shard_map/ppermute | solution.py:42
  63.3 1.6 %collective-permute-done.9 = f32[80,512]{1,0:T(8,128)S(1)} collective-permute-done((f32[80,512]{1,0:T(8,128)S(1)}, f32[80,512]{1,0:T(8,128)S(1)}, u32[]{:S(2)}, u32[]{:S(2)}) %collective-permute-start.9) | collective-permute-done | bytes 163872 | tf_op jit(solution)/shard_map/ppermute | solution.py:42
  65.0 1.1 multiply_reduce_fusion
  66.1 1.1 collective-permute-start.12
  67.1 1.1 collective-permute-start.13
  68.3 1.3 collective-permute-start.11
  70.4 1.2 collective-permute-done.13
  71.9 2.8 %collective-permute-start.14 = (bf16[64,512]{1,0:T(8,128)(2,1)S(1)}, bf16[64,512]{1,0:T(8,128)(2,1)S(1)}, u32[]{:S(2)}, u32[]{:S(2)}) collective-permute-start(bf16[64,512]{1,0:T(8,128)(2,1)S(1)} %get-tuple-element.65), channel_id=1, source_target_pairs={{0,2},{1,3},{2,0},{3,1},{4,6},{5,7},{6,4},{7,5},{8,10},{9,11},{10,... | collective-permute-start | bytes 196616 | tf_op jit(solution)/shard_map/ppermute | solution.py:42
  74.8 1.4 %collective-permute-start.16 = (bf16[64,512]{1,0:T(8,128)(2,1)S(1)}, bf16[64,512]{1,0:T(8,128)(2,1)S(1)}, u32[]{:S(2)}, u32[]{:S(2)}) collective-permute-start(bf16[64,512]{1,0:T(8,128)(2,1)S(1)} %get-tuple-element.65), channel_id=1, source_target_pairs={{0,6},{1,7},{2,4},{3,5},{4,2},{5,3},{6,0},{7,1},{8,14},{9,15},{10,... | collective-permute-start | bytes 196616 | tf_op jit(solution)/shard_map/ppermute | solution.py:42
  77.1 5.2 %collective-permute-done.15 = bf16[64,512]{1,0:T(8,128)(2,1)S(1)} collective-permute-done((bf16[64,512]{1,0:T(8,128)(2,1)S(1)}, bf16[64,512]{1,0:T(8,128)(2,1)S(1)}, u32[]{:S(2)}, u32[]{:S(2)}) %collective-permute-start.15) | collective-permute-done | bytes 65568 | tf_op jit(solution)/shard_map/ppermute | solution.py:42
  82.3 1.7 %collective-permute-start.19 = (bf16[272,512]{1,0:T(8,128)(2,1)S(1)}, bf16[272,512]{1,0:T(8,128)(2,1)S(1)}, u32[]{:S(2)}, u32[]{:S(2)}) collective-permute-start(bf16[272,512]{1,0:T(8,128)(2,1)S(1)} %constant_dynamic-update-slice_fusion.4.refs_0_), channel_id=1, source_target_pairs={{0,24},{8,16},{16,8},{24,0},{1,25},{9,17},{17,9},{25,1},{2,26},{10... | collective-permute-start | bytes 835592 | tf_op jit(solution)/shard_map/ppermute | solution.py:42
  84.7 1.2 collective-permute-start.17
  87.7 2.5 %collective-permute-done.19.refs_3_ = bf16[272,512]{1,0:T(8,128)(2,1)S(1)} collective-permute-done((bf16[272,512]{1,0:T(8,128)(2,1)S(1)}, bf16[272,512]{1,0:T(8,128)(2,1)S(1)}, u32[]{:S(2)}, u32[]{:S(2)}) %collective-permute-start.19) | collective-permute-done | bytes 278560 | tf_op jit(solution)/shard_map/ppermute | solution.py:42
  90.2 2.9 %collective-permute-done.18.refs_2_ = bf16[272,512]{1,0:T(8,128)(2,1)S(1)} collective-permute-done((bf16[272,512]{1,0:T(8,128)(2,1)S(1)}, bf16[272,512]{1,0:T(8,128)(2,1)S(1)}, u32[]{:S(2)}, u32[]{:S(2)}) %collective-permute-start.18) | collective-permute-done | bytes 278560 | tf_op jit(solution)/shard_map/ppermute | solution.py:42
  94.1 0.9 collective-permute-done.27
  95.3 8.0 %experts.1 = (bf16[272,512]{1,0:T(8,128)(2,1)S(1)}, bf16[272,512]{1,0:T(8,128)(2,1)S(1)}, bf16[272,512]{1,0:T(8,128)(2,1)S(1)}, bf16[272,512]{1,0:T(8,128)(2,1)S...) custom-call(s32[1]{0:T(128)} %bitcast.head_ref, ...), custom_call_target="tpu_custom_call" | custom-call | tf_op jit(solution)/shard_map/experts/pallas_call | solution.py:364
  109.3 1.0 add_convert_fusion.3
  110.4 1.1 collective-permute-start.30
  111.5 1.1 add_convert_fusion.2
  112.5 0.9 collective-permute-start.32
  113.5 1.7 %collective-permute-start.34 = (bf16[272,512]{1,0:T(8,128)(2,1)S(1)}, bf16[272,512]{1,0:T(8,128)(2,1)S(1)}, u32[]{:S(2)}, u32[]{:S(2)}) collective-permute-start(bf16[272,512]{1,0:T(8,128)(2,1)S(1)} %add_convert_fusion.1), channel_id=1, source_target_pairs={{0,24},{8,16},{16,8},{24,0},{1,25},{9,17},{17,9},{25,1},{2,26},{10... | collective-permute-start | bytes 835592 | tf_op jit(solution)/shard_map/ppermute | solution.py:42
  116.6 3.4 %collective-permute-done.30 = bf16[272,512]{1,0:T(8,128)(2,1)S(1)} collective-permute-done((bf16[272,512]{1,0:T(8,128)(2,1)S(1)}, bf16[272,512]{1,0:T(8,128)(2,1)S(1)}, u32[]{:S(2)}, u32[]{:S(2)}) %collective-permute-start.30) | collective-permute-done | bytes 278560 | tf_op jit(solution)/shard_map/ppermute | solution.py:42
  119.9 7.1 %collective-permute-done.32 = bf16[272,512]{1,0:T(8,128)(2,1)S(1)} collective-permute-done((bf16[272,512]{1,0:T(8,128)(2,1)S(1)}, bf16[272,512]{1,0:T(8,128)(2,1)S(1)}, u32[]{:S(2)}, u32[]{:S(2)}) %collective-permute-start.32) | collective-permute-done | bytes 278560 | tf_op jit(solution)/shard_map/ppermute | solution.py:42
  127.2 1.5 %collective-permute-start.37 = (bf16[80,512]{1,0:T(8,128)(2,1)S(1)}, bf16[80,512]{1,0:T(8,128)(2,1)S(1)}, u32[]{:S(2)}, u32[]{:S(2)}) collective-permute-start(bf16[80,512]{1,0:T(8,128)(2,1)S(1)} %concatenate.62), channel_id=1, source_target_pairs={{0,6},{1,7},{2,4},{3,5},{4,2},{5,3},{6,0},{7,1},{8,14},{9,15},{10,... | collective-permute-start | bytes 245768 | tf_op jit(solution)/shard_map/ppermute | solution.py:42
  128.8 3.0 %collective-permute-start.36 = (bf16[80,512]{1,0:T(8,128)(2,1)S(1)}, bf16[80,512]{1,0:T(8,128)(2,1)S(1)}, u32[]{:S(2)}, u32[]{:S(2)}) collective-permute-start(bf16[80,512]{1,0:T(8,128)(2,1)S(1)} %get-tuple-element.70), channel_id=1, source_target_pairs={{0,4},{1,5},{2,6},{3,7},{4,0},{5,1},{6,2},{7,3},{8,12},{9,13},{10,... | collective-permute-start | bytes 245768 | tf_op jit(solution)/shard_map/ppermute | solution.py:42
  132.4 1.9 %collective-permute-done.37 = bf16[80,512]{1,0:T(8,128)(2,1)S(1)} collective-permute-done((bf16[80,512]{1,0:T(8,128)(2,1)S(1)}, bf16[80,512]{1,0:T(8,128)(2,1)S(1)}, u32[]{:S(2)}, u32[]{:S(2)}) %collective-permute-start.37) | collective-permute-done | bytes 81952 | tf_op jit(solution)/shard_map/ppermute | solution.py:42
  134.3 2.1 %collective-permute-done.36 = bf16[80,512]{1,0:T(8,128)(2,1)S(1)} collective-permute-done((bf16[80,512]{1,0:T(8,128)(2,1)S(1)}, bf16[80,512]{1,0:T(8,128)(2,1)S(1)}, u32[]{:S(2)}, u32[]{:S(2)}) %collective-permute-start.36) | collective-permute-done | bytes 81952 | tf_op jit(solution)/shard_map/ppermute | solution.py:42
  (155 shorter events, 22.8 us)
Async XLA Ops:
  6.2 8.9 %copy-start.10 = (s32[8]{0:T(128)S(1)}, s32[8]{0:T(128)}, u32[]{:S(2)}) copy-start(s32[8]{0:T(128)} %owner_ref.1) | copy-start | bytes 100
  9.1 11.1 %copy-start.15 = (bf16[80,4,64]{2,1,0:T(4,128)(2,1)}, bf16[80,4,64]{2,1,0:T(4,128)(2,1)S(1)}, u32[]{:S(2)}) copy-start(bf16[80,4,64]{2,1,0:T(4,128)(2,1)S(1)} %get-tuple-element.59) | copy-start | bytes 122884
  9.1 11.1 %copy-start.17 = (bf16[80,4,64]{2,1,0:T(4,128)(2,1)}, bf16[80,4,64]{2,1,0:T(4,128)(2,1)S(1)}, u32[]{:S(2)}) copy-start(bf16[80,4,64]{2,1,0:T(4,128)(2,1)S(1)} %get-tuple-element.60) | copy-start | bytes 122884
  9.3 10.7 %collective-permute-start.2 = (bf16[64,512]{1,0:T(8,128)(2,1)S(1)}, bf16[64,512]{1,0:T(8,128)(2,1)S(1)}, u32[]{:S(2)}, u32[]{:S(2)}) collective-permute-start(bf16[64,512]{1,0:T(8,128)(2,1)S(1)} %bitcast.39), channel_id=1, source_target_pairs={{0,6},{1,7},{2,4},{3,5},{4,2},{5,3},{6,0},{7,1},{8,14},{9,15},{10,... | collective-permute-start | bytes 196616 | tf_op jit(solution)/shard_map/ppermute | solution.py:42
  14.4 5.6 %collective-permute-start.1 = (bf16[64,512]{1,0:T(8,128)(2,1)S(1)}, bf16[64,512]{1,0:T(8,128)(2,1)S(1)}, u32[]{:S(2)}, u32[]{:S(2)}) collective-permute-start(bf16[64,512]{1,0:T(8,128)(2,1)S(1)} %bitcast.40), channel_id=1, source_target_pairs={{0,4},{1,5},{2,6},{3,7},{4,0},{5,1},{6,2},{7,3},{8,12},{9,13},{10,... | collective-permute-start | bytes 196616 | tf_op jit(solution)/shard_map/ppermute | solution.py:42
  14.4 4.3 %collective-permute-start = (bf16[64,512]{1,0:T(8,128)(2,1)S(1)}, bf16[64,512]{1,0:T(8,128)(2,1)S(1)}, u32[]{:S(2)}, u32[]{:S(2)}) collective-permute-start(bf16[64,512]{1,0:T(8,128)(2,1)S(1)} %bitcast.41), channel_id=1, source_target_pairs={{0,2},{1,3},{2,0},{3,1},{4,6},{5,7},{6,4},{7,5},{8,10},{9,11},{10,... | collective-permute-start | bytes 196616 | tf_op jit(solution)/shard_map/ppermute | solution.py:42
  17.4 20.7 %copy-start.19 = (bf16[80,512]{1,0:T(8,128)(2,1)}, bf16[80,512]{1,0:T(8,128)(2,1)S(1)}, u32[]{:S(2)}) copy-start(bf16[80,512]{1,0:T(8,128)(2,1)S(1)} %convolution_convert_fusion) | copy-start | bytes 245764
  20.1 1.6 %collective-permute-start.3 = (bf16[256,512]{1,0:T(8,128)(2,1)S(1)}, bf16[256,512]{1,0:T(8,128)(2,1)S(1)}, u32[]{:S(2)}, u32[]{:S(2)}) collective-permute-start(bf16[256,512]{1,0:T(8,128)(2,1)S(1)} %constant_dynamic-update-slice_fusion.query_a), channel_id=1, source_target_pairs={{0,1},{1,0},{2,3},{3,2},{4,5},{5,4},{6,7},{7,6},{8,9},{9,8},{10,11... | collective-permute-start | bytes 786440 | tf_op jit(solution)/shard_map/ppermute | solution.py:42
  38.1 2.2 %collective-permute-start.4 = (f32[272,640]{1,0:T(8,128)S(1)}, f32[272,640]{1,0:T(8,128)S(1)}, u32[]{:S(2)}, u32[]{:S(2)}) collective-permute-start(f32[272,640]{1,0:T(8,128)S(1)} %get-tuple-element.23), channel_id=1, source_target_pairs={{0,1},{1,0},{2,3},{3,2},{4,5},{5,4},{6,7},{7,6},{8,9},{9,8},{10,11... | collective-permute-start | bytes 2088968 | tf_op jit(solution)/shard_map/ppermute | solution.py:42
  41.2 6.2 %collective-permute-start.5 = (bf16[80,640]{1,0:T(8,128)(2,1)S(1)}, bf16[80,640]{1,0:T(8,128)(2,1)S(1)}, u32[]{:S(2)}, u32[]{:S(2)}) collective-permute-start(bf16[80,640]{1,0:T(8,128)(2,1)S(1)} %get-tuple-element.25), channel_id=1, source_target_pairs={{0,2},{1,3},{2,0},{3,1},{4,6},{5,7},{6,4},{7,5},{8,10},{9,11},{10,... | collective-permute-start | bytes 307208 | tf_op jit(solution)/shard_map/ppermute | solution.py:42
  41.3 11.1 %collective-permute-start.6 = (bf16[80,640]{1,0:T(8,128)(2,1)S(1)}, bf16[80,640]{1,0:T(8,128)(2,1)S(1)}, u32[]{:S(2)}, u32[]{:S(2)}) collective-permute-start(bf16[80,640]{1,0:T(8,128)(2,1)S(1)} %get-tuple-element.26), channel_id=1, source_target_pairs={{0,4},{1,5},{2,6},{3,7},{4,0},{5,1},{6,2},{7,3},{8,12},{9,13},{10,... | collective-permute-start | bytes 307208 | tf_op jit(solution)/shard_map/ppermute | solution.py:42
  42.3 10.1 %collective-permute-start.7 = (bf16[80,640]{1,0:T(8,128)(2,1)S(1)}, bf16[80,640]{1,0:T(8,128)(2,1)S(1)}, u32[]{:S(2)}, u32[]{:S(2)}) collective-permute-start(bf16[80,640]{1,0:T(8,128)(2,1)S(1)} %get-tuple-element.27), channel_id=1, source_target_pairs={{0,6},{1,7},{2,4},{3,5},{4,2},{5,3},{6,0},{7,1},{8,14},{9,15},{10,... | collective-permute-start | bytes 307208 | tf_op jit(solution)/shard_map/ppermute | solution.py:42
  54.9 8.4 %collective-permute-start.8 = (f32[80,512]{1,0:T(8,128)S(1)}, f32[80,512]{1,0:T(8,128)S(1)}, u32[]{:S(2)}, u32[]{:S(2)}) collective-permute-start(f32[80,512]{1,0:T(8,128)S(1)} %get-tuple-element.29), channel_id=1, source_target_pairs={{0,8},{8,0},{16,24},{24,16},{1,9},{9,1},{17,25},{25,17},{2,10},{10... | collective-permute-start | bytes 491528 | tf_op jit(solution)/shard_map/ppermute | solution.py:42
  56.5 8.5 %collective-permute-start.9 = (f32[80,512]{1,0:T(8,128)S(1)}, f32[80,512]{1,0:T(8,128)S(1)}, u32[]{:S(2)}, u32[]{:S(2)}) collective-permute-start(f32[80,512]{1,0:T(8,128)S(1)} %get-tuple-element.30), channel_id=1, source_target_pairs={{0,16},{8,24},{16,0},{24,8},{1,17},{9,25},{17,1},{25,9},{2,18},{10... | collective-permute-start | bytes 491528 | tf_op jit(solution)/shard_map/ppermute | solution.py:42
  58.0 7.0 %collective-permute-start.10 = (f32[80,512]{1,0:T(8,128)S(1)}, f32[80,512]{1,0:T(8,128)}, u32[]{:S(2)}, u32[]{:S(2)}) collective-permute-start(f32[80,512]{1,0:T(8,128)S(1)} %get-tuple-element.31), channel_id=1, source_target_pairs={{0,24},{8,16},{16,8},{24,0},{1,25},{9,17},{17,9},{25,1},{2,26},{10... | collective-permute-start | bytes 491528 | tf_op jit(solution)/shard_map/ppermute | solution.py:42
  59.8 27.6 %collective-permute-start.26 = (bf16[64,16]{0,1:T(8,128)(2,1)S(1)}, bf16[64,16]{0,1:T(8,128)(2,1)S(1)}, u32[]{:S(2)}, u32[]{:S(2)}) collective-permute-start(bf16[64,16]{0,1:T(8,128)(2,1)S(1)} %select_reduce_fusion), channel_id=1, source_target_pairs={{0,6},{1,7},{2,4},{3,5},{4,2},{5,3},{6,0},{7,1},{8,14},{9,15},{10,... | collective-permute-start | bytes 6152 | tf_op jit(solution)/shard_map/ppermute | solution.py:42
  61.3 26.4 %collective-permute-start.25 = (bf16[64,16]{0,1:T(8,128)(2,1)S(1)}, bf16[64,16]{0,1:T(8,128)(2,1)S(1)}, u32[]{:S(2)}, u32[]{:S(2)}) collective-permute-start(bf16[64,16]{0,1:T(8,128)(2,1)S(1)} %select_reduce_fusion), channel_id=1, source_target_pairs={{0,4},{1,5},{2,6},{3,7},{4,0},{5,1},{6,2},{7,3},{8,12},{9,13},{10,... | collective-permute-start | bytes 6152 | tf_op jit(solution)/shard_map/ppermute | solution.py:42
  66.0 16.2 %copy-start.13 = (f32[80,512]{1,0:T(8,128)}, f32[80,512]{1,0:T(8,128)S(1)}, u32[]{:S(2)}) copy-start(f32[80,512]{1,0:T(8,128)S(1)} %get-tuple-element.53) | copy-start | bytes 491524
  66.1 4.3 %collective-permute-start.12 = (f32[1,80]{1,0:T(1,128)S(1)}, f32[1,80]{1,0:T(1,128)S(1)}, u32[]{:S(2)}, u32[]{:S(2)}) collective-permute-start(f32[1,80]{1,0:T(1,128)S(1)} %bitcast.42), channel_id=1, source_target_pairs={{0,16},{8,24},{16,0},{24,8},{1,17},{9,25},{17,1},{25,9},{2,18},{10... | collective-permute-start | bytes 968 | tf_op jit(solution)/shard_map/ppermute | solution.py:42
  67.1 4.4 %collective-permute-start.13 = (f32[1,80]{1,0:T(1,128)S(1)}, f32[1,80]{1,0:T(1,128)S(1)}, u32[]{:S(2)}, u32[]{:S(2)}) collective-permute-start(f32[1,80]{1,0:T(1,128)S(1)} %bitcast.43), channel_id=1, source_target_pairs={{0,24},{8,16},{16,8},{24,0},{1,25},{9,17},{17,9},{25,1},{2,26},{10... | collective-permute-start | bytes 968 | tf_op jit(solution)/shard_map/ppermute | solution.py:42
  68.3 3.5 %collective-permute-start.11 = (f32[1,80]{1,0:T(1,128)S(1)}, f32[1,80]{1,0:T(1,128)S(1)}, u32[]{:S(2)}, u32[]{:S(2)}) collective-permute-start(f32[1,80]{1,0:T(1,128)S(1)} %bitcast.44), channel_id=1, source_target_pairs={{0,8},{8,0},{16,24},{24,16},{1,9},{9,1},{17,25},{25,17},{2,10},{10... | collective-permute-start | bytes 968 | tf_op jit(solution)/shard_map/ppermute | solution.py:42
  71.9 5.1 %collective-permute-start.14 = (bf16[64,512]{1,0:T(8,128)(2,1)S(1)}, bf16[64,512]{1,0:T(8,128)(2,1)S(1)}, u32[]{:S(2)}, u32[]{:S(2)}) collective-permute-start(bf16[64,512]{1,0:T(8,128)(2,1)S(1)} %get-tuple-element.65), channel_id=1, source_target_pairs={{0,2},{1,3},{2,0},{3,1},{4,6},{5,7},{6,4},{7,5},{8,10},{9,11},{10,... | collective-permute-start | bytes 196616 | tf_op jit(solution)/shard_map/ppermute | solution.py:42
  74.8 7.5 %collective-permute-start.16 = (bf16[64,512]{1,0:T(8,128)(2,1)S(1)}, bf16[64,512]{1,0:T(8,128)(2,1)S(1)}, u32[]{:S(2)}, u32[]{:S(2)}) collective-permute-start(bf16[64,512]{1,0:T(8,128)(2,1)S(1)} %get-tuple-element.65), channel_id=1, source_target_pairs={{0,6},{1,7},{2,4},{3,5},{4,2},{5,3},{6,0},{7,1},{8,14},{9,15},{10,... | collective-permute-start | bytes 196616 | tf_op jit(solution)/shard_map/ppermute | solution.py:42
  76.1 6.1 %collective-permute-start.15 = (bf16[64,512]{1,0:T(8,128)(2,1)S(1)}, bf16[64,512]{1,0:T(8,128)(2,1)S(1)}, u32[]{:S(2)}, u32[]{:S(2)}) collective-permute-start(bf16[64,512]{1,0:T(8,128)(2,1)S(1)} %get-tuple-element.65), channel_id=1, source_target_pairs={{0,4},{1,5},{2,6},{3,7},{4,0},{5,1},{6,2},{7,3},{8,12},{9,13},{10,... | collective-permute-start | bytes 196616 | tf_op jit(solution)/shard_map/ppermute | solution.py:42
  82.3 7.9 %collective-permute-start.19 = (bf16[272,512]{1,0:T(8,128)(2,1)S(1)}, bf16[272,512]{1,0:T(8,128)(2,1)S(1)}, u32[]{:S(2)}, u32[]{:S(2)}) collective-permute-start(bf16[272,512]{1,0:T(8,128)(2,1)S(1)} %constant_dynamic-update-slice_fusion.4.refs_0_), channel_id=1, source_target_pairs={{0,24},{8,16},{16,8},{24,0},{1,25},{9,17},{17,9},{25,1},{2,26},{10... | collective-permute-start | bytes 835592 | tf_op jit(solution)/shard_map/ppermute | solution.py:42
  84.0 9.1 %collective-permute-start.18 = (bf16[272,512]{1,0:T(8,128)(2,1)S(1)}, bf16[272,512]{1,0:T(8,128)(2,1)S(1)}, u32[]{:S(2)}, u32[]{:S(2)}) collective-permute-start(bf16[272,512]{1,0:T(8,128)(2,1)S(1)} %constant_dynamic-update-slice_fusion.4.refs_0_), channel_id=1, source_target_pairs={{0,16},{8,24},{16,0},{24,8},{1,17},{9,25},{17,1},{25,9},{2,18},{10... | collective-permute-start | bytes 835592 | tf_op jit(solution)/shard_map/ppermute | solution.py:42
  84.7 8.4 %collective-permute-start.17 = (bf16[272,512]{1,0:T(8,128)(2,1)S(1)}, bf16[272,512]{1,0:T(8,128)(2,1)S(1)}, u32[]{:S(2)}, u32[]{:S(2)}) collective-permute-start(bf16[272,512]{1,0:T(8,128)(2,1)S(1)} %constant_dynamic-update-slice_fusion.4.refs_0_), channel_id=1, source_target_pairs={{0,8},{8,0},{16,24},{24,16},{1,9},{9,1},{17,25},{25,17},{2,10},{10... | collective-permute-start | bytes 835592 | tf_op jit(solution)/shard_map/ppermute | solution.py:42
  87.4 6.1 %collective-permute-start.24 = (bf16[64,16]{0,1:T(8,128)(2,1)S(1)}, bf16[64,16]{0,1:T(8,128)(2,1)S(1)}, u32[]{:S(2)}, u32[]{:S(2)}) collective-permute-start(bf16[64,16]{0,1:T(8,128)(2,1)S(1)} %select_reduce_fusion), channel_id=1, source_target_pairs={{0,2},{1,3},{2,0},{3,1},{4,6},{5,7},{6,4},{7,5},{8,10},{9,11},{10,... | collective-permute-start | bytes 6152 | tf_op jit(solution)/shard_map/ppermute | solution.py:42
  87.7 7.6 %collective-permute-start.20 = (bf16[272,512]{1,0:T(8,128)(2,1)S(1)}, bf16[272,512]{1,0:T(8,128)(2,1)}, u32[]{:S(2)}, u32[]{:S(2)}) collective-permute-start(bf16[272,512]{1,0:T(8,128)(2,1)S(1)} %constant_dynamic-update-slice_fusion.4.refs_0_), channel_id=1, source_target_pairs={{0,1},{1,0},{2,3},{3,2},{4,5},{5,4},{6,7},{7,6},{8,9},{9,8},{10,11... | collective-permute-start | bytes 835592 | tf_op jit(solution)/shard_map/ppermute | solution.py:42
  90.2 5.1 %collective-permute-start.23 = (bf16[272,512]{1,0:T(8,128)(2,1)S(1)}, bf16[272,512]{1,0:T(8,128)(2,1)}, u32[]{:S(2)}, u32[]{:S(2)}) collective-permute-start(bf16[272,512]{1,0:T(8,128)(2,1)S(1)} %collective-permute-done.19.refs_3_), channel_id=1, source_target_pairs={{0,1},{1,0},{2,3},{3,2},{4,5},{5,4},{6,7},{7,6},{8,9},{9,8},{10,11... | collective-permute-start | bytes 835592 | tf_op jit(solution)/shard_map/ppermute | solution.py:42
  93.1 2.3 %collective-permute-start.22 = (bf16[272,512]{1,0:T(8,128)(2,1)S(1)}, bf16[272,512]{1,0:T(8,128)(2,1)}, u32[]{:S(2)}, u32[]{:S(2)}) collective-permute-start(bf16[272,512]{1,0:T(8,128)(2,1)S(1)} %collective-permute-done.18.refs_2_), channel_id=1, source_target_pairs={{0,1},{1,0},{2,3},{3,2},{4,5},{5,4},{6,7},{7,6},{8,9},{9,8},{10,11... | collective-permute-start | bytes 835592 | tf_op jit(solution)/shard_map/ppermute | solution.py:42
  93.1 2.3 %collective-permute-start.21 = (bf16[272,512]{1,0:T(8,128)(2,1)S(1)}, bf16[272,512]{1,0:T(8,128)(2,1)}, u32[]{:S(2)}, u32[]{:S(2)}) collective-permute-start(bf16[272,512]{1,0:T(8,128)(2,1)S(1)} %collective-permute-done.17.refs_1_), channel_id=1, source_target_pairs={{0,1},{1,0},{2,3},{3,2},{4,5},{5,4},{6,7},{7,6},{8,9},{9,8},{10,11... | collective-permute-start | bytes 835592 | tf_op jit(solution)/shard_map/ppermute | solution.py:42
  93.8 1.3 collective-permute-start.27
  95.3 12.8 %copy-start.16 = (bf16[80,4,64]{2,1,0:T(4,128)(2,1)S(1)}, bf16[80,4,64]{2,1,0:T(4,128)(2,1)}, u32[]{:S(2)}) copy-start(bf16[80,4,64]{2,1,0:T(4,128)(2,1)} %copy-done.15) | copy-start | bytes 122884
  95.3 12.8 %copy-start.18 = (bf16[80,4,64]{2,1,0:T(4,128)(2,1)S(1)}, bf16[80,4,64]{2,1,0:T(4,128)(2,1)}, u32[]{:S(2)}) copy-start(bf16[80,4,64]{2,1,0:T(4,128)(2,1)} %copy-done.17) | copy-start | bytes 122884
  107.6 19.4 %copy-start.5 = (bf16[272,512]{1,0:T(8,128)(2,1)S(1)}, bf16[272,512]{1,0:T(8,128)(2,1)}, u32[]{:S(2)}) copy-start(bf16[272,512]{1,0:T(8,128)(2,1)} %copy-done.4) | copy-start | bytes 835588
  107.6 1.8 %collective-permute-start.29 = (bf16[272,512]{1,0:T(8,128)(2,1)}, bf16[272,512]{1,0:T(8,128)(2,1)S(1)}, u32[]{:S(2)}, u32[]{:S(2)}) collective-permute-start(bf16[272,512]{1,0:T(8,128)(2,1)} %get-tuple-element.35), channel_id=1, source_target_pairs={{0,1},{1,0},{2,3},{3,2},{4,5},{5,4},{6,7},{7,6},{8,9},{9,8},{10,11... | collective-permute-start | bytes 835592 | tf_op jit(solution)/shard_map/ppermute | solution.py:42
  107.7 3.7 %collective-permute-start.31 = (bf16[272,512]{1,0:T(8,128)(2,1)}, bf16[272,512]{1,0:T(8,128)(2,1)S(1)}, u32[]{:S(2)}, u32[]{:S(2)}) collective-permute-start(bf16[272,512]{1,0:T(8,128)(2,1)} %get-tuple-element.37), channel_id=1, source_target_pairs={{0,1},{1,0},{2,3},{3,2},{4,5},{5,4},{6,7},{7,6},{8,9},{9,8},{10,11... | collective-permute-start | bytes 835592 | tf_op jit(solution)/shard_map/ppermute | solution.py:42
  108.2 8.4 %collective-permute-start.28 = (bf16[272,512]{1,0:T(8,128)(2,1)}, bf16[272,512]{1,0:T(8,128)(2,1)S(1)}, u32[]{:S(2)}, u32[]{:S(2)}) collective-permute-start(bf16[272,512]{1,0:T(8,128)(2,1)} %copy-done.11), channel_id=1, source_target_pairs={{0,1},{1,0},{2,3},{3,2},{4,5},{5,4},{6,7},{7,6},{8,9},{9,8},{10,11... | collective-permute-start | bytes 835592 | tf_op jit(solution)/shard_map/ppermute | solution.py:42
  108.4 5.0 %collective-permute-start.33 = (bf16[272,512]{1,0:T(8,128)(2,1)}, bf16[272,512]{1,0:T(8,128)(2,1)S(1)}, u32[]{:S(2)}, u32[]{:S(2)}) collective-permute-start(bf16[272,512]{1,0:T(8,128)(2,1)} %copy-done.12), channel_id=1, source_target_pairs={{0,1},{1,0},{2,3},{3,2},{4,5},{5,4},{6,7},{7,6},{8,9},{9,8},{10,11... | collective-permute-start | bytes 835592 | tf_op jit(solution)/shard_map/ppermute | solution.py:42
  110.4 9.6 %collective-permute-start.30 = (bf16[272,512]{1,0:T(8,128)(2,1)S(1)}, bf16[272,512]{1,0:T(8,128)(2,1)S(1)}, u32[]{:S(2)}, u32[]{:S(2)}) collective-permute-start(bf16[272,512]{1,0:T(8,128)(2,1)S(1)} %add_convert_fusion.3), channel_id=1, source_target_pairs={{0,8},{8,0},{16,24},{24,16},{1,9},{9,1},{17,25},{25,17},{2,10},{10... | collective-permute-start | bytes 835592 | tf_op jit(solution)/shard_map/ppermute | solution.py:42
  111.5 20.3 %copy-start.20 = (bf16[1,64,512]{2,1,0:T(8,128)(2,1)S(1)}, bf16[1,64,512]{2,1,0:T(8,128)(2,1)}, u32[]{:S(2)}) copy-start(bf16[1,64,512]{2,1,0:T(8,128)(2,1)} %get-tuple-element.63) | copy-start | bytes 196612
  112.5 23.9 %copy-start.14 = (f32[80,512]{1,0:T(8,128)S(1)}, f32[80,512]{1,0:T(8,128)}, u32[]{:S(2)}) copy-start(f32[80,512]{1,0:T(8,128)} %copy-done.13) | copy-start | bytes 491524
  112.5 14.5 %collective-permute-start.32 = (bf16[272,512]{1,0:T(8,128)(2,1)S(1)}, bf16[272,512]{1,0:T(8,128)(2,1)S(1)}, u32[]{:S(2)}, u32[]{:S(2)}) collective-permute-start(bf16[272,512]{1,0:T(8,128)(2,1)S(1)} %add_convert_fusion.2), channel_id=1, source_target_pairs={{0,16},{8,24},{16,0},{24,8},{1,17},{9,25},{17,1},{25,9},{2,18},{10... | collective-permute-start | bytes 835592 | tf_op jit(solution)/shard_map/ppermute | solution.py:42
  113.5 13.5 %collective-permute-start.34 = (bf16[272,512]{1,0:T(8,128)(2,1)S(1)}, bf16[272,512]{1,0:T(8,128)(2,1)S(1)}, u32[]{:S(2)}, u32[]{:S(2)}) collective-permute-start(bf16[272,512]{1,0:T(8,128)(2,1)S(1)} %add_convert_fusion.1), channel_id=1, source_target_pairs={{0,24},{8,16},{16,8},{24,0},{1,25},{9,17},{17,9},{25,1},{2,26},{10... | collective-permute-start | bytes 835592 | tf_op jit(solution)/shard_map/ppermute | solution.py:42
  127.2 7.1 %collective-permute-start.37 = (bf16[80,512]{1,0:T(8,128)(2,1)S(1)}, bf16[80,512]{1,0:T(8,128)(2,1)S(1)}, u32[]{:S(2)}, u32[]{:S(2)}) collective-permute-start(bf16[80,512]{1,0:T(8,128)(2,1)S(1)} %concatenate.62), channel_id=1, source_target_pairs={{0,6},{1,7},{2,4},{3,5},{4,2},{5,3},{6,0},{7,1},{8,14},{9,15},{10,... | collective-permute-start | bytes 245768 | tf_op jit(solution)/shard_map/ppermute | solution.py:42
  128.7 5.6 %collective-permute-start.35 = (bf16[80,512]{1,0:T(8,128)(2,1)S(1)}, bf16[80,512]{1,0:T(8,128)(2,1)S(1)}, u32[]{:S(2)}, u32[]{:S(2)}) collective-permute-start(bf16[80,512]{1,0:T(8,128)(2,1)S(1)} %get-tuple-element.69), channel_id=1, source_target_pairs={{0,2},{1,3},{2,0},{3,1},{4,6},{5,7},{6,4},{7,5},{8,10},{9,11},{10,... | collective-permute-start | bytes 245768 | tf_op jit(solution)/shard_map/ppermute | solution.py:42
  128.8 7.6 %collective-permute-start.36 = (bf16[80,512]{1,0:T(8,128)(2,1)S(1)}, bf16[80,512]{1,0:T(8,128)(2,1)S(1)}, u32[]{:S(2)}, u32[]{:S(2)}) collective-permute-start(bf16[80,512]{1,0:T(8,128)(2,1)S(1)} %get-tuple-element.70), channel_id=1, source_target_pairs={{0,4},{1,5},{2,6},{3,7},{4,0},{5,1},{6,2},{7,3},{8,12},{9,13},{10,... | collective-permute-start | bytes 245768 | tf_op jit(solution)/shard_map/ppermute | solution.py:42
  (14 other events, 42.3 us)

commit v2 on v0

v2 whole, which is shorter than its diff:
```python
import functools

import jax
import jax.numpy as jnp
from jax import lax
from jax.experimental import pallas as pl
from jax.experimental.pallas import tpu as pltpu
from jax.sharding import PartitionSpec as P

HD = 128
PRE = 1
DEC = 12
REQS = 13
DPAD = 16
TILE = 256

eps_norm = 1e-06
rope_base = 50000.0
neg_fill = -1e30
bf16 = jnp.bfloat16
f32 = jnp.float32


def swap(value, axis, mask):
    count = lax.axis_size(axis)
    return lax.ppermute(value, axis, [(i, i ^ mask) for i in range(count)])


def span(index, size):
    return pl.ds(pl.multiple_of(index * size, size), size)


def lanes(head):
    return slice(head * HD, (head + 1) * HD)


def tree_sum(values):
    values = list(values)
    while len(values) > 1:
        values = [a + b for a, b in zip(values[::2], values[1::2])]
    return values[0]


VMEM = pl.BlockSpec(memory_space=pltpu.VMEM)
SMEM = pl.BlockSpec(memory_space=pltpu.SMEM)
HBM = pl.BlockSpec(memory_space=pltpu.HBM)


def call(body, outs, ins, args, name, limit, scratch=(), cost=None):
    args = [
        pltpu.with_memory_space_constraint(arg, pltpu.HBM) if spec is HBM else arg
        for spec, arg in zip(ins, args)
    ]
    return pl.pallas_call(
        body,
        out_shape=tuple(jax.ShapeDtypeStruct(shape, dtype) for shape, dtype in outs),
        in_specs=list(ins),
        out_specs=tuple(VMEM for _ in outs),
        scratch_shapes=list(scratch),
        compiler_params=pltpu.CompilerParams(vmem_limit_bytes=limit << 20),
        cost_estimate=cost,
        name=name,
    )(*args)


def turn(flat, cosine, sine):
    heads = []
    for head in range(flat.shape[1] // HD):
        block = flat[:, lanes(head)]
        heads.append(block * cosine + pltpu.roll(block, HD // 2, 1) * sine)
    return jnp.concatenate(heads, axis=1).astype(bf16)


def gate_lanes(ids, gates, width):
    names = ids[...]
    values = gates[...].astype(f32)
    place = lax.broadcasted_iota(jnp.int32, (width, names.shape[1]), 0)
    table = jnp.zeros(place.shape, f32)
    for k in range(names.shape[0]):
        table = jnp.where(place == names[k : k + 1], values[k : k + 1], table)
    shape = (width, width)
    eye = lax.broadcasted_iota(jnp.int32, shape, 0) == lax.broadcasted_iota(jnp.int32, shape, 1)
    return lax.dot_general(
        table.astype(bf16),
        eye.astype(f32).astype(bf16),
        (((0,), (0,)), ((), ())),
        preferred_element_type=f32,
    ).astype(bf16)


def query_kernel(
    pre, dec, gain, weight_hbm, cosine, sine, ids, gates, dec_ids, dec_gates,
    message, query_d, table_d, normed, weight, sem,
):
    copy = pltpu.make_async_copy(weight_hbm, weight, sem)
    copy.start()
    tok = pre.shape[0]
    width = weight.shape[1]

    def norm(rows):
        values = rows.astype(f32)
        meansq = jnp.mean(values * values, axis=-1, keepdims=True)
        return (values * lax.rsqrt(meansq + eps_norm) * gain[...]).astype(bf16)

    normed[0:tok, :] = norm(pre[...])
    normed[tok:, :] = jnp.zeros_like(normed[tok:, :])
    normed[tok : tok + DEC, :] = norm(dec[...])
    message[:, width:] = gate_lanes(ids, gates, message.shape[1] - width)
    table_d[...] = jnp.zeros_like(table_d)
    table_d[0:DEC, :] = gate_lanes(dec_ids, dec_gates, table_d.shape[1])
    copy.wait()
    query = jnp.dot(normed[...], weight[...], preferred_element_type=f32)
    query = turn(query, cosine[...], sine[...])
    message[:, :width] = query[:tok]
    query_d[...] = query[tok:]


def key_kernel(
    normed, key_hbm, value_hbm, cosine, sine, new, dec, key_d, value_d, w_key, w_value, sems
):
    tok = new.shape[1]
    copies = [
        pltpu.make_async_copy(key_hbm, w_key, sems.at[0]),
        pltpu.make_async_copy(value_hbm, w_value, sems.at[1]),
    ]
    for copy in copies:
        copy.start()
    for copy in copies:
        copy.wait()
    key = turn(jnp.dot(normed[...], w_key[...], preferred_element_type=f32), cosine[...], sine[...])
    value = jnp.dot(normed[...], w_value[...], preferred_element_type=f32).astype(bf16)
    for index, (rows, padded) in enumerate(((key, key_d), (value, value_d))):
        new[index] = rows[:tok]
        dec[index] = rows[tok : tok + DEC]
        padded[...] = rows[tok:]


def group(query, keys, values, live):
    scores = lax.dot_general(
        query, keys, (((1,), (1,)), ((), ())), preferred_element_type=f32
    ) * HD ** (-0.5)
    top = jnp.max(jnp.where(live, scores, neg_fill), axis=-1, keepdims=True)
    weights = jnp.where(live, jnp.exp(scores - top), 0.0)
    total = jnp.sum(weights, axis=-1, keepdims=True)
    acc = jnp.dot(weights.astype(bf16), values, preferred_element_type=f32)
    return top, total, acc


def group_turned(query, keys, values, live):
    scores = lax.dot_general(
        keys, query, (((1,), (1,)), ((), ())), preferred_element_type=f32
    ) * HD ** (-0.5)
    top = jnp.max(
        scores if live is None else jnp.where(live, scores, neg_fill), axis=0, keepdims=True
    )
    weights = jnp.exp(scores - top)
    if live is not None:
        weights = jnp.where(live, weights, 0.0)
    total = jnp.sum(weights, axis=0, keepdims=True)
    acc = lax.dot_general(
        values, weights.astype(bf16), (((0,), (0,)), ((), ())), preferred_element_type=f32
    )
    return top, total, acc


def attention_kernel(
    owner_ref, slot_ref, lens_ref, blk_ref, query_a, query_b, query_d, new, key_dec, value_dec,
    cache_k, cache_v, keep, send, dec, key_buf, value_buf, tops, totals, sems,
):
    blocks, block_len, width = cache_k.shape
    heads = width // HD
    half = query_a.shape[0]
    tile = min(TILE, half)
    sides = ((query_a, keep), (query_b, send))

    def copies(index):
        return (
            pltpu.make_async_copy(cache_k.at[index], key_buf.at[index], sems.at[0, index]),
            pltpu.make_async_copy(cache_v.at[index], value_buf.at[index], sems.at[1, index]),
        )

    for index in range(blocks):
        for copy in copies(index):
            copy.start()

    def over_tiles(body):
        for query, state in sides:
            for row in range(0, half, tile):
                for head in range(heads):
                    body(query[row : row + tile, lanes(head)], state, slice(row, row + tile), head)

    def start(query, state, columns, head):
        top, total, acc = group_turned(query, new[0, :, lanes(head)], new[1, :, lanes(head)], None)
        state[width + head : width + head + 1, columns] = top
        state[width + heads + head : width + heads + head + 1, columns] = total
        state[lanes(head), columns] = acc

    over_tiles(start)
    mine = blk_ref[0] == 0
    for head in range(heads):
        own = jnp.sum(
            query_d[:, lanes(head)].astype(f32) * key_dec[:, lanes(head)].astype(f32),
            axis=-1,
            keepdims=True,
        ) * HD ** (-0.5)
        tops[head] = jnp.where(mine, own, neg_fill)
        totals[head] = jnp.where(mine, jnp.ones_like(own), jnp.zeros_like(own))
        dec[:, lanes(head)] = jnp.where(mine, value_dec[:, lanes(head)].astype(f32), 0.0)

    @pl.loop(0, blocks)
    def _(index):
        for copy in copies(index):
            copy.wait()
        owner = owner_ref[index]
        length = lens_ref[jnp.minimum(owner, REQS - 1)]
        count = jnp.clip(length - slot_ref[index] * block_len, 0, block_len)

        def add(live, query, state, columns, head):
            top, total, acc = group_turned(
                query, key_buf[index, :, lanes(head)], value_buf[index, :, lanes(head)], live
            )
            top_row = slice(width + head, width + head + 1)
            total_row = slice(width + heads + head, width + heads + head + 1)
            old_top = state[top_row, columns]
            best = jnp.maximum(old_top, top)
            old_scale = jnp.exp(old_top - best)
            scale = jnp.exp(top - best)
            state[top_row, columns] = best
            state[total_row, columns] = state[total_row, columns] * old_scale + total * scale
            state[lanes(head), columns] = state[lanes(head), columns] * old_scale + acc * scale

        @pl.when((owner < PRE) & (count == block_len))
        def _():
            over_tiles(functools.partial(add, None))

        @pl.when((owner < PRE) & (count < block_len))
        def _():
            live = lax.broadcasted_iota(jnp.int32, (block_len, tile), 0) < count
            over_tiles(functools.partial(add, live))

        @pl.when((owner >= PRE) & (owner < REQS))
        def _():
            shape = (DPAD, block_len)
            live = (lax.broadcasted_iota(jnp.int32, shape, 1) < count) & (
                lax.broadcasted_iota(jnp.int32, shape, 0) == owner - PRE
            )
            for head in range(heads):
                top, total, acc = group(
                    query_d[:, lanes(head)],
                    key_buf[index, :, lanes(head)],
                    value_buf[index, :, lanes(head)],
                    live,
                )
                old_top = tops[head]
                best = jnp.maximum(old_top, top)
                old_scale = jnp.exp(old_top - best)
                scale = jnp.exp(top - best)
                tops[head] = best
                totals[head] = totals[head] * old_scale + total * scale
                dec[:, lanes(head)] = dec[:, lanes(head)] * old_scale + acc * scale

    place = lax.broadcasted_iota(jnp.int32, (DPAD, HD), 1)
    packed = jnp.zeros((DPAD, HD), f32)
    for head in range(heads):
        packed = jnp.where(place == head, tops[head], packed)
        packed = jnp.where(place == heads + head, totals[head], packed)
    dec[:, width:] = packed


def attention(query_a, query_b, query_d, new, key_d, value_d, cache_keys, cache_values, scalars):
    half = query_a.shape[0]
    blocks, block_len, width = cache_keys.shape
    heads = width // HD
    state = ((width + 2 * heads, half), f32)
    return call(
        attention_kernel,
        (state, state, ((DPAD, width + HD), f32)),
        [SMEM] * 4 + [VMEM] * 6 + [HBM] * 2,
        (*scalars, query_a, query_b, query_d, new, key_d, value_d, cache_keys, cache_values),
        "attention",
        24,
        [
            pltpu.VMEM((blocks, block_len, width), bf16),
            pltpu.VMEM((blocks, block_len, width), bf16),
            pltpu.VMEM((heads, DPAD, 1), f32),
            pltpu.VMEM((heads, DPAD, 1), f32),
            pltpu.SemaphoreType.DMA((2, blocks)),
        ],
    )


def split(values):
    high = values.astype(bf16).astype(f32)
    middle = (values - high).astype(bf16).astype(f32)
    return high, middle, (values - high) - middle


def merge_core_kernel(mine, other, dec_mine, dec_other, *outs):
    full = dec_mine.shape[1]
    width = full - HD
    heads = width // HD
    half = mine.shape[1]
    tok = half // len(outs)

    def put(where, turned, dec):
        value = turned.T.astype(bf16)
        for index, out in enumerate(outs):
            out[0:tok, where] = value[index * tok : (index + 1) * tok]
            out[tok : tok + DPAD, where] = dec.astype(bf16)

    place = lax.broadcasted_iota(jnp.int32, (DPAD, HD), 1)
    packed = jnp.zeros((DPAD, HD), f32)
    stats_a = dec_mine[:, width:]
    stats_b = dec_other[:, width:]
    top_rows = slice(width, width + heads)
    total_rows = slice(width + heads, width + 2 * heads)
    best = jnp.maximum(mine[top_rows, :], other[top_rows, :])
    scale_a = jnp.exp(mine[top_rows, :] - best)
    scale_b = jnp.exp(other[top_rows, :] - best)
    total = mine[total_rows, :] * scale_a + other[total_rows, :] * scale_b
    for head in range(heads):
        one = slice(head, head + 1)
        two = slice(heads + head, heads + head + 1)
        turned = mine[lanes(head), :] * scale_a[one] + other[lanes(head), :] * scale_b[one]
        dec_best = jnp.maximum(stats_a[:, one], stats_b[:, one])
        dec_a = jnp.exp(stats_a[:, one] - dec_best)
        dec_b = jnp.exp(stats_b[:, one] - dec_best)
        packed = jnp.where(place == head, dec_best, packed)
        packed = jnp.where(place == heads + head, stats_a[:, two] * dec_a + stats_b[:, two] * dec_b, packed)
        put(lanes(head), turned, dec_mine[:, lanes(head)] * dec_a + dec_other[:, lanes(head)] * dec_b)
    coded = [*split(jnp.concatenate([best, total], axis=0))]
    coded.append(jnp.zeros((HD - 6 * heads, half), f32))
    high, middle, low = split(packed)
    put(
        slice(width, full),
        jnp.concatenate(coded, axis=0),
        high + pltpu.roll(middle, 2 * heads, 1) + pltpu.roll(low, 4 * heads, 1),
    )


def merge_core(mine, other, dec_mine, dec_other, parts):
    full = dec_mine.shape[1]
    tok = mine.shape[1] // parts
    return call(
        merge_core_kernel,
        (((tok + DPAD, full), bf16),) * parts,
        [VMEM] * 4,
        (mine, other, dec_mine, dec_other),
        "merge_core",
        12,
    )


def project_kernel(parts, head_ref, *refs):
    pieces = refs[:parts]
    weight_hbm = refs[parts]
    weight, sem = refs[-2:]
    outs = refs[parts + 1 : -2]
    copy = pltpu.make_async_copy(weight_hbm, weight, sem)
    copy.start()
    rows, full = pieces[0].shape
    width = full - HD
    heads = width // HD
    columns = outs[0].shape[1]
    stats = []
    for piece in pieces:
        coded = piece[:, width:].astype(f32)
        stats.append(
            (coded + pltpu.roll(coded, HD - 2 * heads, 1)) + pltpu.roll(coded, HD - 4 * heads, 1)
        )
    attended = []
    for head in range(heads):
        tops = [s[:, head : head + 1] for s in stats]
        best = functools.reduce(jnp.maximum, tops)
        scales = [jnp.exp(top - best) for top in tops]
        total = tree_sum([s[:, heads + head : heads + head + 1] * c for s, c in zip(stats, scales)])
        acc = tree_sum([piece[:, lanes(head)].astype(f32) * c for piece, c in zip(pieces, scales)])
        attended.append((acc / total).astype(bf16))
    attended = jnp.concatenate(attended, axis=1)
    copy.wait()
    for offset, out in enumerate(outs):
        place = lax.bitwise_xor(head_ref[0], offset)
        out[...] = jnp.dot(attended, weight[:, span(place, columns)], preferred_element_type=f32)


def project_out(pieces, w_output, head_index, head_count):
    rows = pieces[0].shape[0]
    columns = w_output.shape[1] // head_count
    return call(
        functools.partial(project_kernel, len(pieces)),
        (((rows, columns), f32),) * head_count,
        [SMEM] + [VMEM] * len(pieces) + [HBM],
        (head_index, *pieces, w_output),
        "project_out",
        12,
        [pltpu.VMEM(w_output.shape, bf16), pltpu.SemaphoreType.DMA],
    )


def mid_kernel(head_ref, pre, dec, *refs):
    parts, (mid, square) = refs[:-2], refs[-2:]
    tok, width = pre.shape[0], mid.shape[1]
    here = span(head_ref[0], width)
    total = tree_sum([part[...] for part in parts])
    mid[0:tok, :] = pre[:, here].astype(f32) + total[:tok]
    mid[tok : tok + DEC, :] = dec[:, here].astype(f32) + total[tok : tok + DEC]
    mid[tok + DEC :, :] = jnp.zeros_like(mid[tok + DEC :, :])
    values = mid[...]
    values = values * values
    square[...] = tree_sum([values[:, lanes(part)] for part in range(width // HD)])


def norm_kernel(model_width, head_ref, mid, gain, *refs):
    squares, (tokens, dec) = refs[:-2], refs[-2:]
    tok, width = tokens.shape
    total = jnp.sum(tree_sum([square[...] for square in squares]), axis=-1, keepdims=True)
    scaled = mid[...] * lax.rsqrt(total / model_width + eps_norm) * gain[:, span(head_ref[0], width)]
    scaled = scaled.astype(bf16)
    tokens[...] = scaled[:tok]
    dec[...] = scaled[tok:]


def experts_kernel(chunks, scalar_ref, *refs):
    data = refs[:chunks]
    query, table_d = refs[chunks : chunks + 2]
    table = query.at[:, query.shape[1] - table_d.shape[1] :]
    hbm = refs[chunks + 2 : chunks + 8]
    outs = refs[chunks + 8 : 2 * chunks + 8]
    bufs = refs[2 * chunks + 8 : 2 * chunks + 11]
    gates, first, second, sems = refs[2 * chunks + 11 :]
    each = hbm[0].shape[0]
    experts = 2 * each
    rows, width = data[0].shape
    half = rows - DPAD
    tile = min(TILE, half)
    places = [lax.bitwise_xor(scalar_ref[0], offset) for offset in range(chunks)]

    def copies(expert):
        source = hbm[:3] if expert < each else hbm[3:]
        return [
            pltpu.make_async_copy(src.at[expert % each], buf.at[expert], sems.at[kind, expert])
            for kind, (src, buf) in enumerate(zip(source, bufs))
        ]

    for expert in range(experts):
        for copy in copies(expert):
            copy.start()
    w_gate, w_up, w_down = bufs
    for expert in range(experts):
        number = lax.bitwise_xor(scalar_ref[1], expert // each) * each + expert % each
        for ref, row in ((table, 0), (table_d, half)):
            place = lax.broadcasted_iota(jnp.int32, ref.shape, 1)
            found = jnp.where(place == number, ref[...].astype(f32), 0.0)
            gates[expert, row : row + ref.shape[0], :] = jnp.sum(found, axis=-1, keepdims=True)
    for expert in range(experts):
        for copy in copies(expert):
            copy.wait()
        total = first if expert < each else second
        for row in range(0, half, tile):
            size = tile + (DPAD if row + tile == half else 0)
            gate = up = None
            for part, place in zip(data, places):
                block = part[row : row + size, :]
                g = jnp.dot(block, w_gate[expert, span(place, width), :], preferred_element_type=f32)
                u = jnp.dot(block, w_up[expert, span(place, width), :], preferred_element_type=f32)
                gate = g if gate is None else gate + g
                up = u if up is None else up + u
            act = (gate / (1.0 + jnp.exp(-gate)) * up).astype(bf16)
            factor = gates[expert, row : row + size, :]
            for index, place in enumerate(places):
                down = jnp.dot(act, w_down[expert, :, span(place, width)], preferred_element_type=f32)
                down = down.astype(bf16).astype(f32) * factor
                if expert % each:
                    down = total[index, row : row + size, :] + down
                if expert == experts - 1:
                    down = first[index, row : row + size, :] + down
                    outs[index][row : row + size, :] = down.astype(bf16)
                else:
                    total[index, row : row + size, :] = down


def run_experts(data, query, table_d, own, other, scalars):
    chunks = len(data)
    rows, width = data[0].shape
    experts = 2 * own[0].shape[0]
    return call(
        functools.partial(experts_kernel, chunks),
        (((rows, width), bf16),) * chunks,
        [SMEM] + [VMEM] * (chunks + 2) + [HBM] * 6,
        (scalars, *data, query, table_d, *own, *other),
        "experts",
        32,
        [pltpu.VMEM((experts, *w.shape[1:]), bf16) for w in own]
        + [
            pltpu.VMEM((experts, rows, 1), f32),
            pltpu.VMEM((chunks, rows, width), f32),
            pltpu.VMEM((chunks, rows, width), f32),
            pltpu.SemaphoreType.DMA((3, experts)),
        ],
    )


def head_sum_kernel(parts, *refs):
    total = tree_sum([ref[...].astype(f32) for ref in refs[:parts]]).astype(bf16)
    outs = refs[parts:]
    half = total.shape[0] - DPAD
    tok = half // len(outs)
    for index, out in enumerate(outs):
        out[0:tok, :] = total[index * tok : (index + 1) * tok]
        out[tok:, :] = total[half:]


def final_kernel(mid, *refs):
    parts, (hidden, dec) = refs[:-2], refs[-2:]
    tok = hidden.shape[0]
    total = mid[...] + tree_sum([part[...].astype(f32) for part in parts])
    hidden[...] = total[:tok].astype(bf16)
    dec[...] = total[tok : tok + DEC].astype(bf16)


def per_device(
    pre_tokens, dec_tokens, attn_gain, w_query, w_key, w_value, w_output, cache_keys, cache_values,
    block_request, block_slot, cache_lens, moe_gain, expert_ids, expert_gates, dec_expert_ids,
    dec_expert_gates, w_gate, w_up, w_down,
):
    tok, model_width = pre_tokens.shape
    width = w_query.shape[1]
    blk_count = lax.axis_size("blk")
    blk_index = lax.axis_index("blk").astype(jnp.int32)
    head_count = lax.axis_size("head")
    head_index = lax.axis_index("head").astype(jnp.int32)
    chips = blk_count // 2
    head_scalar = head_index.reshape(1)
    scalars = jnp.stack([head_index, blk_index])
    part_width = model_width // head_count
    tables = -(-w_gate.shape[0] * blk_count // HD) * HD
    rows = tok + DPAD

    row = jnp.arange(rows, dtype=jnp.int32)
    request = jnp.maximum(row - tok + PRE, 0)[:, None] == jnp.arange(REQS, dtype=jnp.int32)
    positions = jnp.sum(jnp.where(request, cache_lens, 0), axis=1)
    positions = positions + jnp.where(row < tok, blk_index * tok + row, 0)
    frequencies = rope_base ** (-jnp.arange(HD // 2, dtype=f32) / (HD // 2))
    angles = positions.astype(f32)[:, None] * frequencies[None, :]
    cosine = jnp.cos(angles)
    sine = jnp.sin(angles)
    cosine = jnp.concatenate([cosine, cosine], axis=1)
    sine = jnp.concatenate([-sine, sine], axis=1)

    message, query_d, table_d, normed = call(
        query_kernel,
        (
            ((tok, width + tables), bf16),
            ((DPAD, width), bf16),
            ((DPAD, tables), bf16),
            ((rows, model_width), bf16),
        ),
        [VMEM] * 3 + [HBM] + [VMEM] * 6,
        (
            pre_tokens, dec_tokens, attn_gain[None, :], w_query, cosine, sine,
            expert_ids.T, expert_gates.T, dec_expert_ids.T, dec_expert_gates.T,
        ),
        "queries",
        16,
        [pltpu.VMEM(w_query.shape, bf16), pltpu.SemaphoreType.DMA],
    )

    def exchange(pieces, axis, step):
        return [pieces[0]] + [swap(pieces[o], axis, step * o) for o in range(1, len(pieces))]

    new_cache, dec_cache, key_d, value_d = call(
        key_kernel,
        (
            ((2, tok, width), bf16),
            ((2, DEC, width), bf16),
            ((DPAD, width), bf16),
            ((DPAD, width), bf16),
        ),
        [VMEM] + [HBM] * 2 + [VMEM] * 2,
        (normed, w_key, w_value, cosine, sine),
        "keys",
        16,
        [
            pltpu.VMEM(w_key.shape, bf16),
            pltpu.VMEM(w_value.shape, bf16),
            pltpu.SemaphoreType.DMA((2,)),
        ],
        pl.CostEstimate(
            flops=4 * rows * model_width * width,
            transcendentals=0,
            bytes_accessed=4 * model_width * width,
        ),
    )
    gate_other = swap(w_gate, "blk", 1)
    pieces = exchange([message] * chips, "blk", 2)
    new_cache, *pieces = lax.optimization_barrier((new_cache, *pieces))
    query_a = jnp.concatenate(pieces, axis=0)
    query_b = swap(query_a, "blk", 1)
    query_b, gate_other, up_source = lax.optimization_barrier((query_b, gate_other, w_up))
    up_other = swap(up_source, "blk", 1)

    keep, send, dec = attention(
        query_a, query_b, query_d, new_cache, key_d, value_d, cache_keys, cache_values,
        (block_request, block_slot, cache_lens, blk_index.reshape(1)),
    )
    send, up_other = lax.optimization_barrier((send, up_other))
    pieces = merge_core(keep, swap(send, "blk", 1), dec, swap(dec, "blk", 1), chips)
    *pieces, down_source = lax.optimization_barrier((*pieces, w_down))
    down_other = swap(down_source, "blk", 1)
    pieces = exchange(pieces, "blk", 2)
    partial = exchange(project_out(pieces, w_output, head_scalar, head_count), "head", 1)
    mid, square = call(
        mid_kernel,
        (((rows, part_width), f32), ((rows, HD), f32)),
        [SMEM] + [VMEM] * (2 + head_count),
        (head_scalar, pre_tokens, dec_tokens, *partial),
        "mid",
        8,
    )
    squares = exchange([square] * head_count, "head", 1)
    moe_tok, moe_dec = call(
        functools.partial(norm_kernel, model_width),
        (((tok, part_width), bf16), ((DPAD, part_width), bf16)),
        [SMEM] + [VMEM] * (2 + head_count),
        (head_scalar, mid, moe_gain[None, :], *squares),
        "moe_norm",
        8,
    )
    gathered = jnp.concatenate([*exchange([moe_tok] * chips, "blk", 2), moe_dec], axis=0)
    data = exchange([gathered] * head_count, "head", 1)
    results = run_experts(
        data, query_a, table_d, (w_gate, w_up, w_down), (gate_other, up_other, down_other), scalars
    )
    results = exchange(results, "head", 1)
    final = call(
        functools.partial(head_sum_kernel, head_count),
        (((rows, part_width), bf16),) * chips,
        [VMEM] * head_count,
        results,
        "head_sum",
        8,
    )
    final = exchange(final, "blk", 2)
    hidden, dec_hidden = call(
        final_kernel,
        (((tok, part_width), bf16), ((DEC, part_width), bf16)),
        [VMEM] * (1 + chips),
        (mid, *final),
        "final",
        8,
    )
    return (hidden, dec_hidden, new_cache, dec_cache)


def solution(mesh):
    placed = (
        P("blk", None),
        P(),
        P(),
        P(None, "head"),
        P(None, "head"),
        P(None, "head"),
        P("head", None),
        P("blk", None, "head"),
        P("blk", None, "head"),
        P("blk"),
        P("blk"),
        P(),
        P(),
        P("blk", None),
        P("blk", None),
        P(),
        P(),
        P("blk", None, "head"),
        P("blk", None, "head"),
        P("blk", "head", None),
    )
    return jax.shard_map(
        per_device,
        mesh=mesh,
        in_specs=placed,
        out_specs=(
            P("blk", "head"),
            P(None, "head"),
            P(None, "blk", "head"),
            P(None, None, "head"),
        ),
        check_vma=False,
    )
```

time: 566 us -> 117 us (0.21)
  blocking collectives: 202 us -> 0 us
  waiting for transfers between devices: 158 us -> 46.5 us
  other arithmetic: 56.4 us -> 1.16 us
  local copies, waits for them, and re-layouts: 61.3 us -> 8.22 us
  matrix products: 51.8 us -> 0 us
  starting transfers between devices: 4.85 us -> 34.7 us
  Pallas kernels: 0 us -> 24.1 us
  between operations: 15.2 us -> 0.88 us
  loops' own time: 11 us -> 0 us
    all_to_all x1 -> x0, blocking collectives: 98.6 us -> none  [per_device(): lax.all_to_all(dispatched, 'blk', split_axis=0, concat_axis=0, tiled=True)]
    all_to_all x1 -> x0, waiting for transfers between devices: 89.3 us -> none  [per_device(): lax.all_to_all(produced, 'blk', split_axis=0, concat_axis=0, tiled=True)]
    psum x3 -> x0, blocking collectives: 69.8 us -> none  [the longest x1 27.2 us: per_device(): moe_dec = lax.psum(moe_dec.astype(jnp.bfloat16), 'blk').astype(jnp.float32)]
    dot_general x34 -> x0, matrix products: 51.8 us -> none  [the longest x10 9.23 us: group_stats(): jnp.einsum('qhk,khd->qhd', weights.astype(jnp.bfloat16), v_heads, preferr...]
    ppermute x0 -> x30, waiting for transfers between devices: none -> 46.5 us  [swap(): return lax.ppermute(value, axis, [(i, i ^ mask) for i in range(count)])]
    psum x2 -> x0, waiting for transfers between devices: 43.1 us -> none  [the longest x1 43.1 us: per_device(): out_pre, out_dec = lax.psum((out_pre, out_dec), 'head')]
    ppermute x0 -> x30, starting transfers between devices: none -> 34.7 us  [swap(): return lax.ppermute(value, axis, [(i, i ^ mask) for i in range(count)])]
    dynamic_slice x40 -> x0, local copies, waits for them, and re-layouts: 31.1 us -> none  [the longest x8 10.4 us: add_block(): live_keys = block_slot[block_index] * block_len + key_offsets < length_limit]
  transfers between devices with their start and end apart: 5 -> 30, of which waited for: 3 -> 17; matrix products, arithmetic and copies ran while one was open for 3% -> 2% of each run, Pallas kernels for 0% -> 13%
where the time goes in v2:
time: 117 us; the launch traced here: 116 us
  waiting for transfers between devices  46.5 us (40%)
  starting transfers between devices  34.7 us (30%)
  Pallas kernels  24.1 us (21%)
  local copies, waits for them, and re-layouts  8.22 us (7%)
    ppermute x30, waiting for transfers between devices, swap(): return lax.ppermute(value, axis, [(i, i ^ mask) for i in range(count)])  46.5 us
    ppermute x30, starting transfers between devices, swap(): return lax.ppermute(value, axis, [(i, i ^ mask) for i in range(count)])  34.7 us
    pallas_call x10, Pallas kernels, call(): pl.pallas_call(body, out_shape=tuple((jax.ShapeDtypeStruct(shape, dtype)...  24.1 us
    unnamed x42, local copies, waits for them, and re-layouts  8.2 us
  transfers between devices with their start and end apart: 30, of which 17 were waited for; matrix products, arithmetic and copies ran while one was open for 2% of the time, Pallas kernels for 13%

profile of v2, /device:TPU:0, one launch (start us, length us, event | category | flops | bytes accessed | tf_op | source)
XLA Modules:
  0.0 115.6 jit_solution(7270022196104777964)
XLA Ops:
  1.2 0.7 select_reduce_fusion
  2.3 0.9 copy-done
  3.2 0.8 copy-done.2
  4.0 0.7 copy-done.5
  4.7 0.7 copy-done.7
  5.4 0.7 copy-done.8
  6.1 0.7 copy-done.9
  7.5 2.2 %queries.1 = (bf16[64,640]{1,0:T(8,128)(2,1)S(1)}, bf16[16,512]{1,0:T(8,128)(2,1)S(1)}, bf16[16,128]{1,0:T(8,128)(2,1)S(1)}, bf16[80,2048]{1,0:T(8,128)(2,1)S(1)}) custom-call(bf16[64,2048]{1,0:T(8,128)(2,1)S(1)} %copy-done, bf16[12,2048]{1,0:T(8,128)(2,1)S(1)} %copy-done.2, f32[1,2048]{1,0:T(1,128)S(1)} %bitcast.8, bf16[2048,512]{1,0:T(8,128)(2,1)} %weight_hbm.1, ...), custom_call_target="tpu_custom_call" | custom-call | tf_op jit(solution)/shard_map/queries/pallas_call | solution.py:54
  9.7 4.7 %collective-permute-start.2 = (bf16[64,640]{1,0:T(8,128)(2,1)S(1)}, bf16[64,640]{1,0:T(8,128)(2,1)S(1)}, u32[]{:S(2)}, u32[]{:S(2)}) collective-permute-start(bf16[64,640]{1,0:T(8,128)(2,1)S(1)} %get-tuple-element.55), channel_id=1, source_target_pairs={{0,6},{1,7},{2,4},{3,5},{4,2},{5,3},{6,0},{7,1},{8,14},{9,15},{10,... | collective-permute-start | bytes 245768 | tf_op jit(solution)/shard_map/ppermute | solution.py:26
  15.0 3.9 %keys.1 = (bf16[2,64,512]{2,1,0:T(8,128)(2,1)}, bf16[2,12,512]{2,1,0:T(8,128)(2,1)S(1)}, bf16[16,512]{1,0:T(8,128)(2,1)S(1)}, bf16[16,512]{1,0:T(8,128)(2,1)S(1)}) custom-call(bf16[80,2048]{1,0:T(8,128)(2,1)S(1)} %get-tuple-element.52.normed, bf16[2048,512]{1,0:T(8,128)(2,1)} %key_hbm.1, bf16[2048,512]{1,0:T(8,128)(2,1)} %value_hbm.1, ...), custom_call_target="tpu_custom_call" | custom-call | flops 335544320 | bytes 4194304 | tf_op jit(solution)/shard_map/keys/pallas_call | solution.py:54
  18.9 2.9 %collective-permute-done.1 = bf16[64,640]{1,0:T(8,128)(2,1)S(1)} collective-permute-done((bf16[64,640]{1,0:T(8,128)(2,1)S(1)}, bf16[64,640]{1,0:T(8,128)(2,1)S(1)}, u32[]{:S(2)}, u32[]{:S(2)}) %collective-permute-start.1) | collective-permute-done | bytes 81952 | tf_op jit(solution)/shard_map/ppermute | solution.py:26
  22.0 1.6 %collective-permute-done.3.query_b = bf16[256,640]{1,0:T(8,128)(2,1)S(1)} collective-permute-done((bf16[256,640]{1,0:T(8,128)(2,1)S(1)}, bf16[256,640]{1,0:T(8,128)(2,1)S(1)}, u32[]{:S(2)}, u32[]{:S(2)}) %collective-permute-start.3) | collective-permute-done | bytes 327712 | tf_op jit(solution)/shard_map/ppermute | solution.py:26
  23.8 0.9 copy-done.4
  24.7 7.2 %attention.1 = (f32[520,256]{1,0:T(8,128)S(1)}, f32[520,256]{1,0:T(8,128)S(1)}, f32[16,640]{1,0:T(8,128)S(1)}) custom-call(s32[8]{0:T(128)S(1)} %copy-done.11, s32[8]{0:T(128)S(1)} %copy-done.12, s32[13]{0:T(128)S(1)} %copy-done.13, s32[1]{0:T(128)} %bitcast.1.blk_ref, bf16[256,640]{1,0:T(8,128)(2,1)S(1)} %constant_dynamic-update-slice_fusion.query_a.refs_4_, ...), custom_call_target="tpu_custom_call" | custom-call | tf_op jit(solution)/shard_map/attention/pallas_call | solution.py:54
  32.6 1.5 %collective-permute-done.7.dec_other = f32[16,640]{1,0:T(8,128)S(1)} collective-permute-done((f32[16,640]{1,0:T(8,128)S(1)}, f32[16,640]{1,0:T(8,128)S(1)}, u32[]{:S(2)}, u32[]{:S(2)}) %collective-permute-start.7) | collective-permute-done | bytes 40992 | tf_op jit(solution)/shard_map/ppermute | solution.py:26
  34.6 2.1 %collective-permute-start.8 = (bf16[80,640]{1,0:T(8,128)(2,1)S(1)}, bf16[80,640]{1,0:T(8,128)(2,1)S(1)}, u32[]{:S(2)}, u32[]{:S(2)}) collective-permute-start(bf16[80,640]{1,0:T(8,128)(2,1)S(1)} %get-tuple-element.74), channel_id=1, source_target_pairs={{0,2},{1,3},{2,0},{3,1},{4,6},{5,7},{6,4},{7,5},{8,10},{9,11},{10,... | collective-permute-start | bytes 307208 | tf_op jit(solution)/shard_map/ppermute | solution.py:26
  36.8 2.6 %collective-permute-start.9 = (bf16[80,640]{1,0:T(8,128)(2,1)S(1)}, bf16[80,640]{1,0:T(8,128)(2,1)S(1)}, u32[]{:S(2)}, u32[]{:S(2)}) collective-permute-start(bf16[80,640]{1,0:T(8,128)(2,1)S(1)} %get-tuple-element.75), channel_id=1, source_target_pairs={{0,4},{1,5},{2,6},{3,7},{4,0},{5,1},{6,2},{7,3},{8,12},{9,13},{10,... | collective-permute-start | bytes 307208 | tf_op jit(solution)/shard_map/ppermute | solution.py:26
  40.0 7.8 %collective-permute-done.9.refs_2_ = bf16[80,640]{1,0:T(8,128)(2,1)S(1)} collective-permute-done((bf16[80,640]{1,0:T(8,128)(2,1)S(1)}, bf16[80,640]{1,0:T(8,128)(2,1)S(1)}, u32[]{:S(2)}, u32[]{:S(2)}) %collective-permute-start.9) | collective-permute-done | bytes 102432 | tf_op jit(solution)/shard_map/ppermute | solution.py:26
  47.8 2.1 %project_out.1 = (f32[80,512]{1,0:T(8,128)S(1)}, f32[80,512]{1,0:T(8,128)S(1)}, f32[80,512]{1,0:T(8,128)S(1)}, f32[80,512]{1,0:T(8,128)S(1)}) custom-call(s32[1]{0:T(128)} %bitcast.head_ref, bf16[80,640]{1,0:T(8,128)(2,1)S(1)} %get-tuple-element.73.refs_0_, bf16[80,640]{1,0:T(8,128)(2,1)S(1)} %collective-permute-done.8.refs_1_, ...), custom_call_target="tpu_custom_call" | custom-call | tf_op jit(solution)/shard_map/project_out/pallas_call | solution.py:54
  49.9 1.6 %collective-permute-start.11 = (f32[80,512]{1,0:T(8,128)S(1)}, f32[80,512]{1,0:T(8,128)S(1)}, u32[]{:S(2)}, u32[]{:S(2)}) collective-permute-start(f32[80,512]{1,0:T(8,128)S(1)} %get-tuple-element.78), channel_id=1, source_target_pairs={{0,8},{8,0},{16,24},{24,16},{1,9},{9,1},{17,25},{25,17},{2,10},{10... | collective-permute-start | bytes 491528 | tf_op jit(solution)/shard_map/ppermute | solution.py:26
  51.5 1.5 %collective-permute-start.12 = (f32[80,512]{1,0:T(8,128)S(1)}, f32[80,512]{1,0:T(8,128)S(1)}, u32[]{:S(2)}, u32[]{:S(2)}) collective-permute-start(f32[80,512]{1,0:T(8,128)S(1)} %get-tuple-element.79), channel_id=1, source_target_pairs={{0,16},{8,24},{16,0},{24,8},{1,17},{9,25},{17,1},{25,9},{2,18},{10... | collective-permute-start | bytes 491528 | tf_op jit(solution)/shard_map/ppermute | solution.py:26
  53.5 3.5 %collective-permute-done.11.refs_1_ = f32[80,512]{1,0:T(8,128)S(1)} collective-permute-done((f32[80,512]{1,0:T(8,128)S(1)}, f32[80,512]{1,0:T(8,128)S(1)}, u32[]{:S(2)}, u32[]{:S(2)}) %collective-permute-start.11) | collective-permute-done | bytes 163872 | tf_op jit(solution)/shard_map/ppermute | solution.py:26
  57.0 3.1 %collective-permute-done.12.refs_2_ = f32[80,512]{1,0:T(8,128)S(1)} collective-permute-done((f32[80,512]{1,0:T(8,128)S(1)}, f32[80,512]{1,0:T(8,128)S(1)}, u32[]{:S(2)}, u32[]{:S(2)}) %collective-permute-start.12) | collective-permute-done | bytes 163872 | tf_op jit(solution)/shard_map/ppermute | solution.py:26
  60.1 0.9 collective-permute-start.16
  61.1 1.2 %collective-permute-start.15 = (f32[80,128]{1,0:T(8,128)S(1)}, f32[80,128]{1,0:T(8,128)S(1)}, u32[]{:S(2)}, u32[]{:S(2)}) collective-permute-start(f32[80,128]{1,0:T(8,128)S(1)} %get-tuple-element.82.refs_0_), channel_id=1, source_target_pairs={{0,16},{8,24},{16,0},{24,8},{1,17},{9,25},{17,1},{25,9},{2,18},{10... | collective-permute-start | bytes 122888 | tf_op jit(solution)/shard_map/ppermute | solution.py:26
  62.3 1.4 %collective-permute-start.14 = (f32[80,128]{1,0:T(8,128)S(1)}, f32[80,128]{1,0:T(8,128)S(1)}, u32[]{:S(2)}, u32[]{:S(2)}) collective-permute-start(f32[80,128]{1,0:T(8,128)S(1)} %get-tuple-element.82.refs_0_), channel_id=1, source_target_pairs={{0,8},{8,0},{16,24},{24,16},{1,9},{9,1},{17,25},{25,17},{2,10},{10... | collective-permute-start | bytes 122888 | tf_op jit(solution)/shard_map/ppermute | solution.py:26
  63.7 1.5 %collective-permute-done.16.refs_3_ = f32[80,128]{1,0:T(8,128)S(1)} collective-permute-done((f32[80,128]{1,0:T(8,128)S(1)}, f32[80,128]{1,0:T(8,128)S(1)}, u32[]{:S(2)}, u32[]{:S(2)}) %collective-permute-start.16) | collective-permute-done | bytes 40992 | tf_op jit(solution)/shard_map/ppermute | solution.py:26
  65.5 0.8 collective-permute-done.14.refs_1_
  66.4 2.5 %collective-permute-start.19 = (bf16[64,512]{1,0:T(8,128)(2,1)S(1)}, bf16[64,512]{1,0:T(8,128)(2,1)S(1)}, u32[]{:S(2)}, u32[]{:S(2)}) collective-permute-start(bf16[64,512]{1,0:T(8,128)(2,1)S(1)} %get-tuple-element.83), channel_id=1, source_target_pairs={{0,6},{1,7},{2,4},{3,5},{4,2},{5,3},{6,0},{7,1},{8,14},{9,15},{10,... | collective-permute-start | bytes 196616 | tf_op jit(solution)/shard_map/ppermute | solution.py:26
  68.9 1.4 %collective-permute-start.18 = (bf16[64,512]{1,0:T(8,128)(2,1)S(1)}, bf16[64,512]{1,0:T(8,128)(2,1)S(1)}, u32[]{:S(2)}, u32[]{:S(2)}) collective-permute-start(bf16[64,512]{1,0:T(8,128)(2,1)S(1)} %get-tuple-element.83), channel_id=1, source_target_pairs={{0,4},{1,5},{2,6},{3,7},{4,0},{5,1},{6,2},{7,3},{8,12},{9,13},{10,... | collective-permute-start | bytes 196616 | tf_op jit(solution)/shard_map/ppermute | solution.py:26
  70.9 3.9 %collective-permute-done.17 = bf16[64,512]{1,0:T(8,128)(2,1)S(1)} collective-permute-done((bf16[64,512]{1,0:T(8,128)(2,1)S(1)}, bf16[64,512]{1,0:T(8,128)(2,1)S(1)}, u32[]{:S(2)}, u32[]{:S(2)}) %collective-permute-start.17) | collective-permute-done | bytes 65568 | tf_op jit(solution)/shard_map/ppermute | solution.py:26
  74.8 1.8 %collective-permute-start.22 = (bf16[272,512]{1,0:T(8,128)(2,1)S(1)}, bf16[272,512]{1,0:T(8,128)(2,1)S(1)}, u32[]{:S(2)}, u32[]{:S(2)}) collective-permute-start(bf16[272,512]{1,0:T(8,128)(2,1)S(1)} %constant_dynamic-update-slice_fusion.4.refs_0_), channel_id=1, source_target_pairs={{0,24},{8,16},{16,8},{24,0},{1,25},{9,17},{17,9},{25,1},{2,26},{10... | collective-permute-start | bytes 835592 | tf_op jit(solution)/shard_map/ppermute | solution.py:26
  76.6 0.9 collective-permute-start.21
  77.5 0.8 collective-permute-start.20
  78.4 4.3 %collective-permute-done.22.refs_3_ = bf16[272,512]{1,0:T(8,128)(2,1)S(1)} collective-permute-done((bf16[272,512]{1,0:T(8,128)(2,1)S(1)}, bf16[272,512]{1,0:T(8,128)(2,1)S(1)}, u32[]{:S(2)}, u32[]{:S(2)}) %collective-permute-start.22) | collective-permute-done | bytes 278560 | tf_op jit(solution)/shard_map/ppermute | solution.py:26
  82.7 2.9 %collective-permute-done.21.refs_2_ = bf16[272,512]{1,0:T(8,128)(2,1)S(1)} collective-permute-done((bf16[272,512]{1,0:T(8,128)(2,1)S(1)}, bf16[272,512]{1,0:T(8,128)(2,1)S(1)}, u32[]{:S(2)}, u32[]{:S(2)}) %collective-permute-start.21) | collective-permute-done | bytes 278560 | tf_op jit(solution)/shard_map/ppermute | solution.py:26
  85.6 1.4 %copy-done.16 = bf16[2,256,2048]{2,1,0:T(8,128)(2,1)} copy-done((bf16[2,256,2048]{2,1,0:T(8,128)(2,1)}, bf16[2,256,2048]{2,1,0:T(8,128)(2,1)S(1)}, u32[]{:S(2)}) %copy-start.16) | copy-done | bytes 2097176
  87.0 7.4 %experts.1 = (bf16[272,512]{1,0:T(8,128)(2,1)S(1)}, bf16[272,512]{1,0:T(8,128)(2,1)S(1)}, bf16[272,512]{1,0:T(8,128)(2,1)S(1)}, bf16[272,512]{1,0:T(8,128)(2,1)S(1)}) custom-call(s32[2]{0:T(128)S(1)} %pad_add_fusion.scalar_ref, bf16[272,512]{1,0:T(8,128)(2,1)S(1)} %constant_dynamic-update-slice_fusion.4.refs_0_, ...), custom_call_target="tpu_custom_call" | custom-call | tf_op jit(solution)/shard_map/experts/pallas_call | solution.py:54
  94.3 1.1 collective-permute-start.24
  95.4 1.0 collective-permute-start.25
  96.4 1.5 %collective-permute-start.26 = (bf16[272,512]{1,0:T(8,128)(2,1)S(1)}, bf16[272,512]{1,0:T(8,128)(2,1)S(1)}, u32[]{:S(2)}, u32[]{:S(2)}) collective-permute-start(bf16[272,512]{1,0:T(8,128)(2,1)S(1)} %get-tuple-element.92), channel_id=1, source_target_pairs={{0,24},{8,16},{16,8},{24,0},{1,25},{9,17},{17,9},{25,1},{2,26},{10... | collective-permute-start | bytes 835592 | tf_op jit(solution)/shard_map/ppermute | solution.py:26
  97.9 3.1 %collective-permute-done.24.refs_1_ = bf16[272,512]{1,0:T(8,128)(2,1)S(1)} collective-permute-done((bf16[272,512]{1,0:T(8,128)(2,1)S(1)}, bf16[272,512]{1,0:T(8,128)(2,1)S(1)}, u32[]{:S(2)}, u32[]{:S(2)}) %collective-permute-start.24) | collective-permute-done | bytes 278560 | tf_op jit(solution)/shard_map/ppermute | solution.py:26
  100.9 4.0 %collective-permute-done.25.refs_2_ = bf16[272,512]{1,0:T(8,128)(2,1)S(1)} collective-permute-done((bf16[272,512]{1,0:T(8,128)(2,1)S(1)}, bf16[272,512]{1,0:T(8,128)(2,1)S(1)}, u32[]{:S(2)}, u32[]{:S(2)}) %collective-permute-start.25) | collective-permute-done | bytes 278560 | tf_op jit(solution)/shard_map/ppermute | solution.py:26
  105.1 1.1 collective-permute-start.27
  106.2 2.4 %collective-permute-start.28 = (bf16[80,512]{1,0:T(8,128)(2,1)S(1)}, bf16[80,512]{1,0:T(8,128)(2,1)S(1)}, u32[]{:S(2)}, u32[]{:S(2)}) collective-permute-start(bf16[80,512]{1,0:T(8,128)(2,1)S(1)} %get-tuple-element.95), channel_id=1, source_target_pairs={{0,4},{1,5},{2,6},{3,7},{4,0},{5,1},{6,2},{7,3},{8,12},{9,13},{10,... | collective-permute-start | bytes 245768 | tf_op jit(solution)/shard_map/ppermute | solution.py:26
  108.6 0.9 collective-permute-start.29
  110.2 2.3 %collective-permute-done.28.refs_2_ = bf16[80,512]{1,0:T(8,128)(2,1)S(1)} collective-permute-done((bf16[80,512]{1,0:T(8,128)(2,1)S(1)}, bf16[80,512]{1,0:T(8,128)(2,1)S(1)}, u32[]{:S(2)}, u32[]{:S(2)}) %collective-permute-start.28) | collective-permute-done | bytes 81952 | tf_op jit(solution)/shard_map/ppermute | solution.py:26
  112.5 2.4 %collective-permute-done.29.refs_3_ = bf16[80,512]{1,0:T(8,128)(2,1)S(1)} collective-permute-done((bf16[80,512]{1,0:T(8,128)(2,1)S(1)}, bf16[80,512]{1,0:T(8,128)(2,1)S(1)}, u32[]{:S(2)}, u32[]{:S(2)}) %collective-permute-start.29) | collective-permute-done | bytes 81952 | tf_op jit(solution)/shard_map/ppermute | solution.py:26
  (73 shorter events, 7.3 us)
Async XLA Ops:
  0.6 23.0 %collective-permute-start.4 = (bf16[2,2048,256]{2,1,0:T(8,128)(2,1)}, bf16[2,2048,256]{2,1,0:T(8,128)(2,1)}, u32[]{:S(2)}, u32[]{:S(2)}) collective-permute-start(bf16[2,2048,256]{2,1,0:T(8,128)(2,1)} %refs_6_.1), channel_id=1, source_target_pairs={{0,1},{1,0},{2,3},{3,2},{4,5},{5,4},{6,7},{7,6},{8,9},{9,8},{10,11... | collective-permute-start | bytes 6291464 | tf_op jit(solution)/shard_map/ppermute | solution.py:26
  2.2 1.0 copy-start
  3.2 0.8 copy-start.2
  4.0 0.7 copy-start.5
  4.7 0.7 copy-start.7
  5.4 0.7 copy-start.8
  6.1 0.7 copy-start.9
  6.8 0.7 copy-start.10
  9.7 9.2 %collective-permute-start.2 = (bf16[64,640]{1,0:T(8,128)(2,1)S(1)}, bf16[64,640]{1,0:T(8,128)(2,1)S(1)}, u32[]{:S(2)}, u32[]{:S(2)}) collective-permute-start(bf16[64,640]{1,0:T(8,128)(2,1)S(1)} %get-tuple-element.55), channel_id=1, source_target_pairs={{0,6},{1,7},{2,4},{3,5},{4,2},{5,3},{6,0},{7,1},{8,14},{9,15},{10,... | collective-permute-start | bytes 245768 | tf_op jit(solution)/shard_map/ppermute | solution.py:26
  14.4 7.5 %collective-permute-start.1 = (bf16[64,640]{1,0:T(8,128)(2,1)S(1)}, bf16[64,640]{1,0:T(8,128)(2,1)S(1)}, u32[]{:S(2)}, u32[]{:S(2)}) collective-permute-start(bf16[64,640]{1,0:T(8,128)(2,1)S(1)} %get-tuple-element.55), channel_id=1, source_target_pairs={{0,4},{1,5},{2,6},{3,7},{4,0},{5,1},{6,2},{7,3},{8,12},{9,13},{10,... | collective-permute-start | bytes 245768 | tf_op jit(solution)/shard_map/ppermute | solution.py:26
  14.4 7.5 %collective-permute-start = (bf16[64,640]{1,0:T(8,128)(2,1)S(1)}, bf16[64,640]{1,0:T(8,128)(2,1)S(1)}, u32[]{:S(2)}, u32[]{:S(2)}) collective-permute-start(bf16[64,640]{1,0:T(8,128)(2,1)S(1)} %get-tuple-element.55), channel_id=1, source_target_pairs={{0,2},{1,3},{2,0},{3,1},{4,6},{5,7},{6,4},{7,5},{8,10},{9,11},{10,... | collective-permute-start | bytes 245768 | tf_op jit(solution)/shard_map/ppermute | solution.py:26
  15.0 8.6 %copy-start.14 = (bf16[2,2048,256]{2,1,0:T(8,128)(2,1)S(1)}, bf16[2,2048,256]{2,1,0:T(8,128)(2,1)}, u32[]{:S(2)}) copy-start(bf16[2,2048,256]{2,1,0:T(8,128)(2,1)} %refs_7_.1) | copy-start | bytes 6291460
  15.0 8.8 %copy-start.11 = (s32[8]{0:T(128)S(1)}, s32[8]{0:T(128)}, u32[]{:S(2)}) copy-start(s32[8]{0:T(128)} %owner_ref.1) | copy-start | bytes 100
  15.0 8.8 %copy-start.12 = (s32[8]{0:T(128)S(1)}, s32[8]{0:T(128)}, u32[]{:S(2)}) copy-start(s32[8]{0:T(128)} %slot_ref.1) | copy-start | bytes 100
  15.0 8.8 %copy-start.13 = (s32[13]{0:T(128)S(1)}, s32[13]{0:T(128)}, u32[]{:S(2)}) copy-start(s32[13]{0:T(128)} %lens_ref.1) | copy-start | bytes 160
  22.0 1.7 %collective-permute-start.3 = (bf16[256,640]{1,0:T(8,128)(2,1)S(1)}, bf16[256,640]{1,0:T(8,128)(2,1)S(1)}, u32[]{:S(2)}, u32[]{:S(2)}) collective-permute-start(bf16[256,640]{1,0:T(8,128)(2,1)S(1)} %constant_dynamic-update-slice_fusion.query_a.refs_4_), channel_id=1, source_target_pairs={{0,1},{1,0},{2,3},{3,2},{4,5},{5,4},{6,7},{7,6},{8,9},{9,8},{10,11... | collective-permute-start | bytes 983048 | tf_op jit(solution)/shard_map/ppermute | solution.py:26
  23.7 8.3 %collective-permute-start.5 = (bf16[2,2048,256]{2,1,0:T(8,128)(2,1)S(1)}, bf16[2,2048,256]{2,1,0:T(8,128)(2,1)S(1)}, u32[]{:S(2)}, u32[]{:S(2)}) collective-permute-start(bf16[2,2048,256]{2,1,0:T(8,128)(2,1)S(1)} %copy-done.14), channel_id=1, source_target_pairs={{0,1},{1,0},{2,3},{3,2},{4,5},{5,4},{6,7},{7,6},{8,9},{9,8},{10,11... | collective-permute-start | bytes 6291464 | tf_op jit(solution)/shard_map/ppermute | solution.py:26
  23.8 0.9 copy-start.4
  31.9 28.1 %copy-start.1 = (bf16[64,2048]{1,0:T(8,128)(2,1)S(1)}, bf16[64,2048]{1,0:T(8,128)(2,1)}, u32[]{:S(2)}) copy-start(bf16[64,2048]{1,0:T(8,128)(2,1)} %pre.3) | copy-start | bytes 786436
  31.9 28.1 %copy-start.3 = (bf16[12,2048]{1,0:T(8,128)(2,1)S(1)}, bf16[12,2048]{1,0:T(8,128)(2,1)}, u32[]{:S(2)}) copy-start(bf16[12,2048]{1,0:T(8,128)(2,1)} %dec.3) | copy-start | bytes 147460
  32.0 7.4 %copy-start.15 = (bf16[2,2048,256]{2,1,0:T(8,128)(2,1)}, bf16[2,2048,256]{2,1,0:T(8,128)(2,1)S(1)}, u32[]{:S(2)}) copy-start(bf16[2,2048,256]{2,1,0:T(8,128)(2,1)S(1)} %collective-permute-done.5.refs_10_) | copy-start | bytes 6291460
  32.0 2.0 %collective-permute-start.6 = (f32[520,256]{1,0:T(8,128)S(1)}, f32[520,256]{1,0:T(8,128)S(1)}, u32[]{:S(2)}, u32[]{:S(2)}) collective-permute-start(f32[520,256]{1,0:T(8,128)S(1)} %get-tuple-element.67), channel_id=1, source_target_pairs={{0,1},{1,0},{2,3},{3,2},{4,5},{5,4},{6,7},{7,6},{8,9},{9,8},{10,11... | collective-permute-start | bytes 1597448 | tf_op jit(solution)/shard_map/ppermute | solution.py:26
  32.1 1.9 %collective-permute-start.7 = (f32[16,640]{1,0:T(8,128)S(1)}, f32[16,640]{1,0:T(8,128)S(1)}, u32[]{:S(2)}, u32[]{:S(2)}) collective-permute-start(f32[16,640]{1,0:T(8,128)S(1)} %get-tuple-element.68.dec_mine), channel_id=1, source_target_pairs={{0,1},{1,0},{2,3},{3,2},{4,5},{5,4},{6,7},{7,6},{8,9},{9,8},{10,11... | collective-permute-start | bytes 122888 | tf_op jit(solution)/shard_map/ppermute | solution.py:26
  34.0 32.3 %copy-start.6 = (f32[2048]{0:T(1024)S(1)}, f32[2048]{0:T(1024)}, u32[]{:S(2)}) copy-start(f32[2048]{0:T(1024)} %param.32) | copy-start | bytes 24580
  34.4 51.2 %collective-permute-start.23 = (bf16[2,256,2048]{2,1,0:T(8,128)(2,1)}, bf16[2,256,2048]{2,1,0:T(8,128)(2,1)S(1)}, u32[]{:S(2)}, u32[]{:S(2)}) collective-permute-start(bf16[2,256,2048]{2,1,0:T(8,128)(2,1)} %refs_8_.1), channel_id=1, source_target_pairs={{0,1},{1,0},{2,3},{3,2},{4,5},{5,4},{6,7},{7,6},{8,9},{9,8},{10,11... | collective-permute-start | bytes 6291464 | tf_op jit(solution)/shard_map/ppermute | solution.py:26
  34.6 5.3 %collective-permute-start.8 = (bf16[80,640]{1,0:T(8,128)(2,1)S(1)}, bf16[80,640]{1,0:T(8,128)(2,1)S(1)}, u32[]{:S(2)}, u32[]{:S(2)}) collective-permute-start(bf16[80,640]{1,0:T(8,128)(2,1)S(1)} %get-tuple-element.74), channel_id=1, source_target_pairs={{0,2},{1,3},{2,0},{3,1},{4,6},{5,7},{6,4},{7,5},{8,10},{9,11},{10,... | collective-permute-start | bytes 307208 | tf_op jit(solution)/shard_map/ppermute | solution.py:26
  36.8 11.0 %collective-permute-start.9 = (bf16[80,640]{1,0:T(8,128)(2,1)S(1)}, bf16[80,640]{1,0:T(8,128)(2,1)S(1)}, u32[]{:S(2)}, u32[]{:S(2)}) collective-permute-start(bf16[80,640]{1,0:T(8,128)(2,1)S(1)} %get-tuple-element.75), channel_id=1, source_target_pairs={{0,4},{1,5},{2,6},{3,7},{4,0},{5,1},{6,2},{7,3},{8,12},{9,13},{10,... | collective-permute-start | bytes 307208 | tf_op jit(solution)/shard_map/ppermute | solution.py:26
  39.4 8.4 %collective-permute-start.10 = (bf16[80,640]{1,0:T(8,128)(2,1)S(1)}, bf16[80,640]{1,0:T(8,128)(2,1)S(1)}, u32[]{:S(2)}, u32[]{:S(2)}) collective-permute-start(bf16[80,640]{1,0:T(8,128)(2,1)S(1)} %get-tuple-element.76), channel_id=1, source_target_pairs={{0,6},{1,7},{2,4},{3,5},{4,2},{5,3},{6,0},{7,1},{8,14},{9,15},{10,... | collective-permute-start | bytes 307208 | tf_op jit(solution)/shard_map/ppermute | solution.py:26
  49.9 7.1 %collective-permute-start.11 = (f32[80,512]{1,0:T(8,128)S(1)}, f32[80,512]{1,0:T(8,128)S(1)}, u32[]{:S(2)}, u32[]{:S(2)}) collective-permute-start(f32[80,512]{1,0:T(8,128)S(1)} %get-tuple-element.78), channel_id=1, source_target_pairs={{0,8},{8,0},{16,24},{24,16},{1,9},{9,1},{17,25},{25,17},{2,10},{10... | collective-permute-start | bytes 491528 | tf_op jit(solution)/shard_map/ppermute | solution.py:26
  51.5 8.6 %collective-permute-start.12 = (f32[80,512]{1,0:T(8,128)S(1)}, f32[80,512]{1,0:T(8,128)S(1)}, u32[]{:S(2)}, u32[]{:S(2)}) collective-permute-start(f32[80,512]{1,0:T(8,128)S(1)} %get-tuple-element.79), channel_id=1, source_target_pairs={{0,16},{8,24},{16,0},{24,8},{1,17},{9,25},{17,1},{25,9},{2,18},{10... | collective-permute-start | bytes 491528 | tf_op jit(solution)/shard_map/ppermute | solution.py:26
  53.0 7.1 %collective-permute-start.13 = (f32[80,512]{1,0:T(8,128)S(1)}, f32[80,512]{1,0:T(8,128)S(1)}, u32[]{:S(2)}, u32[]{:S(2)}) collective-permute-start(f32[80,512]{1,0:T(8,128)S(1)} %get-tuple-element.80), channel_id=1, source_target_pairs={{0,24},{8,16},{16,8},{24,0},{1,25},{9,17},{17,9},{25,1},{2,26},{10... | collective-permute-start | bytes 491528 | tf_op jit(solution)/shard_map/ppermute | solution.py:26
  60.1 5.1 %collective-permute-start.16 = (f32[80,128]{1,0:T(8,128)S(1)}, f32[80,128]{1,0:T(8,128)S(1)}, u32[]{:S(2)}, u32[]{:S(2)}) collective-permute-start(f32[80,128]{1,0:T(8,128)S(1)} %get-tuple-element.82.refs_0_), channel_id=1, source_target_pairs={{0,24},{8,16},{16,8},{24,0},{1,25},{9,17},{17,9},{25,1},{2,26},{10... | collective-permute-start | bytes 122888 | tf_op jit(solution)/shard_map/ppermute | solution.py:26
  61.1 4.4 %collective-permute-start.15 = (f32[80,128]{1,0:T(8,128)S(1)}, f32[80,128]{1,0:T(8,128)S(1)}, u32[]{:S(2)}, u32[]{:S(2)}) collective-permute-start(f32[80,128]{1,0:T(8,128)S(1)} %get-tuple-element.82.refs_0_), channel_id=1, source_target_pairs={{0,16},{8,24},{16,0},{24,8},{1,17},{9,25},{17,1},{25,9},{2,18},{10... | collective-permute-start | bytes 122888 | tf_op jit(solution)/shard_map/ppermute | solution.py:26
  62.3 4.0 %collective-permute-start.14 = (f32[80,128]{1,0:T(8,128)S(1)}, f32[80,128]{1,0:T(8,128)S(1)}, u32[]{:S(2)}, u32[]{:S(2)}) collective-permute-start(f32[80,128]{1,0:T(8,128)S(1)} %get-tuple-element.82.refs_0_), channel_id=1, source_target_pairs={{0,8},{8,0},{16,24},{24,16},{1,9},{9,1},{17,25},{25,17},{2,10},{10... | collective-permute-start | bytes 122888 | tf_op jit(solution)/shard_map/ppermute | solution.py:26
  66.4 8.4 %collective-permute-start.19 = (bf16[64,512]{1,0:T(8,128)(2,1)S(1)}, bf16[64,512]{1,0:T(8,128)(2,1)S(1)}, u32[]{:S(2)}, u32[]{:S(2)}) collective-permute-start(bf16[64,512]{1,0:T(8,128)(2,1)S(1)} %get-tuple-element.83), channel_id=1, source_target_pairs={{0,6},{1,7},{2,4},{3,5},{4,2},{5,3},{6,0},{7,1},{8,14},{9,15},{10,... | collective-permute-start | bytes 196616 | tf_op jit(solution)/shard_map/ppermute | solution.py:26
  68.9 5.9 %collective-permute-start.18 = (bf16[64,512]{1,0:T(8,128)(2,1)S(1)}, bf16[64,512]{1,0:T(8,128)(2,1)S(1)}, u32[]{:S(2)}, u32[]{:S(2)}) collective-permute-start(bf16[64,512]{1,0:T(8,128)(2,1)S(1)} %get-tuple-element.83), channel_id=1, source_target_pairs={{0,4},{1,5},{2,6},{3,7},{4,0},{5,1},{6,2},{7,3},{8,12},{9,13},{10,... | collective-permute-start | bytes 196616 | tf_op jit(solution)/shard_map/ppermute | solution.py:26
  70.3 4.4 %collective-permute-start.17 = (bf16[64,512]{1,0:T(8,128)(2,1)S(1)}, bf16[64,512]{1,0:T(8,128)(2,1)S(1)}, u32[]{:S(2)}, u32[]{:S(2)}) collective-permute-start(bf16[64,512]{1,0:T(8,128)(2,1)S(1)} %get-tuple-element.83), channel_id=1, source_target_pairs={{0,2},{1,3},{2,0},{3,1},{4,6},{5,7},{6,4},{7,5},{8,10},{9,11},{10,... | collective-permute-start | bytes 196616 | tf_op jit(solution)/shard_map/ppermute | solution.py:26
  74.8 7.9 %collective-permute-start.22 = (bf16[272,512]{1,0:T(8,128)(2,1)S(1)}, bf16[272,512]{1,0:T(8,128)(2,1)S(1)}, u32[]{:S(2)}, u32[]{:S(2)}) collective-permute-start(bf16[272,512]{1,0:T(8,128)(2,1)S(1)} %constant_dynamic-update-slice_fusion.4.refs_0_), channel_id=1, source_target_pairs={{0,24},{8,16},{16,8},{24,0},{1,25},{9,17},{17,9},{25,1},{2,26},{10... | collective-permute-start | bytes 835592 | tf_op jit(solution)/shard_map/ppermute | solution.py:26
  76.6 9.0 %collective-permute-start.21 = (bf16[272,512]{1,0:T(8,128)(2,1)S(1)}, bf16[272,512]{1,0:T(8,128)(2,1)S(1)}, u32[]{:S(2)}, u32[]{:S(2)}) collective-permute-start(bf16[272,512]{1,0:T(8,128)(2,1)S(1)} %constant_dynamic-update-slice_fusion.4.refs_0_), channel_id=1, source_target_pairs={{0,16},{8,24},{16,0},{24,8},{1,17},{9,25},{17,1},{25,9},{2,18},{10... | collective-permute-start | bytes 835592 | tf_op jit(solution)/shard_map/ppermute | solution.py:26
  77.5 8.1 %collective-permute-start.20 = (bf16[272,512]{1,0:T(8,128)(2,1)S(1)}, bf16[272,512]{1,0:T(8,128)(2,1)S(1)}, u32[]{:S(2)}, u32[]{:S(2)}) collective-permute-start(bf16[272,512]{1,0:T(8,128)(2,1)S(1)} %constant_dynamic-update-slice_fusion.4.refs_0_), channel_id=1, source_target_pairs={{0,8},{8,0},{16,24},{24,16},{1,9},{9,1},{17,25},{25,17},{2,10},{10... | collective-permute-start | bytes 835592 | tf_op jit(solution)/shard_map/ppermute | solution.py:26
  85.6 1.4 %copy-start.16 = (bf16[2,256,2048]{2,1,0:T(8,128)(2,1)}, bf16[2,256,2048]{2,1,0:T(8,128)(2,1)S(1)}, u32[]{:S(2)}) copy-start(bf16[2,256,2048]{2,1,0:T(8,128)(2,1)S(1)} %collective-permute-done.23.refs_11_) | copy-start | bytes 6291460
  94.3 6.6 %collective-permute-start.24 = (bf16[272,512]{1,0:T(8,128)(2,1)S(1)}, bf16[272,512]{1,0:T(8,128)(2,1)S(1)}, u32[]{:S(2)}, u32[]{:S(2)}) collective-permute-start(bf16[272,512]{1,0:T(8,128)(2,1)S(1)} %get-tuple-element.90), channel_id=1, source_target_pairs={{0,8},{8,0},{16,24},{24,16},{1,9},{9,1},{17,25},{25,17},{2,10},{10... | collective-permute-start | bytes 835592 | tf_op jit(solution)/shard_map/ppermute | solution.py:26
  95.4 9.5 %collective-permute-start.25 = (bf16[272,512]{1,0:T(8,128)(2,1)S(1)}, bf16[272,512]{1,0:T(8,128)(2,1)S(1)}, u32[]{:S(2)}, u32[]{:S(2)}) collective-permute-start(bf16[272,512]{1,0:T(8,128)(2,1)S(1)} %get-tuple-element.91), channel_id=1, source_target_pairs={{0,16},{8,24},{16,0},{24,8},{1,17},{9,25},{17,1},{25,9},{2,18},{10... | collective-permute-start | bytes 835592 | tf_op jit(solution)/shard_map/ppermute | solution.py:26
  96.4 8.6 %collective-permute-start.26 = (bf16[272,512]{1,0:T(8,128)(2,1)S(1)}, bf16[272,512]{1,0:T(8,128)(2,1)S(1)}, u32[]{:S(2)}, u32[]{:S(2)}) collective-permute-start(bf16[272,512]{1,0:T(8,128)(2,1)S(1)} %get-tuple-element.92), channel_id=1, source_target_pairs={{0,24},{8,16},{16,8},{24,0},{1,25},{9,17},{17,9},{25,1},{2,26},{10... | collective-permute-start | bytes 835592 | tf_op jit(solution)/shard_map/ppermute | solution.py:26
  105.1 5.1 %collective-permute-start.27 = (bf16[80,512]{1,0:T(8,128)(2,1)S(1)}, bf16[80,512]{1,0:T(8,128)(2,1)S(1)}, u32[]{:S(2)}, u32[]{:S(2)}) collective-permute-start(bf16[80,512]{1,0:T(8,128)(2,1)S(1)} %get-tuple-element.94), channel_id=1, source_target_pairs={{0,2},{1,3},{2,0},{3,1},{4,6},{5,7},{6,4},{7,5},{8,10},{9,11},{10,... | collective-permute-start | bytes 245768 | tf_op jit(solution)/shard_map/ppermute | solution.py:26
  106.2 6.2 %collective-permute-start.28 = (bf16[80,512]{1,0:T(8,128)(2,1)S(1)}, bf16[80,512]{1,0:T(8,128)(2,1)S(1)}, u32[]{:S(2)}, u32[]{:S(2)}) collective-permute-start(bf16[80,512]{1,0:T(8,128)(2,1)S(1)} %get-tuple-element.95), channel_id=1, source_target_pairs={{0,4},{1,5},{2,6},{3,7},{4,0},{5,1},{6,2},{7,3},{8,12},{9,13},{10,... | collective-permute-start | bytes 245768 | tf_op jit(solution)/shard_map/ppermute | solution.py:26
  108.6 6.2 %collective-permute-start.29 = (bf16[80,512]{1,0:T(8,128)(2,1)S(1)}, bf16[80,512]{1,0:T(8,128)(2,1)S(1)}, u32[]{:S(2)}, u32[]{:S(2)}) collective-permute-start(bf16[80,512]{1,0:T(8,128)(2,1)S(1)} %get-tuple-element.96), channel_id=1, source_target_pairs={{0,6},{1,7},{2,4},{3,5},{4,2},{5,3},{6,0},{7,1},{8,14},{9,15},{10,... | collective-permute-start | bytes 245768 | tf_op jit(solution)/shard_map/ppermute | solution.py:26

commit v3 on v2

--- a/solution.py
+++ b/solution.py
@@ -17,6 +17,7 @@
 eps_norm = 1e-06
 rope_base = 50000.0
 neg_fill = -1e30
+LOG2E = 1.4426950408889634
 bf16 = jnp.bfloat16
 f32 = jnp.float32
 
@@ -85,30 +86,52 @@
         eye.astype(f32).astype(bf16),
         (((0,), (0,)), ((), ())),
         preferred_element_type=f32,
-    ).astype(bf16)
+    )
 
 
 def query_kernel(
-    pre, dec, gain, weight_hbm, cosine, sine, ids, gates, dec_ids, dec_gates,
-    message, query_d, table_d, normed, weight, sem,
+    pre_hbm, dec_hbm, gain_hbm, weight_hbm, ids_hbm, gates_hbm, dec_ids_hbm, dec_gates_hbm, cosine, sine,
+    message, query_d, table_d, normed, dec_pad,
+    pre, dec, gain, weight, ids, gates, dec_ids, dec_gates, rows, sems,
 ):
-    copy = pltpu.make_async_copy(weight_hbm, weight, sem)
-    copy.start()
+    sources = (pre_hbm, dec_hbm, gain_hbm, ids_hbm, gates_hbm, dec_ids_hbm, dec_gates_hbm)
+    targets = (pre, dec, gain, ids, gates, dec_ids, dec_gates)
+    copies = [
+        pltpu.make_async_copy(source, target, sems.at[index])
+        for index, (source, target) in enumerate(zip(sources, targets))
+    ]
+    depth = weight.shape[0] // 4
+    for part in range(4):
+        here = pl.ds(part * depth, depth)
+        copies.append(
+            pltpu.make_async_copy(weight_hbm.at[here], weight.at[here], sems.at[len(sources) + part])
+        )
+    for copy in copies:
+        copy.start()
     tok = pre.shape[0]
     width = weight.shape[1]
-
-    def norm(rows):
-        values = rows.astype(f32)
+    heads = dec_pad.shape[0] // 8
+    share = DEC // heads
+    for copy in copies[:7]:
+        copy.wait()
+
+    def norm(values):
         meansq = jnp.mean(values * values, axis=-1, keepdims=True)
         return (values * lax.rsqrt(meansq + eps_norm) * gain[...]).astype(bf16)
 
-    normed[0:tok, :] = norm(pre[...])
+    dec_rows = dec[...].astype(f32)
+    normed[0:tok, :] = norm(pre[...].astype(f32))
     normed[tok:, :] = jnp.zeros_like(normed[tok:, :])
-    normed[tok : tok + DEC, :] = norm(dec[...])
-    message[:, width:] = gate_lanes(ids, gates, message.shape[1] - width)
-    table_d[...] = jnp.zeros_like(table_d)
-    table_d[0:DEC, :] = gate_lanes(dec_ids, dec_gates, table_d.shape[1])
-    copy.wait()
+    normed[tok : tok + DEC, :] = norm(dec_rows)
+    dec_table = gate_lanes(dec_ids, dec_gates, table_d.shape[1])
+    message[:, width:] = gate_lanes(ids, gates, message.shape[1] - width).astype(bf16)
+    for out, source in ((dec_pad, dec_rows), (table_d, dec_table)):
+        rows[...] = jnp.zeros_like(rows)
+        for head in range(heads):
+            rows[8 * head : 8 * head + share, : source.shape[1]] = source[share * head : share * (head + 1)]
+        out[...] = rows[:, : source.shape[1]].astype(out.dtype)
+    for copy in copies[7:]:
+        copy.wait()
     query = jnp.dot(normed[...], weight[...], preferred_element_type=f32)
     query = turn(query, cosine[...], sine[...])
     message[:, :width] = query[:tok]
@@ -116,7 +139,7 @@
 
 
 def key_kernel(
-    normed, key_hbm, value_hbm, cosine, sine, new, dec, key_d, value_d, w_key, w_value, sems
+    normed, key_hbm, value_hbm, cosine, sine, new, dec, key_n, value_n, key_d, value_d, w_key, w_value, sems
 ):
     tok = new.shape[1]
     copies = [
@@ -129,8 +152,9 @@
         copy.wait()
     key = turn(jnp.dot(normed[...], w_key[...], preferred_element_type=f32), cosine[...], sine[...])
     value = jnp.dot(normed[...], w_value[...], preferred_element_type=f32).astype(bf16)
-    for index, (rows, padded) in enumerate(((key, key_d), (value, value_d))):
+    for index, (rows, plain, padded) in enumerate(((key, key_n, key_d), (value, value_n, value_d))):
         new[index] = rows[:tok]
+        plain[...] = rows[:tok]
         dec[index] = rows[tok : tok + DEC]
         padded[...] = rows[tok:]
 
@@ -149,11 +173,12 @@
 def group_turned(query, keys, values, live):
     scores = lax.dot_general(
         keys, query, (((1,), (1,)), ((), ())), preferred_element_type=f32
-    ) * HD ** (-0.5)
+    )
     top = jnp.max(
         scores if live is None else jnp.where(live, scores, neg_fill), axis=0, keepdims=True
     )
-    weights = jnp.exp(scores - top)
+    weights = jnp.exp2((scores - top) * (HD ** (-0.5) * LOG2E))
+    top = top * HD ** (-0.5)
     if live is not None:
         weights = jnp.where(live, weights, 0.0)
     total = jnp.sum(weights, axis=0, keepdims=True)
@@ -164,7 +189,7 @@
 
 
 def attention_kernel(
-    owner_ref, slot_ref, lens_ref, blk_ref, query_a, query_b, query_d, new, key_dec, value_dec,
+    owner_ref, slot_ref, lens_ref, blk_ref, query_a, query_b, query_d, key_new, value_new, key_dec, value_dec,
     cache_k, cache_v, keep, send, dec, key_buf, value_buf, tops, totals, sems,
 ):
     blocks, block_len, width = cache_k.shape
@@ -190,7 +215,7 @@
                     body(query[row : row + tile, lanes(head)], state, slice(row, row + tile), head)
 
     def start(query, state, columns, head):
-        top, total, acc = group_turned(query, new[0, :, lanes(head)], new[1, :, lanes(head)], None)
+        top, total, acc = group_turned(query, key_new[:, lanes(head)], value_new[:, lanes(head)], None)
         state[width + head : width + head + 1, columns] = top
         state[width + heads + head : width + heads + head + 1, columns] = total
         state[lanes(head), columns] = acc
@@ -267,7 +292,7 @@
     dec[:, width:] = packed
 
 
-def attention(query_a, query_b, query_d, new, key_d, value_d, cache_keys, cache_values, scalars):
+def attention(query_a, query_b, query_d, new, cache_keys, cache_values, scalars):
     half = query_a.shape[0]
     blocks, block_len, width = cache_keys.shape
     heads = width // HD
@@ -275,8 +300,8 @@
     return call(
         attention_kernel,
         (state, state, ((DPAD, width + HD), f32)),
-        [SMEM] * 4 + [VMEM] * 6 + [HBM] * 2,
-        (*scalars, query_a, query_b, query_d, new, key_d, value_d, cache_keys, cache_values),
+        [SMEM] * 4 + [VMEM] * 7 + [HBM] * 2,
+        (*scalars, query_a, query_b, query_d, *new, cache_keys, cache_values),
         "attention",
         24,
         [
@@ -351,171 +376,252 @@
     )
 
 
+def load_kernel(count, *refs):
+    sources, targets, sems = refs[:count], refs[count + 1 : -1], refs[-1]
+    copies = []
+    for source, target in zip(sources, targets):
+        depth = source.shape[-2] // 4
+        for lead in range(source.shape[0]) if len(source.shape) == 3 else (None,):
+            for part in range(4):
+                here = pl.ds(part * depth, depth)
+                where = here if lead is None else (lead, here)
+                copies.append(
+                    pltpu.make_async_copy(source.at[where], target.at[where], sems.at[len(copies)])
+                )
+    for copy in copies:
+        copy.start()
+    for copy in copies:
+        copy.wait()
+
+
+def load(arrays, after, name):
+    size = sum(arr.size for arr in arrays) * 2
+    count = sum(4 * (arr.shape[0] if arr.ndim == 3 else 1) for arr in arrays)
+    return call(
+        functools.partial(load_kernel, len(arrays)),
+        tuple((arr.shape, arr.dtype) for arr in arrays),
+        [HBM] * len(arrays) + [VMEM],
+        (*arrays, after),
+        name,
+        1,
+        [pltpu.SemaphoreType.DMA((count,))],
+        pl.CostEstimate(flops=0, transcendentals=0, bytes_accessed=2 * size),
+    )
+
+
 def project_kernel(parts, head_ref, *refs):
     pieces = refs[:parts]
-    weight_hbm = refs[parts]
-    weight, sem = refs[-2:]
+    weight = refs[parts]
     outs = refs[parts + 1 : -2]
-    copy = pltpu.make_async_copy(weight_hbm, weight, sem)
-    copy.start()
+    arranged, product = refs[-2:]
     rows, full = pieces[0].shape
     width = full - HD
     heads = width // HD
-    columns = outs[0].shape[1]
+    group_rows = outs[0].shape[0]
+    places = len(outs)
+    share = (rows - DPAD) // places
+    dec_share = DEC // places
     stats = []
     for piece in pieces:
         coded = piece[:, width:].astype(f32)
         stats.append(
             (coded + pltpu.roll(coded, HD - 2 * heads, 1)) + pltpu.roll(coded, HD - 4 * heads, 1)
         )
-    attended = []
+    arranged[...] = jnp.zeros_like(arranged)
     for head in range(heads):
         tops = [s[:, head : head + 1] for s in stats]
         best = functools.reduce(jnp.maximum, tops)
         scales = [jnp.exp(top - best) for top in tops]
         total = tree_sum([s[:, heads + head : heads + head + 1] * c for s, c in zip(stats, scales)])
         acc = tree_sum([piece[:, lanes(head)].astype(f32) * c for piece, c in zip(pieces, scales)])
-        attended.append((acc / total).astype(bf16))
-    attended = jnp.concatenate(attended, axis=1)
-    copy.wait()
+        attended = acc / total
+        for place in range(places):
+            row = group_rows * place
+            arranged[row : row + share, lanes(head)] = attended[share * place : share * (place + 1)]
+            start = rows - DPAD + dec_share * place
+            arranged[row + share : row + share + dec_share, lanes(head)] = attended[start : start + dec_share]
+    product[...] = jnp.dot(arranged[...].astype(bf16), weight[...], preferred_element_type=f32)
     for offset, out in enumerate(outs):
-        place = lax.bitwise_xor(head_ref[0], offset)
-        out[...] = jnp.dot(attended, weight[:, span(place, columns)], preferred_element_type=f32)
+        out[...] = product[span(lax.bitwise_xor(head_ref[0], offset), group_rows), :].astype(out.dtype)
 
 
 def project_out(pieces, w_output, head_index, head_count):
     rows = pieces[0].shape[0]
-    columns = w_output.shape[1] // head_count
+    share = (rows - DPAD) // head_count + 8
+    width, columns = w_output.shape
     return call(
         functools.partial(project_kernel, len(pieces)),
-        (((rows, columns), f32),) * head_count,
-        [SMEM] + [VMEM] * len(pieces) + [HBM],
+        (((share, columns), f32),) + (((share, columns), bf16),) * (head_count - 1),
+        [SMEM] + [VMEM] * (len(pieces) + 1),
         (head_index, *pieces, w_output),
         "project_out",
-        12,
-        [pltpu.VMEM(w_output.shape, bf16), pltpu.SemaphoreType.DMA],
-    )
-
-
-def mid_kernel(head_ref, pre, dec, *refs):
-    parts, (mid, square) = refs[:-2], refs[-2:]
-    tok, width = pre.shape[0], mid.shape[1]
-    here = span(head_ref[0], width)
-    total = tree_sum([part[...] for part in parts])
-    mid[0:tok, :] = pre[:, here].astype(f32) + total[:tok]
-    mid[tok : tok + DEC, :] = dec[:, here].astype(f32) + total[tok : tok + DEC]
-    mid[tok + DEC :, :] = jnp.zeros_like(mid[tok + DEC :, :])
+        8,
+        [pltpu.VMEM((share * head_count, width), f32), pltpu.VMEM((share * head_count, columns), f32)],
+    )
+
+
+def norm_kernel(parts, head_ref, pre_hbm, dec_pad, gain, *refs):
+    arrived = refs[:parts]
+    tokens, dec = refs[parts : parts + 2]
+    mids = refs[parts + 2 : 2 * parts + 2]
+    rows, mid, sem = refs[2 * parts + 2 :]
+    share = rows.shape[0]
+    head = head_ref[0]
+    copy = pltpu.make_async_copy(pre_hbm.at[span(head, share)], rows, sem)
+    copy.start()
+    total = tree_sum([part[...].astype(f32) for part in arrived])
+    copy.wait()
+    mid[0:share, :] = rows[...].astype(f32) + total[:share]
+    mid[share:, :] = dec_pad[span(head, 8), :] + total[share:]
+    for offset, out in enumerate(mids):
+        out[...] = mid[:, span(lax.bitwise_xor(head, offset), out.shape[1])]
     values = mid[...]
-    values = values * values
-    square[...] = tree_sum([values[:, lanes(part)] for part in range(width // HD)])
-
-
-def norm_kernel(model_width, head_ref, mid, gain, *refs):
-    squares, (tokens, dec) = refs[:-2], refs[-2:]
-    tok, width = tokens.shape
-    total = jnp.sum(tree_sum([square[...] for square in squares]), axis=-1, keepdims=True)
-    scaled = mid[...] * lax.rsqrt(total / model_width + eps_norm) * gain[:, span(head_ref[0], width)]
-    scaled = scaled.astype(bf16)
-    tokens[...] = scaled[:tok]
-    dec[...] = scaled[tok:]
-
-
-def experts_kernel(chunks, scalar_ref, *refs):
-    data = refs[:chunks]
-    query, table_d = refs[chunks : chunks + 2]
-    table = query.at[:, query.shape[1] - table_d.shape[1] :]
-    hbm = refs[chunks + 2 : chunks + 8]
-    outs = refs[chunks + 8 : 2 * chunks + 8]
-    bufs = refs[2 * chunks + 8 : 2 * chunks + 11]
-    gates, first, second, sems = refs[2 * chunks + 11 :]
-    each = hbm[0].shape[0]
+    meansq = jnp.mean(values * values, axis=-1, keepdims=True)
+    scaled = values * lax.rsqrt(meansq + eps_norm) * gain[...]
+    tokens[...] = scaled[:share].astype(bf16)
+    dec[...] = scaled[share:].astype(bf16)
+
+
+def experts_kernel(offsets, chunks, chips, scalar_ref, *refs):
+    count = len(offsets)
+    data = refs[:count]
+    query, table_d = refs[count : count + 2]
+    weights = refs[count + 2 : count + 8]
+    outs = refs[count + 8 : count + 8 + chunks]
+    rows_in, table = refs[count + 8 + chunks :]
+    each = weights[0].shape[0]
     experts = 2 * each
-    rows, width = data[0].shape
-    half = rows - DPAD
-    tile = min(TILE, half)
+    piece, depth = data[0].shape
+    width = depth // chunks
+    long = piece - 8
+    share = long // chips
+    tok = share * chunks
+    base = query.shape[1] - table_d.shape[1]
+    rows = count * piece
+    tile = rows if rows <= 320 else piece
     places = [lax.bitwise_xor(scalar_ref[0], offset) for offset in range(chunks)]
-
-    def copies(expert):
-        source = hbm[:3] if expert < each else hbm[3:]
-        return [
-            pltpu.make_async_copy(src.at[expert % each], buf.at[expert], sems.at[kind, expert])
-            for kind, (src, buf) in enumerate(zip(source, bufs))
-        ]
-
-    for expert in range(experts):
-        for copy in copies(expert):
-            copy.start()
-    w_gate, w_up, w_down = bufs
-    for expert in range(experts):
-        number = lax.bitwise_xor(scalar_ref[1], expert // each) * each + expert % each
-        for ref, row in ((table, 0), (table_d, half)):
-            place = lax.broadcasted_iota(jnp.int32, ref.shape, 1)
-            found = jnp.where(place == number, ref[...].astype(f32), 0.0)
-            gates[expert, row : row + ref.shape[0], :] = jnp.sum(found, axis=-1, keepdims=True)
-    for expert in range(experts):
-        for copy in copies(expert):
-            copy.wait()
-        total = first if expert < each else second
-        for row in range(0, half, tile):
-            size = tile + (DPAD if row + tile == half else 0)
-            gate = up = None
-            for part, place in zip(data, places):
-                block = part[row : row + size, :]
-                g = jnp.dot(block, w_gate[expert, span(place, width), :], preferred_element_type=f32)
-                u = jnp.dot(block, w_up[expert, span(place, width), :], preferred_element_type=f32)
-                gate = g if gate is None else gate + g
-                up = u if up is None else up + u
+    for index, offset in enumerate(offsets):
+        rows_in[long * index : long * (index + 1), :] = data[index][:long, :]
+        row = long * count + 8 * index
+        rows_in[row : row + 8, :] = data[index][long:, :]
+        table[row : row + 8, :] = table_d[span(places[offset], 8), :]
+        for chip in range(chips):
+            row = long * index + share * chip
+            start = pl.multiple_of(tok * chip + share * places[offset], share)
+            table[row : row + share, :] = query[pl.ds(start, share), base:].astype(f32)
+    lane = lax.broadcasted_iota(jnp.int32, (tile, table.shape[1]), 1)
+    found = {}
+    for row in range(0, rows, tile):
+        here = slice(row, row + tile)
+        block = rows_in[here, :]
+        for expert in range(experts):
+            w_gate, w_up, _ = weights[:3] if expert < each else weights[3:]
+            local = expert % each
+            number = lax.bitwise_xor(scalar_ref[1], expert // each) * each + local
+            gate = jnp.dot(block, w_gate[local], preferred_element_type=f32)
+            up = jnp.dot(block, w_up[local], preferred_element_type=f32)
             act = (gate / (1.0 + jnp.exp(-gate)) * up).astype(bf16)
-            factor = gates[expert, row : row + size, :]
-            for index, place in enumerate(places):
-                down = jnp.dot(act, w_down[expert, :, span(place, width)], preferred_element_type=f32)
-                down = down.astype(bf16).astype(f32) * factor
-                if expert % each:
-                    down = total[index, row : row + size, :] + down
-                if expert == experts - 1:
-                    down = first[index, row : row + size, :] + down
-                    outs[index][row : row + size, :] = down.astype(bf16)
-                else:
-                    total[index, row : row + size, :] = down
-
-
-def run_experts(data, query, table_d, own, other, scalars):
-    chunks = len(data)
-    rows, width = data[0].shape
-    experts = 2 * own[0].shape[0]
-    return call(
-        functools.partial(experts_kernel, chunks),
-        (((rows, width), bf16),) * chunks,
-        [SMEM] + [VMEM] * (chunks + 2) + [HBM] * 6,
-        (scalars, *data, query, table_d, *own, *other),
-        "experts",
-        32,
-        [pltpu.VMEM((experts, *w.shape[1:]), bf16) for w in own]
-        + [
-            pltpu.VMEM((experts, rows, 1), f32),
-            pltpu.VMEM((chunks, rows, width), f32),
-            pltpu.VMEM((chunks, rows, width), f32),
-            pltpu.SemaphoreType.DMA((3, experts)),
-        ],
-    )
-
-
-def head_sum_kernel(parts, *refs):
-    total = tree_sum([ref[...].astype(f32) for ref in refs[:parts]]).astype(bf16)
-    outs = refs[parts:]
-    half = total.shape[0] - DPAD
-    tok = half // len(outs)
-    for index, out in enumerate(outs):
-        out[0:tok, :] = total[index * tok : (index + 1) * tok]
-        out[tok:, :] = total[half:]
-
-
-def final_kernel(mid, *refs):
-    parts, (hidden, dec) = refs[:-2], refs[-2:]
+            factor = jnp.sum(jnp.where(lane == number, table[here, :], 0.0), axis=-1, keepdims=True)
+            found[row, expert] = act, factor
+    dec_share = DEC // chunks
+    for out, place in zip(outs, places):
+        values = []
+        for row in range(0, rows, tile):
+            sums = []
+            for first in (0, each):
+                total = None
+                for expert in range(first, first + each):
+                    act, factor = found[row, expert]
+                    w_down = weights[2 if first == 0 else 5]
+                    down = jnp.dot(
+                        act, w_down[expert % each, :, span(place, width)], preferred_element_type=f32
+                    )
+                    down = down.astype(bf16).astype(f32) * factor
+                    total = down if total is None else total + down
+                sums.append(total)
+            values.append(sums[0] + sums[1])
+        value = values[0] if len(values) == 1 else jnp.concatenate(values, axis=0)
+        out[: long * count, :] = value[: long * count].astype(bf16)
+        out[long * count :, :] = jnp.zeros_like(out[long * count :, :])
+        for index in range(count):
+            start = long * count + 8 * index
+            row = long * count + dec_share * index
+            out[row : row + dec_share, :] = value[start : start + dec_share].astype(bf16)
+
+
+def run_experts(data, offsets, query, table_d, weights, scalars, chips, chunks, name):
+    count = len(data)
+    piece, depth = data[0].shape
+    width = depth // chunks
+    tail = -(-(DEC // chunks) * count // 8) * 8
+    return list(
+        call(
+            functools.partial(experts_kernel, offsets, chunks, chips),
+            ((((piece - 8) * count + tail, width), bf16),) * chunks,
+            [SMEM] + [VMEM] * (count + 8),
+            (scalars, *data, query, table_d, *weights),
+            name,
+            28,
+            [
+                pltpu.VMEM((count * piece, depth), bf16),
+                pltpu.VMEM((count * piece, table_d.shape[1]), f32),
+            ],
+            pl.CostEstimate(
+                flops=12 * count * piece * depth * weights[0].shape[2],
+                transcendentals=0,
+                bytes_accessed=2 * sum(w.size for w in weights),
+            ),
+        )
+    )
+
+
+def head_sum_kernel(parts, share, *refs):
+    early, late, outs = refs[:parts], refs[parts : 2 * parts], refs[2 * parts :]
+    chips = len(outs)
+    long = share * chips
+    tok = share * parts
+    dec_share = DEC // parts
+    for out in outs:
+        out[tok:, :] = jnp.zeros_like(out[tok:, :])
+    for mine in range(parts):
+        found, found_d = [], []
+        for sender in range(parts):
+            index = mine ^ sender
+            source, count = early[sender], parts - 1
+            if index == parts - 1:
+                source, index, count = late[sender], 0, 1
+            found.append(source[long * index : long * (index + 1), :].astype(f32))
+            row = long * count + dec_share * index
+            found_d.append(source[row : row + dec_share, :].astype(f32))
+        total = tree_sum(found).astype(bf16)
+        total_d = tree_sum(found_d).astype(bf16)
+        for chip, out in enumerate(outs):
+            out[share * mine : share * (mine + 1), :] = total[share * chip : share * (chip + 1)]
+            out[tok + dec_share * mine : tok + dec_share * (mine + 1), :] = total_d
+
+
+def final_kernel(parts, head_ref, *refs):
+    mids, pieces = refs[:parts], refs[parts:-4]
+    hidden, dec, packed, placed = refs[-4:]
     tok = hidden.shape[0]
-    total = mid[...] + tree_sum([part[...].astype(f32) for part in parts])
-    hidden[...] = total[:tok].astype(bf16)
-    dec[...] = total[tok : tok + DEC].astype(bf16)
+    share = tok // parts
+    dec_share = DEC // parts
+    total = tree_sum([piece[...].astype(f32) for piece in pieces])
+    packed[...] = jnp.zeros_like(packed)
+    for offset, mid in enumerate(mids):
+        place = lax.bitwise_xor(head_ref[0], offset)
+        hidden[span(place, share), :] = (
+            mid[0:share, :] + total[share * offset : share * (offset + 1)]
+        ).astype(bf16)
+        start = tok + dec_share * offset
+        packed[8 * offset : 8 * offset + dec_share, :] = (
+            mid[share : share + dec_share, :] + total[start : start + dec_share]
+        )
+        placed[span(place, 8), :] = packed[8 * offset : 8 * offset + 8, :]
+    for place in range(parts):
+        dec[dec_share * place : dec_share * (place + 1), :] = placed[
+            8 * place : 8 * place + dec_share, :
+        ].astype(bf16)
 
 
 def per_device(
@@ -547,32 +653,41 @@
     cosine = jnp.concatenate([cosine, cosine], axis=1)
     sine = jnp.concatenate([-sine, sine], axis=1)
 
-    message, query_d, table_d, normed = call(
+    dec_rows = 8 * head_count
+    sources = (
+        pre_tokens, dec_tokens, attn_gain[None, :], w_query,
+        expert_ids.T, expert_gates.T, dec_expert_ids.T, dec_expert_gates.T,
+    )
+    message, query_d, table_d, normed, dec_pad = call(
         query_kernel,
         (
             ((tok, width + tables), bf16),
             ((DPAD, width), bf16),
-            ((DPAD, tables), bf16),
+            ((dec_rows, tables), f32),
             ((rows, model_width), bf16),
+            ((dec_rows, model_width), f32),
         ),
-        [VMEM] * 3 + [HBM] + [VMEM] * 6,
-        (
-            pre_tokens, dec_tokens, attn_gain[None, :], w_query, cosine, sine,
-            expert_ids.T, expert_gates.T, dec_expert_ids.T, dec_expert_gates.T,
-        ),
+        [HBM] * 8 + [VMEM] * 2,
+        (*sources, cosine, sine),
         "queries",
         16,
-        [pltpu.VMEM(w_query.shape, bf16), pltpu.SemaphoreType.DMA],
+        [
+            *(pltpu.VMEM(source.shape, source.dtype) for source in sources),
+            pltpu.VMEM((dec_rows, model_width), f32),
+            pltpu.SemaphoreType.DMA((len(sources) + 3,)),
+        ],
     )
 
     def exchange(pieces, axis, step):
         return [pieces[0]] + [swap(pieces[o], axis, step * o) for o in range(1, len(pieces))]
 
-    new_cache, dec_cache, key_d, value_d = call(
+    new_cache, dec_cache, *new = call(
         key_kernel,
         (
             ((2, tok, width), bf16),
             ((2, DEC, width), bf16),
+            ((tok, width), bf16),
+            ((tok, width), bf16),
             ((DPAD, width), bf16),
             ((DPAD, width), bf16),
         ),
@@ -596,58 +711,75 @@
     new_cache, *pieces = lax.optimization_barrier((new_cache, *pieces))
     query_a = jnp.concatenate(pieces, axis=0)
     query_b = swap(query_a, "blk", 1)
-    query_b, gate_other, up_source = lax.optimization_barrier((query_b, gate_other, w_up))
+    query_b, gate_other = lax.optimization_barrier((query_b, gate_other))
+
+    keep, send, dec = attention(
+        query_a, query_b, query_d, new, cache_keys, cache_values,
+        (block_request, block_slot, cache_lens, blk_index.reshape(1)),
+    )
+    pieces = merge_core(keep, swap(send, "blk", 1), dec, swap(dec, "blk", 1), chips)
+    *pieces, up_source = lax.optimization_barrier((*pieces, w_up))
     up_other = swap(up_source, "blk", 1)
-
-    keep, send, dec = attention(
-        query_a, query_b, query_d, new_cache, key_d, value_d, cache_keys, cache_values,
-        (block_request, block_slot, cache_lens, blk_index.reshape(1)),
-    )
-    send, up_other = lax.optimization_barrier((send, up_other))
-    pieces = merge_core(keep, swap(send, "blk", 1), dec, swap(dec, "blk", 1), chips)
-    *pieces, down_source = lax.optimization_barrier((*pieces, w_down))
+    (weight,) = load((w_output,), pieces[0], "load_output")
+    pieces = exchange(pieces, "blk", 2)
+    pieces[-1], weight, up_other = lax.optimization_barrier((pieces[-1], weight, up_other))
+    partial = project_out(pieces, weight, head_scalar, head_count)
+    *partial, down_source = lax.optimization_barrier((*partial, w_down))
     down_other = swap(down_source, "blk", 1)
-    pieces = exchange(pieces, "blk", 2)
-    partial = exchange(project_out(pieces, w_output, head_scalar, head_count), "head", 1)
-    mid, square = call(
-        mid_kernel,
-        (((rows, part_width), f32), ((rows, HD), f32)),
-        [SMEM] + [VMEM] * (2 + head_count),
-        (head_scalar, pre_tokens, dec_tokens, *partial),
-        "mid",
-        8,
-    )
-    squares = exchange([square] * head_count, "head", 1)
-    moe_tok, moe_dec = call(
-        functools.partial(norm_kernel, model_width),
-        (((tok, part_width), bf16), ((DPAD, part_width), bf16)),
-        [SMEM] + [VMEM] * (2 + head_count),
-        (head_scalar, mid, moe_gain[None, :], *squares),
+    partial = exchange(partial, "head", 1)
+    partial[-1], down_other = lax.optimization_barrier((partial[-1], down_other))
+    share = tok // head_count
+    moe_tok, moe_dec, *mids = call(
+        functools.partial(norm_kernel, head_count),
+        (
+            ((share, model_width), bf16),
+            ((8, model_width), bf16),
+            *(((share + 8, part_width), f32),) * head_count,
+        ),
+        [SMEM, HBM] + [VMEM] * (2 + head_count),
+        (head_scalar, pre_tokens, dec_pad, moe_gain[None, :], *partial),
         "moe_norm",
         8,
-    )
-    gathered = jnp.concatenate([*exchange([moe_tok] * chips, "blk", 2), moe_dec], axis=0)
+        [
+            pltpu.VMEM((share, model_width), bf16),
+            pltpu.VMEM((share + 8, model_width), f32),
+            pltpu.SemaphoreType.DMA,
+        ],
+    )
+    spread = exchange([moe_tok] * chips, "blk", 2)
+    mids[1:-1] = [swap(mids[o], "head", o) for o in range(1, head_count - 1)]
+    spread[-1], *mids[1:-1] = lax.optimization_barrier((spread[-1], *mids[1:-1]))
+    gathered = jnp.concatenate([*spread, moe_dec], axis=0)
     data = exchange([gathered] * head_count, "head", 1)
-    results = run_experts(
-        data, query_a, table_d, (w_gate, w_up, w_down), (gate_other, up_other, down_other), scalars
-    )
-    results = exchange(results, "head", 1)
+    weights = load((w_gate, w_up, w_down), gathered, "load_experts")
+    data[1], *weights = lax.optimization_barrier((data[1], *weights))
+    weights = (*weights, gate_other, up_other, down_other)
+    offsets = tuple(range(head_count))
+    shared = (query_a, table_d, weights, scalars, chips, head_count)
+    early = run_experts(data[:-1], offsets[:-1], *shared, "experts_early")
+    late = run_experts(data[-1:], offsets[-1:], *shared, "experts_late")
+    early = exchange(early, "head", 1)
+    late = exchange(late, "head", 1)
     final = call(
-        functools.partial(head_sum_kernel, head_count),
+        functools.partial(head_sum_kernel, head_count, share),
         (((rows, part_width), bf16),) * chips,
-        [VMEM] * head_count,
-        results,
+        [VMEM] * (2 * head_count),
+        (*early, *late),
         "head_sum",
         8,
     )
+    final = list(final)
+    *final, mids[-1] = lax.optimization_barrier((*final, mids[-1]))
     final = exchange(final, "blk", 2)
+    mids[-1] = swap(mids[-1], "head", head_count - 1)
     hidden, dec_hidden = call(
-        final_kernel,
+        functools.partial(final_kernel, head_count),
         (((tok, part_width), bf16), ((DEC, part_width), bf16)),
-        [VMEM] * (1 + chips),
-        (mid, *final),
+        [SMEM] + [VMEM] * (head_count + chips),
+        (head_scalar, *mids, *final),
         "final",
         8,
+        [pltpu.VMEM((dec_rows, part_width), f32), pltpu.VMEM((dec_rows, part_width), f32)],
     )
     return (hidden, dec_hidden, new_cache, dec_cache)
 

time: 117 us -> 111 us (0.949)
  waiting for transfers between devices: 46.5 us -> 33.1 us
  Pallas kernels: 24.1 us -> 32.9 us
  local copies, waits for them, and re-layouts: 8.22 us -> 0.74 us
  starting transfers between devices: 34.7 us -> 41.9 us
    ppermute x30 -> x33, waiting for transfers between devices: 46.5 us -> 33.1 us  [swap(): return lax.ppermute(value, axis, [(i, i ^ mask) for i in range(count)])]
    pallas_call x10 -> x12, Pallas kernels: 24.1 us -> 32.9 us  [call(): pl.pallas_call(body, out_shape=tuple((jax.ShapeDtypeStruct(shape, dtype)...]
    unnamed x42 -> x18, local copies, waits for them, and re-layouts: 8.2 us -> 0.72 us
    ppermute x30 -> x33, starting transfers between devices: 34.7 us -> 41.9 us  [swap(): return lax.ppermute(value, axis, [(i, i ^ mask) for i in range(count)])]
  transfers between devices with their start and end apart: 30 -> 33, of which waited for: 17 -> 16; matrix products, arithmetic and copies ran while one was open for 2% -> 2% of each run, Pallas kernels for 13% -> 18%
where the time goes in v3:
time: 111 us
  starting transfers between devices  41.9 us (38%)
  waiting for transfers between devices  33.1 us (30%)
  Pallas kernels  32.9 us (30%)
  other arithmetic  1.16 us (1%)
    ppermute x33, starting transfers between devices, swap(): return lax.ppermute(value, axis, [(i, i ^ mask) for i in range(count)])  41.9 us
    ppermute x33, waiting for transfers between devices, swap(): return lax.ppermute(value, axis, [(i, i ^ mask) for i in range(count)])  33.1 us
    pallas_call x12, Pallas kernels, call(): pl.pallas_call(body, out_shape=tuple((jax.ShapeDtypeStruct(shape, dtype)...  32.9 us
  transfers between devices with their start and end apart: 33, of which 16 were waited for; matrix products, arithmetic and copies ran while one was open for 2% of the time, Pallas kernels for 18%

profile of v3, /device:TPU:0, one launch (start us, length us, event | category | flops | bytes accessed | tf_op | source)
XLA Modules:
  0.0 110.6 jit_solution(13803369092369257609)
XLA Ops:
  1.2 0.7 select_reduce_fusion
  2.2 2.4 %queries.1 = (bf16[64,640]{1,0:T(8,128)(2,1)S(1)}, bf16[16,512]{1,0:T(8,128)(2,1)S(1)}, f32[32,128]{1,0:T(8,128)S(1)}, bf16[80,2048]{1,0:T(8,128)(2,1)S(1)}, f32[32,2048]{1,0:T(8,128)S(1)}) custom-call(bf16[64,2048]{1,0:T(8,128)(2,1)} %pre_hbm.3, bf16[12,2048]{1,0:T(8,128)(2,1)} %dec_hbm.1, f32[1,2048]{1,0:T(1,128)} %bitcast.9, ...), custom_call_target="tpu_custom_call" | custom-call | tf_op jit(solution)/shard_map/queries/pallas_call | solution.py:55
  4.7 2.7 %collective-permute-start = (bf16[64,640]{1,0:T(8,128)(2,1)S(1)}, bf16[64,640]{1,0:T(8,128)(2,1)S(1)}, u32[]{:S(2)}, u32[]{:S(2)}) collective-permute-start(bf16[64,640]{1,0:T(8,128)(2,1)S(1)} %get-tuple-element.87), channel_id=1, source_target_pairs={{0,2},{1,3},{2,0},{3,1},{4,6},{5,7},{6,4},{7,5},{8,10},{9,11},{10,... | collective-permute-start | bytes 245768 | tf_op jit(solution)/shard_map/ppermute | solution.py:27
  7.3 2.6 %collective-permute-start.1 = (bf16[64,640]{1,0:T(8,128)(2,1)S(1)}, bf16[64,640]{1,0:T(8,128)(2,1)S(1)}, u32[]{:S(2)}, u32[]{:S(2)}) collective-permute-start(bf16[64,640]{1,0:T(8,128)(2,1)S(1)} %get-tuple-element.87), channel_id=1, source_target_pairs={{0,4},{1,5},{2,6},{3,7},{4,0},{5,1},{6,2},{7,3},{8,12},{9,13},{10,... | collective-permute-start | bytes 245768 | tf_op jit(solution)/shard_map/ppermute | solution.py:27
  9.9 3.8 %keys.1 = (bf16[2,64,512]{2,1,0:T(8,128)(2,1)}, bf16[2,12,512]{2,1,0:T(8,128)(2,1)S(1)}, bf16[64,512]{1,0:T(8,128)(2,1)S(1)}, bf16[64,512]{1,0:T(8,128)(2,1)S(1)...) custom-call(bf16[80,2048]{1,0:T(8,128)(2,1)S(1)} %get-tuple-element.84.normed, bf16[2048,512]{1,0:T(8,128)(2,1)} %key_hbm.1, ...), custom_call_target="tpu_custom_call" | custom-call | flops 335544320 | bytes 4194304 | tf_op jit(solution)/shard_map/keys/pallas_call | solution.py:55
  13.7 3.2 %collective-permute-done.1 = bf16[64,640]{1,0:T(8,128)(2,1)S(1)} collective-permute-done((bf16[64,640]{1,0:T(8,128)(2,1)S(1)}, bf16[64,640]{1,0:T(8,128)(2,1)S(1)}, u32[]{:S(2)}, u32[]{:S(2)}) %collective-permute-start.1) | collective-permute-done | bytes 81952 | tf_op jit(solution)/shard_map/ppermute | solution.py:27
  17.0 1.6 %collective-permute-done.3.query_b = bf16[256,640]{1,0:T(8,128)(2,1)S(1)} collective-permute-done((bf16[256,640]{1,0:T(8,128)(2,1)S(1)}, bf16[256,640]{1,0:T(8,128)(2,1)S(1)}, u32[]{:S(2)}, u32[]{:S(2)}) %collective-permute-start.3) | collective-permute-done | bytes 327712 | tf_op jit(solution)/shard_map/ppermute | solution.py:27
  18.7 10.0 %attention.1 = (f32[520,256]{1,0:T(8,128)S(1)}, f32[520,256]{1,0:T(8,128)S(1)}, f32[16,640]{1,0:T(8,128)S(1)}) custom-call(s32[8]{0:T(128)S(1)} %copy-done.2, s32[8]{0:T(128)S(1)} %copy-done.3, s32[13]{0:T(128)S(1)} %copy-done.1, s32[1]{0:T(128)} %bitcast.7.blk_ref, bf16[256,640]{1,0:T(8,128)(2,1)S(1)} %constant_dynamic-update-slice_fusion.query_a.refs_3_.refs_1_, ...), custom_call_target="tpu_custom_call" | custom-call | tf_op jit(solution)/shard_map/attention/pallas_call | solution.py:55
  29.3 1.5 %collective-permute-done.6.dec_other = f32[16,640]{1,0:T(8,128)S(1)} collective-permute-done((f32[16,640]{1,0:T(8,128)S(1)}, f32[16,640]{1,0:T(8,128)S(1)}, u32[]{:S(2)}, u32[]{:S(2)}) %collective-permute-start.6) | collective-permute-done | bytes 40992 | tf_op jit(solution)/shard_map/ppermute | solution.py:27
  31.4 3.2 %collective-permute-start.9 = (bf16[80,640]{1,0:T(8,128)(2,1)S(1)}, bf16[80,640]{1,0:T(8,128)(2,1)S(1)}, u32[]{:S(2)}, u32[]{:S(2)}) collective-permute-start(bf16[80,640]{1,0:T(8,128)(2,1)S(1)} %get-tuple-element.107), channel_id=1, source_target_pairs={{0,6},{1,7},{2,4},{3,5},{4,2},{5,3},{6,0},{7,1},{8,14},{9,15},{10,... | collective-permute-start | bytes 307208 | tf_op jit(solution)/shard_map/ppermute | solution.py:27
  34.6 1.1 %collective-permute-start.8 = (bf16[80,640]{1,0:T(8,128)(2,1)S(1)}, bf16[80,640]{1,0:T(8,128)(2,1)S(1)}, u32[]{:S(2)}, u32[]{:S(2)}) collective-permute-start(bf16[80,640]{1,0:T(8,128)(2,1)S(1)} %get-tuple-element.106), channel_id=1, source_target_pairs={{0,4},{1,5},{2,6},{3,7},{4,0},{5,1},{6,2},{7,3},{8,12},{9,13},{10,... | collective-permute-start | bytes 307208 | tf_op jit(solution)/shard_map/ppermute | solution.py:27
  35.8 1.5 %load_output.1.refs_4_ = bf16[512,2048]{1,0:T(8,128)(2,1)S(1)} custom-call(bf16[512,2048]{1,0:T(8,128)(2,1)} %refs_0_.2, bf16[80,640]{1,0:T(8,128)(2,1)S(1)} %get-tuple-element.104.refs_1_.refs_0_), custom_call_target="tpu_custom_call" | custom-call | bytes 4194304 | tf_op jit(solution)/shard_map/load_output/pallas_call | solution.py:55
  37.3 1.6 %collective-permute-done.9.refs_3_ = bf16[80,640]{1,0:T(8,128)(2,1)S(1)} collective-permute-done((bf16[80,640]{1,0:T(8,128)(2,1)S(1)}, bf16[80,640]{1,0:T(8,128)(2,1)S(1)}, u32[]{:S(2)}, u32[]{:S(2)}) %collective-permute-start.9) | collective-permute-done | bytes 102432 | tf_op jit(solution)/shard_map/ppermute | solution.py:27
  38.9 2.7 %collective-permute-done.7.refs_1_ = bf16[80,640]{1,0:T(8,128)(2,1)S(1)} collective-permute-done((bf16[80,640]{1,0:T(8,128)(2,1)S(1)}, bf16[80,640]{1,0:T(8,128)(2,1)S(1)}, u32[]{:S(2)}, u32[]{:S(2)}) %collective-permute-start.7) | collective-permute-done | bytes 102432 | tf_op jit(solution)/shard_map/ppermute | solution.py:27
  41.6 2.4 %collective-permute-done.8.refs_2_ = bf16[80,640]{1,0:T(8,128)(2,1)S(1)} collective-permute-done((bf16[80,640]{1,0:T(8,128)(2,1)S(1)}, bf16[80,640]{1,0:T(8,128)(2,1)S(1)}, u32[]{:S(2)}, u32[]{:S(2)}) %collective-permute-start.8) | collective-permute-done | bytes 102432 | tf_op jit(solution)/shard_map/ppermute | solution.py:27
  44.0 0.9 project_out.1
  45.1 2.5 %collective-permute-start.13 = (bf16[24,2048]{1,0:T(8,128)(2,1)S(1)}, bf16[24,2048]{1,0:T(8,128)(2,1)S(1)}, u32[]{:S(2)}, u32[]{:S(2)}) collective-permute-start(bf16[24,2048]{1,0:T(8,128)(2,1)S(1)} %get-tuple-element.118), channel_id=1, source_target_pairs={{0,24},{8,16},{16,8},{24,0},{1,25},{9,17},{17,9},{25,1},{2,26},{10... | collective-permute-start | bytes 294920 | tf_op jit(solution)/shard_map/ppermute | solution.py:27
  48.6 3.0 %collective-permute-done.13.refs_3_ = bf16[24,2048]{1,0:T(8,128)(2,1)S(1)} collective-permute-done((bf16[24,2048]{1,0:T(8,128)(2,1)S(1)}, bf16[24,2048]{1,0:T(8,128)(2,1)S(1)}, u32[]{:S(2)}, u32[]{:S(2)}) %collective-permute-start.13) | collective-permute-done | bytes 98336 | tf_op jit(solution)/shard_map/ppermute | solution.py:27
  51.6 1.7 %collective-permute-done.11.refs_1_ = bf16[24,2048]{1,0:T(8,128)(2,1)S(1)} collective-permute-done((bf16[24,2048]{1,0:T(8,128)(2,1)S(1)}, bf16[24,2048]{1,0:T(8,128)(2,1)S(1)}, u32[]{:S(2)}, u32[]{:S(2)}) %collective-permute-start.11) | collective-permute-done | bytes 98336 | tf_op jit(solution)/shard_map/ppermute | solution.py:27
  53.4 1.0 moe_norm.1
  54.3 2.7 %collective-permute-start.15 = (bf16[16,2048]{1,0:T(8,128)(2,1)S(1)}, bf16[16,2048]{1,0:T(8,128)(2,1)S(1)}, u32[]{:S(2)}, u32[]{:S(2)}) collective-permute-start(bf16[16,2048]{1,0:T(8,128)(2,1)S(1)} %get-tuple-element.122), channel_id=1, source_target_pairs={{0,6},{1,7},{2,4},{3,5},{4,2},{5,3},{6,0},{7,1},{8,14},{9,15},{10,... | collective-permute-start | bytes 196616 | tf_op jit(solution)/shard_map/ppermute | solution.py:27
  57.1 1.7 %collective-permute-start.19 = (bf16[16,2048]{1,0:T(8,128)(2,1)S(1)}, bf16[16,2048]{1,0:T(8,128)(2,1)S(1)}, u32[]{:S(2)}, u32[]{:S(2)}) collective-permute-start(bf16[16,2048]{1,0:T(8,128)(2,1)S(1)} %get-tuple-element.122), channel_id=1, source_target_pairs={{0,4},{1,5},{2,6},{3,7},{4,0},{5,1},{6,2},{7,3},{8,12},{9,13},{10,... | collective-permute-start | bytes 196616 | tf_op jit(solution)/shard_map/ppermute | solution.py:27
  58.8 1.5 %collective-permute-start.16 = (f32[24,512]{1,0:T(8,128)S(1)}, f32[24,512]{1,0:T(8,128)S(1)}, u32[]{:S(2)}, u32[]{:S(2)}) collective-permute-start(f32[24,512]{1,0:T(8,128)S(1)} %get-tuple-element.123), channel_id=1, source_target_pairs={{0,8},{8,0},{16,24},{24,16},{1,9},{9,1},{17,25},{25,17},{2,10},{10... | collective-permute-start | bytes 147464 | tf_op jit(solution)/shard_map/ppermute | solution.py:27
  60.3 1.5 %collective-permute-start.17 = (f32[24,512]{1,0:T(8,128)S(1)}, f32[24,512]{1,0:T(8,128)S(1)}, u32[]{:S(2)}, u32[]{:S(2)}) collective-permute-start(f32[24,512]{1,0:T(8,128)S(1)} %get-tuple-element.124), channel_id=1, source_target_pairs={{0,16},{8,24},{16,0},{24,8},{1,17},{9,25},{17,1},{25,9},{2,18},{10... | collective-permute-start | bytes 147464 | tf_op jit(solution)/shard_map/ppermute | solution.py:27
  62.0 0.9 collective-permute-done.16.refs_1_
  62.9 1.5 %collective-permute-done.17.refs_2_ = f32[24,512]{1,0:T(8,128)S(1)} collective-permute-done((f32[24,512]{1,0:T(8,128)S(1)}, f32[24,512]{1,0:T(8,128)S(1)}, u32[]{:S(2)}, u32[]{:S(2)}) %collective-permute-start.17) | collective-permute-done | bytes 49184 | tf_op jit(solution)/shard_map/ppermute | solution.py:27
  64.4 0.6 collective-permute-start.20
  65.0 1.5 %collective-permute-start.21 = (bf16[72,2048]{1,0:T(8,128)(2,1)S(1)}, bf16[72,2048]{1,0:T(8,128)(2,1)S(1)}, u32[]{:S(2)}, u32[]{:S(2)}) collective-permute-start(bf16[72,2048]{1,0:T(8,128)(2,1)S(1)} %constant_dynamic-update-slice_fusion.4.refs_3_.refs_0_), channel_id=1, source_target_pairs={{0,16},{8,24},{16,0},{24,8},{1,17},{9,25},{17,1},{25,9},{2,18},{10... | collective-permute-start | bytes 884744 | tf_op jit(solution)/shard_map/ppermute | solution.py:27
  66.5 1.5 %collective-permute-start.25 = (bf16[72,2048]{1,0:T(8,128)(2,1)S(1)}, bf16[72,2048]{1,0:T(8,128)(2,1)S(1)}, u32[]{:S(2)}, u32[]{:S(2)}) collective-permute-start(bf16[72,2048]{1,0:T(8,128)(2,1)S(1)} %constant_dynamic-update-slice_fusion.4.refs_3_.refs_0_), channel_id=1, source_target_pairs={{0,24},{8,16},{16,8},{24,0},{1,25},{9,17},{17,9},{25,1},{2,26},{10... | collective-permute-start | bytes 884744 | tf_op jit(solution)/shard_map/ppermute | solution.py:27
  68.1 3.0 %load_experts.1 = (bf16[2,2048,256]{2,1,0:T(8,128)(2,1)S(1)}, bf16[2,2048,256]{2,1,0:T(8,128)(2,1)S(1)}, bf16[2,256,2048]{2,1,0:T(8,128)(2,1)S(1)}) custom-call(bf16[2,2048,256]{2,1,0:T(8,128)(2,1)} %refs_0_.3, bf16[2,2048,256]{2,1,0:T(8,128)(2,1)} %refs_1_.1, bf16[2,256,2048]{2,1,0:T(8,128)(2,1)} %refs_2_.1, ...), custom_call_target="tpu_custom_call" | custom-call | bytes 12582912 | tf_op jit(solution)/shard_map/load_experts/pallas_call | solution.py:55
  71.0 3.3 %collective-permute-done.20.refs_1_ = bf16[72,2048]{1,0:T(8,128)(2,1)S(1)} collective-permute-done((bf16[72,2048]{1,0:T(8,128)(2,1)S(1)}, bf16[72,2048]{1,0:T(8,128)(2,1)S(1)}, u32[]{:S(2)}, u32[]{:S(2)}) %collective-permute-start.20) | collective-permute-done | bytes 294944 | tf_op jit(solution)/shard_map/ppermute | solution.py:27
  74.3 3.3 %collective-permute-done.21.refs_2_ = bf16[72,2048]{1,0:T(8,128)(2,1)S(1)} collective-permute-done((bf16[72,2048]{1,0:T(8,128)(2,1)S(1)}, bf16[72,2048]{1,0:T(8,128)(2,1)S(1)}, u32[]{:S(2)}, u32[]{:S(2)}) %collective-permute-start.21) | collective-permute-done | bytes 294944 | tf_op jit(solution)/shard_map/ppermute | solution.py:27
  77.6 4.9 %experts_early.1 = (bf16[208,512]{1,0:T(8,128)(2,1)S(1)}, bf16[208,512]{1,0:T(8,128)(2,1)S(1)}, bf16[208,512]{1,0:T(8,128)(2,1)S(1)}, bf16[208,512]{1,0:T(8,128)(2,1)S(1)}) custom-call(s32[2]{0:T(128)S(1)} %pad_add_fusion.scalar_ref, bf16[72,2048]{1,0:T(8,128)(2,1)S(1)} %constant_dynamic-update-slice_fusion.4.refs_3_.refs_0_, ...), custom_call_target="tpu_custom_call" | custom-call | flops 1358954496 | bytes 12582912 | tf_op jit(solution)/shard_map/experts_early/pallas_call | solution.py:55
  82.5 1.0 collective-permute-start.22
  83.5 2.5 %collective-permute-start.23 = (bf16[208,512]{1,0:T(8,128)(2,1)S(1)}, bf16[208,512]{1,0:T(8,128)(2,1)S(1)}, u32[]{:S(2)}, u32[]{:S(2)}) collective-permute-start(bf16[208,512]{1,0:T(8,128)(2,1)S(1)} %get-tuple-element.142), channel_id=1, source_target_pairs={{0,16},{8,24},{16,0},{24,8},{1,17},{9,25},{17,1},{25,9},{2,18},{10... | collective-permute-start | bytes 638984 | tf_op jit(solution)/shard_map/ppermute | solution.py:27
  86.5 4.0 %experts_late.1 = (bf16[72,512]{1,0:T(8,128)(2,1)S(1)}, bf16[72,512]{1,0:T(8,128)(2,1)S(1)}, bf16[72,512]{1,0:T(8,128)(2,1)S(1)}, bf16[72,512]{1,0:T(8,128)(2,1)S(1)}) custom-call(s32[2]{0:T(128)S(1)} %pad_add_fusion.scalar_ref, bf16[72,2048]{1,0:T(8,128)(2,1)S(1)} %collective-permute-done.25.refs_0_, ...), custom_call_target="tpu_custom_call" | custom-call | flops 452984832 | bytes 12582912 | tf_op jit(solution)/shard_map/experts_late/pallas_call | solution.py:55
  90.5 1.0 collective-permute-start.26
  91.5 2.0 %collective-permute-start.27 = (bf16[72,512]{1,0:T(8,128)(2,1)S(1)}, bf16[72,512]{1,0:T(8,128)(2,1)S(1)}, u32[]{:S(2)}, u32[]{:S(2)}) collective-permute-start(bf16[72,512]{1,0:T(8,128)(2,1)S(1)} %get-tuple-element.146), channel_id=1, source_target_pairs={{0,16},{8,24},{16,0},{24,8},{1,17},{9,25},{17,1},{25,9},{2,18},{10... | collective-permute-start | bytes 221192 | tf_op jit(solution)/shard_map/ppermute | solution.py:27
  93.5 1.4 %collective-permute-done.26.refs_5_ = bf16[72,512]{1,0:T(8,128)(2,1)S(1)} collective-permute-done((bf16[72,512]{1,0:T(8,128)(2,1)S(1)}, bf16[72,512]{1,0:T(8,128)(2,1)S(1)}, u32[]{:S(2)}, u32[]{:S(2)}) %collective-permute-start.26) | collective-permute-done | bytes 73760 | tf_op jit(solution)/shard_map/ppermute | solution.py:27
  94.9 2.4 %collective-permute-start.28 = (bf16[72,512]{1,0:T(8,128)(2,1)S(1)}, bf16[72,512]{1,0:T(8,128)(2,1)S(1)}, u32[]{:S(2)}, u32[]{:S(2)}) collective-permute-start(bf16[72,512]{1,0:T(8,128)(2,1)S(1)} %get-tuple-element.147), channel_id=1, source_target_pairs={{0,24},{8,16},{16,8},{24,0},{1,25},{9,17},{17,9},{25,1},{2,26},{10... | collective-permute-start | bytes 221192 | tf_op jit(solution)/shard_map/ppermute | solution.py:27
  97.3 2.9 %collective-permute-done.28.refs_7_ = bf16[72,512]{1,0:T(8,128)(2,1)S(1)} collective-permute-done((bf16[72,512]{1,0:T(8,128)(2,1)S(1)}, bf16[72,512]{1,0:T(8,128)(2,1)S(1)}, u32[]{:S(2)}, u32[]{:S(2)}) %collective-permute-start.28) | collective-permute-done | bytes 73760 | tf_op jit(solution)/shard_map/ppermute | solution.py:27
  100.4 0.9 collective-permute-start.30
  101.3 1.9 %collective-permute-start.31 = (bf16[80,512]{1,0:T(8,128)(2,1)S(1)}, bf16[80,512]{1,0:T(8,128)(2,1)S(1)}, u32[]{:S(2)}, u32[]{:S(2)}) collective-permute-start(bf16[80,512]{1,0:T(8,128)(2,1)S(1)} %get-tuple-element.156), channel_id=1, source_target_pairs={{0,4},{1,5},{2,6},{3,7},{4,0},{5,1},{6,2},{7,3},{8,12},{9,13},{10,... | collective-permute-start | bytes 245768 | tf_op jit(solution)/shard_map/ppermute | solution.py:27
  103.3 1.6 %collective-permute-start.32 = (bf16[80,512]{1,0:T(8,128)(2,1)S(1)}, bf16[80,512]{1,0:T(8,128)(2,1)S(1)}, u32[]{:S(2)}, u32[]{:S(2)}) collective-permute-start(bf16[80,512]{1,0:T(8,128)(2,1)S(1)} %get-tuple-element.157), channel_id=1, source_target_pairs={{0,6},{1,7},{2,4},{3,5},{4,2},{5,3},{6,0},{7,1},{8,14},{9,15},{10,... | collective-permute-start | bytes 245768 | tf_op jit(solution)/shard_map/ppermute | solution.py:27
  104.9 2.5 %collective-permute-start.29 = (f32[24,512]{1,0:T(8,128)S(1)}, f32[24,512]{1,0:T(8,128)S(1)}, u32[]{:S(2)}, u32[]{:S(2)}) collective-permute-start(f32[24,512]{1,0:T(8,128)S(1)} %get-tuple-element.153), channel_id=1, source_target_pairs={{0,24},{8,16},{16,8},{24,0},{1,25},{9,17},{17,9},{25,1},{2,26},{10... | collective-permute-start | bytes 147464 | tf_op jit(solution)/shard_map/ppermute | solution.py:27
  107.4 0.6 copy.25
  108.0 1.9 %collective-permute-done.29.refs_3_ = f32[24,512]{1,0:T(8,128)S(1)} collective-permute-done((f32[24,512]{1,0:T(8,128)S(1)}, f32[24,512]{1,0:T(8,128)S(1)}, u32[]{:S(2)}, u32[]{:S(2)}) %collective-permute-start.29) | collective-permute-done | bytes 49184 | tf_op jit(solution)/shard_map/ppermute | solution.py:27
  109.9 0.7 final.1
  (57 shorter events, 4.6 us)
Async XLA Ops:
  0.6 18.0 %collective-permute-start.4 = (bf16[2,2048,256]{2,1,0:T(8,128)(2,1)}, bf16[2,2048,256]{2,1,0:T(8,128)(2,1)S(1)}, u32[]{:S(2)}, u32[]{:S(2)}) collective-permute-start(bf16[2,2048,256]{2,1,0:T(8,128)(2,1)} %refs_0_.3), channel_id=1, source_target_pairs={{0,1},{1,0},{2,3},{3,2},{4,5},{5,4},{6,7},{7,6},{8,9},{9,8},{10,11... | collective-permute-start | bytes 6291464 | tf_op jit(solution)/shard_map/ppermute | solution.py:27
  4.7 9.0 %collective-permute-start = (bf16[64,640]{1,0:T(8,128)(2,1)S(1)}, bf16[64,640]{1,0:T(8,128)(2,1)S(1)}, u32[]{:S(2)}, u32[]{:S(2)}) collective-permute-start(bf16[64,640]{1,0:T(8,128)(2,1)S(1)} %get-tuple-element.87), channel_id=1, source_target_pairs={{0,2},{1,3},{2,0},{3,1},{4,6},{5,7},{6,4},{7,5},{8,10},{9,11},{10,... | collective-permute-start | bytes 245768 | tf_op jit(solution)/shard_map/ppermute | solution.py:27
  7.3 9.5 %collective-permute-start.1 = (bf16[64,640]{1,0:T(8,128)(2,1)S(1)}, bf16[64,640]{1,0:T(8,128)(2,1)S(1)}, u32[]{:S(2)}, u32[]{:S(2)}) collective-permute-start(bf16[64,640]{1,0:T(8,128)(2,1)S(1)} %get-tuple-element.87), channel_id=1, source_target_pairs={{0,4},{1,5},{2,6},{3,7},{4,0},{5,1},{6,2},{7,3},{8,12},{9,13},{10,... | collective-permute-start | bytes 245768 | tf_op jit(solution)/shard_map/ppermute | solution.py:27
  9.9 7.0 %collective-permute-start.2 = (bf16[64,640]{1,0:T(8,128)(2,1)S(1)}, bf16[64,640]{1,0:T(8,128)(2,1)S(1)}, u32[]{:S(2)}, u32[]{:S(2)}) collective-permute-start(bf16[64,640]{1,0:T(8,128)(2,1)S(1)} %get-tuple-element.87), channel_id=1, source_target_pairs={{0,6},{1,7},{2,4},{3,5},{4,2},{5,3},{6,0},{7,1},{8,14},{9,15},{10,... | collective-permute-start | bytes 245768 | tf_op jit(solution)/shard_map/ppermute | solution.py:27
  9.9 8.7 %copy-start.1 = (s32[13]{0:T(128)S(1)}, s32[13]{0:T(128)}, u32[]{:S(2)}) copy-start(s32[13]{0:T(128)} %lens_ref.1) | copy-start | bytes 160
  9.9 8.7 %copy-start.2 = (s32[8]{0:T(128)S(1)}, s32[8]{0:T(128)}, u32[]{:S(2)}) copy-start(s32[8]{0:T(128)} %owner_ref.1) | copy-start | bytes 100
  9.9 8.7 %copy-start.3 = (s32[8]{0:T(128)S(1)}, s32[8]{0:T(128)}, u32[]{:S(2)}) copy-start(s32[8]{0:T(128)} %slot_ref.1) | copy-start | bytes 100
  16.9 1.7 %collective-permute-start.3 = (bf16[256,640]{1,0:T(8,128)(2,1)S(1)}, bf16[256,640]{1,0:T(8,128)(2,1)S(1)}, u32[]{:S(2)}, u32[]{:S(2)}) collective-permute-start(bf16[256,640]{1,0:T(8,128)(2,1)S(1)} %constant_dynamic-update-slice_fusion.query_a.refs_3_.refs_1_), channel_id=1, source_target_pairs={{0,1},{1,0},{2,3},{3,2},{4,5},{5,4},{6,7},{7,6},{8,9},{9,8},{10,11... | collective-permute-start | bytes 983048 | tf_op jit(solution)/shard_map/ppermute | solution.py:27
  28.7 2.0 %collective-permute-start.5 = (f32[520,256]{1,0:T(8,128)S(1)}, f32[520,256]{1,0:T(8,128)S(1)}, u32[]{:S(2)}, u32[]{:S(2)}) collective-permute-start(f32[520,256]{1,0:T(8,128)S(1)} %get-tuple-element.98), channel_id=1, source_target_pairs={{0,1},{1,0},{2,3},{3,2},{4,5},{5,4},{6,7},{7,6},{8,9},{9,8},{10,11... | collective-permute-start | bytes 1597448 | tf_op jit(solution)/shard_map/ppermute | solution.py:27
  28.8 2.0 %collective-permute-start.6 = (f32[16,640]{1,0:T(8,128)S(1)}, f32[16,640]{1,0:T(8,128)S(1)}, u32[]{:S(2)}, u32[]{:S(2)}) collective-permute-start(f32[16,640]{1,0:T(8,128)S(1)} %get-tuple-element.99.dec_mine), channel_id=1, source_target_pairs={{0,1},{1,0},{2,3},{3,2},{4,5},{5,4},{6,7},{7,6},{8,9},{9,8},{10,11... | collective-permute-start | bytes 122888 | tf_op jit(solution)/shard_map/ppermute | solution.py:27
  31.2 7.8 %collective-permute-start.10 = (bf16[2,2048,256]{2,1,0:T(8,128)(2,1)}, bf16[2,2048,256]{2,1,0:T(8,128)(2,1)}, u32[]{:S(2)}, u32[]{:S(2)}) collective-permute-start(bf16[2,2048,256]{2,1,0:T(8,128)(2,1)} %refs_1_.1), channel_id=1, source_target_pairs={{0,1},{1,0},{2,3},{3,2},{4,5},{5,4},{6,7},{7,6},{8,9},{9,8},{10,11... | collective-permute-start | bytes 6291464 | tf_op jit(solution)/shard_map/ppermute | solution.py:27
  31.4 7.6 %collective-permute-start.9 = (bf16[80,640]{1,0:T(8,128)(2,1)S(1)}, bf16[80,640]{1,0:T(8,128)(2,1)S(1)}, u32[]{:S(2)}, u32[]{:S(2)}) collective-permute-start(bf16[80,640]{1,0:T(8,128)(2,1)S(1)} %get-tuple-element.107), channel_id=1, source_target_pairs={{0,6},{1,7},{2,4},{3,5},{4,2},{5,3},{6,0},{7,1},{8,14},{9,15},{10,... | collective-permute-start | bytes 307208 | tf_op jit(solution)/shard_map/ppermute | solution.py:27
  34.5 7.1 %collective-permute-start.7 = (bf16[80,640]{1,0:T(8,128)(2,1)S(1)}, bf16[80,640]{1,0:T(8,128)(2,1)S(1)}, u32[]{:S(2)}, u32[]{:S(2)}) collective-permute-start(bf16[80,640]{1,0:T(8,128)(2,1)S(1)} %get-tuple-element.105), channel_id=1, source_target_pairs={{0,2},{1,3},{2,0},{3,1},{4,6},{5,7},{6,4},{7,5},{8,10},{9,11},{10,... | collective-permute-start | bytes 307208 | tf_op jit(solution)/shard_map/ppermute | solution.py:27
  34.6 9.4 %collective-permute-start.8 = (bf16[80,640]{1,0:T(8,128)(2,1)S(1)}, bf16[80,640]{1,0:T(8,128)(2,1)S(1)}, u32[]{:S(2)}, u32[]{:S(2)}) collective-permute-start(bf16[80,640]{1,0:T(8,128)(2,1)S(1)} %get-tuple-element.106), channel_id=1, source_target_pairs={{0,4},{1,5},{2,6},{3,7},{4,0},{5,1},{6,2},{7,3},{8,12},{9,13},{10,... | collective-permute-start | bytes 307208 | tf_op jit(solution)/shard_map/ppermute | solution.py:27
  37.3 7.7 %copy-start.4 = (bf16[2,256,2048]{2,1,0:T(8,128)(2,1)S(1)}, bf16[2,256,2048]{2,1,0:T(8,128)(2,1)}, u32[]{:S(2)}) copy-start(bf16[2,256,2048]{2,1,0:T(8,128)(2,1)} %refs_2_.1) | copy-start | bytes 6291460
  37.3 16.0 %copy-start = (f32[2048]{0:T(1024)S(1)}, f32[2048]{0:T(1024)}, u32[]{:S(2)}) copy-start(f32[2048]{0:T(1024)} %param.32) | copy-start | bytes 24580
  45.0 6.6 %collective-permute-start.14 = (bf16[2,256,2048]{2,1,0:T(8,128)(2,1)S(1)}, bf16[2,256,2048]{2,1,0:T(8,128)(2,1)S(1)}, u32[]{:S(2)}, u32[]{:S(2)}) collective-permute-start(bf16[2,256,2048]{2,1,0:T(8,128)(2,1)S(1)} %copy-done.4), channel_id=1, source_target_pairs={{0,1},{1,0},{2,3},{3,2},{4,5},{5,4},{6,7},{7,6},{8,9},{9,8},{10,11... | collective-permute-start | bytes 6291464 | tf_op jit(solution)/shard_map/ppermute | solution.py:27
  45.1 6.6 %collective-permute-start.13 = (bf16[24,2048]{1,0:T(8,128)(2,1)S(1)}, bf16[24,2048]{1,0:T(8,128)(2,1)S(1)}, u32[]{:S(2)}, u32[]{:S(2)}) collective-permute-start(bf16[24,2048]{1,0:T(8,128)(2,1)S(1)} %get-tuple-element.118), channel_id=1, source_target_pairs={{0,24},{8,16},{16,8},{24,0},{1,25},{9,17},{17,9},{25,1},{2,26},{10... | collective-permute-start | bytes 294920 | tf_op jit(solution)/shard_map/ppermute | solution.py:27
  47.6 5.8 %collective-permute-start.11 = (bf16[24,2048]{1,0:T(8,128)(2,1)S(1)}, bf16[24,2048]{1,0:T(8,128)(2,1)S(1)}, u32[]{:S(2)}, u32[]{:S(2)}) collective-permute-start(bf16[24,2048]{1,0:T(8,128)(2,1)S(1)} %get-tuple-element.116), channel_id=1, source_target_pairs={{0,8},{8,0},{16,24},{24,16},{1,9},{9,1},{17,25},{25,17},{2,10},{10... | collective-permute-start | bytes 294920 | tf_op jit(solution)/shard_map/ppermute | solution.py:27
  48.1 5.2 %collective-permute-start.12 = (bf16[24,2048]{1,0:T(8,128)(2,1)S(1)}, bf16[24,2048]{1,0:T(8,128)(2,1)S(1)}, u32[]{:S(2)}, u32[]{:S(2)}) collective-permute-start(bf16[24,2048]{1,0:T(8,128)(2,1)S(1)} %get-tuple-element.117), channel_id=1, source_target_pairs={{0,16},{8,24},{16,0},{24,8},{1,17},{9,25},{17,1},{25,9},{2,18},{10... | collective-permute-start | bytes 294920 | tf_op jit(solution)/shard_map/ppermute | solution.py:27
  54.3 10.0 %collective-permute-start.15 = (bf16[16,2048]{1,0:T(8,128)(2,1)S(1)}, bf16[16,2048]{1,0:T(8,128)(2,1)S(1)}, u32[]{:S(2)}, u32[]{:S(2)}) collective-permute-start(bf16[16,2048]{1,0:T(8,128)(2,1)S(1)} %get-tuple-element.122), channel_id=1, source_target_pairs={{0,6},{1,7},{2,4},{3,5},{4,2},{5,3},{6,0},{7,1},{8,14},{9,15},{10,... | collective-permute-start | bytes 196616 | tf_op jit(solution)/shard_map/ppermute | solution.py:27
  57.1 5.0 %collective-permute-start.18 = (bf16[16,2048]{1,0:T(8,128)(2,1)S(1)}, bf16[16,2048]{1,0:T(8,128)(2,1)S(1)}, u32[]{:S(2)}, u32[]{:S(2)}) collective-permute-start(bf16[16,2048]{1,0:T(8,128)(2,1)S(1)} %get-tuple-element.122), channel_id=1, source_target_pairs={{0,2},{1,3},{2,0},{3,1},{4,6},{5,7},{6,4},{7,5},{8,10},{9,11},{10,... | collective-permute-start | bytes 196616 | tf_op jit(solution)/shard_map/ppermute | solution.py:27
  57.1 7.3 %collective-permute-start.19 = (bf16[16,2048]{1,0:T(8,128)(2,1)S(1)}, bf16[16,2048]{1,0:T(8,128)(2,1)S(1)}, u32[]{:S(2)}, u32[]{:S(2)}) collective-permute-start(bf16[16,2048]{1,0:T(8,128)(2,1)S(1)} %get-tuple-element.122), channel_id=1, source_target_pairs={{0,4},{1,5},{2,6},{3,7},{4,0},{5,1},{6,2},{7,3},{8,12},{9,13},{10,... | collective-permute-start | bytes 196616 | tf_op jit(solution)/shard_map/ppermute | solution.py:27
  58.8 4.1 %collective-permute-start.16 = (f32[24,512]{1,0:T(8,128)S(1)}, f32[24,512]{1,0:T(8,128)S(1)}, u32[]{:S(2)}, u32[]{:S(2)}) collective-permute-start(f32[24,512]{1,0:T(8,128)S(1)} %get-tuple-element.123), channel_id=1, source_target_pairs={{0,8},{8,0},{16,24},{24,16},{1,9},{9,1},{17,25},{25,17},{2,10},{10... | collective-permute-start | bytes 147464 | tf_op jit(solution)/shard_map/ppermute | solution.py:27
  60.3 4.1 %collective-permute-start.17 = (f32[24,512]{1,0:T(8,128)S(1)}, f32[24,512]{1,0:T(8,128)S(1)}, u32[]{:S(2)}, u32[]{:S(2)}) collective-permute-start(f32[24,512]{1,0:T(8,128)S(1)} %get-tuple-element.124), channel_id=1, source_target_pairs={{0,16},{8,24},{16,0},{24,8},{1,17},{9,25},{17,1},{25,9},{2,18},{10... | collective-permute-start | bytes 147464 | tf_op jit(solution)/shard_map/ppermute | solution.py:27
  64.4 9.9 %collective-permute-start.20 = (bf16[72,2048]{1,0:T(8,128)(2,1)S(1)}, bf16[72,2048]{1,0:T(8,128)(2,1)S(1)}, u32[]{:S(2)}, u32[]{:S(2)}) collective-permute-start(bf16[72,2048]{1,0:T(8,128)(2,1)S(1)} %constant_dynamic-update-slice_fusion.4.refs_3_.refs_0_), channel_id=1, source_target_pairs={{0,8},{8,0},{16,24},{24,16},{1,9},{9,1},{17,25},{25,17},{2,10},{10... | collective-permute-start | bytes 884744 | tf_op jit(solution)/shard_map/ppermute | solution.py:27
  65.0 12.6 %collective-permute-start.21 = (bf16[72,2048]{1,0:T(8,128)(2,1)S(1)}, bf16[72,2048]{1,0:T(8,128)(2,1)S(1)}, u32[]{:S(2)}, u32[]{:S(2)}) collective-permute-start(bf16[72,2048]{1,0:T(8,128)(2,1)S(1)} %constant_dynamic-update-slice_fusion.4.refs_3_.refs_0_), channel_id=1, source_target_pairs={{0,16},{8,24},{16,0},{24,8},{1,17},{9,25},{17,1},{25,9},{2,18},{10... | collective-permute-start | bytes 884744 | tf_op jit(solution)/shard_map/ppermute | solution.py:27
  66.5 20.0 %collective-permute-start.25 = (bf16[72,2048]{1,0:T(8,128)(2,1)S(1)}, bf16[72,2048]{1,0:T(8,128)(2,1)S(1)}, u32[]{:S(2)}, u32[]{:S(2)}) collective-permute-start(bf16[72,2048]{1,0:T(8,128)(2,1)S(1)} %constant_dynamic-update-slice_fusion.4.refs_3_.refs_0_), channel_id=1, source_target_pairs={{0,24},{8,16},{16,8},{24,0},{1,25},{9,17},{17,9},{25,1},{2,26},{10... | collective-permute-start | bytes 884744 | tf_op jit(solution)/shard_map/ppermute | solution.py:27
  82.5 17.7 %collective-permute-start.22 = (bf16[208,512]{1,0:T(8,128)(2,1)S(1)}, bf16[208,512]{1,0:T(8,128)(2,1)S(1)}, u32[]{:S(2)}, u32[]{:S(2)}) collective-permute-start(bf16[208,512]{1,0:T(8,128)(2,1)S(1)} %get-tuple-element.141), channel_id=1, source_target_pairs={{0,8},{8,0},{16,24},{24,16},{1,9},{9,1},{17,25},{25,17},{2,10},{10... | collective-permute-start | bytes 638984 | tf_op jit(solution)/shard_map/ppermute | solution.py:27
  83.5 16.7 %collective-permute-start.23 = (bf16[208,512]{1,0:T(8,128)(2,1)S(1)}, bf16[208,512]{1,0:T(8,128)(2,1)S(1)}, u32[]{:S(2)}, u32[]{:S(2)}) collective-permute-start(bf16[208,512]{1,0:T(8,128)(2,1)S(1)} %get-tuple-element.142), channel_id=1, source_target_pairs={{0,16},{8,24},{16,0},{24,8},{1,17},{9,25},{17,1},{25,9},{2,18},{10... | collective-permute-start | bytes 638984 | tf_op jit(solution)/shard_map/ppermute | solution.py:27
  86.0 14.2 %collective-permute-start.24 = (bf16[208,512]{1,0:T(8,128)(2,1)S(1)}, bf16[208,512]{1,0:T(8,128)(2,1)S(1)}, u32[]{:S(2)}, u32[]{:S(2)}) collective-permute-start(bf16[208,512]{1,0:T(8,128)(2,1)S(1)} %get-tuple-element.143), channel_id=1, source_target_pairs={{0,24},{8,16},{16,8},{24,0},{1,25},{9,17},{17,9},{25,1},{2,26},{10... | collective-permute-start | bytes 638984 | tf_op jit(solution)/shard_map/ppermute | solution.py:27
  90.5 4.4 %collective-permute-start.26 = (bf16[72,512]{1,0:T(8,128)(2,1)S(1)}, bf16[72,512]{1,0:T(8,128)(2,1)S(1)}, u32[]{:S(2)}, u32[]{:S(2)}) collective-permute-start(bf16[72,512]{1,0:T(8,128)(2,1)S(1)} %get-tuple-element.145), channel_id=1, source_target_pairs={{0,8},{8,0},{16,24},{24,16},{1,9},{9,1},{17,25},{25,17},{2,10},{10... | collective-permute-start | bytes 221192 | tf_op jit(solution)/shard_map/ppermute | solution.py:27
  91.5 5.8 %collective-permute-start.27 = (bf16[72,512]{1,0:T(8,128)(2,1)S(1)}, bf16[72,512]{1,0:T(8,128)(2,1)S(1)}, u32[]{:S(2)}, u32[]{:S(2)}) collective-permute-start(bf16[72,512]{1,0:T(8,128)(2,1)S(1)} %get-tuple-element.146), channel_id=1, source_target_pairs={{0,16},{8,24},{16,0},{24,8},{1,17},{9,25},{17,1},{25,9},{2,18},{10... | collective-permute-start | bytes 221192 | tf_op jit(solution)/shard_map/ppermute | solution.py:27
  94.9 5.3 %collective-permute-start.28 = (bf16[72,512]{1,0:T(8,128)(2,1)S(1)}, bf16[72,512]{1,0:T(8,128)(2,1)S(1)}, u32[]{:S(2)}, u32[]{:S(2)}) collective-permute-start(bf16[72,512]{1,0:T(8,128)(2,1)S(1)} %get-tuple-element.147), channel_id=1, source_target_pairs={{0,24},{8,16},{16,8},{24,0},{1,25},{9,17},{17,9},{25,1},{2,26},{10... | collective-permute-start | bytes 221192 | tf_op jit(solution)/shard_map/ppermute | solution.py:27
  100.4 9.4 %collective-permute-start.30 = (bf16[80,512]{1,0:T(8,128)(2,1)S(1)}, bf16[80,512]{1,0:T(8,128)(2,1)S(1)}, u32[]{:S(2)}, u32[]{:S(2)}) collective-permute-start(bf16[80,512]{1,0:T(8,128)(2,1)S(1)} %get-tuple-element.155), channel_id=1, source_target_pairs={{0,2},{1,3},{2,0},{3,1},{4,6},{5,7},{6,4},{7,5},{8,10},{9,11},{10,... | collective-permute-start | bytes 245768 | tf_op jit(solution)/shard_map/ppermute | solution.py:27
  101.3 8.6 %collective-permute-start.31 = (bf16[80,512]{1,0:T(8,128)(2,1)S(1)}, bf16[80,512]{1,0:T(8,128)(2,1)S(1)}, u32[]{:S(2)}, u32[]{:S(2)}) collective-permute-start(bf16[80,512]{1,0:T(8,128)(2,1)S(1)} %get-tuple-element.156), channel_id=1, source_target_pairs={{0,4},{1,5},{2,6},{3,7},{4,0},{5,1},{6,2},{7,3},{8,12},{9,13},{10,... | collective-permute-start | bytes 245768 | tf_op jit(solution)/shard_map/ppermute | solution.py:27
  103.3 6.6 %collective-permute-start.32 = (bf16[80,512]{1,0:T(8,128)(2,1)S(1)}, bf16[80,512]{1,0:T(8,128)(2,1)S(1)}, u32[]{:S(2)}, u32[]{:S(2)}) collective-permute-start(bf16[80,512]{1,0:T(8,128)(2,1)S(1)} %get-tuple-element.157), channel_id=1, source_target_pairs={{0,6},{1,7},{2,4},{3,5},{4,2},{5,3},{6,0},{7,1},{8,14},{9,15},{10,... | collective-permute-start | bytes 245768 | tf_op jit(solution)/shard_map/ppermute | solution.py:27
  104.9 5.0 %collective-permute-start.29 = (f32[24,512]{1,0:T(8,128)S(1)}, f32[24,512]{1,0:T(8,128)S(1)}, u32[]{:S(2)}, u32[]{:S(2)}) collective-permute-start(f32[24,512]{1,0:T(8,128)S(1)} %get-tuple-element.153), channel_id=1, source_target_pairs={{0,24},{8,16},{16,8},{24,0},{1,25},{9,17},{17,9},{25,1},{2,26},{10... | collective-permute-start | bytes 147464 | tf_op jit(solution)/shard_map/ppermute | solution.py:27

commit v4 on v3

--- a/solution.py
+++ b/solution.py
@@ -159,44 +159,32 @@
         padded[...] = rows[tok:]
 
 
-def group(query, keys, values, live):
-    scores = lax.dot_general(
-        query, keys, (((1,), (1,)), ((), ())), preferred_element_type=f32
-    ) * HD ** (-0.5)
-    top = jnp.max(jnp.where(live, scores, neg_fill), axis=-1, keepdims=True)
-    weights = jnp.where(live, jnp.exp(scores - top), 0.0)
-    total = jnp.sum(weights, axis=-1, keepdims=True)
-    acc = jnp.dot(weights.astype(bf16), values, preferred_element_type=f32)
-    return top, total, acc
-
-
-def group_turned(query, keys, values, live):
-    scores = lax.dot_general(
-        keys, query, (((1,), (1,)), ((), ())), preferred_element_type=f32
-    )
+def group_turned(keys, turned_query, turned_values, live):
+    scores = jnp.dot(keys, turned_query, preferred_element_type=f32)
     top = jnp.max(
         scores if live is None else jnp.where(live, scores, neg_fill), axis=0, keepdims=True
     )
     weights = jnp.exp2((scores - top) * (HD ** (-0.5) * LOG2E))
-    top = top * HD ** (-0.5)
     if live is not None:
         weights = jnp.where(live, weights, 0.0)
     total = jnp.sum(weights, axis=0, keepdims=True)
-    acc = lax.dot_general(
-        values, weights.astype(bf16), (((0,), (0,)), ((), ())), preferred_element_type=f32
-    )
-    return top, total, acc
+    acc = jnp.dot(turned_values, weights.astype(bf16), preferred_element_type=f32)
+    return top * HD ** (-0.5), total, acc
+
+
+def turned(values):
+    return values.astype(f32).T.astype(bf16)
 
 
 def attention_kernel(
     owner_ref, slot_ref, lens_ref, blk_ref, query_a, query_b, query_d, key_new, value_new, key_dec, value_dec,
-    cache_k, cache_v, keep, send, dec, key_buf, value_buf, tops, totals, sems,
+    cache_k, cache_v, keep, send, dec, key_buf, value_buf, turn_a, turn_b, spread, dec_acc, dec_stats, sems,
 ):
     blocks, block_len, width = cache_k.shape
     heads = width // HD
     half = query_a.shape[0]
     tile = min(TILE, half)
-    sides = ((query_a, keep), (query_b, send))
+    sides = ((turn_a, keep), (turn_b, send))
 
     def copies(index):
         return (
@@ -208,29 +196,37 @@
         for copy in copies(index):
             copy.start()
 
-    def over_tiles(body):
-        for query, state in sides:
-            for row in range(0, half, tile):
-                for head in range(heads):
-                    body(query[row : row + tile, lanes(head)], state, slice(row, row + tile), head)
-
-    def start(query, state, columns, head):
-        top, total, acc = group_turned(query, key_new[:, lanes(head)], value_new[:, lanes(head)], None)
+    for query, turn_ref in ((query_a, turn_a), (query_b, turn_b)):
+        for row in range(0, half, tile):
+            turn_ref[:, row : row + tile] = turned(query[row : row + tile, :width])
+
+    def over_tiles(keys, values, body):
+        for head in range(heads):
+            key_head = keys[:, lanes(head)]
+            value_head = turned(values[:, lanes(head)])
+            for query, state in sides:
+                for row in range(0, half, tile):
+                    columns = slice(row, row + tile)
+                    body(key_head, query[lanes(head), columns], value_head, state, columns, head)
+
+    def start(keys, query, values, state, columns, head):
+        top, total, acc = group_turned(keys, query, values, None)
         state[width + head : width + head + 1, columns] = top
         state[width + heads + head : width + heads + head + 1, columns] = total
         state[lanes(head), columns] = acc
 
-    over_tiles(start)
-    mine = blk_ref[0] == 0
+    over_tiles(key_new, value_new, start)
+
+    lines = lax.broadcasted_iota(jnp.int32, (DPAD, width), 1)
+    spread[...] = jnp.zeros_like(spread)
     for head in range(heads):
-        own = jnp.sum(
-            query_d[:, lanes(head)].astype(f32) * key_dec[:, lanes(head)].astype(f32),
-            axis=-1,
-            keepdims=True,
-        ) * HD ** (-0.5)
-        tops[head] = jnp.where(mine, own, neg_fill)
-        totals[head] = jnp.where(mine, jnp.ones_like(own), jnp.zeros_like(own))
-        dec[:, lanes(head)] = jnp.where(mine, value_dec[:, lanes(head)].astype(f32), 0.0)
+        here = (lines >= head * HD) & (lines < (head + 1) * HD)
+        spread[head * DPAD : (head + 1) * DPAD, :] = jnp.where(
+            here, query_d[...].astype(f32), 0.0
+        ).astype(bf16)
+    dec_acc[...] = jnp.zeros_like(dec_acc)
+    dec_stats[0:1, :] = jnp.full((1, HD), neg_fill, f32)
+    dec_stats[1:, :] = jnp.zeros_like(dec_stats[1:, :])
 
     @pl.loop(0, blocks)
     def _(index):
@@ -240,10 +236,8 @@
         length = lens_ref[jnp.minimum(owner, REQS - 1)]
         count = jnp.clip(length - slot_ref[index] * block_len, 0, block_len)
 
-        def add(live, query, state, columns, head):
-            top, total, acc = group_turned(
-                query, key_buf[index, :, lanes(head)], value_buf[index, :, lanes(head)], live
-            )
+        def add(live, keys, query, values, state, columns, head):
+            top, total, acc = group_turned(keys, query, values, live)
             top_row = slice(width + head, width + head + 1)
             total_row = slice(width + heads + head, width + heads + head + 1)
             old_top = state[top_row, columns]
@@ -256,39 +250,63 @@
 
         @pl.when((owner < PRE) & (count == block_len))
         def _():
-            over_tiles(functools.partial(add, None))
+            over_tiles(key_buf.at[index], value_buf.at[index], functools.partial(add, None))
 
         @pl.when((owner < PRE) & (count < block_len))
         def _():
             live = lax.broadcasted_iota(jnp.int32, (block_len, tile), 0) < count
-            over_tiles(functools.partial(add, live))
+            over_tiles(key_buf.at[index], value_buf.at[index], functools.partial(add, live))
 
         @pl.when((owner >= PRE) & (owner < REQS))
         def _():
-            shape = (DPAD, block_len)
-            live = (lax.broadcasted_iota(jnp.int32, shape, 1) < count) & (
-                lax.broadcasted_iota(jnp.int32, shape, 0) == owner - PRE
+            shape = (block_len, HD)
+            lane = lax.broadcasted_iota(jnp.int32, shape, 1)
+            live = (lax.broadcasted_iota(jnp.int32, shape, 0) < count) & (
+                lax.rem(lane, DPAD) == owner - PRE
+            ) & (lane < heads * DPAD)
+            scores = lax.dot_general(
+                key_buf[index], spread[...], (((1,), (1,)), ((), ())), preferred_element_type=f32
             )
+            top = jnp.max(jnp.where(live, scores, neg_fill), axis=0, keepdims=True)
+            weights = jnp.where(live, jnp.exp2((scores - top) * (HD ** (-0.5) * LOG2E)), 0.0)
+            top = top * HD ** (-0.5)
+            total = jnp.sum(weights, axis=0, keepdims=True)
+            mixed = lax.dot_general(
+                value_buf[index], weights.astype(bf16), (((0,), (0,)), ((), ())), preferred_element_type=f32
+            )
+            place = lax.broadcasted_iota(jnp.int32, (HD, HD), 1)
+            acc = jnp.zeros((HD, HD), f32)
             for head in range(heads):
-                top, total, acc = group(
-                    query_d[:, lanes(head)],
-                    key_buf[index, :, lanes(head)],
-                    value_buf[index, :, lanes(head)],
-                    live,
-                )
-                old_top = tops[head]
-                best = jnp.maximum(old_top, top)
-                old_scale = jnp.exp(old_top - best)
-                scale = jnp.exp(top - best)
-                tops[head] = best
-                totals[head] = totals[head] * old_scale + total * scale
-                dec[:, lanes(head)] = dec[:, lanes(head)] * old_scale + acc * scale
-
+                here = (place >= head * DPAD) & (place < (head + 1) * DPAD)
+                acc = jnp.where(here, mixed[lanes(head)], acc)
+            old_top = dec_stats[0:1, :]
+            best = jnp.maximum(old_top, top)
+            old_scale = jnp.exp(old_top - best)
+            scale = jnp.exp(top - best)
+            dec_stats[0:1, :] = best
+            dec_stats[1:2, :] = dec_stats[1:2, :] * old_scale + total * scale
+            dec_acc[...] = dec_acc[...] * old_scale + acc * scale
+
+    mine = blk_ref[0] == 0
+    plain = dec_acc[...].T
+    stats = jnp.concatenate([dec_stats[...], jnp.zeros((HD - 8, HD), f32)], axis=0).T
     place = lax.broadcasted_iota(jnp.int32, (DPAD, HD), 1)
     packed = jnp.zeros((DPAD, HD), f32)
     for head in range(heads):
-        packed = jnp.where(place == head, tops[head], packed)
-        packed = jnp.where(place == heads + head, totals[head], packed)
+        rows = slice(head * DPAD, (head + 1) * DPAD)
+        own = jnp.sum(
+            query_d[:, lanes(head)].astype(f32) * key_dec[:, lanes(head)].astype(f32),
+            axis=-1,
+            keepdims=True,
+        ) * HD ** (-0.5)
+        own = jnp.where(mine, own, neg_fill)
+        top = stats[rows, 0:1]
+        best = jnp.maximum(top, own)
+        scale = jnp.exp(top - best)
+        own_scale = jnp.where(mine, jnp.exp(own - best), 0.0)
+        packed = jnp.where(place == head, best, packed)
+        packed = jnp.where(place == heads + head, stats[rows, 1:2] * scale + own_scale, packed)
+        dec[:, lanes(head)] = plain[rows] * scale + value_dec[:, lanes(head)].astype(f32) * own_scale
     dec[:, width:] = packed
 
 
@@ -307,8 +325,11 @@
         [
             pltpu.VMEM((blocks, block_len, width), bf16),
             pltpu.VMEM((blocks, block_len, width), bf16),
-            pltpu.VMEM((heads, DPAD, 1), f32),
-            pltpu.VMEM((heads, DPAD, 1), f32),
+            pltpu.VMEM((width, half), bf16),
+            pltpu.VMEM((width, half), bf16),
+            pltpu.VMEM((HD, width), bf16),
+            pltpu.VMEM((HD, HD), f32),
+            pltpu.VMEM((8, HD), f32),
             pltpu.SemaphoreType.DMA((2, blocks)),
         ],
     )

time: 111 us -> 110 us (level)
  starting transfers between devices: 41.9 us -> 47.9 us
  Pallas kernels: 32.9 us -> 28.2 us
  waiting for transfers between devices: 33.1 us -> 30.7 us
    ppermute x33, starting transfers between devices: 41.9 us -> 47.9 us  [swap(): return lax.ppermute(value, axis, [(i, i ^ mask) for i in range(count)])]
    pallas_call x12, Pallas kernels: 32.9 us -> 28.2 us  [call(): pl.pallas_call(body, out_shape=tuple((jax.ShapeDtypeStruct(shape, dtype)...]
    ppermute x33, waiting for transfers between devices: 33.1 us -> 30.7 us  [swap(): return lax.ppermute(value, axis, [(i, i ^ mask) for i in range(count)])]
where the time goes in v4:
time: 110 us
  starting transfers between devices  47.9 us (44%)
  waiting for transfers between devices  30.7 us (28%)
  Pallas kernels  28.2 us (26%)
  other arithmetic  1.16 us (1%)
    ppermute x33, starting transfers between devices, swap(): return lax.ppermute(value, axis, [(i, i ^ mask) for i in range(count)])  47.9 us
    ppermute x33, waiting for transfers between devices, swap(): return lax.ppermute(value, axis, [(i, i ^ mask) for i in range(count)])  30.7 us
    pallas_call x12, Pallas kernels, call(): pl.pallas_call(body, out_shape=tuple((jax.ShapeDtypeStruct(shape, dtype)...  28.2 us
  transfers between devices with their start and end apart: 33, of which 16 were waited for; matrix products, arithmetic and copies ran while one was open for 2% of the time, Pallas kernels for 18%

profile of v4, /device:TPU:0, one launch (start us, length us, event | category | flops | bytes accessed | tf_op | source)
XLA Modules:
  0.0 109.7 jit_solution(3249371531380450838)
XLA Ops:
  1.2 0.7 select_reduce_fusion
  2.2 2.4 %queries.1 = (bf16[64,640]{1,0:T(8,128)(2,1)S(1)}, bf16[16,512]{1,0:T(8,128)(2,1)S(1)}, f32[32,128]{1,0:T(8,128)S(1)}, bf16[80,2048]{1,0:T(8,128)(2,1)S(1)}, f32[32,2048]{1,0:T(8,128)S(1)}) custom-call(bf16[64,2048]{1,0:T(8,128)(2,1)} %pre_hbm.3, bf16[12,2048]{1,0:T(8,128)(2,1)} %dec_hbm.1, f32[1,2048]{1,0:T(1,128)} %bitcast.9, ...), custom_call_target="tpu_custom_call" | custom-call | tf_op jit(solution)/shard_map/queries/pallas_call | solution.py:55
  4.7 2.7 %collective-permute-start = (bf16[64,640]{1,0:T(8,128)(2,1)S(1)}, bf16[64,640]{1,0:T(8,128)(2,1)S(1)}, u32[]{:S(2)}, u32[]{:S(2)}) collective-permute-start(bf16[64,640]{1,0:T(8,128)(2,1)S(1)} %get-tuple-element.87), channel_id=1, source_target_pairs={{0,2},{1,3},{2,0},{3,1},{4,6},{5,7},{6,4},{7,5},{8,10},{9,11},{10,... | collective-permute-start | bytes 245768 | tf_op jit(solution)/shard_map/ppermute | solution.py:27
  7.3 2.6 %collective-permute-start.1 = (bf16[64,640]{1,0:T(8,128)(2,1)S(1)}, bf16[64,640]{1,0:T(8,128)(2,1)S(1)}, u32[]{:S(2)}, u32[]{:S(2)}) collective-permute-start(bf16[64,640]{1,0:T(8,128)(2,1)S(1)} %get-tuple-element.87), channel_id=1, source_target_pairs={{0,4},{1,5},{2,6},{3,7},{4,0},{5,1},{6,2},{7,3},{8,12},{9,13},{10,... | collective-permute-start | bytes 245768 | tf_op jit(solution)/shard_map/ppermute | solution.py:27
  9.9 3.8 %keys.1 = (bf16[2,64,512]{2,1,0:T(8,128)(2,1)}, bf16[2,12,512]{2,1,0:T(8,128)(2,1)S(1)}, bf16[64,512]{1,0:T(8,128)(2,1)S(1)}, bf16[64,512]{1,0:T(8,128)(2,1)S(1)...) custom-call(bf16[80,2048]{1,0:T(8,128)(2,1)S(1)} %get-tuple-element.84.normed, bf16[2048,512]{1,0:T(8,128)(2,1)} %key_hbm.1, ...), custom_call_target="tpu_custom_call" | custom-call | flops 335544320 | bytes 4194304 | tf_op jit(solution)/shard_map/keys/pallas_call | solution.py:55
  13.7 3.2 %collective-permute-done.1 = bf16[64,640]{1,0:T(8,128)(2,1)S(1)} collective-permute-done((bf16[64,640]{1,0:T(8,128)(2,1)S(1)}, bf16[64,640]{1,0:T(8,128)(2,1)S(1)}, u32[]{:S(2)}, u32[]{:S(2)}) %collective-permute-start.1) | collective-permute-done | bytes 81952 | tf_op jit(solution)/shard_map/ppermute | solution.py:27
  17.0 1.6 %collective-permute-done.3.query_b = bf16[256,640]{1,0:T(8,128)(2,1)S(1)} collective-permute-done((bf16[256,640]{1,0:T(8,128)(2,1)S(1)}, bf16[256,640]{1,0:T(8,128)(2,1)S(1)}, u32[]{:S(2)}, u32[]{:S(2)}) %collective-permute-start.3) | collective-permute-done | bytes 327712 | tf_op jit(solution)/shard_map/ppermute | solution.py:27
  18.7 5.4 %attention.1 = (f32[520,256]{1,0:T(8,128)S(1)}, f32[520,256]{1,0:T(8,128)S(1)}, f32[16,640]{1,0:T(8,128)S(1)}) custom-call(s32[8]{0:T(128)S(1)} %copy-done.2, s32[8]{0:T(128)S(1)} %copy-done.3, s32[13]{0:T(128)S(1)} %copy-done.1, s32[1]{0:T(128)} %bitcast.7.blk_ref, bf16[256,640]{1,0:T(8,128)(2,1)S(1)} %constant_dynamic-update-slice_fusion.query_a.refs_3_.refs_1_, ...), custom_call_target="tpu_custom_call" | custom-call | tf_op jit(solution)/shard_map/attention/pallas_call | solution.py:55
  24.0 1.8 %collective-permute-start.5 = (f32[520,256]{1,0:T(8,128)S(1)}, f32[520,256]{1,0:T(8,128)S(1)}, u32[]{:S(2)}, u32[]{:S(2)}) collective-permute-start(f32[520,256]{1,0:T(8,128)S(1)} %get-tuple-element.98), channel_id=1, source_target_pairs={{0,1},{1,0},{2,3},{3,2},{4,5},{5,4},{6,7},{7,6},{8,9},{9,8},{10,11... | collective-permute-start | bytes 1597448 | tf_op jit(solution)/shard_map/ppermute | solution.py:27
  25.9 1.5 %collective-permute-done.6.dec_other = f32[16,640]{1,0:T(8,128)S(1)} collective-permute-done((f32[16,640]{1,0:T(8,128)S(1)}, f32[16,640]{1,0:T(8,128)S(1)}, u32[]{:S(2)}, u32[]{:S(2)}) %collective-permute-start.6) | collective-permute-done | bytes 40992 | tf_op jit(solution)/shard_map/ppermute | solution.py:27
  28.3 2.1 %collective-permute-start.9 = (bf16[80,640]{1,0:T(8,128)(2,1)S(1)}, bf16[80,640]{1,0:T(8,128)(2,1)S(1)}, u32[]{:S(2)}, u32[]{:S(2)}) collective-permute-start(bf16[80,640]{1,0:T(8,128)(2,1)S(1)} %get-tuple-element.107), channel_id=1, source_target_pairs={{0,6},{1,7},{2,4},{3,5},{4,2},{5,3},{6,0},{7,1},{8,14},{9,15},{10,... | collective-permute-start | bytes 307208 | tf_op jit(solution)/shard_map/ppermute | solution.py:27
  30.4 4.0 %collective-permute-start.7 = (bf16[80,640]{1,0:T(8,128)(2,1)S(1)}, bf16[80,640]{1,0:T(8,128)(2,1)S(1)}, u32[]{:S(2)}, u32[]{:S(2)}) collective-permute-start(bf16[80,640]{1,0:T(8,128)(2,1)S(1)} %get-tuple-element.105), channel_id=1, source_target_pairs={{0,2},{1,3},{2,0},{3,1},{4,6},{5,7},{6,4},{7,5},{8,10},{9,11},{10,... | collective-permute-start | bytes 307208 | tf_op jit(solution)/shard_map/ppermute | solution.py:27
  34.4 1.5 %collective-permute-start.8 = (bf16[80,640]{1,0:T(8,128)(2,1)S(1)}, bf16[80,640]{1,0:T(8,128)(2,1)S(1)}, u32[]{:S(2)}, u32[]{:S(2)}) collective-permute-start(bf16[80,640]{1,0:T(8,128)(2,1)S(1)} %get-tuple-element.106), channel_id=1, source_target_pairs={{0,4},{1,5},{2,6},{3,7},{4,0},{5,1},{6,2},{7,3},{8,12},{9,13},{10,... | collective-permute-start | bytes 307208 | tf_op jit(solution)/shard_map/ppermute | solution.py:27
  35.9 1.5 %load_output.1.refs_4_ = bf16[512,2048]{1,0:T(8,128)(2,1)S(1)} custom-call(bf16[512,2048]{1,0:T(8,128)(2,1)} %refs_0_.2, bf16[80,640]{1,0:T(8,128)(2,1)S(1)} %get-tuple-element.104.refs_1_.refs_0_), custom_call_target="tpu_custom_call" | custom-call | bytes 4194304 | tf_op jit(solution)/shard_map/load_output/pallas_call | solution.py:55
  37.8 5.6 %collective-permute-done.8.refs_2_ = bf16[80,640]{1,0:T(8,128)(2,1)S(1)} collective-permute-done((bf16[80,640]{1,0:T(8,128)(2,1)S(1)}, bf16[80,640]{1,0:T(8,128)(2,1)S(1)}, u32[]{:S(2)}, u32[]{:S(2)}) %collective-permute-start.8) | collective-permute-done | bytes 102432 | tf_op jit(solution)/shard_map/ppermute | solution.py:27
  43.4 0.9 project_out.1
  44.4 2.5 %collective-permute-start.13 = (bf16[24,2048]{1,0:T(8,128)(2,1)S(1)}, bf16[24,2048]{1,0:T(8,128)(2,1)S(1)}, u32[]{:S(2)}, u32[]{:S(2)}) collective-permute-start(bf16[24,2048]{1,0:T(8,128)(2,1)S(1)} %get-tuple-element.118), channel_id=1, source_target_pairs={{0,24},{8,16},{16,8},{24,0},{1,25},{9,17},{17,9},{25,1},{2,26},{10... | collective-permute-start | bytes 294920 | tf_op jit(solution)/shard_map/ppermute | solution.py:27
  48.0 3.0 %collective-permute-done.13.refs_3_ = bf16[24,2048]{1,0:T(8,128)(2,1)S(1)} collective-permute-done((bf16[24,2048]{1,0:T(8,128)(2,1)S(1)}, bf16[24,2048]{1,0:T(8,128)(2,1)S(1)}, u32[]{:S(2)}, u32[]{:S(2)}) %collective-permute-start.13) | collective-permute-done | bytes 98336 | tf_op jit(solution)/shard_map/ppermute | solution.py:27
  51.0 1.7 %collective-permute-done.11.refs_1_ = bf16[24,2048]{1,0:T(8,128)(2,1)S(1)} collective-permute-done((bf16[24,2048]{1,0:T(8,128)(2,1)S(1)}, bf16[24,2048]{1,0:T(8,128)(2,1)S(1)}, u32[]{:S(2)}, u32[]{:S(2)}) %collective-permute-start.11) | collective-permute-done | bytes 98336 | tf_op jit(solution)/shard_map/ppermute | solution.py:27
  52.7 1.0 moe_norm.1
  53.7 1.7 %collective-permute-start.15 = (bf16[16,2048]{1,0:T(8,128)(2,1)S(1)}, bf16[16,2048]{1,0:T(8,128)(2,1)S(1)}, u32[]{:S(2)}, u32[]{:S(2)}) collective-permute-start(bf16[16,2048]{1,0:T(8,128)(2,1)S(1)} %get-tuple-element.122), channel_id=1, source_target_pairs={{0,6},{1,7},{2,4},{3,5},{4,2},{5,3},{6,0},{7,1},{8,14},{9,15},{10,... | collective-permute-start | bytes 196616 | tf_op jit(solution)/shard_map/ppermute | solution.py:27
  55.4 2.7 %collective-permute-start.19 = (bf16[16,2048]{1,0:T(8,128)(2,1)S(1)}, bf16[16,2048]{1,0:T(8,128)(2,1)S(1)}, u32[]{:S(2)}, u32[]{:S(2)}) collective-permute-start(bf16[16,2048]{1,0:T(8,128)(2,1)S(1)} %get-tuple-element.122), channel_id=1, source_target_pairs={{0,4},{1,5},{2,6},{3,7},{4,0},{5,1},{6,2},{7,3},{8,12},{9,13},{10,... | collective-permute-start | bytes 196616 | tf_op jit(solution)/shard_map/ppermute | solution.py:27
  58.2 1.5 %collective-permute-start.16 = (f32[24,512]{1,0:T(8,128)S(1)}, f32[24,512]{1,0:T(8,128)S(1)}, u32[]{:S(2)}, u32[]{:S(2)}) collective-permute-start(f32[24,512]{1,0:T(8,128)S(1)} %get-tuple-element.123), channel_id=1, source_target_pairs={{0,8},{8,0},{16,24},{24,16},{1,9},{9,1},{17,25},{25,17},{2,10},{10... | collective-permute-start | bytes 147464 | tf_op jit(solution)/shard_map/ppermute | solution.py:27
  59.6 1.5 %collective-permute-start.17 = (f32[24,512]{1,0:T(8,128)S(1)}, f32[24,512]{1,0:T(8,128)S(1)}, u32[]{:S(2)}, u32[]{:S(2)}) collective-permute-start(f32[24,512]{1,0:T(8,128)S(1)} %get-tuple-element.124), channel_id=1, source_target_pairs={{0,16},{8,24},{16,0},{24,8},{1,17},{9,25},{17,1},{25,9},{2,18},{10... | collective-permute-start | bytes 147464 | tf_op jit(solution)/shard_map/ppermute | solution.py:27
  61.6 0.7 collective-permute-done.16.refs_1_
  62.2 1.5 %collective-permute-done.17.refs_2_ = f32[24,512]{1,0:T(8,128)S(1)} collective-permute-done((f32[24,512]{1,0:T(8,128)S(1)}, f32[24,512]{1,0:T(8,128)S(1)}, u32[]{:S(2)}, u32[]{:S(2)}) %collective-permute-start.17) | collective-permute-done | bytes 49184 | tf_op jit(solution)/shard_map/ppermute | solution.py:27
  63.8 0.6 collective-permute-start.20
  64.4 1.5 %collective-permute-start.21 = (bf16[72,2048]{1,0:T(8,128)(2,1)S(1)}, bf16[72,2048]{1,0:T(8,128)(2,1)S(1)}, u32[]{:S(2)}, u32[]{:S(2)}) collective-permute-start(bf16[72,2048]{1,0:T(8,128)(2,1)S(1)} %constant_dynamic-update-slice_fusion.4.refs_3_.refs_0_), channel_id=1, source_target_pairs={{0,16},{8,24},{16,0},{24,8},{1,17},{9,25},{17,1},{25,9},{2,18},{10... | collective-permute-start | bytes 884744 | tf_op jit(solution)/shard_map/ppermute | solution.py:27
  65.8 1.5 %collective-permute-start.25 = (bf16[72,2048]{1,0:T(8,128)(2,1)S(1)}, bf16[72,2048]{1,0:T(8,128)(2,1)S(1)}, u32[]{:S(2)}, u32[]{:S(2)}) collective-permute-start(bf16[72,2048]{1,0:T(8,128)(2,1)S(1)} %constant_dynamic-update-slice_fusion.4.refs_3_.refs_0_), channel_id=1, source_target_pairs={{0,24},{8,16},{16,8},{24,0},{1,25},{9,17},{17,9},{25,1},{2,26},{10... | collective-permute-start | bytes 884744 | tf_op jit(solution)/shard_map/ppermute | solution.py:27
  67.4 3.0 %load_experts.1 = (bf16[2,2048,256]{2,1,0:T(8,128)(2,1)S(1)}, bf16[2,2048,256]{2,1,0:T(8,128)(2,1)S(1)}, bf16[2,256,2048]{2,1,0:T(8,128)(2,1)S(1)}) custom-call(bf16[2,2048,256]{2,1,0:T(8,128)(2,1)} %refs_0_.3, bf16[2,2048,256]{2,1,0:T(8,128)(2,1)} %refs_1_.1, bf16[2,256,2048]{2,1,0:T(8,128)(2,1)} %refs_2_.1, ...), custom_call_target="tpu_custom_call" | custom-call | bytes 12582912 | tf_op jit(solution)/shard_map/load_experts/pallas_call | solution.py:55
  70.4 3.3 %collective-permute-done.20.refs_1_ = bf16[72,2048]{1,0:T(8,128)(2,1)S(1)} collective-permute-done((bf16[72,2048]{1,0:T(8,128)(2,1)S(1)}, bf16[72,2048]{1,0:T(8,128)(2,1)S(1)}, u32[]{:S(2)}, u32[]{:S(2)}) %collective-permute-start.20) | collective-permute-done | bytes 294944 | tf_op jit(solution)/shard_map/ppermute | solution.py:27
  73.7 2.8 %collective-permute-done.21.refs_2_ = bf16[72,2048]{1,0:T(8,128)(2,1)S(1)} collective-permute-done((bf16[72,2048]{1,0:T(8,128)(2,1)S(1)}, bf16[72,2048]{1,0:T(8,128)(2,1)S(1)}, u32[]{:S(2)}, u32[]{:S(2)}) %collective-permute-start.21) | collective-permute-done | bytes 294944 | tf_op jit(solution)/shard_map/ppermute | solution.py:27
  76.4 4.9 %experts_early.1 = (bf16[208,512]{1,0:T(8,128)(2,1)S(1)}, bf16[208,512]{1,0:T(8,128)(2,1)S(1)}, bf16[208,512]{1,0:T(8,128)(2,1)S(1)}, bf16[208,512]{1,0:T(8,128)(2,1)S(1)}) custom-call(s32[2]{0:T(128)S(1)} %pad_add_fusion.scalar_ref, bf16[72,2048]{1,0:T(8,128)(2,1)S(1)} %constant_dynamic-update-slice_fusion.4.refs_3_.refs_0_, ...), custom_call_target="tpu_custom_call" | custom-call | flops 1358954496 | bytes 12582912 | tf_op jit(solution)/shard_map/experts_early/pallas_call | solution.py:55
  81.4 2.5 %collective-permute-start.22 = (bf16[208,512]{1,0:T(8,128)(2,1)S(1)}, bf16[208,512]{1,0:T(8,128)(2,1)S(1)}, u32[]{:S(2)}, u32[]{:S(2)}) collective-permute-start(bf16[208,512]{1,0:T(8,128)(2,1)S(1)} %get-tuple-element.141), channel_id=1, source_target_pairs={{0,8},{8,0},{16,24},{24,16},{1,9},{9,1},{17,25},{25,17},{2,10},{10... | collective-permute-start | bytes 638984 | tf_op jit(solution)/shard_map/ppermute | solution.py:27
  83.9 1.5 %collective-permute-start.23 = (bf16[208,512]{1,0:T(8,128)(2,1)S(1)}, bf16[208,512]{1,0:T(8,128)(2,1)S(1)}, u32[]{:S(2)}, u32[]{:S(2)}) collective-permute-start(bf16[208,512]{1,0:T(8,128)(2,1)S(1)} %get-tuple-element.142), channel_id=1, source_target_pairs={{0,16},{8,24},{16,0},{24,8},{1,17},{9,25},{17,1},{25,9},{2,18},{10... | collective-permute-start | bytes 638984 | tf_op jit(solution)/shard_map/ppermute | solution.py:27
  85.4 4.0 %experts_late.1 = (bf16[72,512]{1,0:T(8,128)(2,1)S(1)}, bf16[72,512]{1,0:T(8,128)(2,1)S(1)}, bf16[72,512]{1,0:T(8,128)(2,1)S(1)}, bf16[72,512]{1,0:T(8,128)(2,1)S(1)}) custom-call(s32[2]{0:T(128)S(1)} %pad_add_fusion.scalar_ref, bf16[72,2048]{1,0:T(8,128)(2,1)S(1)} %collective-permute-done.25.refs_0_, ...), custom_call_target="tpu_custom_call" | custom-call | flops 452984832 | bytes 12582912 | tf_op jit(solution)/shard_map/experts_late/pallas_call | solution.py:55
  89.4 2.0 %collective-permute-start.26 = (bf16[72,512]{1,0:T(8,128)(2,1)S(1)}, bf16[72,512]{1,0:T(8,128)(2,1)S(1)}, u32[]{:S(2)}, u32[]{:S(2)}) collective-permute-start(bf16[72,512]{1,0:T(8,128)(2,1)S(1)} %get-tuple-element.145), channel_id=1, source_target_pairs={{0,8},{8,0},{16,24},{24,16},{1,9},{9,1},{17,25},{25,17},{2,10},{10... | collective-permute-start | bytes 221192 | tf_op jit(solution)/shard_map/ppermute | solution.py:27
  91.4 1.5 %collective-permute-start.27 = (bf16[72,512]{1,0:T(8,128)(2,1)S(1)}, bf16[72,512]{1,0:T(8,128)(2,1)S(1)}, u32[]{:S(2)}, u32[]{:S(2)}) collective-permute-start(bf16[72,512]{1,0:T(8,128)(2,1)S(1)} %get-tuple-element.146), channel_id=1, source_target_pairs={{0,16},{8,24},{16,0},{24,8},{1,17},{9,25},{17,1},{25,9},{2,18},{10... | collective-permute-start | bytes 221192 | tf_op jit(solution)/shard_map/ppermute | solution.py:27
  92.9 1.0 collective-permute-done.26.refs_5_
  93.8 2.8 %collective-permute-start.28 = (bf16[72,512]{1,0:T(8,128)(2,1)S(1)}, bf16[72,512]{1,0:T(8,128)(2,1)S(1)}, u32[]{:S(2)}, u32[]{:S(2)}) collective-permute-start(bf16[72,512]{1,0:T(8,128)(2,1)S(1)} %get-tuple-element.147), channel_id=1, source_target_pairs={{0,24},{8,16},{16,8},{24,0},{1,25},{9,17},{17,9},{25,1},{2,26},{10... | collective-permute-start | bytes 221192 | tf_op jit(solution)/shard_map/ppermute | solution.py:27
  96.7 2.4 %collective-permute-done.28.refs_7_ = bf16[72,512]{1,0:T(8,128)(2,1)S(1)} collective-permute-done((bf16[72,512]{1,0:T(8,128)(2,1)S(1)}, bf16[72,512]{1,0:T(8,128)(2,1)S(1)}, u32[]{:S(2)}, u32[]{:S(2)}) %collective-permute-start.28) | collective-permute-done | bytes 73760 | tf_op jit(solution)/shard_map/ppermute | solution.py:27
  99.3 0.9 collective-permute-start.30
  100.2 2.5 %collective-permute-start.31 = (bf16[80,512]{1,0:T(8,128)(2,1)S(1)}, bf16[80,512]{1,0:T(8,128)(2,1)S(1)}, u32[]{:S(2)}, u32[]{:S(2)}) collective-permute-start(bf16[80,512]{1,0:T(8,128)(2,1)S(1)} %get-tuple-element.156), channel_id=1, source_target_pairs={{0,4},{1,5},{2,6},{3,7},{4,0},{5,1},{6,2},{7,3},{8,12},{9,13},{10,... | collective-permute-start | bytes 245768 | tf_op jit(solution)/shard_map/ppermute | solution.py:27
  102.7 1.0 collective-permute-start.32
  103.8 2.8 %collective-permute-start.29 = (f32[24,512]{1,0:T(8,128)S(1)}, f32[24,512]{1,0:T(8,128)S(1)}, u32[]{:S(2)}, u32[]{:S(2)}) collective-permute-start(f32[24,512]{1,0:T(8,128)S(1)} %get-tuple-element.153), channel_id=1, source_target_pairs={{0,24},{8,16},{16,8},{24,0},{1,25},{9,17},{17,9},{25,1},{2,26},{10... | collective-permute-start | bytes 147464 | tf_op jit(solution)/shard_map/ppermute | solution.py:27
  106.6 0.6 copy.25
  107.2 1.5 %collective-permute-done.29.refs_3_ = f32[24,512]{1,0:T(8,128)S(1)} collective-permute-done((f32[24,512]{1,0:T(8,128)S(1)}, f32[24,512]{1,0:T(8,128)S(1)}, u32[]{:S(2)}, u32[]{:S(2)}) %collective-permute-start.29) | collective-permute-done | bytes 49184 | tf_op jit(solution)/shard_map/ppermute | solution.py:27
  109.0 0.7 final.1
  (57 shorter events, 4.5 us)
Async XLA Ops:
  0.6 18.0 %collective-permute-start.4 = (bf16[2,2048,256]{2,1,0:T(8,128)(2,1)}, bf16[2,2048,256]{2,1,0:T(8,128)(2,1)S(1)}, u32[]{:S(2)}, u32[]{:S(2)}) collective-permute-start(bf16[2,2048,256]{2,1,0:T(8,128)(2,1)} %refs_0_.3), channel_id=1, source_target_pairs={{0,1},{1,0},{2,3},{3,2},{4,5},{5,4},{6,7},{7,6},{8,9},{9,8},{10,11... | collective-permute-start | bytes 6291464 | tf_op jit(solution)/shard_map/ppermute | solution.py:27
  4.7 9.0 %collective-permute-start = (bf16[64,640]{1,0:T(8,128)(2,1)S(1)}, bf16[64,640]{1,0:T(8,128)(2,1)S(1)}, u32[]{:S(2)}, u32[]{:S(2)}) collective-permute-start(bf16[64,640]{1,0:T(8,128)(2,1)S(1)} %get-tuple-element.87), channel_id=1, source_target_pairs={{0,2},{1,3},{2,0},{3,1},{4,6},{5,7},{6,4},{7,5},{8,10},{9,11},{10,... | collective-permute-start | bytes 245768 | tf_op jit(solution)/shard_map/ppermute | solution.py:27
  7.3 9.5 %collective-permute-start.1 = (bf16[64,640]{1,0:T(8,128)(2,1)S(1)}, bf16[64,640]{1,0:T(8,128)(2,1)S(1)}, u32[]{:S(2)}, u32[]{:S(2)}) collective-permute-start(bf16[64,640]{1,0:T(8,128)(2,1)S(1)} %get-tuple-element.87), channel_id=1, source_target_pairs={{0,4},{1,5},{2,6},{3,7},{4,0},{5,1},{6,2},{7,3},{8,12},{9,13},{10,... | collective-permute-start | bytes 245768 | tf_op jit(solution)/shard_map/ppermute | solution.py:27
  9.9 7.0 %collective-permute-start.2 = (bf16[64,640]{1,0:T(8,128)(2,1)S(1)}, bf16[64,640]{1,0:T(8,128)(2,1)S(1)}, u32[]{:S(2)}, u32[]{:S(2)}) collective-permute-start(bf16[64,640]{1,0:T(8,128)(2,1)S(1)} %get-tuple-element.87), channel_id=1, source_target_pairs={{0,6},{1,7},{2,4},{3,5},{4,2},{5,3},{6,0},{7,1},{8,14},{9,15},{10,... | collective-permute-start | bytes 245768 | tf_op jit(solution)/shard_map/ppermute | solution.py:27
  9.9 8.7 %copy-start.1 = (s32[13]{0:T(128)S(1)}, s32[13]{0:T(128)}, u32[]{:S(2)}) copy-start(s32[13]{0:T(128)} %lens_ref.1) | copy-start | bytes 160
  9.9 8.7 %copy-start.2 = (s32[8]{0:T(128)S(1)}, s32[8]{0:T(128)}, u32[]{:S(2)}) copy-start(s32[8]{0:T(128)} %owner_ref.1) | copy-start | bytes 100
  9.9 8.7 %copy-start.3 = (s32[8]{0:T(128)S(1)}, s32[8]{0:T(128)}, u32[]{:S(2)}) copy-start(s32[8]{0:T(128)} %slot_ref.1) | copy-start | bytes 100
  16.9 1.7 %collective-permute-start.3 = (bf16[256,640]{1,0:T(8,128)(2,1)S(1)}, bf16[256,640]{1,0:T(8,128)(2,1)S(1)}, u32[]{:S(2)}, u32[]{:S(2)}) collective-permute-start(bf16[256,640]{1,0:T(8,128)(2,1)S(1)} %constant_dynamic-update-slice_fusion.query_a.refs_3_.refs_1_), channel_id=1, source_target_pairs={{0,1},{1,0},{2,3},{3,2},{4,5},{5,4},{6,7},{7,6},{8,9},{9,8},{10,11... | collective-permute-start | bytes 983048 | tf_op jit(solution)/shard_map/ppermute | solution.py:27
  24.0 3.4 %collective-permute-start.5 = (f32[520,256]{1,0:T(8,128)S(1)}, f32[520,256]{1,0:T(8,128)S(1)}, u32[]{:S(2)}, u32[]{:S(2)}) collective-permute-start(f32[520,256]{1,0:T(8,128)S(1)} %get-tuple-element.98), channel_id=1, source_target_pairs={{0,1},{1,0},{2,3},{3,2},{4,5},{5,4},{6,7},{7,6},{8,9},{9,8},{10,11... | collective-permute-start | bytes 1597448 | tf_op jit(solution)/shard_map/ppermute | solution.py:27
  25.8 1.6 %collective-permute-start.6 = (f32[16,640]{1,0:T(8,128)S(1)}, f32[16,640]{1,0:T(8,128)S(1)}, u32[]{:S(2)}, u32[]{:S(2)}) collective-permute-start(f32[16,640]{1,0:T(8,128)S(1)} %get-tuple-element.99.dec_mine), channel_id=1, source_target_pairs={{0,1},{1,0},{2,3},{3,2},{4,5},{5,4},{6,7},{7,6},{8,9},{9,8},{10,11... | collective-permute-start | bytes 122888 | tf_op jit(solution)/shard_map/ppermute | solution.py:27
  27.9 9.6 %collective-permute-start.10 = (bf16[2,2048,256]{2,1,0:T(8,128)(2,1)}, bf16[2,2048,256]{2,1,0:T(8,128)(2,1)}, u32[]{:S(2)}, u32[]{:S(2)}) collective-permute-start(bf16[2,2048,256]{2,1,0:T(8,128)(2,1)} %refs_1_.1), channel_id=1, source_target_pairs={{0,1},{1,0},{2,3},{3,2},{4,5},{5,4},{6,7},{7,6},{8,9},{9,8},{10,11... | collective-permute-start | bytes 6291464 | tf_op jit(solution)/shard_map/ppermute | solution.py:27
  28.3 9.2 %collective-permute-start.9 = (bf16[80,640]{1,0:T(8,128)(2,1)S(1)}, bf16[80,640]{1,0:T(8,128)(2,1)S(1)}, u32[]{:S(2)}, u32[]{:S(2)}) collective-permute-start(bf16[80,640]{1,0:T(8,128)(2,1)S(1)} %get-tuple-element.107), channel_id=1, source_target_pairs={{0,6},{1,7},{2,4},{3,5},{4,2},{5,3},{6,0},{7,1},{8,14},{9,15},{10,... | collective-permute-start | bytes 307208 | tf_op jit(solution)/shard_map/ppermute | solution.py:27
  30.4 7.4 %collective-permute-start.7 = (bf16[80,640]{1,0:T(8,128)(2,1)S(1)}, bf16[80,640]{1,0:T(8,128)(2,1)S(1)}, u32[]{:S(2)}, u32[]{:S(2)}) collective-permute-start(bf16[80,640]{1,0:T(8,128)(2,1)S(1)} %get-tuple-element.105), channel_id=1, source_target_pairs={{0,2},{1,3},{2,0},{3,1},{4,6},{5,7},{6,4},{7,5},{8,10},{9,11},{10,... | collective-permute-start | bytes 307208 | tf_op jit(solution)/shard_map/ppermute | solution.py:27
  34.4 9.0 %collective-permute-start.8 = (bf16[80,640]{1,0:T(8,128)(2,1)S(1)}, bf16[80,640]{1,0:T(8,128)(2,1)S(1)}, u32[]{:S(2)}, u32[]{:S(2)}) collective-permute-start(bf16[80,640]{1,0:T(8,128)(2,1)S(1)} %get-tuple-element.106), channel_id=1, source_target_pairs={{0,4},{1,5},{2,6},{3,7},{4,0},{5,1},{6,2},{7,3},{8,12},{9,13},{10,... | collective-permute-start | bytes 307208 | tf_op jit(solution)/shard_map/ppermute | solution.py:27
  37.4 6.9 %copy-start.4 = (bf16[2,256,2048]{2,1,0:T(8,128)(2,1)S(1)}, bf16[2,256,2048]{2,1,0:T(8,128)(2,1)}, u32[]{:S(2)}) copy-start(bf16[2,256,2048]{2,1,0:T(8,128)(2,1)} %refs_2_.1) | copy-start | bytes 6291460
  37.5 15.3 %copy-start = (f32[2048]{0:T(1024)S(1)}, f32[2048]{0:T(1024)}, u32[]{:S(2)}) copy-start(f32[2048]{0:T(1024)} %param.32) | copy-start | bytes 24580
  44.4 6.6 %collective-permute-start.14 = (bf16[2,256,2048]{2,1,0:T(8,128)(2,1)S(1)}, bf16[2,256,2048]{2,1,0:T(8,128)(2,1)S(1)}, u32[]{:S(2)}, u32[]{:S(2)}) collective-permute-start(bf16[2,256,2048]{2,1,0:T(8,128)(2,1)S(1)} %copy-done.4), channel_id=1, source_target_pairs={{0,1},{1,0},{2,3},{3,2},{4,5},{5,4},{6,7},{7,6},{8,9},{9,8},{10,11... | collective-permute-start | bytes 6291464 | tf_op jit(solution)/shard_map/ppermute | solution.py:27
  44.4 6.6 %collective-permute-start.13 = (bf16[24,2048]{1,0:T(8,128)(2,1)S(1)}, bf16[24,2048]{1,0:T(8,128)(2,1)S(1)}, u32[]{:S(2)}, u32[]{:S(2)}) collective-permute-start(bf16[24,2048]{1,0:T(8,128)(2,1)S(1)} %get-tuple-element.118), channel_id=1, source_target_pairs={{0,24},{8,16},{16,8},{24,0},{1,25},{9,17},{17,9},{25,1},{2,26},{10... | collective-permute-start | bytes 294920 | tf_op jit(solution)/shard_map/ppermute | solution.py:27
  46.9 5.8 %collective-permute-start.11 = (bf16[24,2048]{1,0:T(8,128)(2,1)S(1)}, bf16[24,2048]{1,0:T(8,128)(2,1)S(1)}, u32[]{:S(2)}, u32[]{:S(2)}) collective-permute-start(bf16[24,2048]{1,0:T(8,128)(2,1)S(1)} %get-tuple-element.116), channel_id=1, source_target_pairs={{0,8},{8,0},{16,24},{24,16},{1,9},{9,1},{17,25},{25,17},{2,10},{10... | collective-permute-start | bytes 294920 | tf_op jit(solution)/shard_map/ppermute | solution.py:27
  47.5 5.2 %collective-permute-start.12 = (bf16[24,2048]{1,0:T(8,128)(2,1)S(1)}, bf16[24,2048]{1,0:T(8,128)(2,1)S(1)}, u32[]{:S(2)}, u32[]{:S(2)}) collective-permute-start(bf16[24,2048]{1,0:T(8,128)(2,1)S(1)} %get-tuple-element.117), channel_id=1, source_target_pairs={{0,16},{8,24},{16,0},{24,8},{1,17},{9,25},{17,1},{25,9},{2,18},{10... | collective-permute-start | bytes 294920 | tf_op jit(solution)/shard_map/ppermute | solution.py:27
  53.7 10.0 %collective-permute-start.15 = (bf16[16,2048]{1,0:T(8,128)(2,1)S(1)}, bf16[16,2048]{1,0:T(8,128)(2,1)S(1)}, u32[]{:S(2)}, u32[]{:S(2)}) collective-permute-start(bf16[16,2048]{1,0:T(8,128)(2,1)S(1)} %get-tuple-element.122), channel_id=1, source_target_pairs={{0,6},{1,7},{2,4},{3,5},{4,2},{5,3},{6,0},{7,1},{8,14},{9,15},{10,... | collective-permute-start | bytes 196616 | tf_op jit(solution)/shard_map/ppermute | solution.py:27
  55.4 6.2 %collective-permute-start.18 = (bf16[16,2048]{1,0:T(8,128)(2,1)S(1)}, bf16[16,2048]{1,0:T(8,128)(2,1)S(1)}, u32[]{:S(2)}, u32[]{:S(2)}) collective-permute-start(bf16[16,2048]{1,0:T(8,128)(2,1)S(1)} %get-tuple-element.122), channel_id=1, source_target_pairs={{0,2},{1,3},{2,0},{3,1},{4,6},{5,7},{6,4},{7,5},{8,10},{9,11},{10,... | collective-permute-start | bytes 196616 | tf_op jit(solution)/shard_map/ppermute | solution.py:27
  55.4 8.3 %collective-permute-start.19 = (bf16[16,2048]{1,0:T(8,128)(2,1)S(1)}, bf16[16,2048]{1,0:T(8,128)(2,1)S(1)}, u32[]{:S(2)}, u32[]{:S(2)}) collective-permute-start(bf16[16,2048]{1,0:T(8,128)(2,1)S(1)} %get-tuple-element.122), channel_id=1, source_target_pairs={{0,4},{1,5},{2,6},{3,7},{4,0},{5,1},{6,2},{7,3},{8,12},{9,13},{10,... | collective-permute-start | bytes 196616 | tf_op jit(solution)/shard_map/ppermute | solution.py:27
  58.2 4.1 %collective-permute-start.16 = (f32[24,512]{1,0:T(8,128)S(1)}, f32[24,512]{1,0:T(8,128)S(1)}, u32[]{:S(2)}, u32[]{:S(2)}) collective-permute-start(f32[24,512]{1,0:T(8,128)S(1)} %get-tuple-element.123), channel_id=1, source_target_pairs={{0,8},{8,0},{16,24},{24,16},{1,9},{9,1},{17,25},{25,17},{2,10},{10... | collective-permute-start | bytes 147464 | tf_op jit(solution)/shard_map/ppermute | solution.py:27
  59.6 4.1 %collective-permute-start.17 = (f32[24,512]{1,0:T(8,128)S(1)}, f32[24,512]{1,0:T(8,128)S(1)}, u32[]{:S(2)}, u32[]{:S(2)}) collective-permute-start(f32[24,512]{1,0:T(8,128)S(1)} %get-tuple-element.124), channel_id=1, source_target_pairs={{0,16},{8,24},{16,0},{24,8},{1,17},{9,25},{17,1},{25,9},{2,18},{10... | collective-permute-start | bytes 147464 | tf_op jit(solution)/shard_map/ppermute | solution.py:27
  63.8 9.9 %collective-permute-start.20 = (bf16[72,2048]{1,0:T(8,128)(2,1)S(1)}, bf16[72,2048]{1,0:T(8,128)(2,1)S(1)}, u32[]{:S(2)}, u32[]{:S(2)}) collective-permute-start(bf16[72,2048]{1,0:T(8,128)(2,1)S(1)} %constant_dynamic-update-slice_fusion.4.refs_3_.refs_0_), channel_id=1, source_target_pairs={{0,8},{8,0},{16,24},{24,16},{1,9},{9,1},{17,25},{25,17},{2,10},{10... | collective-permute-start | bytes 884744 | tf_op jit(solution)/shard_map/ppermute | solution.py:27
  64.4 12.1 %collective-permute-start.21 = (bf16[72,2048]{1,0:T(8,128)(2,1)S(1)}, bf16[72,2048]{1,0:T(8,128)(2,1)S(1)}, u32[]{:S(2)}, u32[]{:S(2)}) collective-permute-start(bf16[72,2048]{1,0:T(8,128)(2,1)S(1)} %constant_dynamic-update-slice_fusion.4.refs_3_.refs_0_), channel_id=1, source_target_pairs={{0,16},{8,24},{16,0},{24,8},{1,17},{9,25},{17,1},{25,9},{2,18},{10... | collective-permute-start | bytes 884744 | tf_op jit(solution)/shard_map/ppermute | solution.py:27
  65.8 19.6 %collective-permute-start.25 = (bf16[72,2048]{1,0:T(8,128)(2,1)S(1)}, bf16[72,2048]{1,0:T(8,128)(2,1)S(1)}, u32[]{:S(2)}, u32[]{:S(2)}) collective-permute-start(bf16[72,2048]{1,0:T(8,128)(2,1)S(1)} %constant_dynamic-update-slice_fusion.4.refs_3_.refs_0_), channel_id=1, source_target_pairs={{0,24},{8,16},{16,8},{24,0},{1,25},{9,17},{17,9},{25,1},{2,26},{10... | collective-permute-start | bytes 884744 | tf_op jit(solution)/shard_map/ppermute | solution.py:27
  81.4 17.7 %collective-permute-start.22 = (bf16[208,512]{1,0:T(8,128)(2,1)S(1)}, bf16[208,512]{1,0:T(8,128)(2,1)S(1)}, u32[]{:S(2)}, u32[]{:S(2)}) collective-permute-start(bf16[208,512]{1,0:T(8,128)(2,1)S(1)} %get-tuple-element.141), channel_id=1, source_target_pairs={{0,8},{8,0},{16,24},{24,16},{1,9},{9,1},{17,25},{25,17},{2,10},{10... | collective-permute-start | bytes 638984 | tf_op jit(solution)/shard_map/ppermute | solution.py:27
  83.9 15.2 %collective-permute-start.23 = (bf16[208,512]{1,0:T(8,128)(2,1)S(1)}, bf16[208,512]{1,0:T(8,128)(2,1)S(1)}, u32[]{:S(2)}, u32[]{:S(2)}) collective-permute-start(bf16[208,512]{1,0:T(8,128)(2,1)S(1)} %get-tuple-element.142), channel_id=1, source_target_pairs={{0,16},{8,24},{16,0},{24,8},{1,17},{9,25},{17,1},{25,9},{2,18},{10... | collective-permute-start | bytes 638984 | tf_op jit(solution)/shard_map/ppermute | solution.py:27
  85.3 13.8 %collective-permute-start.24 = (bf16[208,512]{1,0:T(8,128)(2,1)S(1)}, bf16[208,512]{1,0:T(8,128)(2,1)S(1)}, u32[]{:S(2)}, u32[]{:S(2)}) collective-permute-start(bf16[208,512]{1,0:T(8,128)(2,1)S(1)} %get-tuple-element.143), channel_id=1, source_target_pairs={{0,24},{8,16},{16,8},{24,0},{1,25},{9,17},{17,9},{25,1},{2,26},{10... | collective-permute-start | bytes 638984 | tf_op jit(solution)/shard_map/ppermute | solution.py:27
  89.4 4.4 %collective-permute-start.26 = (bf16[72,512]{1,0:T(8,128)(2,1)S(1)}, bf16[72,512]{1,0:T(8,128)(2,1)S(1)}, u32[]{:S(2)}, u32[]{:S(2)}) collective-permute-start(bf16[72,512]{1,0:T(8,128)(2,1)S(1)} %get-tuple-element.145), channel_id=1, source_target_pairs={{0,8},{8,0},{16,24},{24,16},{1,9},{9,1},{17,25},{25,17},{2,10},{10... | collective-permute-start | bytes 221192 | tf_op jit(solution)/shard_map/ppermute | solution.py:27
  91.4 5.2 %collective-permute-start.27 = (bf16[72,512]{1,0:T(8,128)(2,1)S(1)}, bf16[72,512]{1,0:T(8,128)(2,1)S(1)}, u32[]{:S(2)}, u32[]{:S(2)}) collective-permute-start(bf16[72,512]{1,0:T(8,128)(2,1)S(1)} %get-tuple-element.146), channel_id=1, source_target_pairs={{0,16},{8,24},{16,0},{24,8},{1,17},{9,25},{17,1},{25,9},{2,18},{10... | collective-permute-start | bytes 221192 | tf_op jit(solution)/shard_map/ppermute | solution.py:27
  93.8 5.3 %collective-permute-start.28 = (bf16[72,512]{1,0:T(8,128)(2,1)S(1)}, bf16[72,512]{1,0:T(8,128)(2,1)S(1)}, u32[]{:S(2)}, u32[]{:S(2)}) collective-permute-start(bf16[72,512]{1,0:T(8,128)(2,1)S(1)} %get-tuple-element.147), channel_id=1, source_target_pairs={{0,24},{8,16},{16,8},{24,0},{1,25},{9,17},{17,9},{25,1},{2,26},{10... | collective-permute-start | bytes 221192 | tf_op jit(solution)/shard_map/ppermute | solution.py:27
  99.3 9.4 %collective-permute-start.30 = (bf16[80,512]{1,0:T(8,128)(2,1)S(1)}, bf16[80,512]{1,0:T(8,128)(2,1)S(1)}, u32[]{:S(2)}, u32[]{:S(2)}) collective-permute-start(bf16[80,512]{1,0:T(8,128)(2,1)S(1)} %get-tuple-element.155), channel_id=1, source_target_pairs={{0,2},{1,3},{2,0},{3,1},{4,6},{5,7},{6,4},{7,5},{8,10},{9,11},{10,... | collective-permute-start | bytes 245768 | tf_op jit(solution)/shard_map/ppermute | solution.py:27
  100.2 8.5 %collective-permute-start.31 = (bf16[80,512]{1,0:T(8,128)(2,1)S(1)}, bf16[80,512]{1,0:T(8,128)(2,1)S(1)}, u32[]{:S(2)}, u32[]{:S(2)}) collective-permute-start(bf16[80,512]{1,0:T(8,128)(2,1)S(1)} %get-tuple-element.156), channel_id=1, source_target_pairs={{0,4},{1,5},{2,6},{3,7},{4,0},{5,1},{6,2},{7,3},{8,12},{9,13},{10,... | collective-permute-start | bytes 245768 | tf_op jit(solution)/shard_map/ppermute | solution.py:27
  102.7 6.2 %collective-permute-start.32 = (bf16[80,512]{1,0:T(8,128)(2,1)S(1)}, bf16[80,512]{1,0:T(8,128)(2,1)S(1)}, u32[]{:S(2)}, u32[]{:S(2)}) collective-permute-start(bf16[80,512]{1,0:T(8,128)(2,1)S(1)} %get-tuple-element.157), channel_id=1, source_target_pairs={{0,6},{1,7},{2,4},{3,5},{4,2},{5,3},{6,0},{7,1},{8,14},{9,15},{10,... | collective-permute-start | bytes 245768 | tf_op jit(solution)/shard_map/ppermute | solution.py:27
  103.8 5.0 %collective-permute-start.29 = (f32[24,512]{1,0:T(8,128)S(1)}, f32[24,512]{1,0:T(8,128)S(1)}, u32[]{:S(2)}, u32[]{:S(2)}) collective-permute-start(f32[24,512]{1,0:T(8,128)S(1)} %get-tuple-element.153), channel_id=1, source_target_pairs={{0,24},{8,16},{16,8},{24,0},{1,25},{9,17},{17,9},{25,1},{2,26},{10... | collective-permute-start | bytes 147464 | tf_op jit(solution)/shard_map/ppermute | solution.py:27

commit v5 on v4

--- a/solution.py
+++ b/solution.py
@@ -771,15 +771,19 @@
     mids[1:-1] = [swap(mids[o], "head", o) for o in range(1, head_count - 1)]
     spread[-1], *mids[1:-1] = lax.optimization_barrier((spread[-1], *mids[1:-1]))
     gathered = jnp.concatenate([*spread, moe_dec], axis=0)
-    data = exchange([gathered] * head_count, "head", 1)
+    data = [gathered, swap(gathered, "head", 1), swap(gathered, "head", 2)]
     weights = load((w_gate, w_up, w_down), gathered, "load_experts")
-    data[1], *weights = lax.optimization_barrier((data[1], *weights))
+    data[1], data[2], *weights = lax.optimization_barrier((data[1], data[2], *weights))
+    cut = gathered.shape[0] // 16 * 8
+    relayed = [swap(data[1][:cut], "head", 2), swap(data[2][cut:], "head", 1)]
+    data.append(jnp.concatenate(relayed, axis=0))
     weights = (*weights, gate_other, up_other, down_other)
     offsets = tuple(range(head_count))
     shared = (query_a, table_d, weights, scalars, chips, head_count)
     early = run_experts(data[:-1], offsets[:-1], *shared, "experts_early")
     late = run_experts(data[-1:], offsets[-1:], *shared, "experts_late")
     early = exchange(early, "head", 1)
+    late[1], early[1] = lax.optimization_barrier((late[1], early[1]))
     late = exchange(late, "head", 1)
     final = call(
         functools.partial(head_sum_kernel, head_count, share),

time: 110 us -> 102 us (0.927); the launches traced: 110 us -> 103 us
  starting transfers between devices: 47.9 us -> 40.6 us
  Pallas kernels: 28.2 us -> 30.8 us
  waiting for transfers between devices: 30.7 us -> 29.1 us
    ppermute x33 -> x34, starting transfers between devices: 47.9 us -> 40.6 us  [swap(): return lax.ppermute(value, axis, [(i, i ^ mask) for i in range(count)])]
    pallas_call x12, Pallas kernels: 28.2 us -> 30.8 us  [call(): pl.pallas_call(body, out_shape=tuple((jax.ShapeDtypeStruct(shape, dtype)...]
    ppermute x33 -> x34, waiting for transfers between devices: 30.7 us -> 29.1 us  [swap(): return lax.ppermute(value, axis, [(i, i ^ mask) for i in range(count)])]
  transfers between devices with their start and end apart: 33 -> 34, of which waited for: 16 -> 17; matrix products, arithmetic and copies ran while one was open for 2% -> 2% of each run, Pallas kernels for 18% -> 19%
where the time goes in v5:
time: 102 us; the launch traced here: 103 us
  starting transfers between devices  40.6 us (40%)
  Pallas kernels  30.8 us (30%)
  waiting for transfers between devices  29.1 us (29%)
  other arithmetic  1.18 us (1%)
    ppermute x34, starting transfers between devices, swap(): return lax.ppermute(value, axis, [(i, i ^ mask) for i in range(count)])  40.6 us
    pallas_call x12, Pallas kernels, call(): pl.pallas_call(body, out_shape=tuple((jax.ShapeDtypeStruct(shape, dtype)...  30.8 us
    ppermute x34, waiting for transfers between devices, swap(): return lax.ppermute(value, axis, [(i, i ^ mask) for i in range(count)])  29.1 us
  transfers between devices with their start and end apart: 34, of which 17 were waited for; matrix products, arithmetic and copies ran while one was open for 2% of the time, Pallas kernels for 19%

profile of v5, /device:TPU:0, one launch (start us, length us, event | category | flops | bytes accessed | tf_op | source)
XLA Modules:
  0.0 103.4 jit_solution(7826944815214335684)
XLA Ops:
  1.2 0.7 select_reduce_fusion
  2.2 2.4 %queries.1 = (bf16[64,640]{1,0:T(8,128)(2,1)S(1)}, bf16[16,512]{1,0:T(8,128)(2,1)S(1)}, f32[32,128]{1,0:T(8,128)S(1)}, bf16[80,2048]{1,0:T(8,128)(2,1)S(1)}, f32[32,2048]{1,0:T(8,128)S(1)}) custom-call(bf16[64,2048]{1,0:T(8,128)(2,1)} %pre_hbm.3, bf16[12,2048]{1,0:T(8,128)(2,1)} %dec_hbm.1, f32[1,2048]{1,0:T(1,128)} %bitcast.9, ...), custom_call_target="tpu_custom_call" | custom-call | tf_op jit(solution)/shard_map/queries/pallas_call | solution.py:55
  4.7 2.7 %collective-permute-start = (bf16[64,640]{1,0:T(8,128)(2,1)S(1)}, bf16[64,640]{1,0:T(8,128)(2,1)S(1)}, u32[]{:S(2)}, u32[]{:S(2)}) collective-permute-start(bf16[64,640]{1,0:T(8,128)(2,1)S(1)} %get-tuple-element.90), channel_id=1, source_target_pairs={{0,2},{1,3},{2,0},{3,1},{4,6},{5,7},{6,4},{7,5},{8,10},{9,11},{10,... | collective-permute-start | bytes 245768 | tf_op jit(solution)/shard_map/ppermute | solution.py:27
  7.3 2.6 %collective-permute-start.1 = (bf16[64,640]{1,0:T(8,128)(2,1)S(1)}, bf16[64,640]{1,0:T(8,128)(2,1)S(1)}, u32[]{:S(2)}, u32[]{:S(2)}) collective-permute-start(bf16[64,640]{1,0:T(8,128)(2,1)S(1)} %get-tuple-element.90), channel_id=1, source_target_pairs={{0,4},{1,5},{2,6},{3,7},{4,0},{5,1},{6,2},{7,3},{8,12},{9,13},{10,... | collective-permute-start | bytes 245768 | tf_op jit(solution)/shard_map/ppermute | solution.py:27
  9.9 3.8 %keys.1 = (bf16[2,64,512]{2,1,0:T(8,128)(2,1)}, bf16[2,12,512]{2,1,0:T(8,128)(2,1)S(1)}, bf16[64,512]{1,0:T(8,128)(2,1)S(1)}, bf16[64,512]{1,0:T(8,128)(2,1)S(1)...) custom-call(bf16[80,2048]{1,0:T(8,128)(2,1)S(1)} %get-tuple-element.87.normed, bf16[2048,512]{1,0:T(8,128)(2,1)} %key_hbm.1, ...), custom_call_target="tpu_custom_call" | custom-call | flops 335544320 | bytes 4194304 | tf_op jit(solution)/shard_map/keys/pallas_call | solution.py:55
  13.7 3.2 %collective-permute-done.1 = bf16[64,640]{1,0:T(8,128)(2,1)S(1)} collective-permute-done((bf16[64,640]{1,0:T(8,128)(2,1)S(1)}, bf16[64,640]{1,0:T(8,128)(2,1)S(1)}, u32[]{:S(2)}, u32[]{:S(2)}) %collective-permute-start.1) | collective-permute-done | bytes 81952 | tf_op jit(solution)/shard_map/ppermute | solution.py:27
  17.0 1.6 %collective-permute-done.3.query_b = bf16[256,640]{1,0:T(8,128)(2,1)S(1)} collective-permute-done((bf16[256,640]{1,0:T(8,128)(2,1)S(1)}, bf16[256,640]{1,0:T(8,128)(2,1)S(1)}, u32[]{:S(2)}, u32[]{:S(2)}) %collective-permute-start.3) | collective-permute-done | bytes 327712 | tf_op jit(solution)/shard_map/ppermute | solution.py:27
  18.7 8.0 %attention.1 = (f32[520,256]{1,0:T(8,128)S(1)}, f32[520,256]{1,0:T(8,128)S(1)}, f32[16,640]{1,0:T(8,128)S(1)}) custom-call(s32[8]{0:T(128)S(1)} %copy-done.2, s32[8]{0:T(128)S(1)} %copy-done.3, s32[13]{0:T(128)S(1)} %copy-done.1, s32[1]{0:T(128)} %bitcast.7.blk_ref, bf16[256,640]{1,0:T(8,128)(2,1)S(1)} %constant_dynamic-update-slice_fusion.query_a.refs_3_.refs_1_, ...), custom_call_target="tpu_custom_call" | custom-call | tf_op jit(solution)/shard_map/attention/pallas_call | solution.py:55
  27.2 1.5 %collective-permute-done.6.dec_other = f32[16,640]{1,0:T(8,128)S(1)} collective-permute-done((f32[16,640]{1,0:T(8,128)S(1)}, f32[16,640]{1,0:T(8,128)S(1)}, u32[]{:S(2)}, u32[]{:S(2)}) %collective-permute-start.6) | collective-permute-done | bytes 40992 | tf_op jit(solution)/shard_map/ppermute | solution.py:27
  29.3 1.7 %collective-permute-start.9 = (bf16[80,640]{1,0:T(8,128)(2,1)S(1)}, bf16[80,640]{1,0:T(8,128)(2,1)S(1)}, u32[]{:S(2)}, u32[]{:S(2)}) collective-permute-start(bf16[80,640]{1,0:T(8,128)(2,1)S(1)} %get-tuple-element.110), channel_id=1, source_target_pairs={{0,6},{1,7},{2,4},{3,5},{4,2},{5,3},{6,0},{7,1},{8,14},{9,15},{10,... | collective-permute-start | bytes 307208 | tf_op jit(solution)/shard_map/ppermute | solution.py:27
  31.0 3.2 %collective-permute-start.7 = (bf16[80,640]{1,0:T(8,128)(2,1)S(1)}, bf16[80,640]{1,0:T(8,128)(2,1)S(1)}, u32[]{:S(2)}, u32[]{:S(2)}) collective-permute-start(bf16[80,640]{1,0:T(8,128)(2,1)S(1)} %get-tuple-element.108), channel_id=1, source_target_pairs={{0,2},{1,3},{2,0},{3,1},{4,6},{5,7},{6,4},{7,5},{8,10},{9,11},{10,... | collective-permute-start | bytes 307208 | tf_op jit(solution)/shard_map/ppermute | solution.py:27
  34.1 1.5 %load_output.1.refs_4_ = bf16[512,2048]{1,0:T(8,128)(2,1)S(1)} custom-call(bf16[512,2048]{1,0:T(8,128)(2,1)} %refs_0_.2, bf16[80,640]{1,0:T(8,128)(2,1)S(1)} %get-tuple-element.107.refs_1_.refs_0_), custom_call_target="tpu_custom_call" | custom-call | bytes 4194304 | tf_op jit(solution)/shard_map/load_output/pallas_call | solution.py:55
  35.7 0.9 collective-permute-done.9.refs_3_
  36.6 1.9 %collective-permute-done.7.refs_1_ = bf16[80,640]{1,0:T(8,128)(2,1)S(1)} collective-permute-done((bf16[80,640]{1,0:T(8,128)(2,1)S(1)}, bf16[80,640]{1,0:T(8,128)(2,1)S(1)}, u32[]{:S(2)}, u32[]{:S(2)}) %collective-permute-start.7) | collective-permute-done | bytes 102432 | tf_op jit(solution)/shard_map/ppermute | solution.py:27
  38.5 4.4 %collective-permute-done.8.refs_2_ = bf16[80,640]{1,0:T(8,128)(2,1)S(1)} collective-permute-done((bf16[80,640]{1,0:T(8,128)(2,1)S(1)}, bf16[80,640]{1,0:T(8,128)(2,1)S(1)}, u32[]{:S(2)}, u32[]{:S(2)}) %collective-permute-start.8) | collective-permute-done | bytes 102432 | tf_op jit(solution)/shard_map/ppermute | solution.py:27
  42.9 0.9 project_out.1
  44.0 2.5 %collective-permute-start.13 = (bf16[24,2048]{1,0:T(8,128)(2,1)S(1)}, bf16[24,2048]{1,0:T(8,128)(2,1)S(1)}, u32[]{:S(2)}, u32[]{:S(2)}) collective-permute-start(bf16[24,2048]{1,0:T(8,128)(2,1)S(1)} %get-tuple-element.121), channel_id=1, source_target_pairs={{0,24},{8,16},{16,8},{24,0},{1,25},{9,17},{17,9},{25,1},{2,26},{10... | collective-permute-start | bytes 294920 | tf_op jit(solution)/shard_map/ppermute | solution.py:27
  47.5 3.0 %collective-permute-done.13.refs_3_ = bf16[24,2048]{1,0:T(8,128)(2,1)S(1)} collective-permute-done((bf16[24,2048]{1,0:T(8,128)(2,1)S(1)}, bf16[24,2048]{1,0:T(8,128)(2,1)S(1)}, u32[]{:S(2)}, u32[]{:S(2)}) %collective-permute-start.13) | collective-permute-done | bytes 98336 | tf_op jit(solution)/shard_map/ppermute | solution.py:27
  50.5 1.7 %collective-permute-done.11.refs_1_ = bf16[24,2048]{1,0:T(8,128)(2,1)S(1)} collective-permute-done((bf16[24,2048]{1,0:T(8,128)(2,1)S(1)}, bf16[24,2048]{1,0:T(8,128)(2,1)S(1)}, u32[]{:S(2)}, u32[]{:S(2)}) %collective-permute-start.11) | collective-permute-done | bytes 98336 | tf_op jit(solution)/shard_map/ppermute | solution.py:27
  52.2 1.0 moe_norm.1
  53.2 1.5 %collective-permute-start.15 = (bf16[16,2048]{1,0:T(8,128)(2,1)S(1)}, bf16[16,2048]{1,0:T(8,128)(2,1)S(1)}, u32[]{:S(2)}, u32[]{:S(2)}) collective-permute-start(bf16[16,2048]{1,0:T(8,128)(2,1)S(1)} %get-tuple-element.125), channel_id=1, source_target_pairs={{0,6},{1,7},{2,4},{3,5},{4,2},{5,3},{6,0},{7,1},{8,14},{9,15},{10,... | collective-permute-start | bytes 196616 | tf_op jit(solution)/shard_map/ppermute | solution.py:27
  54.7 3.0 %collective-permute-start.19 = (bf16[16,2048]{1,0:T(8,128)(2,1)S(1)}, bf16[16,2048]{1,0:T(8,128)(2,1)S(1)}, u32[]{:S(2)}, u32[]{:S(2)}) collective-permute-start(bf16[16,2048]{1,0:T(8,128)(2,1)S(1)} %get-tuple-element.125), channel_id=1, source_target_pairs={{0,4},{1,5},{2,6},{3,7},{4,0},{5,1},{6,2},{7,3},{8,12},{9,13},{10,... | collective-permute-start | bytes 196616 | tf_op jit(solution)/shard_map/ppermute | solution.py:27
  57.6 1.5 %collective-permute-start.16 = (f32[24,512]{1,0:T(8,128)S(1)}, f32[24,512]{1,0:T(8,128)S(1)}, u32[]{:S(2)}, u32[]{:S(2)}) collective-permute-start(f32[24,512]{1,0:T(8,128)S(1)} %get-tuple-element.126), channel_id=1, source_target_pairs={{0,8},{8,0},{16,24},{24,16},{1,9},{9,1},{17,25},{25,17},{2,10},{10... | collective-permute-start | bytes 147464 | tf_op jit(solution)/shard_map/ppermute | solution.py:27
  59.1 1.5 %collective-permute-start.17 = (f32[24,512]{1,0:T(8,128)S(1)}, f32[24,512]{1,0:T(8,128)S(1)}, u32[]{:S(2)}, u32[]{:S(2)}) collective-permute-start(f32[24,512]{1,0:T(8,128)S(1)} %get-tuple-element.127), channel_id=1, source_target_pairs={{0,16},{8,24},{16,0},{24,8},{1,17},{9,25},{17,1},{25,9},{2,18},{10... | collective-permute-start | bytes 147464 | tf_op jit(solution)/shard_map/ppermute | solution.py:27
  60.7 1.0 %collective-permute-done.16.refs_1_ = f32[24,512]{1,0:T(8,128)S(1)} collective-permute-done((f32[24,512]{1,0:T(8,128)S(1)}, f32[24,512]{1,0:T(8,128)S(1)}, u32[]{:S(2)}, u32[]{:S(2)}) %collective-permute-start.16) | collective-permute-done | bytes 49184 | tf_op jit(solution)/shard_map/ppermute | solution.py:27
  61.7 1.5 %collective-permute-done.17.refs_2_ = f32[24,512]{1,0:T(8,128)S(1)} collective-permute-done((f32[24,512]{1,0:T(8,128)S(1)}, f32[24,512]{1,0:T(8,128)S(1)}, u32[]{:S(2)}, u32[]{:S(2)}) %collective-permute-start.17) | collective-permute-done | bytes 49184 | tf_op jit(solution)/shard_map/ppermute | solution.py:27
  63.3 0.6 collective-permute-start.20
  63.9 1.5 %collective-permute-start.21 = (bf16[72,2048]{1,0:T(8,128)(2,1)S(1)}, bf16[72,2048]{1,0:T(8,128)(2,1)S(1)}, u32[]{:S(2)}, u32[]{:S(2)}) collective-permute-start(bf16[72,2048]{1,0:T(8,128)(2,1)S(1)} %constant_dynamic-update-slice_fusion.4.refs_3_.refs_0_), channel_id=1, source_target_pairs={{0,16},{8,24},{16,0},{24,8},{1,17},{9,25},{17,1},{25,9},{2,18},{10... | collective-permute-start | bytes 884744 | tf_op jit(solution)/shard_map/ppermute | solution.py:27
  65.3 3.0 %load_experts.1 = (bf16[2,2048,256]{2,1,0:T(8,128)(2,1)S(1)}, bf16[2,2048,256]{2,1,0:T(8,128)(2,1)S(1)}, bf16[2,256,2048]{2,1,0:T(8,128)(2,1)S(1)}) custom-call(bf16[2,2048,256]{2,1,0:T(8,128)(2,1)} %refs_0_.3, bf16[2,2048,256]{2,1,0:T(8,128)(2,1)} %refs_1_.1, bf16[2,256,2048]{2,1,0:T(8,128)(2,1)} %refs_2_.1, ...), custom_call_target="tpu_custom_call" | custom-call | bytes 12582912 | tf_op jit(solution)/shard_map/load_experts/pallas_call | solution.py:55
  68.3 1.8 %collective-permute-done.20.refs_1_ = bf16[72,2048]{1,0:T(8,128)(2,1)S(1)} collective-permute-done((bf16[72,2048]{1,0:T(8,128)(2,1)S(1)}, bf16[72,2048]{1,0:T(8,128)(2,1)S(1)}, u32[]{:S(2)}, u32[]{:S(2)}) %collective-permute-start.20) | collective-permute-done | bytes 294944 | tf_op jit(solution)/shard_map/ppermute | solution.py:27
  70.6 1.8 %collective-permute-start.23 = (bf16[40,2048]{1,0:T(8,128)(2,1)S(1)}, bf16[40,2048]{1,0:T(8,128)(2,1)S(1)}, u32[]{:S(2)}, u32[]{:S(2)}) collective-permute-start(bf16[40,2048]{1,0:T(8,128)(2,1)S(1)} %slice.7), channel_id=1, source_target_pairs={{0,8},{8,0},{16,24},{24,16},{1,9},{9,1},{17,25},{25,17},{2,10},{10... | collective-permute-start | bytes 491528 | tf_op jit(solution)/shard_map/ppermute | solution.py:27
  72.4 1.3 %collective-permute-start.22 = (bf16[32,2048]{1,0:T(8,128)(2,1)S(1)}, bf16[32,2048]{1,0:T(8,128)(2,1)S(1)}, u32[]{:S(2)}, u32[]{:S(2)}) collective-permute-start(bf16[32,2048]{1,0:T(8,128)(2,1)S(1)} %slice.6), channel_id=1, source_target_pairs={{0,16},{8,24},{16,0},{24,8},{1,17},{9,25},{17,1},{25,9},{2,18},{10... | collective-permute-start | bytes 393224 | tf_op jit(solution)/shard_map/ppermute | solution.py:27
  73.8 4.9 %experts_early.1 = (bf16[208,512]{1,0:T(8,128)(2,1)S(1)}, bf16[208,512]{1,0:T(8,128)(2,1)S(1)}, bf16[208,512]{1,0:T(8,128)(2,1)S(1)}, bf16[208,512]{1,0:T(8,128)(2,1)S(1)}) custom-call(s32[2]{0:T(128)S(1)} %pad_add_fusion.scalar_ref, bf16[72,2048]{1,0:T(8,128)(2,1)S(1)} %constant_dynamic-update-slice_fusion.4.refs_3_.refs_0_, ...), custom_call_target="tpu_custom_call" | custom-call | flops 1358954496 | bytes 12582912 | tf_op jit(solution)/shard_map/experts_early/pallas_call | solution.py:55
  78.7 0.6 collective-permute-start.24
  79.9 2.4 %collective-permute-start.26 = (bf16[208,512]{1,0:T(8,128)(2,1)S(1)}, bf16[208,512]{1,0:T(8,128)(2,1)S(1)}, u32[]{:S(2)}, u32[]{:S(2)}) collective-permute-start(bf16[208,512]{1,0:T(8,128)(2,1)S(1)} %get-tuple-element.149), channel_id=1, source_target_pairs={{0,24},{8,16},{16,8},{24,0},{1,25},{9,17},{17,9},{25,1},{2,26},{10... | collective-permute-start | bytes 638984 | tf_op jit(solution)/shard_map/ppermute | solution.py:27
  82.3 4.0 %experts_late.1 = (bf16[72,512]{1,0:T(8,128)(2,1)S(1)}, bf16[72,512]{1,0:T(8,128)(2,1)S(1)}, bf16[72,512]{1,0:T(8,128)(2,1)S(1)}, bf16[72,512]{1,0:T(8,128)(2,1)S(1)}) custom-call(s32[2]{0:T(128)S(1)} %pad_add_fusion.scalar_ref, bf16[72,2048]{1,0:T(8,128)(2,1)S(1)} %pad_maximum_fusion.refs_0_, ...), custom_call_target="tpu_custom_call" | custom-call | flops 452984832 | bytes 12582912 | tf_op jit(solution)/shard_map/experts_late/pallas_call | solution.py:55
  86.3 0.9 collective-permute-start.28
  87.2 1.2 %collective-permute-start.29 = (bf16[72,512]{1,0:T(8,128)(2,1)S(1)}, bf16[72,512]{1,0:T(8,128)(2,1)S(1)}, u32[]{:S(2)}, u32[]{:S(2)}) collective-permute-start(bf16[72,512]{1,0:T(8,128)(2,1)S(1)} %get-tuple-element.153), channel_id=1, source_target_pairs={{0,24},{8,16},{16,8},{24,0},{1,25},{9,17},{17,9},{25,1},{2,26},{10... | collective-permute-start | bytes 221192 | tf_op jit(solution)/shard_map/ppermute | solution.py:27
  88.4 1.5 %collective-permute-start.27 = (bf16[72,512]{1,0:T(8,128)(2,1)S(1)}, bf16[72,512]{1,0:T(8,128)(2,1)S(1)}, u32[]{:S(2)}, u32[]{:S(2)}) collective-permute-start(bf16[72,512]{1,0:T(8,128)(2,1)S(1)} %get-tuple-element.151), channel_id=1, source_target_pairs={{0,8},{8,0},{16,24},{24,16},{1,9},{9,1},{17,25},{25,17},{2,10},{10... | collective-permute-start | bytes 221192 | tf_op jit(solution)/shard_map/ppermute | solution.py:27
  89.9 0.9 collective-permute-done.28.refs_6_
  90.7 1.7 %collective-permute-done.29.refs_7_ = bf16[72,512]{1,0:T(8,128)(2,1)S(1)} collective-permute-done((bf16[72,512]{1,0:T(8,128)(2,1)S(1)}, bf16[72,512]{1,0:T(8,128)(2,1)S(1)}, u32[]{:S(2)}, u32[]{:S(2)}) %collective-permute-start.29) | collective-permute-done | bytes 73760 | tf_op jit(solution)/shard_map/ppermute | solution.py:27
  93.2 0.7 collective-permute-start.31
  93.9 1.8 %collective-permute-start.32 = (bf16[80,512]{1,0:T(8,128)(2,1)S(1)}, bf16[80,512]{1,0:T(8,128)(2,1)S(1)}, u32[]{:S(2)}, u32[]{:S(2)}) collective-permute-start(bf16[80,512]{1,0:T(8,128)(2,1)S(1)} %get-tuple-element.162), channel_id=1, source_target_pairs={{0,4},{1,5},{2,6},{3,7},{4,0},{5,1},{6,2},{7,3},{8,12},{9,13},{10,... | collective-permute-start | bytes 245768 | tf_op jit(solution)/shard_map/ppermute | solution.py:27
  95.7 1.9 %collective-permute-start.33 = (bf16[80,512]{1,0:T(8,128)(2,1)S(1)}, bf16[80,512]{1,0:T(8,128)(2,1)S(1)}, u32[]{:S(2)}, u32[]{:S(2)}) collective-permute-start(bf16[80,512]{1,0:T(8,128)(2,1)S(1)} %get-tuple-element.163), channel_id=1, source_target_pairs={{0,6},{1,7},{2,4},{3,5},{4,2},{5,3},{6,0},{7,1},{8,14},{9,15},{10,... | collective-permute-start | bytes 245768 | tf_op jit(solution)/shard_map/ppermute | solution.py:27
  97.7 1.5 %collective-permute-start.30 = (f32[24,512]{1,0:T(8,128)S(1)}, f32[24,512]{1,0:T(8,128)S(1)}, u32[]{:S(2)}, u32[]{:S(2)}) collective-permute-start(f32[24,512]{1,0:T(8,128)S(1)} %get-tuple-element.159), channel_id=1, source_target_pairs={{0,24},{8,16},{16,8},{24,0},{1,25},{9,17},{17,9},{25,1},{2,26},{10... | collective-permute-start | bytes 147464 | tf_op jit(solution)/shard_map/ppermute | solution.py:27
  99.1 0.6 copy.25
  99.8 2.9 %collective-permute-done.30.refs_3_ = f32[24,512]{1,0:T(8,128)S(1)} collective-permute-done((f32[24,512]{1,0:T(8,128)S(1)}, f32[24,512]{1,0:T(8,128)S(1)}, u32[]{:S(2)}, u32[]{:S(2)}) %collective-permute-start.30) | collective-permute-done | bytes 49184 | tf_op jit(solution)/shard_map/ppermute | solution.py:27
  102.7 0.7 final.1
  (62 shorter events, 5.4 us)
Async XLA Ops:
  0.6 18.0 %collective-permute-start.4 = (bf16[2,2048,256]{2,1,0:T(8,128)(2,1)}, bf16[2,2048,256]{2,1,0:T(8,128)(2,1)S(1)}, u32[]{:S(2)}, u32[]{:S(2)}) collective-permute-start(bf16[2,2048,256]{2,1,0:T(8,128)(2,1)} %refs_0_.3), channel_id=1, source_target_pairs={{0,1},{1,0},{2,3},{3,2},{4,5},{5,4},{6,7},{7,6},{8,9},{9,8},{10,11... | collective-permute-start | bytes 6291464 | tf_op jit(solution)/shard_map/ppermute | solution.py:27
  4.7 9.0 %collective-permute-start = (bf16[64,640]{1,0:T(8,128)(2,1)S(1)}, bf16[64,640]{1,0:T(8,128)(2,1)S(1)}, u32[]{:S(2)}, u32[]{:S(2)}) collective-permute-start(bf16[64,640]{1,0:T(8,128)(2,1)S(1)} %get-tuple-element.90), channel_id=1, source_target_pairs={{0,2},{1,3},{2,0},{3,1},{4,6},{5,7},{6,4},{7,5},{8,10},{9,11},{10,... | collective-permute-start | bytes 245768 | tf_op jit(solution)/shard_map/ppermute | solution.py:27
  7.3 9.5 %collective-permute-start.1 = (bf16[64,640]{1,0:T(8,128)(2,1)S(1)}, bf16[64,640]{1,0:T(8,128)(2,1)S(1)}, u32[]{:S(2)}, u32[]{:S(2)}) collective-permute-start(bf16[64,640]{1,0:T(8,128)(2,1)S(1)} %get-tuple-element.90), channel_id=1, source_target_pairs={{0,4},{1,5},{2,6},{3,7},{4,0},{5,1},{6,2},{7,3},{8,12},{9,13},{10,... | collective-permute-start | bytes 245768 | tf_op jit(solution)/shard_map/ppermute | solution.py:27
  9.9 7.0 %collective-permute-start.2 = (bf16[64,640]{1,0:T(8,128)(2,1)S(1)}, bf16[64,640]{1,0:T(8,128)(2,1)S(1)}, u32[]{:S(2)}, u32[]{:S(2)}) collective-permute-start(bf16[64,640]{1,0:T(8,128)(2,1)S(1)} %get-tuple-element.90), channel_id=1, source_target_pairs={{0,6},{1,7},{2,4},{3,5},{4,2},{5,3},{6,0},{7,1},{8,14},{9,15},{10,... | collective-permute-start | bytes 245768 | tf_op jit(solution)/shard_map/ppermute | solution.py:27
  9.9 8.7 %copy-start.1 = (s32[13]{0:T(128)S(1)}, s32[13]{0:T(128)}, u32[]{:S(2)}) copy-start(s32[13]{0:T(128)} %lens_ref.1) | copy-start | bytes 160
  9.9 8.7 %copy-start.2 = (s32[8]{0:T(128)S(1)}, s32[8]{0:T(128)}, u32[]{:S(2)}) copy-start(s32[8]{0:T(128)} %owner_ref.1) | copy-start | bytes 100
  9.9 8.7 %copy-start.3 = (s32[8]{0:T(128)S(1)}, s32[8]{0:T(128)}, u32[]{:S(2)}) copy-start(s32[8]{0:T(128)} %slot_ref.1) | copy-start | bytes 100
  16.9 1.7 %collective-permute-start.3 = (bf16[256,640]{1,0:T(8,128)(2,1)S(1)}, bf16[256,640]{1,0:T(8,128)(2,1)S(1)}, u32[]{:S(2)}, u32[]{:S(2)}) collective-permute-start(bf16[256,640]{1,0:T(8,128)(2,1)S(1)} %constant_dynamic-update-slice_fusion.query_a.refs_3_.refs_1_), channel_id=1, source_target_pairs={{0,1},{1,0},{2,3},{3,2},{4,5},{5,4},{6,7},{7,6},{8,9},{9,8},{10,11... | collective-permute-start | bytes 983048 | tf_op jit(solution)/shard_map/ppermute | solution.py:27
  26.7 2.0 %collective-permute-start.5 = (f32[520,256]{1,0:T(8,128)S(1)}, f32[520,256]{1,0:T(8,128)S(1)}, u32[]{:S(2)}, u32[]{:S(2)}) collective-permute-start(f32[520,256]{1,0:T(8,128)S(1)} %get-tuple-element.101), channel_id=1, source_target_pairs={{0,1},{1,0},{2,3},{3,2},{4,5},{5,4},{6,7},{7,6},{8,9},{9,8},{10,11... | collective-permute-start | bytes 1597448 | tf_op jit(solution)/shard_map/ppermute | solution.py:27
  26.7 2.0 %collective-permute-start.6 = (f32[16,640]{1,0:T(8,128)S(1)}, f32[16,640]{1,0:T(8,128)S(1)}, u32[]{:S(2)}, u32[]{:S(2)}) collective-permute-start(f32[16,640]{1,0:T(8,128)S(1)} %get-tuple-element.102.dec_mine), channel_id=1, source_target_pairs={{0,1},{1,0},{2,3},{3,2},{4,5},{5,4},{6,7},{7,6},{8,9},{9,8},{10,11... | collective-permute-start | bytes 122888 | tf_op jit(solution)/shard_map/ppermute | solution.py:27
  29.1 7.5 %collective-permute-start.10 = (bf16[2,2048,256]{2,1,0:T(8,128)(2,1)}, bf16[2,2048,256]{2,1,0:T(8,128)(2,1)}, u32[]{:S(2)}, u32[]{:S(2)}) collective-permute-start(bf16[2,2048,256]{2,1,0:T(8,128)(2,1)} %refs_1_.1), channel_id=1, source_target_pairs={{0,1},{1,0},{2,3},{3,2},{4,5},{5,4},{6,7},{7,6},{8,9},{9,8},{10,11... | collective-permute-start | bytes 6291464 | tf_op jit(solution)/shard_map/ppermute | solution.py:27
  29.3 7.2 %collective-permute-start.9 = (bf16[80,640]{1,0:T(8,128)(2,1)S(1)}, bf16[80,640]{1,0:T(8,128)(2,1)S(1)}, u32[]{:S(2)}, u32[]{:S(2)}) collective-permute-start(bf16[80,640]{1,0:T(8,128)(2,1)S(1)} %get-tuple-element.110), channel_id=1, source_target_pairs={{0,6},{1,7},{2,4},{3,5},{4,2},{5,3},{6,0},{7,1},{8,14},{9,15},{10,... | collective-permute-start | bytes 307208 | tf_op jit(solution)/shard_map/ppermute | solution.py:27
  31.0 7.5 %collective-permute-start.7 = (bf16[80,640]{1,0:T(8,128)(2,1)S(1)}, bf16[80,640]{1,0:T(8,128)(2,1)S(1)}, u32[]{:S(2)}, u32[]{:S(2)}) collective-permute-start(bf16[80,640]{1,0:T(8,128)(2,1)S(1)} %get-tuple-element.108), channel_id=1, source_target_pairs={{0,2},{1,3},{2,0},{3,1},{4,6},{5,7},{6,4},{7,5},{8,10},{9,11},{10,... | collective-permute-start | bytes 307208 | tf_op jit(solution)/shard_map/ppermute | solution.py:27
  34.1 8.7 %collective-permute-start.8 = (bf16[80,640]{1,0:T(8,128)(2,1)S(1)}, bf16[80,640]{1,0:T(8,128)(2,1)S(1)}, u32[]{:S(2)}, u32[]{:S(2)}) collective-permute-start(bf16[80,640]{1,0:T(8,128)(2,1)S(1)} %get-tuple-element.109), channel_id=1, source_target_pairs={{0,4},{1,5},{2,6},{3,7},{4,0},{5,1},{6,2},{7,3},{8,12},{9,13},{10,... | collective-permute-start | bytes 307208 | tf_op jit(solution)/shard_map/ppermute | solution.py:27
  35.7 8.1 %copy-start.4 = (bf16[2,256,2048]{2,1,0:T(8,128)(2,1)S(1)}, bf16[2,256,2048]{2,1,0:T(8,128)(2,1)}, u32[]{:S(2)}) copy-start(bf16[2,256,2048]{2,1,0:T(8,128)(2,1)} %refs_2_.1) | copy-start | bytes 6291460
  35.7 16.5 %copy-start = (f32[2048]{0:T(1024)S(1)}, f32[2048]{0:T(1024)}, u32[]{:S(2)}) copy-start(f32[2048]{0:T(1024)} %param.32) | copy-start | bytes 24580
  43.8 6.7 %collective-permute-start.14 = (bf16[2,256,2048]{2,1,0:T(8,128)(2,1)S(1)}, bf16[2,256,2048]{2,1,0:T(8,128)(2,1)S(1)}, u32[]{:S(2)}, u32[]{:S(2)}) collective-permute-start(bf16[2,256,2048]{2,1,0:T(8,128)(2,1)S(1)} %copy-done.4), channel_id=1, source_target_pairs={{0,1},{1,0},{2,3},{3,2},{4,5},{5,4},{6,7},{7,6},{8,9},{9,8},{10,11... | collective-permute-start | bytes 6291464 | tf_op jit(solution)/shard_map/ppermute | solution.py:27
  44.0 6.5 %collective-permute-start.13 = (bf16[24,2048]{1,0:T(8,128)(2,1)S(1)}, bf16[24,2048]{1,0:T(8,128)(2,1)S(1)}, u32[]{:S(2)}, u32[]{:S(2)}) collective-permute-start(bf16[24,2048]{1,0:T(8,128)(2,1)S(1)} %get-tuple-element.121), channel_id=1, source_target_pairs={{0,24},{8,16},{16,8},{24,0},{1,25},{9,17},{17,9},{25,1},{2,26},{10... | collective-permute-start | bytes 294920 | tf_op jit(solution)/shard_map/ppermute | solution.py:27
  46.4 5.7 %collective-permute-start.11 = (bf16[24,2048]{1,0:T(8,128)(2,1)S(1)}, bf16[24,2048]{1,0:T(8,128)(2,1)S(1)}, u32[]{:S(2)}, u32[]{:S(2)}) collective-permute-start(bf16[24,2048]{1,0:T(8,128)(2,1)S(1)} %get-tuple-element.119), channel_id=1, source_target_pairs={{0,8},{8,0},{16,24},{24,16},{1,9},{9,1},{17,25},{25,17},{2,10},{10... | collective-permute-start | bytes 294920 | tf_op jit(solution)/shard_map/ppermute | solution.py:27
  47.0 5.2 %collective-permute-start.12 = (bf16[24,2048]{1,0:T(8,128)(2,1)S(1)}, bf16[24,2048]{1,0:T(8,128)(2,1)S(1)}, u32[]{:S(2)}, u32[]{:S(2)}) collective-permute-start(bf16[24,2048]{1,0:T(8,128)(2,1)S(1)} %get-tuple-element.120), channel_id=1, source_target_pairs={{0,16},{8,24},{16,0},{24,8},{1,17},{9,25},{17,1},{25,9},{2,18},{10... | collective-permute-start | bytes 294920 | tf_op jit(solution)/shard_map/ppermute | solution.py:27
  53.2 10.1 %collective-permute-start.15 = (bf16[16,2048]{1,0:T(8,128)(2,1)S(1)}, bf16[16,2048]{1,0:T(8,128)(2,1)S(1)}, u32[]{:S(2)}, u32[]{:S(2)}) collective-permute-start(bf16[16,2048]{1,0:T(8,128)(2,1)S(1)} %get-tuple-element.125), channel_id=1, source_target_pairs={{0,6},{1,7},{2,4},{3,5},{4,2},{5,3},{6,0},{7,1},{8,14},{9,15},{10,... | collective-permute-start | bytes 196616 | tf_op jit(solution)/shard_map/ppermute | solution.py:27
  54.7 6.0 %collective-permute-start.18 = (bf16[16,2048]{1,0:T(8,128)(2,1)S(1)}, bf16[16,2048]{1,0:T(8,128)(2,1)S(1)}, u32[]{:S(2)}, u32[]{:S(2)}) collective-permute-start(bf16[16,2048]{1,0:T(8,128)(2,1)S(1)} %get-tuple-element.125), channel_id=1, source_target_pairs={{0,2},{1,3},{2,0},{3,1},{4,6},{5,7},{6,4},{7,5},{8,10},{9,11},{10,... | collective-permute-start | bytes 196616 | tf_op jit(solution)/shard_map/ppermute | solution.py:27
  54.7 8.6 %collective-permute-start.19 = (bf16[16,2048]{1,0:T(8,128)(2,1)S(1)}, bf16[16,2048]{1,0:T(8,128)(2,1)S(1)}, u32[]{:S(2)}, u32[]{:S(2)}) collective-permute-start(bf16[16,2048]{1,0:T(8,128)(2,1)S(1)} %get-tuple-element.125), channel_id=1, source_target_pairs={{0,4},{1,5},{2,6},{3,7},{4,0},{5,1},{6,2},{7,3},{8,12},{9,13},{10,... | collective-permute-start | bytes 196616 | tf_op jit(solution)/shard_map/ppermute | solution.py:27
  57.6 4.1 %collective-permute-start.16 = (f32[24,512]{1,0:T(8,128)S(1)}, f32[24,512]{1,0:T(8,128)S(1)}, u32[]{:S(2)}, u32[]{:S(2)}) collective-permute-start(f32[24,512]{1,0:T(8,128)S(1)} %get-tuple-element.126), channel_id=1, source_target_pairs={{0,8},{8,0},{16,24},{24,16},{1,9},{9,1},{17,25},{25,17},{2,10},{10... | collective-permute-start | bytes 147464 | tf_op jit(solution)/shard_map/ppermute | solution.py:27
  59.1 4.1 %collective-permute-start.17 = (f32[24,512]{1,0:T(8,128)S(1)}, f32[24,512]{1,0:T(8,128)S(1)}, u32[]{:S(2)}, u32[]{:S(2)}) collective-permute-start(f32[24,512]{1,0:T(8,128)S(1)} %get-tuple-element.127), channel_id=1, source_target_pairs={{0,16},{8,24},{16,0},{24,8},{1,17},{9,25},{17,1},{25,9},{2,18},{10... | collective-permute-start | bytes 147464 | tf_op jit(solution)/shard_map/ppermute | solution.py:27
  63.3 6.8 %collective-permute-start.20 = (bf16[72,2048]{1,0:T(8,128)(2,1)S(1)}, bf16[72,2048]{1,0:T(8,128)(2,1)S(1)}, u32[]{:S(2)}, u32[]{:S(2)}) collective-permute-start(bf16[72,2048]{1,0:T(8,128)(2,1)S(1)} %constant_dynamic-update-slice_fusion.4.refs_3_.refs_0_), channel_id=1, source_target_pairs={{0,8},{8,0},{16,24},{24,16},{1,9},{9,1},{17,25},{25,17},{2,10},{10... | collective-permute-start | bytes 884744 | tf_op jit(solution)/shard_map/ppermute | solution.py:27
  63.9 6.7 %collective-permute-start.21 = (bf16[72,2048]{1,0:T(8,128)(2,1)S(1)}, bf16[72,2048]{1,0:T(8,128)(2,1)S(1)}, u32[]{:S(2)}, u32[]{:S(2)}) collective-permute-start(bf16[72,2048]{1,0:T(8,128)(2,1)S(1)} %constant_dynamic-update-slice_fusion.4.refs_3_.refs_0_), channel_id=1, source_target_pairs={{0,16},{8,24},{16,0},{24,8},{1,17},{9,25},{17,1},{25,9},{2,18},{10... | collective-permute-start | bytes 884744 | tf_op jit(solution)/shard_map/ppermute | solution.py:27
  70.6 11.7 %collective-permute-start.23 = (bf16[40,2048]{1,0:T(8,128)(2,1)S(1)}, bf16[40,2048]{1,0:T(8,128)(2,1)S(1)}, u32[]{:S(2)}, u32[]{:S(2)}) collective-permute-start(bf16[40,2048]{1,0:T(8,128)(2,1)S(1)} %slice.7), channel_id=1, source_target_pairs={{0,8},{8,0},{16,24},{24,16},{1,9},{9,1},{17,25},{25,17},{2,10},{10... | collective-permute-start | bytes 491528 | tf_op jit(solution)/shard_map/ppermute | solution.py:27
  72.4 9.9 %collective-permute-start.22 = (bf16[32,2048]{1,0:T(8,128)(2,1)S(1)}, bf16[32,2048]{1,0:T(8,128)(2,1)S(1)}, u32[]{:S(2)}, u32[]{:S(2)}) collective-permute-start(bf16[32,2048]{1,0:T(8,128)(2,1)S(1)} %slice.6), channel_id=1, source_target_pairs={{0,16},{8,24},{16,0},{24,8},{1,17},{9,25},{17,1},{25,9},{2,18},{10... | collective-permute-start | bytes 393224 | tf_op jit(solution)/shard_map/ppermute | solution.py:27
  78.7 9.7 %collective-permute-start.24 = (bf16[208,512]{1,0:T(8,128)(2,1)S(1)}, bf16[208,512]{1,0:T(8,128)(2,1)S(1)}, u32[]{:S(2)}, u32[]{:S(2)}) collective-permute-start(bf16[208,512]{1,0:T(8,128)(2,1)S(1)} %get-tuple-element.146), channel_id=1, source_target_pairs={{0,8},{8,0},{16,24},{24,16},{1,9},{9,1},{17,25},{25,17},{2,10},{10... | collective-permute-start | bytes 638984 | tf_op jit(solution)/shard_map/ppermute | solution.py:27
  79.3 10.5 %collective-permute-start.25 = (bf16[208,512]{1,0:T(8,128)(2,1)S(1)}, bf16[208,512]{1,0:T(8,128)(2,1)S(1)}, u32[]{:S(2)}, u32[]{:S(2)}) collective-permute-start(bf16[208,512]{1,0:T(8,128)(2,1)S(1)} %get-tuple-element.148), channel_id=1, source_target_pairs={{0,16},{8,24},{16,0},{24,8},{1,17},{9,25},{17,1},{25,9},{2,18},{10... | collective-permute-start | bytes 638984 | tf_op jit(solution)/shard_map/ppermute | solution.py:27
  79.9 10.0 %collective-permute-start.26 = (bf16[208,512]{1,0:T(8,128)(2,1)S(1)}, bf16[208,512]{1,0:T(8,128)(2,1)S(1)}, u32[]{:S(2)}, u32[]{:S(2)}) collective-permute-start(bf16[208,512]{1,0:T(8,128)(2,1)S(1)} %get-tuple-element.149), channel_id=1, source_target_pairs={{0,24},{8,16},{16,8},{24,0},{1,25},{9,17},{17,9},{25,1},{2,26},{10... | collective-permute-start | bytes 638984 | tf_op jit(solution)/shard_map/ppermute | solution.py:27
  86.3 4.4 %collective-permute-start.28 = (bf16[72,512]{1,0:T(8,128)(2,1)S(1)}, bf16[72,512]{1,0:T(8,128)(2,1)S(1)}, u32[]{:S(2)}, u32[]{:S(2)}) collective-permute-start(bf16[72,512]{1,0:T(8,128)(2,1)S(1)} %get-tuple-element.152), channel_id=1, source_target_pairs={{0,16},{8,24},{16,0},{24,8},{1,17},{9,25},{17,1},{25,9},{2,18},{10... | collective-permute-start | bytes 221192 | tf_op jit(solution)/shard_map/ppermute | solution.py:27
  87.2 5.3 %collective-permute-start.29 = (bf16[72,512]{1,0:T(8,128)(2,1)S(1)}, bf16[72,512]{1,0:T(8,128)(2,1)S(1)}, u32[]{:S(2)}, u32[]{:S(2)}) collective-permute-start(bf16[72,512]{1,0:T(8,128)(2,1)S(1)} %get-tuple-element.153), channel_id=1, source_target_pairs={{0,24},{8,16},{16,8},{24,0},{1,25},{9,17},{17,9},{25,1},{2,26},{10... | collective-permute-start | bytes 221192 | tf_op jit(solution)/shard_map/ppermute | solution.py:27
  88.4 4.6 %collective-permute-start.27 = (bf16[72,512]{1,0:T(8,128)(2,1)S(1)}, bf16[72,512]{1,0:T(8,128)(2,1)S(1)}, u32[]{:S(2)}, u32[]{:S(2)}) collective-permute-start(bf16[72,512]{1,0:T(8,128)(2,1)S(1)} %get-tuple-element.151), channel_id=1, source_target_pairs={{0,8},{8,0},{16,24},{24,16},{1,9},{9,1},{17,25},{25,17},{2,10},{10... | collective-permute-start | bytes 221192 | tf_op jit(solution)/shard_map/ppermute | solution.py:27
  93.2 9.4 %collective-permute-start.31 = (bf16[80,512]{1,0:T(8,128)(2,1)S(1)}, bf16[80,512]{1,0:T(8,128)(2,1)S(1)}, u32[]{:S(2)}, u32[]{:S(2)}) collective-permute-start(bf16[80,512]{1,0:T(8,128)(2,1)S(1)} %get-tuple-element.161), channel_id=1, source_target_pairs={{0,2},{1,3},{2,0},{3,1},{4,6},{5,7},{6,4},{7,5},{8,10},{9,11},{10,... | collective-permute-start | bytes 245768 | tf_op jit(solution)/shard_map/ppermute | solution.py:27
  93.9 8.7 %collective-permute-start.32 = (bf16[80,512]{1,0:T(8,128)(2,1)S(1)}, bf16[80,512]{1,0:T(8,128)(2,1)S(1)}, u32[]{:S(2)}, u32[]{:S(2)}) collective-permute-start(bf16[80,512]{1,0:T(8,128)(2,1)S(1)} %get-tuple-element.162), channel_id=1, source_target_pairs={{0,4},{1,5},{2,6},{3,7},{4,0},{5,1},{6,2},{7,3},{8,12},{9,13},{10,... | collective-permute-start | bytes 245768 | tf_op jit(solution)/shard_map/ppermute | solution.py:27
  95.7 6.9 %collective-permute-start.33 = (bf16[80,512]{1,0:T(8,128)(2,1)S(1)}, bf16[80,512]{1,0:T(8,128)(2,1)S(1)}, u32[]{:S(2)}, u32[]{:S(2)}) collective-permute-start(bf16[80,512]{1,0:T(8,128)(2,1)S(1)} %get-tuple-element.163), channel_id=1, source_target_pairs={{0,6},{1,7},{2,4},{3,5},{4,2},{5,3},{6,0},{7,1},{8,14},{9,15},{10,... | collective-permute-start | bytes 245768 | tf_op jit(solution)/shard_map/ppermute | solution.py:27
  97.7 5.0 %collective-permute-start.30 = (f32[24,512]{1,0:T(8,128)S(1)}, f32[24,512]{1,0:T(8,128)S(1)}, u32[]{:S(2)}, u32[]{:S(2)}) collective-permute-start(f32[24,512]{1,0:T(8,128)S(1)} %get-tuple-element.159), channel_id=1, source_target_pairs={{0,24},{8,16},{16,8},{24,0},{1,25},{9,17},{17,9},{25,1},{2,26},{10... | collective-permute-start | bytes 147464 | tf_op jit(solution)/shard_map/ppermute | solution.py:27

commit v6 on v5

--- a/solution.py
+++ b/solution.py
@@ -193,8 +193,11 @@
         )
 
     for index in range(blocks):
-        for copy in copies(index):
-            copy.start()
+
+        @pl.when(owner_ref[index] < REQS)
+        def _():
+            for copy in copies(index):
+                copy.start()
 
     for query, turn_ref in ((query_a, turn_a), (query_b, turn_b)):
         for row in range(0, half, tile):
@@ -230,9 +233,13 @@
 
     @pl.loop(0, blocks)
     def _(index):
-        for copy in copies(index):
-            copy.wait()
         owner = owner_ref[index]
+
+        @pl.when(owner < REQS)
+        def _():
+            for copy in copies(index):
+                copy.wait()
+
         length = lens_ref[jnp.minimum(owner, REQS - 1)]
         count = jnp.clip(length - slot_ref[index] * block_len, 0, block_len)
 

time: 102 us -> 104 us (1.020); the launches traced: 103 us -> 103 us
  Pallas kernels: 30.8 us -> 33.6 us
  waiting for transfers between devices: 29.1 us -> 27.1 us
  starting transfers between devices: 40.6 us -> 39.5 us
    pallas_call x12, Pallas kernels: 30.8 us -> 33.6 us  [call(): pl.pallas_call(body, out_shape=tuple((jax.ShapeDtypeStruct(shape, dtype)...]
    ppermute x34, waiting for transfers between devices: 29.1 us -> 27.1 us  [swap(): return lax.ppermute(value, axis, [(i, i ^ mask) for i in range(count)])]
    ppermute x34, starting transfers between devices: 40.6 us -> 39.5 us  [swap(): return lax.ppermute(value, axis, [(i, i ^ mask) for i in range(count)])]
  transfers between devices with their start and end apart: 34 -> 34, of which waited for: 17 -> 18; matrix products, arithmetic and copies ran while one was open for 2% -> 2% of each run, Pallas kernels for 19% -> 19%
where the time goes in v6:
time: 104 us; the launch traced here: 103 us
  starting transfers between devices  39.5 us (38%)
  Pallas kernels  33.6 us (32%)
  waiting for transfers between devices  27.1 us (26%)
  other arithmetic  1.18 us (1%)
    ppermute x34, starting transfers between devices, swap(): return lax.ppermute(value, axis, [(i, i ^ mask) for i in range(count)])  39.5 us
    pallas_call x12, Pallas kernels, call(): pl.pallas_call(body, out_shape=tuple((jax.ShapeDtypeStruct(shape, dtype)...  33.6 us
    ppermute x34, waiting for transfers between devices, swap(): return lax.ppermute(value, axis, [(i, i ^ mask) for i in range(count)])  27.1 us
  transfers between devices with their start and end apart: 34, of which 18 were waited for; matrix products, arithmetic and copies ran while one was open for 2% of the time, Pallas kernels for 19%

profile of v6, /device:TPU:0, one launch (start us, length us, event | category | flops | bytes accessed | tf_op | source)
XLA Modules:
  0.0 103.1 jit_solution(11553849939807157644)
XLA Ops:
  1.2 0.7 select_reduce_fusion
  2.2 2.4 %queries.1 = (bf16[64,640]{1,0:T(8,128)(2,1)S(1)}, bf16[16,512]{1,0:T(8,128)(2,1)S(1)}, f32[32,128]{1,0:T(8,128)S(1)}, bf16[80,2048]{1,0:T(8,128)(2,1)S(1)}, f32[32,2048]{1,0:T(8,128)S(1)}) custom-call(bf16[64,2048]{1,0:T(8,128)(2,1)} %pre_hbm.3, bf16[12,2048]{1,0:T(8,128)(2,1)} %dec_hbm.1, f32[1,2048]{1,0:T(1,128)} %bitcast.9, ...), custom_call_target="tpu_custom_call" | custom-call | tf_op jit(solution)/shard_map/queries/pallas_call | solution.py:55
  4.7 2.7 %collective-permute-start = (bf16[64,640]{1,0:T(8,128)(2,1)S(1)}, bf16[64,640]{1,0:T(8,128)(2,1)S(1)}, u32[]{:S(2)}, u32[]{:S(2)}) collective-permute-start(bf16[64,640]{1,0:T(8,128)(2,1)S(1)} %get-tuple-element.90), channel_id=1, source_target_pairs={{0,2},{1,3},{2,0},{3,1},{4,6},{5,7},{6,4},{7,5},{8,10},{9,11},{10,... | collective-permute-start | bytes 245768 | tf_op jit(solution)/shard_map/ppermute | solution.py:27
  7.3 2.6 %collective-permute-start.1 = (bf16[64,640]{1,0:T(8,128)(2,1)S(1)}, bf16[64,640]{1,0:T(8,128)(2,1)S(1)}, u32[]{:S(2)}, u32[]{:S(2)}) collective-permute-start(bf16[64,640]{1,0:T(8,128)(2,1)S(1)} %get-tuple-element.90), channel_id=1, source_target_pairs={{0,4},{1,5},{2,6},{3,7},{4,0},{5,1},{6,2},{7,3},{8,12},{9,13},{10,... | collective-permute-start | bytes 245768 | tf_op jit(solution)/shard_map/ppermute | solution.py:27
  9.9 3.8 %keys.1 = (bf16[2,64,512]{2,1,0:T(8,128)(2,1)}, bf16[2,12,512]{2,1,0:T(8,128)(2,1)S(1)}, bf16[64,512]{1,0:T(8,128)(2,1)S(1)}, bf16[64,512]{1,0:T(8,128)(2,1)S(1)...) custom-call(bf16[80,2048]{1,0:T(8,128)(2,1)S(1)} %get-tuple-element.87.normed, bf16[2048,512]{1,0:T(8,128)(2,1)} %key_hbm.1, ...), custom_call_target="tpu_custom_call" | custom-call | flops 335544320 | bytes 4194304 | tf_op jit(solution)/shard_map/keys/pallas_call | solution.py:55
  13.7 3.2 %collective-permute-done.1 = bf16[64,640]{1,0:T(8,128)(2,1)S(1)} collective-permute-done((bf16[64,640]{1,0:T(8,128)(2,1)S(1)}, bf16[64,640]{1,0:T(8,128)(2,1)S(1)}, u32[]{:S(2)}, u32[]{:S(2)}) %collective-permute-start.1) | collective-permute-done | bytes 81952 | tf_op jit(solution)/shard_map/ppermute | solution.py:27
  17.0 1.6 %collective-permute-done.3.query_b = bf16[256,640]{1,0:T(8,128)(2,1)S(1)} collective-permute-done((bf16[256,640]{1,0:T(8,128)(2,1)S(1)}, bf16[256,640]{1,0:T(8,128)(2,1)S(1)}, u32[]{:S(2)}, u32[]{:S(2)}) %collective-permute-start.3) | collective-permute-done | bytes 327712 | tf_op jit(solution)/shard_map/ppermute | solution.py:27
  18.7 10.8 %attention.1 = (f32[520,256]{1,0:T(8,128)S(1)}, f32[520,256]{1,0:T(8,128)S(1)}, f32[16,640]{1,0:T(8,128)S(1)}) custom-call(s32[8]{0:T(128)S(1)} %copy-done.2, s32[8]{0:T(128)S(1)} %copy-done.3, s32[13]{0:T(128)S(1)} %copy-done.1, s32[1]{0:T(128)} %bitcast.7.blk_ref, bf16[256,640]{1,0:T(8,128)(2,1)S(1)} %constant_dynamic-update-slice_fusion.query_a.refs_3_.refs_1_, ...), custom_call_target="tpu_custom_call" | custom-call | tf_op jit(solution)/shard_map/attention/pallas_call | solution.py:55
  30.0 1.5 %collective-permute-done.6.dec_other = f32[16,640]{1,0:T(8,128)S(1)} collective-permute-done((f32[16,640]{1,0:T(8,128)S(1)}, f32[16,640]{1,0:T(8,128)S(1)}, u32[]{:S(2)}, u32[]{:S(2)}) %collective-permute-start.6) | collective-permute-done | bytes 40992 | tf_op jit(solution)/shard_map/ppermute | solution.py:27
  32.3 0.8 collective-permute-start.7
  33.1 3.4 %collective-permute-start.8 = (bf16[80,640]{1,0:T(8,128)(2,1)S(1)}, bf16[80,640]{1,0:T(8,128)(2,1)S(1)}, u32[]{:S(2)}, u32[]{:S(2)}) collective-permute-start(bf16[80,640]{1,0:T(8,128)(2,1)S(1)} %get-tuple-element.109), channel_id=1, source_target_pairs={{0,4},{1,5},{2,6},{3,7},{4,0},{5,1},{6,2},{7,3},{8,12},{9,13},{10,... | collective-permute-start | bytes 307208 | tf_op jit(solution)/shard_map/ppermute | solution.py:27
  36.5 1.5 %load_output.1.refs_4_ = bf16[512,2048]{1,0:T(8,128)(2,1)S(1)} custom-call(bf16[512,2048]{1,0:T(8,128)(2,1)} %refs_0_.2, bf16[80,640]{1,0:T(8,128)(2,1)S(1)} %get-tuple-element.107.refs_1_.refs_0_), custom_call_target="tpu_custom_call" | custom-call | bytes 4194304 | tf_op jit(solution)/shard_map/load_output/pallas_call | solution.py:55
  38.1 1.6 %collective-permute-done.9.refs_3_ = bf16[80,640]{1,0:T(8,128)(2,1)S(1)} collective-permute-done((bf16[80,640]{1,0:T(8,128)(2,1)S(1)}, bf16[80,640]{1,0:T(8,128)(2,1)S(1)}, u32[]{:S(2)}, u32[]{:S(2)}) %collective-permute-start.9) | collective-permute-done | bytes 102432 | tf_op jit(solution)/shard_map/ppermute | solution.py:27
  39.7 1.7 %collective-permute-done.7.refs_1_ = bf16[80,640]{1,0:T(8,128)(2,1)S(1)} collective-permute-done((bf16[80,640]{1,0:T(8,128)(2,1)S(1)}, bf16[80,640]{1,0:T(8,128)(2,1)S(1)}, u32[]{:S(2)}, u32[]{:S(2)}) %collective-permute-start.7) | collective-permute-done | bytes 102432 | tf_op jit(solution)/shard_map/ppermute | solution.py:27
  41.9 0.9 project_out.1
  42.9 2.5 %collective-permute-start.13 = (bf16[24,2048]{1,0:T(8,128)(2,1)S(1)}, bf16[24,2048]{1,0:T(8,128)(2,1)S(1)}, u32[]{:S(2)}, u32[]{:S(2)}) collective-permute-start(bf16[24,2048]{1,0:T(8,128)(2,1)S(1)} %get-tuple-element.121), channel_id=1, source_target_pairs={{0,24},{8,16},{16,8},{24,0},{1,25},{9,17},{17,9},{25,1},{2,26},{10... | collective-permute-start | bytes 294920 | tf_op jit(solution)/shard_map/ppermute | solution.py:27
  46.5 3.0 %collective-permute-done.13.refs_3_ = bf16[24,2048]{1,0:T(8,128)(2,1)S(1)} collective-permute-done((bf16[24,2048]{1,0:T(8,128)(2,1)S(1)}, bf16[24,2048]{1,0:T(8,128)(2,1)S(1)}, u32[]{:S(2)}, u32[]{:S(2)}) %collective-permute-start.13) | collective-permute-done | bytes 98336 | tf_op jit(solution)/shard_map/ppermute | solution.py:27
  49.5 1.7 %collective-permute-done.11.refs_1_ = bf16[24,2048]{1,0:T(8,128)(2,1)S(1)} collective-permute-done((bf16[24,2048]{1,0:T(8,128)(2,1)S(1)}, bf16[24,2048]{1,0:T(8,128)(2,1)S(1)}, u32[]{:S(2)}, u32[]{:S(2)}) %collective-permute-start.11) | collective-permute-done | bytes 98336 | tf_op jit(solution)/shard_map/ppermute | solution.py:27
  51.2 1.0 moe_norm.1
  52.2 3.3 %collective-permute-start.15 = (bf16[16,2048]{1,0:T(8,128)(2,1)S(1)}, bf16[16,2048]{1,0:T(8,128)(2,1)S(1)}, u32[]{:S(2)}, u32[]{:S(2)}) collective-permute-start(bf16[16,2048]{1,0:T(8,128)(2,1)S(1)} %get-tuple-element.125), channel_id=1, source_target_pairs={{0,6},{1,7},{2,4},{3,5},{4,2},{5,3},{6,0},{7,1},{8,14},{9,15},{10,... | collective-permute-start | bytes 196616 | tf_op jit(solution)/shard_map/ppermute | solution.py:27
  55.5 1.1 %collective-permute-start.19 = (bf16[16,2048]{1,0:T(8,128)(2,1)S(1)}, bf16[16,2048]{1,0:T(8,128)(2,1)S(1)}, u32[]{:S(2)}, u32[]{:S(2)}) collective-permute-start(bf16[16,2048]{1,0:T(8,128)(2,1)S(1)} %get-tuple-element.125), channel_id=1, source_target_pairs={{0,4},{1,5},{2,6},{3,7},{4,0},{5,1},{6,2},{7,3},{8,12},{9,13},{10,... | collective-permute-start | bytes 196616 | tf_op jit(solution)/shard_map/ppermute | solution.py:27
  56.6 1.5 %collective-permute-start.16 = (f32[24,512]{1,0:T(8,128)S(1)}, f32[24,512]{1,0:T(8,128)S(1)}, u32[]{:S(2)}, u32[]{:S(2)}) collective-permute-start(f32[24,512]{1,0:T(8,128)S(1)} %get-tuple-element.126), channel_id=1, source_target_pairs={{0,8},{8,0},{16,24},{24,16},{1,9},{9,1},{17,25},{25,17},{2,10},{10... | collective-permute-start | bytes 147464 | tf_op jit(solution)/shard_map/ppermute | solution.py:27
  58.1 1.5 %collective-permute-start.17 = (f32[24,512]{1,0:T(8,128)S(1)}, f32[24,512]{1,0:T(8,128)S(1)}, u32[]{:S(2)}, u32[]{:S(2)}) collective-permute-start(f32[24,512]{1,0:T(8,128)S(1)} %get-tuple-element.127), channel_id=1, source_target_pairs={{0,16},{8,24},{16,0},{24,8},{1,17},{9,25},{17,1},{25,9},{2,18},{10... | collective-permute-start | bytes 147464 | tf_op jit(solution)/shard_map/ppermute | solution.py:27
  59.6 0.8 collective-permute-done.18
  60.7 1.5 %collective-permute-done.17.refs_2_ = f32[24,512]{1,0:T(8,128)S(1)} collective-permute-done((f32[24,512]{1,0:T(8,128)S(1)}, f32[24,512]{1,0:T(8,128)S(1)}, u32[]{:S(2)}, u32[]{:S(2)}) %collective-permute-start.17) | collective-permute-done | bytes 49184 | tf_op jit(solution)/shard_map/ppermute | solution.py:27
  62.9 1.6 %collective-permute-start.21 = (bf16[72,2048]{1,0:T(8,128)(2,1)S(1)}, bf16[72,2048]{1,0:T(8,128)(2,1)S(1)}, u32[]{:S(2)}, u32[]{:S(2)}) collective-permute-start(bf16[72,2048]{1,0:T(8,128)(2,1)S(1)} %constant_dynamic-update-slice_fusion.4.refs_3_.refs_0_), channel_id=1, source_target_pairs={{0,16},{8,24},{16,0},{24,8},{1,17},{9,25},{17,1},{25,9},{2,18},{10... | collective-permute-start | bytes 884744 | tf_op jit(solution)/shard_map/ppermute | solution.py:27
  64.5 3.0 %load_experts.1 = (bf16[2,2048,256]{2,1,0:T(8,128)(2,1)S(1)}, bf16[2,2048,256]{2,1,0:T(8,128)(2,1)S(1)}, bf16[2,256,2048]{2,1,0:T(8,128)(2,1)S(1)}) custom-call(bf16[2,2048,256]{2,1,0:T(8,128)(2,1)} %refs_0_.3, bf16[2,2048,256]{2,1,0:T(8,128)(2,1)} %refs_1_.1, bf16[2,256,2048]{2,1,0:T(8,128)(2,1)} %refs_2_.1, ...), custom_call_target="tpu_custom_call" | custom-call | bytes 12582912 | tf_op jit(solution)/shard_map/load_experts/pallas_call | solution.py:55
  67.4 1.6 %collective-permute-done.20.refs_1_ = bf16[72,2048]{1,0:T(8,128)(2,1)S(1)} collective-permute-done((bf16[72,2048]{1,0:T(8,128)(2,1)S(1)}, bf16[72,2048]{1,0:T(8,128)(2,1)S(1)}, u32[]{:S(2)}, u32[]{:S(2)}) %collective-permute-start.20) | collective-permute-done | bytes 294944 | tf_op jit(solution)/shard_map/ppermute | solution.py:27
  69.1 0.8 collective-permute-done.21.refs_2_
  69.9 1.3 %collective-permute-start.23 = (bf16[40,2048]{1,0:T(8,128)(2,1)S(1)}, bf16[40,2048]{1,0:T(8,128)(2,1)S(1)}, u32[]{:S(2)}, u32[]{:S(2)}) collective-permute-start(bf16[40,2048]{1,0:T(8,128)(2,1)S(1)} %slice.7), channel_id=1, source_target_pairs={{0,8},{8,0},{16,24},{24,16},{1,9},{9,1},{17,25},{25,17},{2,10},{10... | collective-permute-start | bytes 491528 | tf_op jit(solution)/shard_map/ppermute | solution.py:27
  71.2 1.5 %collective-permute-start.22 = (bf16[32,2048]{1,0:T(8,128)(2,1)S(1)}, bf16[32,2048]{1,0:T(8,128)(2,1)S(1)}, u32[]{:S(2)}, u32[]{:S(2)}) collective-permute-start(bf16[32,2048]{1,0:T(8,128)(2,1)S(1)} %slice.6), channel_id=1, source_target_pairs={{0,16},{8,24},{16,0},{24,8},{1,17},{9,25},{17,1},{25,9},{2,18},{10... | collective-permute-start | bytes 393224 | tf_op jit(solution)/shard_map/ppermute | solution.py:27
  72.8 4.9 %experts_early.1 = (bf16[208,512]{1,0:T(8,128)(2,1)S(1)}, bf16[208,512]{1,0:T(8,128)(2,1)S(1)}, bf16[208,512]{1,0:T(8,128)(2,1)S(1)}, bf16[208,512]{1,0:T(8,128)(2,1)S(1)}) custom-call(s32[2]{0:T(128)S(1)} %pad_add_fusion.scalar_ref, bf16[72,2048]{1,0:T(8,128)(2,1)S(1)} %constant_dynamic-update-slice_fusion.4.refs_3_.refs_0_, ...), custom_call_target="tpu_custom_call" | custom-call | flops 1358954496 | bytes 12582912 | tf_op jit(solution)/shard_map/experts_early/pallas_call | solution.py:55
  77.7 1.2 %collective-permute-start.24 = (bf16[208,512]{1,0:T(8,128)(2,1)S(1)}, bf16[208,512]{1,0:T(8,128)(2,1)S(1)}, u32[]{:S(2)}, u32[]{:S(2)}) collective-permute-start(bf16[208,512]{1,0:T(8,128)(2,1)S(1)} %get-tuple-element.146), channel_id=1, source_target_pairs={{0,8},{8,0},{16,24},{24,16},{1,9},{9,1},{17,25},{25,17},{2,10},{10... | collective-permute-start | bytes 638984 | tf_op jit(solution)/shard_map/ppermute | solution.py:27
  79.2 2.1 %collective-permute-start.26 = (bf16[208,512]{1,0:T(8,128)(2,1)S(1)}, bf16[208,512]{1,0:T(8,128)(2,1)S(1)}, u32[]{:S(2)}, u32[]{:S(2)}) collective-permute-start(bf16[208,512]{1,0:T(8,128)(2,1)S(1)} %get-tuple-element.149), channel_id=1, source_target_pairs={{0,24},{8,16},{16,8},{24,0},{1,25},{9,17},{17,9},{25,1},{2,26},{10... | collective-permute-start | bytes 638984 | tf_op jit(solution)/shard_map/ppermute | solution.py:27
  81.3 4.0 %experts_late.1 = (bf16[72,512]{1,0:T(8,128)(2,1)S(1)}, bf16[72,512]{1,0:T(8,128)(2,1)S(1)}, bf16[72,512]{1,0:T(8,128)(2,1)S(1)}, bf16[72,512]{1,0:T(8,128)(2,1)S(1)}) custom-call(s32[2]{0:T(128)S(1)} %pad_add_fusion.scalar_ref, bf16[72,2048]{1,0:T(8,128)(2,1)S(1)} %pad_maximum_fusion.refs_0_, ...), custom_call_target="tpu_custom_call" | custom-call | flops 452984832 | bytes 12582912 | tf_op jit(solution)/shard_map/experts_late/pallas_call | solution.py:55
  85.3 0.6 collective-permute-start.28
  85.9 2.0 %collective-permute-start.29 = (bf16[72,512]{1,0:T(8,128)(2,1)S(1)}, bf16[72,512]{1,0:T(8,128)(2,1)S(1)}, u32[]{:S(2)}, u32[]{:S(2)}) collective-permute-start(bf16[72,512]{1,0:T(8,128)(2,1)S(1)} %get-tuple-element.153), channel_id=1, source_target_pairs={{0,24},{8,16},{16,8},{24,0},{1,25},{9,17},{17,9},{25,1},{2,26},{10... | collective-permute-start | bytes 221192 | tf_op jit(solution)/shard_map/ppermute | solution.py:27
  87.9 0.9 collective-permute-start.27
  88.9 0.9 collective-permute-done.28.refs_6_
  89.7 1.5 %collective-permute-done.29.refs_7_ = bf16[72,512]{1,0:T(8,128)(2,1)S(1)} collective-permute-done((bf16[72,512]{1,0:T(8,128)(2,1)S(1)}, bf16[72,512]{1,0:T(8,128)(2,1)S(1)}, u32[]{:S(2)}, u32[]{:S(2)}) %collective-permute-start.29) | collective-permute-done | bytes 73760 | tf_op jit(solution)/shard_map/ppermute | solution.py:27
  91.2 1.1 %collective-permute-done.27.refs_5_ = bf16[72,512]{1,0:T(8,128)(2,1)S(1)} collective-permute-done((bf16[72,512]{1,0:T(8,128)(2,1)S(1)}, bf16[72,512]{1,0:T(8,128)(2,1)S(1)}, u32[]{:S(2)}, u32[]{:S(2)}) %collective-permute-start.27) | collective-permute-done | bytes 73760 | tf_op jit(solution)/shard_map/ppermute | solution.py:27
  92.5 1.3 %collective-permute-start.31 = (bf16[80,512]{1,0:T(8,128)(2,1)S(1)}, bf16[80,512]{1,0:T(8,128)(2,1)S(1)}, u32[]{:S(2)}, u32[]{:S(2)}) collective-permute-start(bf16[80,512]{1,0:T(8,128)(2,1)S(1)} %get-tuple-element.161), channel_id=1, source_target_pairs={{0,2},{1,3},{2,0},{3,1},{4,6},{5,7},{6,4},{7,5},{8,10},{9,11},{10,... | collective-permute-start | bytes 245768 | tf_op jit(solution)/shard_map/ppermute | solution.py:27
  93.7 2.4 %collective-permute-start.32 = (bf16[80,512]{1,0:T(8,128)(2,1)S(1)}, bf16[80,512]{1,0:T(8,128)(2,1)S(1)}, u32[]{:S(2)}, u32[]{:S(2)}) collective-permute-start(bf16[80,512]{1,0:T(8,128)(2,1)S(1)} %get-tuple-element.162), channel_id=1, source_target_pairs={{0,4},{1,5},{2,6},{3,7},{4,0},{5,1},{6,2},{7,3},{8,12},{9,13},{10,... | collective-permute-start | bytes 245768 | tf_op jit(solution)/shard_map/ppermute | solution.py:27
  96.1 0.8 collective-permute-start.33
  97.0 0.9 collective-permute-start.30
  97.9 0.6 copy.25
  98.5 3.4 %collective-permute-done.30.refs_3_ = f32[24,512]{1,0:T(8,128)S(1)} collective-permute-done((f32[24,512]{1,0:T(8,128)S(1)}, f32[24,512]{1,0:T(8,128)S(1)}, u32[]{:S(2)}, u32[]{:S(2)}) %collective-permute-start.30) | collective-permute-done | bytes 49184 | tf_op jit(solution)/shard_map/ppermute | solution.py:27
  102.3 0.7 final.1
  (62 shorter events, 6.0 us)
Async XLA Ops:
  0.6 18.0 %collective-permute-start.4 = (bf16[2,2048,256]{2,1,0:T(8,128)(2,1)}, bf16[2,2048,256]{2,1,0:T(8,128)(2,1)S(1)}, u32[]{:S(2)}, u32[]{:S(2)}) collective-permute-start(bf16[2,2048,256]{2,1,0:T(8,128)(2,1)} %refs_0_.3), channel_id=1, source_target_pairs={{0,1},{1,0},{2,3},{3,2},{4,5},{5,4},{6,7},{7,6},{8,9},{9,8},{10,11... | collective-permute-start | bytes 6291464 | tf_op jit(solution)/shard_map/ppermute | solution.py:27
  4.7 9.0 %collective-permute-start = (bf16[64,640]{1,0:T(8,128)(2,1)S(1)}, bf16[64,640]{1,0:T(8,128)(2,1)S(1)}, u32[]{:S(2)}, u32[]{:S(2)}) collective-permute-start(bf16[64,640]{1,0:T(8,128)(2,1)S(1)} %get-tuple-element.90), channel_id=1, source_target_pairs={{0,2},{1,3},{2,0},{3,1},{4,6},{5,7},{6,4},{7,5},{8,10},{9,11},{10,... | collective-permute-start | bytes 245768 | tf_op jit(solution)/shard_map/ppermute | solution.py:27
  7.3 9.5 %collective-permute-start.1 = (bf16[64,640]{1,0:T(8,128)(2,1)S(1)}, bf16[64,640]{1,0:T(8,128)(2,1)S(1)}, u32[]{:S(2)}, u32[]{:S(2)}) collective-permute-start(bf16[64,640]{1,0:T(8,128)(2,1)S(1)} %get-tuple-element.90), channel_id=1, source_target_pairs={{0,4},{1,5},{2,6},{3,7},{4,0},{5,1},{6,2},{7,3},{8,12},{9,13},{10,... | collective-permute-start | bytes 245768 | tf_op jit(solution)/shard_map/ppermute | solution.py:27
  9.9 7.0 %collective-permute-start.2 = (bf16[64,640]{1,0:T(8,128)(2,1)S(1)}, bf16[64,640]{1,0:T(8,128)(2,1)S(1)}, u32[]{:S(2)}, u32[]{:S(2)}) collective-permute-start(bf16[64,640]{1,0:T(8,128)(2,1)S(1)} %get-tuple-element.90), channel_id=1, source_target_pairs={{0,6},{1,7},{2,4},{3,5},{4,2},{5,3},{6,0},{7,1},{8,14},{9,15},{10,... | collective-permute-start | bytes 245768 | tf_op jit(solution)/shard_map/ppermute | solution.py:27
  9.9 8.7 %copy-start.1 = (s32[13]{0:T(128)S(1)}, s32[13]{0:T(128)}, u32[]{:S(2)}) copy-start(s32[13]{0:T(128)} %lens_ref.1) | copy-start | bytes 160
  9.9 8.7 %copy-start.2 = (s32[8]{0:T(128)S(1)}, s32[8]{0:T(128)}, u32[]{:S(2)}) copy-start(s32[8]{0:T(128)} %owner_ref.1) | copy-start | bytes 100
  9.9 8.7 %copy-start.3 = (s32[8]{0:T(128)S(1)}, s32[8]{0:T(128)}, u32[]{:S(2)}) copy-start(s32[8]{0:T(128)} %slot_ref.1) | copy-start | bytes 100
  16.9 1.7 %collective-permute-start.3 = (bf16[256,640]{1,0:T(8,128)(2,1)S(1)}, bf16[256,640]{1,0:T(8,128)(2,1)S(1)}, u32[]{:S(2)}, u32[]{:S(2)}) collective-permute-start(bf16[256,640]{1,0:T(8,128)(2,1)S(1)} %constant_dynamic-update-slice_fusion.query_a.refs_3_.refs_1_), channel_id=1, source_target_pairs={{0,1},{1,0},{2,3},{3,2},{4,5},{5,4},{6,7},{7,6},{8,9},{9,8},{10,11... | collective-permute-start | bytes 983048 | tf_op jit(solution)/shard_map/ppermute | solution.py:27
  29.4 2.0 %collective-permute-start.5 = (f32[520,256]{1,0:T(8,128)S(1)}, f32[520,256]{1,0:T(8,128)S(1)}, u32[]{:S(2)}, u32[]{:S(2)}) collective-permute-start(f32[520,256]{1,0:T(8,128)S(1)} %get-tuple-element.101), channel_id=1, source_target_pairs={{0,1},{1,0},{2,3},{3,2},{4,5},{5,4},{6,7},{7,6},{8,9},{9,8},{10,11... | collective-permute-start | bytes 1597448 | tf_op jit(solution)/shard_map/ppermute | solution.py:27
  29.5 2.0 %collective-permute-start.6 = (f32[16,640]{1,0:T(8,128)S(1)}, f32[16,640]{1,0:T(8,128)S(1)}, u32[]{:S(2)}, u32[]{:S(2)}) collective-permute-start(f32[16,640]{1,0:T(8,128)S(1)} %get-tuple-element.102.dec_mine), channel_id=1, source_target_pairs={{0,1},{1,0},{2,3},{3,2},{4,5},{5,4},{6,7},{7,6},{8,9},{9,8},{10,11... | collective-permute-start | bytes 122888 | tf_op jit(solution)/shard_map/ppermute | solution.py:27
  31.9 7.8 %collective-permute-start.10 = (bf16[2,2048,256]{2,1,0:T(8,128)(2,1)}, bf16[2,2048,256]{2,1,0:T(8,128)(2,1)}, u32[]{:S(2)}, u32[]{:S(2)}) collective-permute-start(bf16[2,2048,256]{2,1,0:T(8,128)(2,1)} %refs_1_.1), channel_id=1, source_target_pairs={{0,1},{1,0},{2,3},{3,2},{4,5},{5,4},{6,7},{7,6},{8,9},{9,8},{10,11... | collective-permute-start | bytes 6291464 | tf_op jit(solution)/shard_map/ppermute | solution.py:27
  32.1 7.6 %collective-permute-start.9 = (bf16[80,640]{1,0:T(8,128)(2,1)S(1)}, bf16[80,640]{1,0:T(8,128)(2,1)S(1)}, u32[]{:S(2)}, u32[]{:S(2)}) collective-permute-start(bf16[80,640]{1,0:T(8,128)(2,1)S(1)} %get-tuple-element.110), channel_id=1, source_target_pairs={{0,6},{1,7},{2,4},{3,5},{4,2},{5,3},{6,0},{7,1},{8,14},{9,15},{10,... | collective-permute-start | bytes 307208 | tf_op jit(solution)/shard_map/ppermute | solution.py:27
  32.3 9.1 %collective-permute-start.7 = (bf16[80,640]{1,0:T(8,128)(2,1)S(1)}, bf16[80,640]{1,0:T(8,128)(2,1)S(1)}, u32[]{:S(2)}, u32[]{:S(2)}) collective-permute-start(bf16[80,640]{1,0:T(8,128)(2,1)S(1)} %get-tuple-element.108), channel_id=1, source_target_pairs={{0,2},{1,3},{2,0},{3,1},{4,6},{5,7},{6,4},{7,5},{8,10},{9,11},{10,... | collective-permute-start | bytes 307208 | tf_op jit(solution)/shard_map/ppermute | solution.py:27
  33.1 8.8 %collective-permute-start.8 = (bf16[80,640]{1,0:T(8,128)(2,1)S(1)}, bf16[80,640]{1,0:T(8,128)(2,1)S(1)}, u32[]{:S(2)}, u32[]{:S(2)}) collective-permute-start(bf16[80,640]{1,0:T(8,128)(2,1)S(1)} %get-tuple-element.109), channel_id=1, source_target_pairs={{0,4},{1,5},{2,6},{3,7},{4,0},{5,1},{6,2},{7,3},{8,12},{9,13},{10,... | collective-permute-start | bytes 307208 | tf_op jit(solution)/shard_map/ppermute | solution.py:27
  38.1 4.8 %copy-start.4 = (bf16[2,256,2048]{2,1,0:T(8,128)(2,1)S(1)}, bf16[2,256,2048]{2,1,0:T(8,128)(2,1)}, u32[]{:S(2)}) copy-start(bf16[2,256,2048]{2,1,0:T(8,128)(2,1)} %refs_2_.1) | copy-start | bytes 6291460
  38.1 13.1 %copy-start = (f32[2048]{0:T(1024)S(1)}, f32[2048]{0:T(1024)}, u32[]{:S(2)}) copy-start(f32[2048]{0:T(1024)} %param.32) | copy-start | bytes 24580
  42.8 6.6 %collective-permute-start.14 = (bf16[2,256,2048]{2,1,0:T(8,128)(2,1)S(1)}, bf16[2,256,2048]{2,1,0:T(8,128)(2,1)S(1)}, u32[]{:S(2)}, u32[]{:S(2)}) collective-permute-start(bf16[2,256,2048]{2,1,0:T(8,128)(2,1)S(1)} %copy-done.4), channel_id=1, source_target_pairs={{0,1},{1,0},{2,3},{3,2},{4,5},{5,4},{6,7},{7,6},{8,9},{9,8},{10,11... | collective-permute-start | bytes 6291464 | tf_op jit(solution)/shard_map/ppermute | solution.py:27
  42.9 6.6 %collective-permute-start.13 = (bf16[24,2048]{1,0:T(8,128)(2,1)S(1)}, bf16[24,2048]{1,0:T(8,128)(2,1)S(1)}, u32[]{:S(2)}, u32[]{:S(2)}) collective-permute-start(bf16[24,2048]{1,0:T(8,128)(2,1)S(1)} %get-tuple-element.121), channel_id=1, source_target_pairs={{0,24},{8,16},{16,8},{24,0},{1,25},{9,17},{17,9},{25,1},{2,26},{10... | collective-permute-start | bytes 294920 | tf_op jit(solution)/shard_map/ppermute | solution.py:27
  45.4 5.8 %collective-permute-start.11 = (bf16[24,2048]{1,0:T(8,128)(2,1)S(1)}, bf16[24,2048]{1,0:T(8,128)(2,1)S(1)}, u32[]{:S(2)}, u32[]{:S(2)}) collective-permute-start(bf16[24,2048]{1,0:T(8,128)(2,1)S(1)} %get-tuple-element.119), channel_id=1, source_target_pairs={{0,8},{8,0},{16,24},{24,16},{1,9},{9,1},{17,25},{25,17},{2,10},{10... | collective-permute-start | bytes 294920 | tf_op jit(solution)/shard_map/ppermute | solution.py:27
  46.0 5.2 %collective-permute-start.12 = (bf16[24,2048]{1,0:T(8,128)(2,1)S(1)}, bf16[24,2048]{1,0:T(8,128)(2,1)S(1)}, u32[]{:S(2)}, u32[]{:S(2)}) collective-permute-start(bf16[24,2048]{1,0:T(8,128)(2,1)S(1)} %get-tuple-element.120), channel_id=1, source_target_pairs={{0,16},{8,24},{16,0},{24,8},{1,17},{9,25},{17,1},{25,9},{2,18},{10... | collective-permute-start | bytes 294920 | tf_op jit(solution)/shard_map/ppermute | solution.py:27
  52.2 10.1 %collective-permute-start.15 = (bf16[16,2048]{1,0:T(8,128)(2,1)S(1)}, bf16[16,2048]{1,0:T(8,128)(2,1)S(1)}, u32[]{:S(2)}, u32[]{:S(2)}) collective-permute-start(bf16[16,2048]{1,0:T(8,128)(2,1)S(1)} %get-tuple-element.125), channel_id=1, source_target_pairs={{0,6},{1,7},{2,4},{3,5},{4,2},{5,3},{6,0},{7,1},{8,14},{9,15},{10,... | collective-permute-start | bytes 196616 | tf_op jit(solution)/shard_map/ppermute | solution.py:27
  55.5 4.8 %collective-permute-start.18 = (bf16[16,2048]{1,0:T(8,128)(2,1)S(1)}, bf16[16,2048]{1,0:T(8,128)(2,1)S(1)}, u32[]{:S(2)}, u32[]{:S(2)}) collective-permute-start(bf16[16,2048]{1,0:T(8,128)(2,1)S(1)} %get-tuple-element.125), channel_id=1, source_target_pairs={{0,2},{1,3},{2,0},{3,1},{4,6},{5,7},{6,4},{7,5},{8,10},{9,11},{10,... | collective-permute-start | bytes 196616 | tf_op jit(solution)/shard_map/ppermute | solution.py:27
  55.5 6.7 %collective-permute-start.19 = (bf16[16,2048]{1,0:T(8,128)(2,1)S(1)}, bf16[16,2048]{1,0:T(8,128)(2,1)S(1)}, u32[]{:S(2)}, u32[]{:S(2)}) collective-permute-start(bf16[16,2048]{1,0:T(8,128)(2,1)S(1)} %get-tuple-element.125), channel_id=1, source_target_pairs={{0,4},{1,5},{2,6},{3,7},{4,0},{5,1},{6,2},{7,3},{8,12},{9,13},{10,... | collective-permute-start | bytes 196616 | tf_op jit(solution)/shard_map/ppermute | solution.py:27
  56.6 4.1 %collective-permute-start.16 = (f32[24,512]{1,0:T(8,128)S(1)}, f32[24,512]{1,0:T(8,128)S(1)}, u32[]{:S(2)}, u32[]{:S(2)}) collective-permute-start(f32[24,512]{1,0:T(8,128)S(1)} %get-tuple-element.126), channel_id=1, source_target_pairs={{0,8},{8,0},{16,24},{24,16},{1,9},{9,1},{17,25},{25,17},{2,10},{10... | collective-permute-start | bytes 147464 | tf_op jit(solution)/shard_map/ppermute | solution.py:27
  58.1 4.1 %collective-permute-start.17 = (f32[24,512]{1,0:T(8,128)S(1)}, f32[24,512]{1,0:T(8,128)S(1)}, u32[]{:S(2)}, u32[]{:S(2)}) collective-permute-start(f32[24,512]{1,0:T(8,128)S(1)} %get-tuple-element.127), channel_id=1, source_target_pairs={{0,16},{8,24},{16,0},{24,8},{1,17},{9,25},{17,1},{25,9},{2,18},{10... | collective-permute-start | bytes 147464 | tf_op jit(solution)/shard_map/ppermute | solution.py:27
  62.3 6.8 %collective-permute-start.20 = (bf16[72,2048]{1,0:T(8,128)(2,1)S(1)}, bf16[72,2048]{1,0:T(8,128)(2,1)S(1)}, u32[]{:S(2)}, u32[]{:S(2)}) collective-permute-start(bf16[72,2048]{1,0:T(8,128)(2,1)S(1)} %constant_dynamic-update-slice_fusion.4.refs_3_.refs_0_), channel_id=1, source_target_pairs={{0,8},{8,0},{16,24},{24,16},{1,9},{9,1},{17,25},{25,17},{2,10},{10... | collective-permute-start | bytes 884744 | tf_op jit(solution)/shard_map/ppermute | solution.py:27
  62.9 7.0 %collective-permute-start.21 = (bf16[72,2048]{1,0:T(8,128)(2,1)S(1)}, bf16[72,2048]{1,0:T(8,128)(2,1)S(1)}, u32[]{:S(2)}, u32[]{:S(2)}) collective-permute-start(bf16[72,2048]{1,0:T(8,128)(2,1)S(1)} %constant_dynamic-update-slice_fusion.4.refs_3_.refs_0_), channel_id=1, source_target_pairs={{0,16},{8,24},{16,0},{24,8},{1,17},{9,25},{17,1},{25,9},{2,18},{10... | collective-permute-start | bytes 884744 | tf_op jit(solution)/shard_map/ppermute | solution.py:27
  69.9 11.4 %collective-permute-start.23 = (bf16[40,2048]{1,0:T(8,128)(2,1)S(1)}, bf16[40,2048]{1,0:T(8,128)(2,1)S(1)}, u32[]{:S(2)}, u32[]{:S(2)}) collective-permute-start(bf16[40,2048]{1,0:T(8,128)(2,1)S(1)} %slice.7), channel_id=1, source_target_pairs={{0,8},{8,0},{16,24},{24,16},{1,9},{9,1},{17,25},{25,17},{2,10},{10... | collective-permute-start | bytes 491528 | tf_op jit(solution)/shard_map/ppermute | solution.py:27
  71.2 10.1 %collective-permute-start.22 = (bf16[32,2048]{1,0:T(8,128)(2,1)S(1)}, bf16[32,2048]{1,0:T(8,128)(2,1)S(1)}, u32[]{:S(2)}, u32[]{:S(2)}) collective-permute-start(bf16[32,2048]{1,0:T(8,128)(2,1)S(1)} %slice.6), channel_id=1, source_target_pairs={{0,16},{8,24},{16,0},{24,8},{1,17},{9,25},{17,1},{25,9},{2,18},{10... | collective-permute-start | bytes 393224 | tf_op jit(solution)/shard_map/ppermute | solution.py:27
  77.7 10.2 %collective-permute-start.24 = (bf16[208,512]{1,0:T(8,128)(2,1)S(1)}, bf16[208,512]{1,0:T(8,128)(2,1)S(1)}, u32[]{:S(2)}, u32[]{:S(2)}) collective-permute-start(bf16[208,512]{1,0:T(8,128)(2,1)S(1)} %get-tuple-element.146), channel_id=1, source_target_pairs={{0,8},{8,0},{16,24},{24,16},{1,9},{9,1},{17,25},{25,17},{2,10},{10... | collective-permute-start | bytes 638984 | tf_op jit(solution)/shard_map/ppermute | solution.py:27
  78.9 10.0 %collective-permute-start.25 = (bf16[208,512]{1,0:T(8,128)(2,1)S(1)}, bf16[208,512]{1,0:T(8,128)(2,1)S(1)}, u32[]{:S(2)}, u32[]{:S(2)}) collective-permute-start(bf16[208,512]{1,0:T(8,128)(2,1)S(1)} %get-tuple-element.148), channel_id=1, source_target_pairs={{0,16},{8,24},{16,0},{24,8},{1,17},{9,25},{17,1},{25,9},{2,18},{10... | collective-permute-start | bytes 638984 | tf_op jit(solution)/shard_map/ppermute | solution.py:27
  79.2 9.7 %collective-permute-start.26 = (bf16[208,512]{1,0:T(8,128)(2,1)S(1)}, bf16[208,512]{1,0:T(8,128)(2,1)S(1)}, u32[]{:S(2)}, u32[]{:S(2)}) collective-permute-start(bf16[208,512]{1,0:T(8,128)(2,1)S(1)} %get-tuple-element.149), channel_id=1, source_target_pairs={{0,24},{8,16},{16,8},{24,0},{1,25},{9,17},{17,9},{25,1},{2,26},{10... | collective-permute-start | bytes 638984 | tf_op jit(solution)/shard_map/ppermute | solution.py:27
  85.3 4.4 %collective-permute-start.28 = (bf16[72,512]{1,0:T(8,128)(2,1)S(1)}, bf16[72,512]{1,0:T(8,128)(2,1)S(1)}, u32[]{:S(2)}, u32[]{:S(2)}) collective-permute-start(bf16[72,512]{1,0:T(8,128)(2,1)S(1)} %get-tuple-element.152), channel_id=1, source_target_pairs={{0,16},{8,24},{16,0},{24,8},{1,17},{9,25},{17,1},{25,9},{2,18},{10... | collective-permute-start | bytes 221192 | tf_op jit(solution)/shard_map/ppermute | solution.py:27
  85.9 5.3 %collective-permute-start.29 = (bf16[72,512]{1,0:T(8,128)(2,1)S(1)}, bf16[72,512]{1,0:T(8,128)(2,1)S(1)}, u32[]{:S(2)}, u32[]{:S(2)}) collective-permute-start(bf16[72,512]{1,0:T(8,128)(2,1)S(1)} %get-tuple-element.153), channel_id=1, source_target_pairs={{0,24},{8,16},{16,8},{24,0},{1,25},{9,17},{17,9},{25,1},{2,26},{10... | collective-permute-start | bytes 221192 | tf_op jit(solution)/shard_map/ppermute | solution.py:27
  87.9 4.4 %collective-permute-start.27 = (bf16[72,512]{1,0:T(8,128)(2,1)S(1)}, bf16[72,512]{1,0:T(8,128)(2,1)S(1)}, u32[]{:S(2)}, u32[]{:S(2)}) collective-permute-start(bf16[72,512]{1,0:T(8,128)(2,1)S(1)} %get-tuple-element.151), channel_id=1, source_target_pairs={{0,8},{8,0},{16,24},{24,16},{1,9},{9,1},{17,25},{25,17},{2,10},{10... | collective-permute-start | bytes 221192 | tf_op jit(solution)/shard_map/ppermute | solution.py:27
  92.5 9.4 %collective-permute-start.31 = (bf16[80,512]{1,0:T(8,128)(2,1)S(1)}, bf16[80,512]{1,0:T(8,128)(2,1)S(1)}, u32[]{:S(2)}, u32[]{:S(2)}) collective-permute-start(bf16[80,512]{1,0:T(8,128)(2,1)S(1)} %get-tuple-element.161), channel_id=1, source_target_pairs={{0,2},{1,3},{2,0},{3,1},{4,6},{5,7},{6,4},{7,5},{8,10},{9,11},{10,... | collective-permute-start | bytes 245768 | tf_op jit(solution)/shard_map/ppermute | solution.py:27
  93.7 8.2 %collective-permute-start.32 = (bf16[80,512]{1,0:T(8,128)(2,1)S(1)}, bf16[80,512]{1,0:T(8,128)(2,1)S(1)}, u32[]{:S(2)}, u32[]{:S(2)}) collective-permute-start(bf16[80,512]{1,0:T(8,128)(2,1)S(1)} %get-tuple-element.162), channel_id=1, source_target_pairs={{0,4},{1,5},{2,6},{3,7},{4,0},{5,1},{6,2},{7,3},{8,12},{9,13},{10,... | collective-permute-start | bytes 245768 | tf_op jit(solution)/shard_map/ppermute | solution.py:27
  96.1 6.2 %collective-permute-start.33 = (bf16[80,512]{1,0:T(8,128)(2,1)S(1)}, bf16[80,512]{1,0:T(8,128)(2,1)S(1)}, u32[]{:S(2)}, u32[]{:S(2)}) collective-permute-start(bf16[80,512]{1,0:T(8,128)(2,1)S(1)} %get-tuple-element.163), channel_id=1, source_target_pairs={{0,6},{1,7},{2,4},{3,5},{4,2},{5,3},{6,0},{7,1},{8,14},{9,15},{10,... | collective-permute-start | bytes 245768 | tf_op jit(solution)/shard_map/ppermute | solution.py:27
  97.0 5.0 %collective-permute-start.30 = (f32[24,512]{1,0:T(8,128)S(1)}, f32[24,512]{1,0:T(8,128)S(1)}, u32[]{:S(2)}, u32[]{:S(2)}) collective-permute-start(f32[24,512]{1,0:T(8,128)S(1)} %get-tuple-element.159), channel_id=1, source_target_pairs={{0,24},{8,16},{16,8},{24,0},{1,25},{9,17},{17,9},{25,1},{2,26},{10... | collective-permute-start | bytes 147464 | tf_op jit(solution)/shard_map/ppermute | solution.py:27
